TPU v7x, 32 devices: a whole 2x2x4 slice. The times are simulated.
32 devices in a mesh: seq: 2 (over x), tp: 4 (over z), dp: 4 (over y, core).
Axes of the slice: x: 2, y: 2, z: 4, core: 2. Of those that a mesh axis runs over, the one named last changes fastest.
Arguments:
- clip_tokens: bfloat16 [2048, 8192], P('tp', ('dp', 'seq')), parts along dimension 1, may hold values from -40 to 40, as said below
- conv_taps: float32 [27, 2048], P(None, 'tp'), may hold values from -3 to 3
- norm_gain: float32 [2048], replicated, may hold values from 0.25 to 1.75
- qkv_weight: bfloat16 [3, 2048, 2048], P(None, 'tp'), may hold values from -1 to 1
- out_weight: bfloat16 [2048, 2048], P('tp'), may hold values from -2 to 2
- tile_mask: int32 [16, 16], replicated, may hold values from 0 to 1, as said below
- stripe_order: int32 [16], replicated, may hold values from 0 to 15, as said below
Outputs:
- attended: bfloat16 [2048, 8192], P('tp', ('dp', 'seq')), parts along dimension 1
There are 4 independent parts, one for each index of `dp`. A program takes and returns all parts, laid end to end along the dimension named above; an argument that names none is the same for every part. Nothing has to cross between parts.
Inputs may be any that keep to these rules, and one draw needn't show every extreme that they name: `clip_tokens`: the clip's values. tile_mask[i, j] is 1 where tiles i and j lie in the same frame, 0 where tile j lies in a later frame than tile i, and 0 or 1 where tile j lies in an earlier frame; a frame is 4 consecutive tiles. `stripe_order`: A permutation of the 16 tiles. Each aligned block of 8 banded positions holds exactly 4 tiles of each aligned block of 8 tile numbers.
All inputs are finite; a program needn't handle non-finite values.
Results may differ from a plain program's by a relative error of at most 0.024.
Values may be sent and summed in bfloat16 or wider, within the bound.
No kernel may reach another device: no remote copies, remote signals or barrier semaphores. Data moves between devices by JAX's collectives and lax.ppermute only.
A program may use at most 64 MiB of HBM per device.

v0:
```python
import functools
import math

import jax
import jax.numpy as jnp
from jax import lax
from jax.experimental import pallas as pl
from jax.experimental.pallas import tpu as pltpu
from jax.sharding import PartitionSpec as P


HEAD = 128
TILE = 128
FH = 16
FW = 32
FRAME = FH * FW
TAPS = 27


EPSILON = 1e-06
MASKED_SCORE = -1e30
LOG2E = math.log2(math.e)

VMEM_LIMIT = 20 * 1024 * 1024
VMEM_WHOLE = 60 * 1024 * 1024


def params(limit=VMEM_LIMIT):
    return pltpu.CompilerParams(vmem_limit_bytes=limit)


def column_shifts(frame, lane):
    column = lane % FW
    left = jnp.where(column > 0, pltpu.roll(frame, 1, 1), 0.0)
    right = jnp.where(column < FW - 1, pltpu.roll(frame, FRAME - 1, 1), 0.0)
    return (left, frame, right)


def row_sum(rows, lane):
    above = jnp.where(lane >= FW, pltpu.roll(rows[0], FW, 1), 0.0)
    below = jnp.where(lane < FRAME - FW, pltpu.roll(rows[2], FRAME - FW, 1), 0.0)
    return rows[1] + above + below


def taps_applied(pairs, taps, lane):
    rows = []
    for row_off in range(3):
        total = None
        for time_off, shifts in pairs:
            for col_off in range(3):
                tap = time_off * 9 + row_off * 3 + col_off
                term = taps[:, tap : tap + 1] * shifts[col_off]
                total = term if total is None else total + term
        rows.append(total)
    return row_sum(rows, lane)


def pack_slots(order_ref, slots_ref, seq_here, tiles_dev, positions):
    half = tiles_dev // 2
    kept = jnp.int32(0)
    sent = jnp.int32(half)
    for position in range(positions):
        tile = order_ref[position]
        mine = tile // tiles_dev == seq_here
        stays = jnp.int32(position // tiles_dev) == seq_here
        slot = jnp.where(stays, kept, sent)

        @pl.when(mine)
        def _(tile=tile, slot=slot):
            slots_ref[tile - seq_here * tiles_dev] = slot

        step = mine.astype(jnp.int32)
        kept = kept + jnp.where(stays, step, 0)
        sent = sent + jnp.where(stays, 0, step)


def conv_body(with_before, seq_ref, order_ref, *refs):
    if with_before:
        tokens_ref, taps_ref, before_ref, part_ref, keep_ref, send_ref, slots_ref, taps_scr, packed = refs
    else:
        tokens_ref, taps_ref, part_ref, keep_ref, send_ref, slots_ref, taps_scr, packed = refs
    channels, tokens = tokens_ref.shape
    tiles_dev = tokens // TILE
    seq_here = seq_ref[0]

    @pl.when(pl.program_id(0) == 0)
    def _():
        pack_slots(order_ref, slots_ref, seq_here, tiles_dev, order_ref.shape[0])

    taps_scr[:, :TAPS] = taps_ref[...].T
    group = 16
    lane = lax.broadcasted_iota(jnp.int32, (group, FRAME), 1)

    def advance(step, carry):
        rows = pl.ds(pl.multiple_of(step * group, group), group)
        taps = taps_scr[rows, :]
        if with_before:
            old = [
                column_shifts(before_ref[rows, f * FRAME : (f + 1) * FRAME].astype(jnp.float32), lane)
                for f in range(2)
            ]
            sums = [
                part_ref[rows, :FRAME] + taps_applied([(0, old[0]), (1, old[1])], taps, lane),
                part_ref[rows, FRAME:] + taps_applied([(0, old[1])], taps, lane),
            ]
        else:
            now = [
                column_shifts(tokens_ref[rows, f * FRAME : (f + 1) * FRAME].astype(jnp.float32), lane)
                for f in range(2)
            ]
            sums = [
                now[0][1] + taps_applied([(2, now[0])], taps, lane),
                now[1][1] + taps_applied([(1, now[0]), (2, now[1])], taps, lane),
            ]
            part_ref[rows, :FRAME] = sums[0]
            part_ref[rows, FRAME:] = sums[1]
        for tile in range(tiles_dev):
            frame, spot = divmod(tile * TILE, FRAME)
            place = pl.ds(pl.multiple_of(slots_ref[tile] * TILE, TILE), TILE)
            packed[rows, place] = sums[frame][:, spot : spot + TILE].astype(jnp.bfloat16)
        return carry

    lax.fori_loop(0, channels // group, advance, 0)
    keep_ref[...] = packed[:, : tokens // 2]
    send_ref[...] = packed[:, tokens // 2 :]


def conv_call(seq_here, stripe_order, tokens, conv_taps, before=None, part=None):
    channels, count = tokens.shape
    block = 128
    wide = pl.BlockSpec((block, count), lambda i, *_: (i, 0))
    slim = pl.BlockSpec((block, count // 2), lambda i, *_: (i, 0))
    taps_spec = pl.BlockSpec((TAPS, block), lambda i, *_: (0, i))
    packed_shape = jax.ShapeDtypeStruct((channels, count // 2), jnp.bfloat16)
    with_before = before is not None
    extra_in, extra_args, out_specs, out_shape = [], [], [slim, slim], [packed_shape, packed_shape]
    if with_before:
        extra_in, extra_args = [wide, wide], [before, part]
    else:
        out_specs = [wide] + out_specs
        out_shape = [jax.ShapeDtypeStruct((channels, count), jnp.float32)] + out_shape
    return pl.pallas_call(
        functools.partial(conv_body, with_before),
        grid_spec=pltpu.PrefetchScalarGridSpec(
            num_scalar_prefetch=2,
            grid=(channels // block,),
            in_specs=[wide, taps_spec] + extra_in,
            out_specs=out_specs,
            scratch_shapes=[
                pltpu.SMEM((count // TILE,), jnp.int32),
                pltpu.VMEM((block, 128), jnp.float32),
                pltpu.VMEM((block, count), jnp.bfloat16),
            ],
        ),
        out_shape=out_shape,
        compiler_params=params(VMEM_LIMIT if with_before else VMEM_WHOLE),
        cost_estimate=pl.CostEstimate(
            flops=channels * count * TAPS, bytes_accessed=channels * count * 8, transcendentals=0
        ),
        name="conv_before" if with_before else "conv_here",
    )(seq_here, stripe_order, tokens, conv_taps, *extra_args)


def prepare_body(blocks_ref, gain_ref, qkv_ref, out_ref, qkv_out, out_out):
    qkv_out[...] = (qkv_ref[...].astype(jnp.float32) * gain_ref[...]).astype(jnp.bfloat16)
    out_out[...] = out_ref[...].T


def prepare_weights(blocks, norm_gain, qkv_weight, out_weight):
    kinds, cols, channels = qkv_weight.shape
    count = blocks.shape[0]
    width = channels // count
    return pl.pallas_call(
        prepare_body,
        grid_spec=pltpu.PrefetchScalarGridSpec(
            num_scalar_prefetch=1,
            grid=(count,),
            in_specs=[
                pl.BlockSpec((1, width), lambda j, b: (0, b[j])),
                pl.BlockSpec((kinds * cols, width), lambda j, b: (0, b[j])),
                pl.BlockSpec((cols, width), lambda j, b: (0, b[j])),
            ],
            out_specs=[
                pl.BlockSpec((kinds * cols, width), lambda j, b: (0, j)),
                pl.BlockSpec((width, cols), lambda j, b: (j, 0)),
            ],
        ),
        out_shape=[
            jax.ShapeDtypeStruct((kinds * cols, channels), jnp.bfloat16),
            jax.ShapeDtypeStruct((channels, cols), jnp.bfloat16),
        ],
        compiler_params=params(),
        cost_estimate=pl.CostEstimate(
            flops=kinds * cols * channels, bytes_accessed=16 * cols * channels, transcendentals=0
        ),
        name="prepare_weights",
    )(blocks, norm_gain[None, :], qkv_weight.reshape(kinds * cols, channels), out_weight)


def project_body(query_steps, weight_ref, *refs):
    shards, out_ref, inverse_ref = refs[:-2], refs[-2], refs[-1]
    width = shards[0].shape[0]
    step = pl.program_id(0)

    @pl.when(step == 0)
    def _():
        squares = None
        for shard in shards:
            wide = shard[...].astype(jnp.float32)
            term = jnp.sum(wide * wide, axis=0, keepdims=True)
            squares = term if squares is None else squares + term
        inverse_ref[...] = lax.rsqrt(squares / (width * len(shards)) + EPSILON)

    total = None
    for index, shard in enumerate(shards):
        term = jnp.dot(
            weight_ref[:, index * width : (index + 1) * width],
            shard[...],
            preferred_element_type=jnp.float32,
        )
        total = term if total is None else total + term
    scale = jnp.where(step < query_steps, LOG2E / math.sqrt(HEAD), 1.0)
    out_ref[...] = (total * (inverse_ref[...] * scale)).astype(jnp.bfloat16)


def project_call(weights, shards):
    rows, channels = weights.shape
    width, tokens = shards[0].shape
    block = 256
    whole = pl.BlockSpec((width, tokens), lambda i: (0, 0))
    return pl.pallas_call(
        functools.partial(project_body, rows // 3 // block),
        grid=(rows // block,),
        in_specs=[pl.BlockSpec((block, channels), lambda i: (i, 0))] + [whole] * len(shards),
        out_specs=pl.BlockSpec((block, tokens), lambda i: (i, 0)),
        out_shape=jax.ShapeDtypeStruct((rows, tokens), jnp.bfloat16),
        scratch_shapes=[pltpu.VMEM((1, tokens), jnp.float32)],
        compiler_params=params(),
        cost_estimate=pl.CostEstimate(
            flops=2 * rows * channels * tokens,
            bytes_accessed=2 * (rows * channels + channels * tokens + rows * tokens),
            transcendentals=0,
        ),
        name="project",
    )(weights, *shards)


def tile_lists(order_ref, ids_ref, seq_here, tiles_dev):
    half = tiles_dev // 2
    for block in range(2):
        first = jnp.int32(0)
        second = jnp.int32(0)
        away = (jnp.int32(block) != seq_here).astype(jnp.int32)
        for spot in range(tiles_dev):
            tile = order_ref[block * tiles_dev + spot]
            late = tile // tiles_dev
            rank = jnp.where(late == 0, first, second)
            ids_ref[(2 * late + away) * half + rank] = tile
            first = first + (1 - late)
            second = second + late


def attend_body(chunk, seq_ref, order_ref, mask_ref, query_ref, *refs):
    count = 2 * (chunk + 1)
    keys, values = refs[:count], refs[count : 2 * count]
    out_ref, ids_ref, scores_ref = refs[2 * count], refs[2 * count + 1], refs[2 * count + 2]
    tokens = query_ref.shape[1]
    half = tokens // TILE

    @pl.when(pl.program_id(0) == 0)
    def _():
        tile_lists(order_ref, ids_ref, seq_ref[0], 2 * half)

    query = query_ref[...]
    lane_tile = lax.broadcasted_iota(jnp.int32, (1, tokens), 1) // TILE
    top = None
    for source in range(count):
        block = jnp.dot(keys[source][...].T, query, preferred_element_type=jnp.float32)
        for spot in range(half):
            key_tile = ids_ref[source * half + spot]
            bias = jnp.zeros((1, tokens), jnp.float32)
            for query_spot in range(half):
                query_tile = ids_ref[2 * chunk * half + query_spot]
                blocked = jnp.where(mask_ref[query_tile, key_tile] == 1, 0.0, MASKED_SCORE)
                bias = jnp.where(lane_tile == query_spot, blocked, bias)
            piece = block[spot * TILE : (spot + 1) * TILE, :] + bias
            scores_ref[source * tokens + spot * TILE : source * tokens + (spot + 1) * TILE, :] = piece
            best = jnp.max(piece, axis=0, keepdims=True)
            top = best if top is None else jnp.maximum(top, best)
    denom = None
    weighted = None
    for source in range(count):
        powers = jnp.exp2(scores_ref[source * tokens : (source + 1) * tokens, :] - top)
        summed = jnp.sum(powers, axis=0, keepdims=True)
        term = jnp.dot(
            values[source][...], powers.astype(jnp.bfloat16), preferred_element_type=jnp.float32
        )
        denom = summed if denom is None else denom + summed
        weighted = term if weighted is None else weighted + term
    out_ref[...] = (weighted / denom).astype(jnp.bfloat16)


def attend_call(chunk, seq_here, stripe_order, tile_mask, own, peers):
    rows, tokens = own[0].shape
    heads = rows // 3 // HEAD
    sources = []
    for mine, other in zip(own, peers):
        sources += [(mine, heads, 2 * heads), (other, 0, heads)]

    def spec(start):
        return pl.BlockSpec((HEAD, tokens), lambda h, *_, start=start: (start + h, 0))

    count = len(sources)
    return pl.pallas_call(
        functools.partial(attend_body, chunk),
        grid_spec=pltpu.PrefetchScalarGridSpec(
            num_scalar_prefetch=3,
            grid=(heads,),
            in_specs=[spec(0)] + [spec(k) for _, k, _ in sources] + [spec(v) for _, _, v in sources],
            out_specs=spec(0),
            scratch_shapes=[
                pltpu.SMEM((4 * tokens // TILE,), jnp.int32),
                pltpu.VMEM((count * tokens, tokens), jnp.float32),
            ],
        ),
        out_shape=jax.ShapeDtypeStruct((heads * HEAD, tokens), jnp.bfloat16),
        compiler_params=params(),
        cost_estimate=pl.CostEstimate(
            flops=4 * heads * HEAD * tokens * tokens * count,
            bytes_accessed=2 * heads * HEAD * tokens * (2 + 2 * count),
            transcendentals=heads * tokens * tokens * count,
        ),
    )(
        seq_here,
        stripe_order,
        tile_mask,
        own[chunk],
        *[array for array, _, _ in sources],
        *[array for array, _, _ in sources],
    )


def place_body(seq_ref, order_ref, ends_ref, first_ref, *refs):
    parts, out_ref, second_ref = refs[:4], refs[4], refs[5]
    _, tokens = first_ref.shape
    tiles_dev = 2 * tokens // TILE
    seq_here = seq_ref[0]
    at_end = ends_ref[0] == 1
    total = (
        parts[0][...].astype(jnp.float32)
        + parts[1][...].astype(jnp.float32)
        + parts[2][...].astype(jnp.float32)
        + jnp.where(at_end, parts[3][...].astype(jnp.float32), 0.0)
    )
    second_ref[...] = total.astype(jnp.bfloat16)
    ranks = [jnp.int32(0), jnp.int32(0)]
    for position in range(tiles_dev):
        late = order_ref[seq_here * tiles_dev + position] // tiles_dev
        spot = pl.ds(pl.multiple_of(jnp.where(late == 0, ranks[0], ranks[1]) * TILE, TILE), TILE)
        here = slice(position * TILE, (position + 1) * TILE)

        @pl.when(late == 0)
        def _(spot=spot, here=here):
            out_ref[:, here] = first_ref[:, spot]

        @pl.when(late == 1)
        def _(spot=spot, here=here):
            out_ref[:, here] = second_ref[:, spot]

        ranks[0] = ranks[0] + (1 - late)
        ranks[1] = ranks[1] + late


def place_call(seq_here, stripe_order, at_end, first, parts):
    channels, tokens = first.shape
    block = 128
    slim = pl.BlockSpec((block, tokens), lambda i, *_: (i, 0))
    return pl.pallas_call(
        place_body,
        grid_spec=pltpu.PrefetchScalarGridSpec(
            num_scalar_prefetch=3,
            grid=(channels // block,),
            in_specs=[slim] * 5,
            out_specs=pl.BlockSpec((block, 2 * tokens), lambda i, *_: (i, 0)),
            scratch_shapes=[pltpu.VMEM((block, tokens), jnp.bfloat16)],
        ),
        out_shape=jax.ShapeDtypeStruct((channels, 2 * tokens), jnp.bfloat16),
        compiler_params=params(),
        cost_estimate=pl.CostEstimate(
            flops=4 * channels * tokens, bytes_accessed=14 * channels * tokens, transcendentals=0
        ),
        name="place",
    )(seq_here, stripe_order, at_end, first, *parts)


FORWARD = [(0, 1), (1, 2), (2, 3), (3, 0)]
BACKWARD = [(1, 0), (2, 1), (3, 2), (0, 3)]
FOLDED = [(0, 1), (1, 3), (3, 2), (2, 0)]
UNFOLDED = [(1, 0), (3, 1), (2, 3), (0, 2)]


def gather_blocks(block, here):
    before = lax.ppermute(block, "tp", FORWARD)
    after = lax.ppermute(block, "tp", BACKWARD)
    relay = jnp.where(here == 2, before, jnp.where(here == 1, after, block))
    across = lax.ppermute(relay, "tp", UNFOLDED)
    return (block, before, after, across)


def plus(a, b, chosen):
    summed = a.astype(jnp.float32) + jnp.where(chosen, b.astype(jnp.float32), 0.0)
    return summed.astype(jnp.bfloat16)


def reduce_blocks(weights, heads_out, here):
    width = weights.shape[0] // 4

    def partial(index):
        block = weights[index * width : (index + 1) * width]
        return jnp.dot(block, heads_out, preferred_element_type=jnp.float32).astype(jnp.bfloat16)

    sent = partial(3)
    across = lax.ppermute(sent, "tp", FOLDED)
    back = lax.ppermute(plus(partial(1), across, here == 2), "tp", BACKWARD)
    onward = lax.ppermute(plus(partial(2), across, here == 1), "tp", FORWARD)
    return (partial(0), back, onward, across)


def per_device_fast(
    clip_tokens, conv_taps, norm_gain, qkv_weight, out_weight, tile_mask, stripe_order
):
    seq = lax.axis_index("seq")
    here = lax.axis_index("tp")
    seq_here = seq.astype(jnp.int32)[None]
    at_end = ((here == 0) | (here == 3)).astype(jnp.int32)[None]
    blocks = jnp.stack([here, (here + 3) % 4, (here + 1) % 4, (here + 2) % 4]).astype(jnp.int32)

    part, keep_a, send_a = conv_call(seq_here, stripe_order, clip_tokens, conv_taps)
    got_a = lax.ppermute(send_a, "seq", [(0, 1)])
    before = lax.ppermute(clip_tokens, "seq", [(0, 1)])
    weights, out_t = prepare_weights(blocks, norm_gain, qkv_weight, out_weight)

    tokens_a = jnp.where(seq == 0, keep_a, got_a)
    shards_a = gather_blocks(tokens_a, here)

    keep_b, send_b = conv_call(seq_here, stripe_order, clip_tokens, conv_taps, before, part)
    got_b = lax.ppermute(send_b, "seq", [(1, 0)])
    tokens_b = jnp.where(seq == 1, keep_b, got_b)

    rows = weights.shape[0]
    cols = rows // 3
    swap = [(0, 1), (1, 0)]
    own_a = project_call(weights, shards_a)
    peer_a = lax.ppermute(own_a[cols:], "seq", swap)
    shards_b = gather_blocks(tokens_b, here)
    out_a = attend_call(0, seq_here, stripe_order, tile_mask, [own_a], [peer_a])
    parts_a = reduce_blocks(out_t, out_a, here)
    own_b = project_call(weights, shards_b)
    peer_b = lax.ppermute(own_b[cols:], "seq", swap)
    out_b = attend_call(1, seq_here, stripe_order, tile_mask, [own_a, own_b], [peer_a, peer_b])
    parts_b = reduce_blocks(out_t, out_b, here)
    first = (
        parts_a[0].astype(jnp.float32)
        + parts_a[1].astype(jnp.float32)
        + parts_a[2].astype(jnp.float32)
        + jnp.where(at_end == 1, parts_a[3].astype(jnp.float32), 0.0)
    ).astype(jnp.bfloat16)
    return place_call(seq_here, stripe_order, at_end, first, parts_b)


def passed_along(block, axis, distance):
    devices = range(lax.axis_size(axis))
    route = [(i - distance, i) for i in devices if i - distance in devices]
    return lax.ppermute(block, axis, route)


def from_partner(block, axis, apart):
    count = lax.axis_size(axis)
    route = []
    for low in range(count):
        high = low | 1 << apart
        if high != low and high < count:
            route += [(low, high), (high, low)]
    return lax.ppermute(block, axis, route)


def causal_conv(local_tokens, before, conv_taps):
    channels = local_tokens.shape[0]
    frames = local_tokens.shape[1] // (FH * FW)
    stacked = (
        jnp.concatenate([before, local_tokens], axis=1)
        .astype(jnp.float32)
        .reshape(channels, frames + 2, FH, FW)
    )
    padded = jnp.pad(stacked, ((0, 0), (0, 0), (1, 1), (1, 1)))
    summed = jnp.zeros((channels, frames, FH, FW), jnp.float32)
    for time_off in range(3):
        for row_off in range(3):
            for col_off in range(3):
                tap_vec = conv_taps[time_off * 9 + row_off * 3 + col_off]
                summed = (
                    summed
                    + tap_vec[:, None, None, None]
                    * padded[
                        :,
                        time_off : time_off + frames,
                        row_off : row_off + FH,
                        col_off : col_off + FW,
                    ]
                )
    return (local_tokens.astype(jnp.float32) + summed.reshape(channels, -1)).astype(jnp.bfloat16)


def stripe_tables(stripe_order, tiles_dev):
    seq_count = lax.axis_size("seq")
    seq_here = lax.axis_index("seq")
    per_source = tiles_dev // seq_count
    blocks = stripe_order.reshape(seq_count, tiles_dev)
    owners = blocks // tiles_dev
    is_mine = (owners == seq_here).astype(jnp.int32)
    rank_of = jnp.cumsum(is_mine, axis=1) - 1
    slot_ids = jnp.arange(per_source, dtype=jnp.int32)
    picked = is_mine[:, None, :] * (rank_of[:, None, :] == slot_ids[None, :, None]).astype(
        jnp.int32
    )
    local_tiles = (blocks - seq_here * tiles_dev)[:, None, :]
    send_order = jnp.sum(picked * local_tiles, axis=2).reshape(-1)
    own_row = lax.dynamic_slice_in_dim(stripe_order, seq_here * tiles_dev, tiles_dev)
    sources = own_row // tiles_dev
    position = jnp.arange(tiles_dev, dtype=jnp.int32)
    earlier = (sources[:, None] == sources[None, :]) & (position[None, :] < position[:, None])
    place_order = sources * per_source + jnp.sum(earlier.astype(jnp.int32), axis=1)
    return (send_order, place_order, own_row)


def regroup(values, send_order, place_order):
    leading = values.shape[0]
    trailing = values.shape[2:]
    in_tiles = values.reshape((leading, values.shape[1] // TILE, TILE) + trailing)
    outgoing = jnp.take(in_tiles, send_order, axis=1)
    arrived = lax.all_to_all(outgoing, "seq", split_axis=1, concat_axis=1, tiled=True)
    placed = jnp.take(arrived, place_order, axis=1)
    return placed.reshape(values.shape)


def project(mixed, norm_gain, qkv_weight):
    channels = norm_gain.shape[0]
    widened = lax.all_gather(mixed, "tp", axis=0, tiled=True).astype(jnp.float32)
    scaled = (widened * norm_gain[:, None]).astype(jnp.bfloat16)
    projected = jnp.einsum("ct,khc->kth", scaled, qkv_weight, preferred_element_type=jnp.float32)
    squares = jnp.sum(widened * widened, axis=0)
    projected, squares = (projected, squares)
    inverse = lax.rsqrt(squares / channels + EPSILON)
    return (projected * inverse[None, :, None]).astype(jnp.bfloat16)


def position_mask(tile_mask, stripe_order, own_half):
    tiles_all = tile_mask.shape[0]
    tile_ids = jnp.arange(tiles_all, dtype=jnp.int32)
    own_onehot = (own_half[:, None] == tile_ids[None, :]).astype(jnp.float32)
    order_onehot = (stripe_order[:, None] == tile_ids[None, :]).astype(jnp.float32)
    rows_mask = jnp.dot(
        own_onehot, tile_mask.astype(jnp.float32), preferred_element_type=jnp.float32
    )
    return jnp.dot(rows_mask, order_onehot.T, preferred_element_type=jnp.float32)


def attend(queries_flat, key_values, pos_mask):
    row_count = queries_flat.shape[0]
    heads_dev = queries_flat.shape[1] // HEAD
    queries = queries_flat.reshape(row_count, heads_dev, HEAD)
    score_scale = 1.0 / math.sqrt(HEAD)
    tiles_dev = row_count // TILE
    tile_ids = jnp.arange(pos_mask.shape[1], dtype=jnp.int32)
    initial = (
        jnp.full((heads_dev, row_count), MASKED_SCORE, jnp.float32),
        jnp.zeros((heads_dev, row_count), jnp.float32),
        jnp.zeros((heads_dev, row_count, HEAD), jnp.float32),
    )
    fetched = lax.all_gather(key_values, "seq", axis=1, tiled=True)
    fetched_count = fetched.shape[1]
    key_block = 512

    def advance(block_index, state_now):
        top_score, denom, weighted = state_now
        offset = block_index * key_block
        key_rows = lax.dynamic_slice_in_dim(fetched[0], offset, key_block).reshape(
            key_block, heads_dev, HEAD
        )
        values = lax.dynamic_slice_in_dim(fetched[1], offset, key_block).reshape(
            key_block, heads_dev, HEAD
        )
        tile_pos = (offset + jnp.arange(key_block, dtype=jnp.int32)) // TILE
        onehot = (tile_pos[:, None] == tile_ids[None, :]).astype(jnp.float32)
        tile_allowed = (
            jnp.einsum("qn,kn->qk", pos_mask, onehot, preferred_element_type=jnp.float32) > 0.5
        )
        visible = jnp.broadcast_to(tile_allowed[:, None, :], (tiles_dev, TILE, key_block)).reshape(
            row_count, key_block
        )
        scores = (
            jnp.einsum("qhd,khd->hqk", queries, key_rows, preferred_element_type=jnp.float32)
            * score_scale
        )
        masked = jnp.where(visible[None], scores, MASKED_SCORE)
        new_top = jnp.maximum(top_score, jnp.max(masked, axis=2))
        powers = jnp.where(visible[None], jnp.exp(masked - new_top[:, :, None]), 0.0)
        shrink = jnp.exp(top_score - new_top)
        denom = denom * shrink + jnp.sum(powers, axis=2)
        weighted = weighted * shrink[:, :, None] + jnp.einsum(
            "hqk,khd->hqd", powers.astype(jnp.bfloat16), values, preferred_element_type=jnp.float32
        )
        return (new_top, denom, weighted)

    _, denom, weighted = lax.fori_loop(0, fetched_count // key_block, advance, initial)
    finished = (weighted / denom[:, :, None]).astype(jnp.bfloat16)
    return jnp.transpose(finished, (1, 0, 2)).reshape(row_count, heads_dev * HEAD)


def per_device_general(clip_tokens, conv_taps, norm_gain, qkv_weight, out_weight, tile_mask, stripe_order):
    tiles_dev = clip_tokens.shape[1] // TILE
    send_order, place_order, own_row = stripe_tables(stripe_order, tiles_dev)
    before = passed_along(clip_tokens, "seq", 1)
    mixed = causal_conv(clip_tokens, before, conv_taps)
    mixed = regroup(mixed, send_order, place_order)
    projected = project(mixed, norm_gain, qkv_weight)
    row_count = projected.shape[1]
    group_cols = projected.shape[2]
    half_rows = row_count // 2
    side = lax.axis_index("tp") % 2
    mine_first = side == 0
    query_send = lax.dynamic_slice_in_dim(projected[0], (1 - side) * half_rows, half_rows, axis=0)
    query_mine = lax.dynamic_slice_in_dim(projected[0], side * half_rows, half_rows, axis=0)
    kv_mine = projected[1:]
    query_other, kv_other = from_partner((query_send, kv_mine), "tp", 0)
    queries = jnp.where(
        mine_first,
        jnp.concatenate([query_mine, query_other], axis=1),
        jnp.concatenate([query_other, query_mine], axis=1),
    )
    key_values = jnp.where(
        mine_first,
        jnp.concatenate([kv_mine, kv_other], axis=2),
        jnp.concatenate([kv_other, kv_mine], axis=2),
    )
    own_half = lax.dynamic_slice_in_dim(own_row, side * (tiles_dev // 2), tiles_dev // 2)
    pos_mask = position_mask(tile_mask, stripe_order, own_half)
    pair_out = attend(queries, key_values, pos_mask)
    give_cols = lax.dynamic_slice_in_dim(pair_out, (1 - side) * group_cols, group_cols, axis=1)
    keep_cols = lax.dynamic_slice_in_dim(pair_out, side * group_cols, group_cols, axis=1)
    got_cols = from_partner(give_cols, "tp", 0)
    heads_out = jnp.where(
        mine_first,
        jnp.concatenate([keep_cols, got_cols], axis=0),
        jnp.concatenate([got_cols, keep_cols], axis=0),
    )
    return lax.psum_scatter(
        jnp.einsum("qg,gc->cq", heads_out, out_weight, preferred_element_type=jnp.float32).astype(
            jnp.bfloat16
        ),
        "tp",
        scatter_dimension=0,
        tiled=True,
    )


def solution(mesh):
    in_specs = (
        P("tp", ("dp", "seq")),
        P(None, "tp"),
        P(),
        P(None, "tp", None),
        P("tp", None),
        P(),
        P(),
    )
    out_specs = P("tp", ("dp", "seq"))

    def run(clip_tokens, conv_taps, norm_gain, qkv_weight, out_weight, tile_mask, stripe_order):
        arguments = (clip_tokens, conv_taps, norm_gain, qkv_weight, out_weight, tile_mask, stripe_order)
        tokens = clip_tokens.shape[1] // (mesh.shape["dp"] * mesh.shape["seq"])
        columns = qkv_weight.shape[1] // mesh.shape["tp"]
        two_halves = mesh.shape["seq"] == 2 and tokens == 2 * FRAME
        fast = two_halves and mesh.shape["tp"] == 4 and columns % HEAD == 0

        def per_device(*local):
            if not fast:
                return per_device_general(*local)
            return per_device_fast(*local)

        step = jax.shard_map(
            per_device, mesh=mesh, in_specs=in_specs, out_specs=out_specs, check_vma=False
        )
        return step(*arguments)

    return run
```

profile of v0, /device:TPU:0, one launch (start us, length us, event | category | flops | bytes accessed | tf_op | source)
XLA Modules:
  0.0 222.0 jit_solution(15607280610575596485)
XLA Ops:
  0.0 4.9 %collective-permute-start.8 = (bf16[512,1024]{1,0:T(8,128)(2,1)}, bf16[512,1024]{1,0:T(8,128)(2,1)S(1)}, u32[]{:S(2)}, u32[]{:S(2)}) collective-permute-start(bf16[512,1024]{1,0:T(8,128)(2,1)} %refs_0_.3), channel_id=1, source_target_pairs={{0,16},{1,17},{2,18},{3,19},{4,20},{5,21},{6,22},{7,23},{8,24},{9,... | collective-permute-start | bytes 3145736 | tf_op jit(solution)/shard_map/ppermute | solution.py:440
  4.9 10.6 %conv_here.1 = (f32[512,1024]{1,0:T(8,128)}, bf16[512,512]{1,0:T(8,128)(2,1)}, bf16[512,512]{1,0:T(8,128)(2,1)}) custom-call(s32[1]{0:T(128)} %bitcast.seq_ref, s32[16]{0:T(128)} %order_ref.9, bf16[512,1024]{1,0:T(8,128)(2,1)} %refs_0_.3, f32[27,512]{1,0:T(8,128)} %refs_1_.3), custom_call_target="tpu_custom_call" | custom-call | flops 14155776 | bytes 4194304 | tf_op jit(solution)/shard_map/conv_here/pallas_call | solution.py:142
  15.5 2.1 collective-permute-start
  17.6 11.1 %collective-permute-done.8.refs_2_ = bf16[512,1024]{1,0:T(8,128)(2,1)S(1)} collective-permute-done((bf16[512,1024]{1,0:T(8,128)(2,1)}, bf16[512,1024]{1,0:T(8,128)(2,1)S(1)}, u32[]{:S(2)}, u32[]{:S(2)}) %collective-permute-start.8) | collective-permute-done | bytes 1048608 | tf_op jit(solution)/shard_map/ppermute | solution.py:440
  28.7 1.2 copy-done.3
  29.9 1.6 copy-done.5
  31.5 0.8 copy-done.10
  32.4 0.7 copy-done.12
  33.0 8.5 %conv_before.1 = (bf16[512,512]{1,0:T(8,128)(2,1)S(1)}, bf16[512,512]{1,0:T(8,128)(2,1)S(1)}) custom-call(s32[1]{0:T(128)} %bitcast.seq_ref, s32[16]{0:T(128)S(1)} %copy-done.12, bf16[512,1024]{1,0:T(8,128)(2,1)S(1)} %copy-done.3, f32[27,512]{1,0:T(8,128)S(1)} %copy-done.10, bf16[512,1024]{1,0:T(8,128)(2,1)S(1)} %collective-permute-done.8.refs_2_, ...), custom_call_target="tpu_custom_call" | custom-call | flops 14155776 | bytes 4194304 | tf_op jit(solution)/shard_map/conv_before/pallas_call | solution.py:142
  41.5 1.3 collective-permute-start.9
  42.9 3.7 %collective-permute-start.2 = (bf16[512,512]{1,0:T(8,128)(2,1)S(1)}, bf16[512,512]{1,0:T(8,128)(2,1)}, u32[]{:S(2)}, u32[]{:S(2)}) collective-permute-start(bf16[512,512]{1,0:T(8,128)(2,1)S(1)} %broadcast_select_fusion.1.refs_0_), channel_id=1, source_target_pairs={{4,0},{8,4},{12,8},{0,12},{5,1},{9,5},{13,9},{1,13},{6,2},{10,6},{... | collective-permute-start | bytes 1572872 | tf_op jit(solution)/shard_map/ppermute | solution.py:404
  46.6 8.5 %collective-permute-done.9 = bf16[512,512]{1,0:T(8,128)(2,1)S(1)} collective-permute-done((bf16[512,512]{1,0:T(8,128)(2,1)S(1)}, bf16[512,512]{1,0:T(8,128)(2,1)S(1)}, u32[]{:S(2)}, u32[]{:S(2)}) %collective-permute-start.9) | collective-permute-done | bytes 524320 | tf_op jit(solution)/shard_map/ppermute | solution.py:447
  55.2 3.7 %collective-permute-start.11 = (bf16[512,512]{1,0:T(8,128)(2,1)S(1)}, bf16[512,512]{1,0:T(8,128)(2,1)}, u32[]{:S(2)}, u32[]{:S(2)}) collective-permute-start(bf16[512,512]{1,0:T(8,128)(2,1)S(1)} %broadcast_select_fusion.refs_0_), channel_id=1, source_target_pairs={{4,0},{8,4},{12,8},{0,12},{5,1},{9,5},{13,9},{1,13},{6,2},{10,6},{... | collective-permute-start | bytes 1572872 | tf_op jit(solution)/shard_map/ppermute | solution.py:404
  58.9 12.3 %collective-permute-done.1.refs_1_ = bf16[512,512]{1,0:T(8,128)(2,1)} collective-permute-done((bf16[512,512]{1,0:T(8,128)(2,1)S(1)}, bf16[512,512]{1,0:T(8,128)(2,1)}, u32[]{:S(2)}, u32[]{:S(2)}) %collective-permute-start.1) | collective-permute-done | bytes 524320 | tf_op jit(solution)/shard_map/ppermute | solution.py:403
  71.2 0.9 select_select_fusion.1
  72.0 3.5 %collective-permute-start.3 = (bf16[512,512]{1,0:T(8,128)(2,1)}, bf16[512,512]{1,0:T(8,128)(2,1)}, u32[]{:S(2)}, u32[]{:S(2)}) collective-permute-start(bf16[512,512]{1,0:T(8,128)(2,1)} %select_select_fusion.1), channel_id=1, source_target_pairs={{4,0},{12,4},{8,12},{0,8},{5,1},{13,5},{9,13},{1,9},{6,2},{14,6},{... | collective-permute-start | bytes 1572872 | tf_op jit(solution)/shard_map/ppermute | solution.py:406
  75.6 5.8 %collective-permute-done.11.refs_2_ = bf16[512,512]{1,0:T(8,128)(2,1)} collective-permute-done((bf16[512,512]{1,0:T(8,128)(2,1)S(1)}, bf16[512,512]{1,0:T(8,128)(2,1)}, u32[]{:S(2)}, u32[]{:S(2)}) %collective-permute-start.11) | collective-permute-done | bytes 524320 | tf_op jit(solution)/shard_map/ppermute | solution.py:404
  81.4 12.3 %collective-permute-done.10.refs_1_ = bf16[512,512]{1,0:T(8,128)(2,1)} collective-permute-done((bf16[512,512]{1,0:T(8,128)(2,1)S(1)}, bf16[512,512]{1,0:T(8,128)(2,1)}, u32[]{:S(2)}, u32[]{:S(2)}) %collective-permute-start.10) | collective-permute-done | bytes 524320 | tf_op jit(solution)/shard_map/ppermute | solution.py:403
  93.9 2.8 %copy-done.2 = bf16[3,512,2048]{2,1,0:T(8,128)(2,1)S(1)} copy-done((bf16[3,512,2048]{2,1,0:T(8,128)(2,1)S(1)}, bf16[3,512,2048]{2,1,0:T(8,128)(2,1)}, u32[]{:S(2)}) %copy-start.2) | copy-done | bytes 6291480
  96.7 4.6 %prepare_weights.1 = (bf16[1536,2048]{1,0:T(8,128)(2,1)S(1)}, bf16[2048,512]{1,0:T(8,128)(2,1)S(1)}) custom-call(s32[4]{0:T(128)S(1)} %pad_add_fusion.blocks_ref, f32[1,2048]{1,0:T(1,128)S(1)} %bitcast.18, bf16[1536,2048]{1,0:T(8,128)(2,1)S(1)} %bitcast.17, bf16[512,2048]{1,0:T(8,128)(2,1)S(1)} %copy-done.4), custom_call_target="tpu_custom_call" | custom-call | flops 3145728 | bytes 16777216 | tf_op jit(solution)/shard_map/prepare_weights/pallas_call | solution.py:173
  101.3 2.6 %collective-permute-done.3.refs_3_ = bf16[512,512]{1,0:T(8,128)(2,1)} collective-permute-done((bf16[512,512]{1,0:T(8,128)(2,1)}, bf16[512,512]{1,0:T(8,128)(2,1)}, u32[]{:S(2)}, u32[]{:S(2)}) %collective-permute-start.3) | collective-permute-done | bytes 524320 | tf_op jit(solution)/shard_map/ppermute | solution.py:406
  104.0 5.9 %project.2.query_ref.refs_0_.refs_2_.refs_4_ = bf16[1536,512]{1,0:T(8,128)(2,1)S(1)} custom-call(bf16[1536,2048]{1,0:T(8,128)(2,1)S(1)} %get-tuple-element.13.weight_ref, bf16[512,512]{1,0:T(8,128)(2,1)S(1)} %broadcast_select_fusion.1.refs_0_, bf16[512,512]{1,0:T(8,128)(2,1)} %collective-permute-done.1.refs_1_, ...), custom_call_target="tpu_custom_call" | custom-call | flops 3221225472 | bytes 9961472 | tf_op jit(solution)/shard_map/project/pallas_call | solution.py:231
  110.0 3.8 %collective-permute-start.4 = (bf16[1024,512]{1,0:T(8,128)(2,1)S(1)}, bf16[1024,512]{1,0:T(8,128)(2,1)S(1)}, u32[]{:S(2)}, u32[]{:S(2)}) collective-permute-start(bf16[1024,512]{1,0:T(8,128)(2,1)S(1)} %slice.28), channel_id=1, source_target_pairs={{0,16},{16,0},{1,17},{17,1},{2,18},{18,2},{3,19},{19,3},{4,20},{20... | collective-permute-start | bytes 3145736 | tf_op jit(solution)/shard_map/ppermute | solution.py:454
  113.7 5.7 %project.3.query_ref.refs_2_.refs_6_ = bf16[1536,512]{1,0:T(8,128)(2,1)S(1)} custom-call(bf16[1536,2048]{1,0:T(8,128)(2,1)S(1)} %get-tuple-element.13.weight_ref, bf16[512,512]{1,0:T(8,128)(2,1)S(1)} %copy-done.7, bf16[512,512]{1,0:T(8,128)(2,1)} %collective-permute-done.10.refs_1_, bf16[512,512]{1,0:T(8,128)(2,1)} %collective-permute-done.11.refs_2_, ...), custom_call_target="tpu_custom_call" | custom-call | flops 3221225472 | bytes 9961472 | tf_op jit(solution)/shard_map/project/pallas_call | solution.py:231
  119.5 1.1 slice.29
  120.6 1.7 collective-permute-start.13
  122.3 15.4 %collective-permute-done.4.refs_1_.refs_3_.refs_5_ = bf16[1024,512]{1,0:T(8,128)(2,1)S(1)} collective-permute-done((bf16[1024,512]{1,0:T(8,128)(2,1)S(1)}, bf16[1024,512]{1,0:T(8,128)(2,1)S(1)}, u32[]{:S(2)}, u32[]{:S(2)}) %collective-permute-start.4) | collective-permute-done | bytes 1048608 | tf_op jit(solution)/shard_map/ppermute | solution.py:454
  137.8 4.8 %shard_map.73 = bf16[512,512]{1,0:T(8,128)(2,1)S(1)} custom-call(s32[1]{0:T(128)} %bitcast.seq_ref, s32[16]{0:T(128)S(1)} %copy-done.13, s32[16,16]{1,0:T(8,128)S(1)} %copy-done.11, bf16[1536,512]{1,0:T(8,128)(2,1)S(1)} %project.2.query_ref.refs_0_.refs_2_.refs_4_, bf16[1536,512]{1,0:T(8,128)(2,1)S(1)} %project.2.query_ref.refs_0_.refs_2_.refs_4_, ...), custom_call_target="tpu_custom_call" | custom-call | flops 1073741824 | bytes 3145728 | tf_op jit(solution)/shard_map/pallas_call | solution.py:314
  142.6 0.8 copy-done.8
  143.3 1.2 convolution_convert_fusion.5
  144.6 1.5 collective-permute-start.5
  146.1 8.0 %collective-permute-done.13.refs_3_.refs_7_ = bf16[1024,512]{1,0:T(8,128)(2,1)} collective-permute-done((bf16[1024,512]{1,0:T(8,128)(2,1)}, bf16[1024,512]{1,0:T(8,128)(2,1)}, u32[]{:S(2)}, u32[]{:S(2)}) %collective-permute-start.13) | collective-permute-done | bytes 1048608 | tf_op jit(solution)/shard_map/ppermute | solution.py:459
  154.1 1.2 copy-done.1
  155.3 9.2 %shard_map.74 = bf16[512,512]{1,0:T(8,128)(2,1)S(1)} custom-call(s32[1]{0:T(128)} %bitcast.seq_ref, s32[16]{0:T(128)S(1)} %copy-done.13, s32[16,16]{1,0:T(8,128)S(1)} %copy-done.11, bf16[1536,512]{1,0:T(8,128)(2,1)S(1)} %project.3.query_ref.refs_2_.refs_6_, bf16[1536,512]{1,0:T(8,128)(2,1)S(1)} %project.2.query_ref.refs_0_.refs_2_.refs_4_, ...), custom_call_target="tpu_custom_call" | custom-call | flops 2147483648 | bytes 5242880 | tf_op jit(solution)/shard_map/pallas_call | solution.py:314
  165.0 0.5 collective-permute-start.14
  165.4 1.5 fusion.15
  166.9 3.5 %collective-permute-start.6 = (bf16[512,512]{1,0:T(8,128)(2,1)S(1)}, bf16[512,512]{1,0:T(8,128)(2,1)S(1)}, u32[]{:S(2)}, u32[]{:S(2)}) collective-permute-start(bf16[512,512]{1,0:T(8,128)(2,1)S(1)} %fusion.15), channel_id=1, source_target_pairs={{4,0},{8,4},{12,8},{0,12},{5,1},{9,5},{13,9},{1,13},{6,2},{10,6},{... | collective-permute-start | bytes 1572872 | tf_op jit(solution)/shard_map/ppermute | solution.py:424
  170.4 1.5 fusion.14
  172.0 11.3 %collective-permute-done.14.refs_3_ = bf16[512,512]{1,0:T(8,128)(2,1)S(1)} collective-permute-done((bf16[512,512]{1,0:T(8,128)(2,1)S(1)}, bf16[512,512]{1,0:T(8,128)(2,1)S(1)}, u32[]{:S(2)}, u32[]{:S(2)}) %collective-permute-start.14) | collective-permute-done | bytes 524320 | tf_op jit(solution)/shard_map/ppermute | solution.py:423
  183.3 0.4 fusion.13
  183.7 11.9 %collective-permute-start.15 = (bf16[512,512]{1,0:T(8,128)(2,1)S(1)}, bf16[512,512]{1,0:T(8,128)(2,1)S(1)}, u32[]{:S(2)}, u32[]{:S(2)}) collective-permute-start(bf16[512,512]{1,0:T(8,128)(2,1)S(1)} %fusion.13), channel_id=1, source_target_pairs={{4,0},{8,4},{12,8},{0,12},{5,1},{9,5},{13,9},{1,13},{6,2},{10,6},{... | collective-permute-start | bytes 1572872 | tf_op jit(solution)/shard_map/ppermute | solution.py:424
  195.6 0.4 fusion.12
  196.1 0.4 convolution_convert_fusion.3.refs_0_
  196.5 7.7 %collective-permute-done.7 = bf16[512,512]{1,0:T(8,128)(2,1)S(1)} collective-permute-done((bf16[512,512]{1,0:T(8,128)(2,1)S(1)}, bf16[512,512]{1,0:T(8,128)(2,1)S(1)}, u32[]{:S(2)}, u32[]{:S(2)}) %collective-permute-start.7) | collective-permute-done | bytes 524320 | tf_op jit(solution)/shard_map/ppermute | solution.py:425
  204.2 1.6 fusion.16.first_ref
  205.8 7.1 %collective-permute-done.15.refs_1_ = bf16[512,512]{1,0:T(8,128)(2,1)S(1)} collective-permute-done((bf16[512,512]{1,0:T(8,128)(2,1)S(1)}, bf16[512,512]{1,0:T(8,128)(2,1)S(1)}, u32[]{:S(2)}, u32[]{:S(2)}) %collective-permute-start.15) | collective-permute-done | bytes 524320 | tf_op jit(solution)/shard_map/ppermute | solution.py:424
  212.9 6.4 %collective-permute-done.16.refs_2_ = bf16[512,512]{1,0:T(8,128)(2,1)S(1)} collective-permute-done((bf16[512,512]{1,0:T(8,128)(2,1)S(1)}, bf16[512,512]{1,0:T(8,128)(2,1)S(1)}, u32[]{:S(2)}, u32[]{:S(2)}) %collective-permute-start.16) | collective-permute-done | bytes 524320 | tf_op jit(solution)/shard_map/ppermute | solution.py:425
  219.3 2.8 %place.1 = bf16[512,1024]{1,0:T(8,128)(2,1)} custom-call(s32[1]{0:T(128)} %bitcast.seq_ref, s32[16]{0:T(128)S(1)} %copy-done.13, s32[1]{0:T(128)} %bitcast.1.ends_ref, bf16[512,512]{1,0:T(8,128)(2,1)S(1)} %fusion.16.first_ref, bf16[512,512]{1,0:T(8,128)(2,1)S(1)} %convolution_convert_fusion.3.refs_0_, bf16[512,512]{1,0:T(8,128)(2,1)S(1)} %collective-permute-done.15.refs_1_, ...), custom_call_target="tpu_custom_call" | custom-call | flops 1048576 | bytes 3670016 | tf_op jit(solution)/shard_map/place/pallas_call | solution.py:378
  (45 shorter events, 1.1 us)
Async XLA Ops:
  0.0 28.7 %collective-permute-start.8 = (bf16[512,1024]{1,0:T(8,128)(2,1)}, bf16[512,1024]{1,0:T(8,128)(2,1)S(1)}, u32[]{:S(2)}, u32[]{:S(2)}) collective-permute-start(bf16[512,1024]{1,0:T(8,128)(2,1)} %refs_0_.3), channel_id=1, source_target_pairs={{0,16},{1,17},{2,18},{3,19},{4,20},{5,21},{6,22},{7,23},{8,24},{9,... | collective-permute-start | bytes 3145736 | tf_op jit(solution)/shard_map/ppermute | solution.py:440
  15.5 27.3 %collective-permute-start = (bf16[512,512]{1,0:T(8,128)(2,1)}, bf16[512,512]{1,0:T(8,128)(2,1)}, u32[]{:S(2)}, u32[]{:S(2)}) collective-permute-start(bf16[512,512]{1,0:T(8,128)(2,1)} %get-tuple-element.15), channel_id=1, source_target_pairs={{0,16},{1,17},{2,18},{3,19},{4,20},{5,21},{6,22},{7,23},{8,24},{9,... | collective-permute-start | bytes 1572872 | tf_op jit(solution)/shard_map/ppermute | solution.py:439
  28.7 1.2 copy-start.3
  29.9 1.6 copy-start.5
  31.5 0.8 copy-start.10
  32.4 0.7 copy-start.12
  33.0 9.8 %copy-start.17 = (bf16[512,512]{1,0:T(8,128)(2,1)S(1)}, bf16[512,512]{1,0:T(8,128)(2,1)}, u32[]{:S(2)}) copy-start(bf16[512,512]{1,0:T(8,128)(2,1)} %get-tuple-element.14) | copy-start | bytes 1572868
  41.5 13.6 %collective-permute-start.9 = (bf16[512,512]{1,0:T(8,128)(2,1)S(1)}, bf16[512,512]{1,0:T(8,128)(2,1)S(1)}, u32[]{:S(2)}, u32[]{:S(2)}) collective-permute-start(bf16[512,512]{1,0:T(8,128)(2,1)S(1)} %get-tuple-element.18), channel_id=1, source_target_pairs={{16,0},{17,1},{18,2},{19,3},{20,4},{21,5},{22,6},{23,7},{24,8},{25... | collective-permute-start | bytes 1572872 | tf_op jit(solution)/shard_map/ppermute | solution.py:447
  42.9 16.0 %collective-permute-start.2 = (bf16[512,512]{1,0:T(8,128)(2,1)S(1)}, bf16[512,512]{1,0:T(8,128)(2,1)}, u32[]{:S(2)}, u32[]{:S(2)}) collective-permute-start(bf16[512,512]{1,0:T(8,128)(2,1)S(1)} %broadcast_select_fusion.1.refs_0_), channel_id=1, source_target_pairs={{4,0},{8,4},{12,8},{0,12},{5,1},{9,5},{13,9},{1,13},{6,2},{10,6},{... | collective-permute-start | bytes 1572872 | tf_op jit(solution)/shard_map/ppermute | solution.py:404
  46.6 24.6 %collective-permute-start.1 = (bf16[512,512]{1,0:T(8,128)(2,1)S(1)}, bf16[512,512]{1,0:T(8,128)(2,1)}, u32[]{:S(2)}, u32[]{:S(2)}) collective-permute-start(bf16[512,512]{1,0:T(8,128)(2,1)S(1)} %broadcast_select_fusion.1.refs_0_), channel_id=1, source_target_pairs={{0,4},{4,8},{8,12},{12,0},{1,5},{5,9},{9,13},{13,1},{2,6},{6,10},{... | collective-permute-start | bytes 1572872 | tf_op jit(solution)/shard_map/ppermute | solution.py:403
  55.2 38.6 %copy-start.6 = (bf16[512,512]{1,0:T(8,128)(2,1)}, bf16[512,512]{1,0:T(8,128)(2,1)S(1)}, u32[]{:S(2)}) copy-start(bf16[512,512]{1,0:T(8,128)(2,1)S(1)} %broadcast_select_fusion.refs_0_) | copy-start | bytes 1572868
  55.2 26.2 %collective-permute-start.11 = (bf16[512,512]{1,0:T(8,128)(2,1)S(1)}, bf16[512,512]{1,0:T(8,128)(2,1)}, u32[]{:S(2)}, u32[]{:S(2)}) collective-permute-start(bf16[512,512]{1,0:T(8,128)(2,1)S(1)} %broadcast_select_fusion.refs_0_), channel_id=1, source_target_pairs={{4,0},{8,4},{12,8},{0,12},{5,1},{9,5},{13,9},{1,13},{6,2},{10,6},{... | collective-permute-start | bytes 1572872 | tf_op jit(solution)/shard_map/ppermute | solution.py:404
  58.8 34.9 %collective-permute-start.10 = (bf16[512,512]{1,0:T(8,128)(2,1)S(1)}, bf16[512,512]{1,0:T(8,128)(2,1)}, u32[]{:S(2)}, u32[]{:S(2)}) collective-permute-start(bf16[512,512]{1,0:T(8,128)(2,1)S(1)} %broadcast_select_fusion.refs_0_), channel_id=1, source_target_pairs={{0,4},{4,8},{8,12},{12,0},{1,5},{5,9},{9,13},{13,1},{2,6},{6,10},{... | collective-permute-start | bytes 1572872 | tf_op jit(solution)/shard_map/ppermute | solution.py:403
  58.8 35.1 %copy-start.4 = (bf16[512,2048]{1,0:T(8,128)(2,1)S(1)}, bf16[512,2048]{1,0:T(8,128)(2,1)}, u32[]{:S(2)}) copy-start(bf16[512,2048]{1,0:T(8,128)(2,1)} %out_ref.1) | copy-start | bytes 6291460
  58.8 35.1 %copy-start.14 = (f32[2048]{0:T(1024)S(1)}, f32[2048]{0:T(1024)}, u32[]{:S(2)}) copy-start(f32[2048]{0:T(1024)} %param.9) | copy-start | bytes 24580
  72.0 31.9 %collective-permute-start.3 = (bf16[512,512]{1,0:T(8,128)(2,1)}, bf16[512,512]{1,0:T(8,128)(2,1)}, u32[]{:S(2)}, u32[]{:S(2)}) collective-permute-start(bf16[512,512]{1,0:T(8,128)(2,1)} %select_select_fusion.1), channel_id=1, source_target_pairs={{4,0},{12,4},{8,12},{0,8},{5,1},{13,5},{9,13},{1,9},{6,2},{14,6},{... | collective-permute-start | bytes 1572872 | tf_op jit(solution)/shard_map/ppermute | solution.py:406
  93.8 20.0 %collective-permute-start.12 = (bf16[512,512]{1,0:T(8,128)(2,1)S(1)}, bf16[512,512]{1,0:T(8,128)(2,1)S(1)}, u32[]{:S(2)}, u32[]{:S(2)}) collective-permute-start(bf16[512,512]{1,0:T(8,128)(2,1)S(1)} %select_select_fusion), channel_id=1, source_target_pairs={{4,0},{12,4},{8,12},{0,8},{5,1},{13,5},{9,13},{1,9},{6,2},{14,6},{... | collective-permute-start | bytes 1572872 | tf_op jit(solution)/shard_map/ppermute | solution.py:406
  93.9 2.8 %copy-start.2 = (bf16[3,512,2048]{2,1,0:T(8,128)(2,1)S(1)}, bf16[3,512,2048]{2,1,0:T(8,128)(2,1)}, u32[]{:S(2)}) copy-start(bf16[3,512,2048]{2,1,0:T(8,128)(2,1)} %param.10) | copy-start | bytes 18874372
  101.3 41.2 %copy-start.15 = (bf16[2048,512]{1,0:T(8,128)(2,1)}, bf16[2048,512]{1,0:T(8,128)(2,1)S(1)}, u32[]{:S(2)}) copy-start(bf16[2048,512]{1,0:T(8,128)(2,1)S(1)} %get-tuple-element.12) | copy-start | bytes 6291460
  109.9 3.9 %copy-start.7 = (bf16[512,512]{1,0:T(8,128)(2,1)S(1)}, bf16[512,512]{1,0:T(8,128)(2,1)}, u32[]{:S(2)}) copy-start(bf16[512,512]{1,0:T(8,128)(2,1)} %copy-done.6) | copy-start | bytes 1572868
  110.0 27.8 %collective-permute-start.4 = (bf16[1024,512]{1,0:T(8,128)(2,1)S(1)}, bf16[1024,512]{1,0:T(8,128)(2,1)S(1)}, u32[]{:S(2)}, u32[]{:S(2)}) collective-permute-start(bf16[1024,512]{1,0:T(8,128)(2,1)S(1)} %slice.28), channel_id=1, source_target_pairs={{0,16},{16,0},{1,17},{17,1},{2,18},{18,2},{3,19},{19,3},{4,20},{20... | collective-permute-start | bytes 3145736 | tf_op jit(solution)/shard_map/ppermute | solution.py:454
  119.5 18.3 %copy-start.11 = (s32[16,16]{1,0:T(8,128)S(1)}, s32[16,16]{1,0:T(8,128)}, u32[]{:S(2)}) copy-start(s32[16,16]{1,0:T(8,128)} %mask_ref.3) | copy-start | bytes 3076
  119.5 18.3 %copy-start.13 = (s32[16]{0:T(128)S(1)}, s32[16]{0:T(128)}, u32[]{:S(2)}) copy-start(s32[16]{0:T(128)} %order_ref.9) | copy-start | bytes 196
  120.6 33.5 %collective-permute-start.13 = (bf16[1024,512]{1,0:T(8,128)(2,1)}, bf16[1024,512]{1,0:T(8,128)(2,1)}, u32[]{:S(2)}, u32[]{:S(2)}) collective-permute-start(bf16[1024,512]{1,0:T(8,128)(2,1)} %slice.29), channel_id=1, source_target_pairs={{0,16},{16,0},{1,17},{17,1},{2,18},{18,2},{3,19},{19,3},{4,20},{20... | collective-permute-start | bytes 3145736 | tf_op jit(solution)/shard_map/ppermute | solution.py:459
  137.8 4.8 %copy-start = (bf16[1024,512]{1,0:T(8,128)(2,1)}, bf16[1024,512]{1,0:T(8,128)(2,1)S(1)}, u32[]{:S(2)}) copy-start(bf16[1024,512]{1,0:T(8,128)(2,1)S(1)} %collective-permute-done.4.refs_1_.refs_3_.refs_5_) | copy-start | bytes 3145732
  142.5 0.8 copy-start.8
  144.6 20.8 %collective-permute-start.5 = (bf16[512,512]{1,0:T(8,128)(2,1)}, bf16[512,512]{1,0:T(8,128)(2,1)}, u32[]{:S(2)}, u32[]{:S(2)}) collective-permute-start(bf16[512,512]{1,0:T(8,128)(2,1)} %convolution_convert_fusion.5), channel_id=1, source_target_pairs={{0,4},{4,12},{12,8},{8,0},{1,5},{5,13},{13,9},{9,1},{2,6},{6,14},{... | collective-permute-start | bytes 1572872 | tf_op jit(solution)/shard_map/ppermute | solution.py:423
  154.1 1.2 copy-start.1
  155.3 9.2 %copy-start.16 = (bf16[2048,512]{1,0:T(8,128)(2,1)S(1)}, bf16[2048,512]{1,0:T(8,128)(2,1)}, u32[]{:S(2)}) copy-start(bf16[2048,512]{1,0:T(8,128)(2,1)} %copy-done.15) | copy-start | bytes 6291460
  155.3 10.1 %copy-start.9 = (bf16[512,512]{1,0:T(8,128)(2,1)S(1)}, bf16[512,512]{1,0:T(8,128)(2,1)}, u32[]{:S(2)}) copy-start(bf16[512,512]{1,0:T(8,128)(2,1)} %copy-done.8) | copy-start | bytes 1572868
  165.0 18.3 %collective-permute-start.14 = (bf16[512,512]{1,0:T(8,128)(2,1)S(1)}, bf16[512,512]{1,0:T(8,128)(2,1)S(1)}, u32[]{:S(2)}, u32[]{:S(2)}) collective-permute-start(bf16[512,512]{1,0:T(8,128)(2,1)S(1)} %convolution_convert_fusion.1), channel_id=1, source_target_pairs={{0,4},{4,12},{12,8},{8,0},{1,5},{5,13},{13,9},{9,1},{2,6},{6,14},{... | collective-permute-start | bytes 1572872 | tf_op jit(solution)/shard_map/ppermute | solution.py:423
  166.9 29.6 %collective-permute-start.6 = (bf16[512,512]{1,0:T(8,128)(2,1)S(1)}, bf16[512,512]{1,0:T(8,128)(2,1)S(1)}, u32[]{:S(2)}, u32[]{:S(2)}) collective-permute-start(bf16[512,512]{1,0:T(8,128)(2,1)S(1)} %fusion.15), channel_id=1, source_target_pairs={{4,0},{8,4},{12,8},{0,12},{5,1},{9,5},{13,9},{1,13},{6,2},{10,6},{... | collective-permute-start | bytes 1572872 | tf_op jit(solution)/shard_map/ppermute | solution.py:424
  171.9 32.3 %collective-permute-start.7 = (bf16[512,512]{1,0:T(8,128)(2,1)S(1)}, bf16[512,512]{1,0:T(8,128)(2,1)S(1)}, u32[]{:S(2)}, u32[]{:S(2)}) collective-permute-start(bf16[512,512]{1,0:T(8,128)(2,1)S(1)} %fusion.14), channel_id=1, source_target_pairs={{0,4},{4,8},{8,12},{12,0},{1,5},{5,9},{9,13},{13,1},{2,6},{6,10},{... | collective-permute-start | bytes 1572872 | tf_op jit(solution)/shard_map/ppermute | solution.py:425
  183.7 29.2 %collective-permute-start.15 = (bf16[512,512]{1,0:T(8,128)(2,1)S(1)}, bf16[512,512]{1,0:T(8,128)(2,1)S(1)}, u32[]{:S(2)}, u32[]{:S(2)}) collective-permute-start(bf16[512,512]{1,0:T(8,128)(2,1)S(1)} %fusion.13), channel_id=1, source_target_pairs={{4,0},{8,4},{12,8},{0,12},{5,1},{9,5},{13,9},{1,13},{6,2},{10,6},{... | collective-permute-start | bytes 1572872 | tf_op jit(solution)/shard_map/ppermute | solution.py:424
  196.0 23.3 %collective-permute-start.16 = (bf16[512,512]{1,0:T(8,128)(2,1)S(1)}, bf16[512,512]{1,0:T(8,128)(2,1)S(1)}, u32[]{:S(2)}, u32[]{:S(2)}) collective-permute-start(bf16[512,512]{1,0:T(8,128)(2,1)S(1)} %fusion.12), channel_id=1, source_target_pairs={{0,4},{4,8},{8,12},{12,0},{1,5},{5,9},{9,13},{13,1},{2,6},{6,10},{... | collective-permute-start | bytes 1572872 | tf_op jit(solution)/shard_map/ppermute | solution.py:425
where the time goes:
time: 223 us; the launch traced here: 222 us
  waiting for transfers between devices  109 us (49%)
  Pallas kernels  52 us (23%)
  starting transfers between devices  42.2 us (19%)
  local copies, waits for them, and re-layouts  10.3 us (5%)
  matrix products  7.49 us (3%)
    ppermute x2, waiting for transfers between devices, gather_blocks(): before = lax.ppermute(block, 'tp', FORWARD)  24.6 us
    pallas_call x2, Pallas kernels, conv_call(): pl.pallas_call(functools.partial(conv_body, with_before), grid_spec=pltpu...  19 us
    ppermute x1, waiting for transfers between devices, per_device_fast(): peer_a = lax.ppermute(own_a[cols:], 'seq', swap)  15.4 us
    ppermute x2, starting transfers between devices, reduce_blocks(): back = lax.ppermute(plus(partial(1), across, here == 2), 'tp', BACKWARD)  15.4 us
    ppermute x2, waiting for transfers between devices, reduce_blocks(): onward = lax.ppermute(plus(partial(2), across, here == 1), 'tp', FORWARD)  14 us
    pallas_call x2, Pallas kernels, attend_call(): pl.pallas_call(functools.partial(attend_body, chunk), grid_spec=pltpu.Pre...  14 us
    pallas_call x2, Pallas kernels, project_call(): pl.pallas_call(functools.partial(project_body, rows // 3 // block), grid=...  11.6 us
    ppermute x2, waiting for transfers between devices, reduce_blocks(): across = lax.ppermute(sent, 'tp', FOLDED)  11.3 us
  transfers between devices with their start and end apart: 17, of which 12 were waited for; matrix products, arithmetic and copies ran while one was open for 4% of the time, Pallas kernels for 22%

commit v1 on v0

--- a/solution.py
+++ b/solution.py
@@ -89,38 +89,43 @@
 
     taps_scr[:, :TAPS] = taps_ref[...].T
     group = 16
-    lane = lax.broadcasted_iota(jnp.int32, (group, FRAME), 1)
+    part = 8
+    lane = lax.broadcasted_iota(jnp.int32, (part, FRAME), 1)
+
+    def frame_of(ref, rows, frame, piece):
+        wide = ref[rows, frame * FRAME : (frame + 1) * FRAME].astype(jnp.float32)
+        return column_shifts(wide[piece * part : (piece + 1) * part], lane)
 
     def advance(step, carry):
-        rows = pl.ds(pl.multiple_of(step * group, group), group)
-        taps = taps_scr[rows, :]
-        if with_before:
-            old = [
-                column_shifts(before_ref[rows, f * FRAME : (f + 1) * FRAME].astype(jnp.float32), lane)
-                for f in range(2)
-            ]
-            sums = [
-                part_ref[rows, :FRAME] + taps_applied([(0, old[0]), (1, old[1])], taps, lane),
-                part_ref[rows, FRAME:] + taps_applied([(0, old[1])], taps, lane),
-            ]
-        else:
-            now = [
-                column_shifts(tokens_ref[rows, f * FRAME : (f + 1) * FRAME].astype(jnp.float32), lane)
-                for f in range(2)
-            ]
-            sums = [
-                now[0][1] + taps_applied([(2, now[0])], taps, lane),
-                now[1][1] + taps_applied([(1, now[0]), (2, now[1])], taps, lane),
-            ]
-            part_ref[rows, :FRAME] = sums[0]
-            part_ref[rows, FRAME:] = sums[1]
+        start = pl.multiple_of(step * group, group)
+        rows = pl.ds(start, group)
+        pieces = []
+        for piece in range(group // part):
+            inner = pl.ds(start + piece * part, part)
+            taps = taps_scr[inner, :]
+            if with_before:
+                old = [frame_of(before_ref, rows, f, piece) for f in range(2)]
+                sums = [
+                    part_ref[inner, :FRAME] + taps_applied([(0, old[0]), (1, old[1])], taps, lane),
+                    part_ref[inner, FRAME:] + taps_applied([(0, old[1])], taps, lane),
+                ]
+            else:
+                now = [frame_of(tokens_ref, rows, f, piece) for f in range(2)]
+                sums = [
+                    now[0][1] + taps_applied([(2, now[0])], taps, lane),
+                    now[1][1] + taps_applied([(1, now[0]), (2, now[1])], taps, lane),
+                ]
+                part_ref[inner, :FRAME] = sums[0]
+                part_ref[inner, FRAME:] = sums[1]
+            pieces.append(sums)
         for tile in range(tiles_dev):
             frame, spot = divmod(tile * TILE, FRAME)
             place = pl.ds(pl.multiple_of(slots_ref[tile] * TILE, TILE), TILE)
-            packed[rows, place] = sums[frame][:, spot : spot + TILE].astype(jnp.bfloat16)
+            joined = jnp.concatenate([sums[frame][:, spot : spot + TILE] for sums in pieces], axis=0)
+            packed[rows, place] = joined.astype(jnp.bfloat16)
         return carry
 
-    lax.fori_loop(0, channels // group, advance, 0)
+    lax.fori_loop(0, channels // group, advance, 0, unroll=2)
     keep_ref[...] = packed[:, : tokens // 2]
     send_ref[...] = packed[:, tokens // 2 :]
 
@@ -189,7 +194,7 @@
             jax.ShapeDtypeStruct((kinds * cols, channels), jnp.bfloat16),
             jax.ShapeDtypeStruct((channels, cols), jnp.bfloat16),
         ],
-        compiler_params=params(),
+        compiler_params=params(VMEM_WHOLE),
         cost_estimate=pl.CostEstimate(
             flops=kinds * cols * channels, bytes_accessed=16 * cols * channels, transcendentals=0
         ),
@@ -197,44 +202,50 @@
     )(blocks, norm_gain[None, :], qkv_weight.reshape(kinds * cols, channels), out_weight)
 
 
-def project_body(query_steps, weight_ref, *refs):
-    shards, out_ref, inverse_ref = refs[:-2], refs[-2], refs[-1]
-    width = shards[0].shape[0]
+def project_body(query_steps, ends_ref, weight_ref, own, before, after, across, far, out_ref, tokens_ref, inverse_ref):
+    width = own.shape[0]
     step = pl.program_id(0)
 
     @pl.when(step == 0)
     def _():
+        at_start, at_stop = ends_ref[0] == 1, ends_ref[1] == 1
         squares = None
-        for shard in shards:
-            wide = shard[...].astype(jnp.float32)
+        shards = (
+            own[...],
+            jnp.where(at_start, far[...], before[...]),
+            jnp.where(at_stop, far[...], after[...]),
+            across[...],
+        )
+        for index, shard in enumerate(shards):
+            tokens_ref[index * width : (index + 1) * width, :] = shard
+            wide = shard.astype(jnp.float32)
             term = jnp.sum(wide * wide, axis=0, keepdims=True)
             squares = term if squares is None else squares + term
         inverse_ref[...] = lax.rsqrt(squares / (width * len(shards)) + EPSILON)
 
-    total = None
-    for index, shard in enumerate(shards):
-        term = jnp.dot(
-            weight_ref[:, index * width : (index + 1) * width],
-            shard[...],
-            preferred_element_type=jnp.float32,
-        )
-        total = term if total is None else total + term
+    total = jnp.dot(weight_ref[...], tokens_ref[...], preferred_element_type=jnp.float32)
     scale = jnp.where(step < query_steps, LOG2E / math.sqrt(HEAD), 1.0)
     out_ref[...] = (total * (inverse_ref[...] * scale)).astype(jnp.bfloat16)
 
 
-def project_call(weights, shards):
+def project_call(ends, weights, shards):
     rows, channels = weights.shape
     width, tokens = shards[0].shape
     block = 256
-    whole = pl.BlockSpec((width, tokens), lambda i: (0, 0))
+    whole = pl.BlockSpec((width, tokens), lambda i, *_: (0, 0))
     return pl.pallas_call(
         functools.partial(project_body, rows // 3 // block),
-        grid=(rows // block,),
-        in_specs=[pl.BlockSpec((block, channels), lambda i: (i, 0))] + [whole] * len(shards),
-        out_specs=pl.BlockSpec((block, tokens), lambda i: (i, 0)),
+        grid_spec=pltpu.PrefetchScalarGridSpec(
+            num_scalar_prefetch=1,
+            grid=(rows // block,),
+            in_specs=[pl.BlockSpec((block, channels), lambda i, *_: (i, 0))] + [whole] * len(shards),
+            out_specs=pl.BlockSpec((block, tokens), lambda i, *_: (i, 0)),
+            scratch_shapes=[
+                pltpu.VMEM((channels, tokens), jnp.bfloat16),
+                pltpu.VMEM((1, tokens), jnp.float32),
+            ],
+        ),
         out_shape=jax.ShapeDtypeStruct((rows, tokens), jnp.bfloat16),
-        scratch_shapes=[pltpu.VMEM((1, tokens), jnp.float32)],
         compiler_params=params(),
         cost_estimate=pl.CostEstimate(
             flops=2 * rows * channels * tokens,
@@ -242,7 +253,7 @@
             transcendentals=0,
         ),
         name="project",
-    )(weights, *shards)
+    )(ends, weights, *shards)
 
 
 def tile_lists(order_ref, ids_ref, seq_here, tiles_dev):
@@ -260,10 +271,17 @@
             second = second + late
 
 
-def attend_body(chunk, seq_ref, order_ref, mask_ref, query_ref, *refs):
-    count = 2 * (chunk + 1)
+def attend_body(chunk, sources, goes_on, ends, seq_ref, order_ref, mask_ref, query_ref, *refs):
+    count = len(sources)
     keys, values = refs[:count], refs[count : 2 * count]
-    out_ref, ids_ref, scores_ref = refs[2 * count], refs[2 * count + 1], refs[2 * count + 2]
+    refs = refs[2 * count :]
+    if goes_on:
+        old_stats, old_weighted, refs = refs[0], refs[1], refs[2:]
+    if ends:
+        out_ref, refs = refs[0], refs[1:]
+    else:
+        new_stats, new_weighted, refs = refs[0], refs[1], refs[2:]
+    ids_ref, scores_ref = refs
     tokens = query_ref.shape[1]
     half = tokens // TILE
 
@@ -273,9 +291,10 @@
 
     query = query_ref[...]
     lane_tile = lax.broadcasted_iota(jnp.int32, (1, tokens), 1) // TILE
-    top = None
-    for source in range(count):
-        block = jnp.dot(keys[source][...].T, query, preferred_element_type=jnp.float32)
+    old_top = old_stats[0, 0:1, :] if goes_on else None
+    top = old_top
+    for index, source in enumerate(sources):
+        block = jnp.dot(keys[index][...].T, query, preferred_element_type=jnp.float32)
         for spot in range(half):
             key_tile = ids_ref[source * half + spot]
             bias = jnp.zeros((1, tokens), jnp.float32)
@@ -284,64 +303,77 @@
                 blocked = jnp.where(mask_ref[query_tile, key_tile] == 1, 0.0, MASKED_SCORE)
                 bias = jnp.where(lane_tile == query_spot, blocked, bias)
             piece = block[spot * TILE : (spot + 1) * TILE, :] + bias
-            scores_ref[source * tokens + spot * TILE : source * tokens + (spot + 1) * TILE, :] = piece
+            scores_ref[index * tokens + spot * TILE : index * tokens + (spot + 1) * TILE, :] = piece
             best = jnp.max(piece, axis=0, keepdims=True)
             top = best if top is None else jnp.maximum(top, best)
     denom = None
     weighted = None
-    for source in range(count):
-        powers = jnp.exp2(scores_ref[source * tokens : (source + 1) * tokens, :] - top)
+    if goes_on:
+        shrink = jnp.exp2(old_top - top)
+        denom = old_stats[0, 1:2, :] * shrink
+        weighted = old_weighted[...] * shrink
+    for index in range(count):
+        powers = jnp.exp2(scores_ref[index * tokens : (index + 1) * tokens, :] - top)
         summed = jnp.sum(powers, axis=0, keepdims=True)
         term = jnp.dot(
-            values[source][...], powers.astype(jnp.bfloat16), preferred_element_type=jnp.float32
+            values[index][...], powers.astype(jnp.bfloat16), preferred_element_type=jnp.float32
         )
         denom = summed if denom is None else denom + summed
         weighted = term if weighted is None else weighted + term
-    out_ref[...] = (weighted / denom).astype(jnp.bfloat16)
-
-
-def attend_call(chunk, seq_here, stripe_order, tile_mask, own, peers):
-    rows, tokens = own[0].shape
+    if ends:
+        out_ref[...] = (weighted / denom).astype(jnp.bfloat16)
+    else:
+        new_stats[0, 0:1, :] = top
+        new_stats[0, 1:2, :] = denom
+        new_weighted[...] = weighted
+
+
+def attend_call(chunk, tables, query_from, sources, state=None, ends=True):
+    rows, tokens = query_from.shape
     heads = rows // 3 // HEAD
-    sources = []
-    for mine, other in zip(own, peers):
-        sources += [(mine, heads, 2 * heads), (other, 0, heads)]
 
     def spec(start):
         return pl.BlockSpec((HEAD, tokens), lambda h, *_, start=start: (start + h, 0))
 
     count = len(sources)
+    stats_spec = pl.BlockSpec((1, 2, tokens), lambda h, *_: (h, 0, 0))
+    state_specs = [stats_spec, spec(0)]
+    state_shapes = [
+        jax.ShapeDtypeStruct((heads, 2, tokens), jnp.float32),
+        jax.ShapeDtypeStruct((heads * HEAD, tokens), jnp.float32),
+    ]
+    goes_on = state is not None
+    in_specs = [spec(0)]
+    in_specs += [spec(first // HEAD) for _, first, _ in sources]
+    in_specs += [spec(first // HEAD + heads) for _, first, _ in sources]
+    arguments = [query_from] + [array for array, _, _ in sources] * 2
+    if goes_on:
+        in_specs += state_specs
+        arguments += list(state)
     return pl.pallas_call(
-        functools.partial(attend_body, chunk),
+        functools.partial(attend_body, chunk, tuple(s for _, _, s in sources), goes_on, ends),
         grid_spec=pltpu.PrefetchScalarGridSpec(
             num_scalar_prefetch=3,
             grid=(heads,),
-            in_specs=[spec(0)] + [spec(k) for _, k, _ in sources] + [spec(v) for _, _, v in sources],
-            out_specs=spec(0),
+            in_specs=in_specs,
+            out_specs=spec(0) if ends else state_specs,
             scratch_shapes=[
                 pltpu.SMEM((4 * tokens // TILE,), jnp.int32),
                 pltpu.VMEM((count * tokens, tokens), jnp.float32),
             ],
         ),
-        out_shape=jax.ShapeDtypeStruct((heads * HEAD, tokens), jnp.bfloat16),
+        out_shape=jax.ShapeDtypeStruct((heads * HEAD, tokens), jnp.bfloat16) if ends else state_shapes,
         compiler_params=params(),
         cost_estimate=pl.CostEstimate(
             flops=4 * heads * HEAD * tokens * tokens * count,
             bytes_accessed=2 * heads * HEAD * tokens * (2 + 2 * count),
             transcendentals=heads * tokens * tokens * count,
         ),
-    )(
-        seq_here,
-        stripe_order,
-        tile_mask,
-        own[chunk],
-        *[array for array, _, _ in sources],
-        *[array for array, _, _ in sources],
-    )
+    )(*tables, *arguments)
 
 
 def place_body(seq_ref, order_ref, ends_ref, first_ref, *refs):
-    parts, out_ref, second_ref = refs[:4], refs[4], refs[5]
+    parts, out_ref, second_ref = refs[:5], refs[5], refs[6]
     _, tokens = first_ref.shape
     tiles_dev = 2 * tokens // TILE
     seq_here = seq_ref[0]
@@ -350,7 +382,8 @@
         parts[0][...].astype(jnp.float32)
         + parts[1][...].astype(jnp.float32)
         + parts[2][...].astype(jnp.float32)
-        + jnp.where(at_end, parts[3][...].astype(jnp.float32), 0.0)
+        + parts[3][...].astype(jnp.float32)
+        + jnp.where(at_end, parts[4][...].astype(jnp.float32), 0.0)
     )
     second_ref[...] = total.astype(jnp.bfloat16)
     ranks = [jnp.int32(0), jnp.int32(0)]
@@ -380,7 +413,7 @@
         grid_spec=pltpu.PrefetchScalarGridSpec(
             num_scalar_prefetch=3,
             grid=(channels // block,),
-            in_specs=[slim] * 5,
+            in_specs=[slim] * 6,
             out_specs=pl.BlockSpec((block, 2 * tokens), lambda i, *_: (i, 0)),
             scratch_shapes=[pltpu.VMEM((block, tokens), jnp.bfloat16)],
         ),
@@ -393,18 +426,20 @@
     )(seq_here, stripe_order, at_end, first, *parts)
 
 
-FORWARD = [(0, 1), (1, 2), (2, 3), (3, 0)]
-BACKWARD = [(1, 0), (2, 1), (3, 2), (0, 3)]
+UP = [(0, 1), (1, 2), (2, 3)]
+DOWN = [(1, 0), (2, 1), (3, 2)]
+ENDS = [(0, 3), (3, 0)]
 FOLDED = [(0, 1), (1, 3), (3, 2), (2, 0)]
 UNFOLDED = [(1, 0), (3, 1), (2, 3), (0, 2)]
 
 
 def gather_blocks(block, here):
-    before = lax.ppermute(block, "tp", FORWARD)
-    after = lax.ppermute(block, "tp", BACKWARD)
+    before = lax.ppermute(block, "tp", UP)
+    after = lax.ppermute(block, "tp", DOWN)
+    far = lax.ppermute(block, "tp", ENDS)
     relay = jnp.where(here == 2, before, jnp.where(here == 1, after, block))
     across = lax.ppermute(relay, "tp", UNFOLDED)
-    return (block, before, after, across)
+    return (block, before, after, across, far)
 
 
 def plus(a, b, chosen):
@@ -421,9 +456,11 @@
 
     sent = partial(3)
     across = lax.ppermute(sent, "tp", FOLDED)
-    back = lax.ppermute(plus(partial(1), across, here == 2), "tp", BACKWARD)
-    onward = lax.ppermute(plus(partial(2), across, here == 1), "tp", FORWARD)
-    return (partial(0), back, onward, across)
+    down, up = lax.optimization_barrier((partial(1), partial(2)))
+    far = lax.ppermute(jnp.where(here == 0, down, up), "tp", ENDS)
+    back = lax.ppermute(plus(down, across, here == 2), "tp", DOWN)
+    onward = lax.ppermute(plus(up, across, here == 1), "tp", UP)
+    return (partial(0), back, onward, far, across)
 
 
 def per_device_fast(
@@ -433,7 +470,9 @@
     here = lax.axis_index("tp")
     seq_here = seq.astype(jnp.int32)[None]
     at_end = ((here == 0) | (here == 3)).astype(jnp.int32)[None]
+    ends = jnp.stack([here == 0, here == 3]).astype(jnp.int32)
     blocks = jnp.stack([here, (here + 3) % 4, (here + 1) % 4, (here + 2) % 4]).astype(jnp.int32)
+    tables = (seq_here, stripe_order, tile_mask)
 
     part, keep_a, send_a = conv_call(seq_here, stripe_order, clip_tokens, conv_taps)
     got_a = lax.ppermute(send_a, "seq", [(0, 1)])
@@ -447,25 +486,22 @@
     got_b = lax.ppermute(send_b, "seq", [(1, 0)])
     tokens_b = jnp.where(seq == 1, keep_b, got_b)
 
-    rows = weights.shape[0]
-    cols = rows // 3
+    cols = weights.shape[0] // 3
     swap = [(0, 1), (1, 0)]
-    own_a = project_call(weights, shards_a)
+    own_a = project_call(ends, weights, shards_a)
     peer_a = lax.ppermute(own_a[cols:], "seq", swap)
     shards_b = gather_blocks(tokens_b, here)
-    out_a = attend_call(0, seq_here, stripe_order, tile_mask, [own_a], [peer_a])
+    out_a = attend_call(0, tables, own_a, [(own_a, cols, 0), (peer_a, 0, 1)])
     parts_a = reduce_blocks(out_t, out_a, here)
-    own_b = project_call(weights, shards_b)
+    own_b = project_call(ends, weights, shards_b)
     peer_b = lax.ppermute(own_b[cols:], "seq", swap)
-    out_b = attend_call(1, seq_here, stripe_order, tile_mask, [own_a, own_b], [peer_a, peer_b])
+    near = [(own_a, cols, 0), (peer_a, 0, 1), (own_b, cols, 2)]
+    state = attend_call(1, tables, own_b, near, ends=False)
+    out_b = attend_call(1, tables, own_b, [(peer_b, 0, 3)], state=state)
     parts_b = reduce_blocks(out_t, out_b, here)
-    first = (
-        parts_a[0].astype(jnp.float32)
-        + parts_a[1].astype(jnp.float32)
-        + parts_a[2].astype(jnp.float32)
-        + jnp.where(at_end == 1, parts_a[3].astype(jnp.float32), 0.0)
-    ).astype(jnp.bfloat16)
-    return place_call(seq_here, stripe_order, at_end, first, parts_b)
+    first = sum(part.astype(jnp.float32) for part in parts_a[:4])
+    first = first + jnp.where(at_end == 1, parts_a[4].astype(jnp.float32), 0.0)
+    return place_call(seq_here, stripe_order, at_end, first.astype(jnp.bfloat16), parts_b)
 
 
 def passed_along(block, axis, distance):

time: 223 us -> 223 us (level)
  waiting for transfers between devices: 109 us -> 65.6 us
  starting transfers between devices: 42.2 us -> 74.8 us
  Pallas kernels: 52 us -> 61.6 us
  matrix products: 7.49 us -> 3.69 us
  other arithmetic: 1.15 us -> 4.28 us
    ppermute x8 -> x12, waiting for transfers between devices: 51.6 us -> 10.8 us  [the longest x2 7.21 us: reduce_blocks(): back = lax.ppermute(plus(down, across, here == 2), 'tp', DOWN)]
    ppermute x8 -> x12, starting transfers between devices: 22.8 us -> 62.2 us  [the longest x2 26.7 us: reduce_blocks(): onward = lax.ppermute(plus(up, across, here == 1), 'tp', UP)]
    ppermute x1, waiting for transfers between devices: 15.4 us -> 0.01 us  [per_device_fast(): peer_a = lax.ppermute(own_a[cols:], 'seq', swap)]
    ppermute x1, waiting for transfers between devices: 0.01 us -> 11.2 us  [per_device_fast(): got_a = lax.ppermute(send_a, 'seq', [(0, 1)])]
    ppermute x1, waiting for transfers between devices: 7.97 us -> 0.01 us  [per_device_fast(): peer_b = lax.ppermute(own_b[cols:], 'seq', swap)]
    ppermute x2, waiting for transfers between devices: 2.64 us -> 9.49 us  [gather_blocks(): across = lax.ppermute(relay, 'tp', UNFOLDED)]
    pallas_call x1, Pallas kernels: 4.6 us -> 8.51 us  [prepare_weights(): pl.pallas_call(prepare_body, grid_spec=pltpu.PrefetchScalarGridSpec(num_s...]
    dot_general x8, matrix products: 7.49 us -> 3.69 us  [partial(): jnp.dot(block, heads_out, preferred_element_type=jnp.float32)]
  transfers between devices with their start and end apart: 17 -> 21, of which waited for: 12 -> 7; matrix products, arithmetic and copies ran while one was open for 4% -> 4% of each run, Pallas kernels for 22% -> 21%
where the time goes in v1:
time: 223 us; the launch traced here: 222 us
  starting transfers between devices  74.8 us (34%)
  waiting for transfers between devices  65.6 us (29%)
  Pallas kernels  61.6 us (28%)
  local copies, waits for them, and re-layouts  12 us (5%)
  other arithmetic  4.28 us (2%)
  matrix products  3.69 us (2%)
    ppermute x2, starting transfers between devices, reduce_blocks(): onward = lax.ppermute(plus(up, across, here == 1), 'tp', UP)  26.7 us
    pallas_call x2, Pallas kernels, conv_call(): pl.pallas_call(functools.partial(conv_body, with_before), grid_spec=pltpu...  22.3 us
    pallas_call x3, Pallas kernels, attend_call(): pl.pallas_call(functools.partial(attend_body, chunk, tuple((s for _, _, s...  15.2 us
    ppermute x1, waiting for transfers between devices, per_device_fast(): before = lax.ppermute(clip_tokens, 'seq', [(0, 1)])  14.6 us
    ppermute x2, starting transfers between devices, gather_blocks(): far = lax.ppermute(block, 'tp', ENDS)  12.8 us
    pallas_call x2, Pallas kernels, project_call(): pl.pallas_call(functools.partial(project_body, rows // 3 // block), grid_...  12.8 us
    ppermute x2, waiting for transfers between devices, reduce_blocks(): across = lax.ppermute(sent, 'tp', FOLDED)  12.3 us
    ppermute x1, waiting for transfers between devices, per_device_fast(): got_a = lax.ppermute(send_a, 'seq', [(0, 1)])  11.2 us
  transfers between devices with their start and end apart: 21, of which 7 were waited for; matrix products, arithmetic and copies ran while one was open for 4% of the time, Pallas kernels for 21%

profile of v1, /device:TPU:0, one launch (start us, length us, event | category | flops | bytes accessed | tf_op | source)
XLA Modules:
  0.0 222.3 jit_solution(5028764357482870984)
XLA Ops:
  0.0 12.0 %conv_here.1 = (f32[512,1024]{1,0:T(8,128)}, bf16[512,512]{1,0:T(8,128)(2,1)}, bf16[512,512]{1,0:T(8,128)(2,1)}) custom-call(s32[1]{0:T(128)} %bitcast.seq_ref, s32[16]{0:T(128)} %order_ref.11, bf16[512,1024]{1,0:T(8,128)(2,1)} %refs_0_.3, f32[27,512]{1,0:T(8,128)} %refs_1_.3), custom_call_target="tpu_custom_call" | custom-call | flops 14155776 | bytes 4194304 | tf_op jit(solution)/shard_map/conv_here/pallas_call | solution.py:147
  12.0 4.9 %collective-permute-start = (bf16[512,512]{1,0:T(8,128)(2,1)}, bf16[512,512]{1,0:T(8,128)(2,1)S(1)}, u32[]{:S(2)}, u32[]{:S(2)}) collective-permute-start(bf16[512,512]{1,0:T(8,128)(2,1)} %get-tuple-element.21), channel_id=1, source_target_pairs={{0,16},{1,17},{2,18},{3,19},{4,20},{5,21},{6,22},{7,23},{8,24},{9,... | collective-permute-start | bytes 1572872 | tf_op jit(solution)/shard_map/ppermute | solution.py:478
  16.9 1.4 collective-permute-start.10
  18.3 11.2 %collective-permute-done = bf16[512,512]{1,0:T(8,128)(2,1)S(1)} collective-permute-done((bf16[512,512]{1,0:T(8,128)(2,1)}, bf16[512,512]{1,0:T(8,128)(2,1)S(1)}, u32[]{:S(2)}, u32[]{:S(2)}) %collective-permute-start) | collective-permute-done | bytes 524320 | tf_op jit(solution)/shard_map/ppermute | solution.py:478
  29.5 1.1 broadcast_select_fusion.3.own
  30.6 4.3 %collective-permute-start.1 = (bf16[512,512]{1,0:T(8,128)(2,1)S(1)}, bf16[512,512]{1,0:T(8,128)(2,1)}, u32[]{:S(2)}, u32[]{:S(2)}) collective-permute-start(bf16[512,512]{1,0:T(8,128)(2,1)S(1)} %broadcast_select_fusion.3.own), channel_id=1, source_target_pairs={{0,4},{4,8},{8,12},{1,5},{5,9},{9,13},{2,6},{6,10},{10,14},{3,7},{... | collective-permute-start | bytes 1572872 | tf_op jit(solution)/shard_map/ppermute | solution.py:437
  34.9 1.3 collective-permute-start.2
  36.2 14.6 %collective-permute-done.10.refs_2_ = bf16[512,1024]{1,0:T(8,128)(2,1)S(1)} collective-permute-done((bf16[512,1024]{1,0:T(8,128)(2,1)}, bf16[512,1024]{1,0:T(8,128)(2,1)S(1)}, u32[]{:S(2)}, u32[]{:S(2)}) %collective-permute-start.10) | collective-permute-done | bytes 1048608 | tf_op jit(solution)/shard_map/ppermute | solution.py:479
  50.8 1.6 copy-done.1
  52.4 10.3 %conv_before.1 = (bf16[512,512]{1,0:T(8,128)(2,1)S(1)}, bf16[512,512]{1,0:T(8,128)(2,1)}) custom-call(s32[1]{0:T(128)} %bitcast.seq_ref, s32[16]{0:T(128)S(1)} %copy-done.6, bf16[512,1024]{1,0:T(8,128)(2,1)S(1)} %copy-done, f32[27,512]{1,0:T(8,128)S(1)} %copy-done.4, bf16[512,1024]{1,0:T(8,128)(2,1)S(1)} %collective-permute-done.10.refs_2_, ...), custom_call_target="tpu_custom_call" | custom-call | flops 14155776 | bytes 4194304 | tf_op jit(solution)/shard_map/conv_before/pallas_call | solution.py:147
  62.7 1.3 collective-permute-start.11
  64.0 5.5 %collective-permute-start.4 = (bf16[512,512]{1,0:T(8,128)(2,1)S(1)}, bf16[512,512]{1,0:T(8,128)(2,1)S(1)}, u32[]{:S(2)}, u32[]{:S(2)}) collective-permute-start(bf16[512,512]{1,0:T(8,128)(2,1)S(1)} %broadcast_select_fusion.3.own), channel_id=1, source_target_pairs={{0,12},{12,0},{1,13},{13,1},{2,14},{14,2},{3,15},{15,3},{16,28},{2... | collective-permute-start | bytes 1572872 | tf_op jit(solution)/shard_map/ppermute | solution.py:439
  69.5 0.9 select_select_fusion.1
  70.4 7.2 %collective-permute-done.11 = bf16[512,512]{1,0:T(8,128)(2,1)S(1)} collective-permute-done((bf16[512,512]{1,0:T(8,128)(2,1)}, bf16[512,512]{1,0:T(8,128)(2,1)S(1)}, u32[]{:S(2)}, u32[]{:S(2)}) %collective-permute-start.11) | collective-permute-done | bytes 524320 | tf_op jit(solution)/shard_map/ppermute | solution.py:486
  77.7 3.5 %collective-permute-start.12 = (bf16[512,512]{1,0:T(8,128)(2,1)S(1)}, bf16[512,512]{1,0:T(8,128)(2,1)S(1)}, u32[]{:S(2)}, u32[]{:S(2)}) collective-permute-start(bf16[512,512]{1,0:T(8,128)(2,1)S(1)} %broadcast_select_fusion.own), channel_id=1, source_target_pairs={{0,4},{4,8},{8,12},{1,5},{5,9},{9,13},{2,6},{6,10},{10,14},{3,7},{... | collective-permute-start | bytes 1572872 | tf_op jit(solution)/shard_map/ppermute | solution.py:437
  81.2 1.3 collective-permute-start.13
  82.5 0.6 pad_add_fusion.blocks_ref
  83.1 8.5 %prepare_weights.1 = (bf16[1536,2048]{1,0:T(8,128)(2,1)}, bf16[2048,512]{1,0:T(8,128)(2,1)}) custom-call(s32[4]{0:T(128)} %pad_add_fusion.blocks_ref, f32[1,2048]{1,0:T(1,128)} %bitcast.20, bf16[1536,2048]{1,0:T(8,128)(2,1)} %bitcast.19, bf16[512,2048]{1,0:T(8,128)(2,1)} %out_ref.1), custom_call_target="tpu_custom_call" | custom-call | flops 3145728 | bytes 16777216 | tf_op jit(solution)/shard_map/prepare_weights/pallas_call | solution.py:178
  91.7 7.3 %collective-permute-start.15 = (bf16[512,512]{1,0:T(8,128)(2,1)S(1)}, bf16[512,512]{1,0:T(8,128)(2,1)}, u32[]{:S(2)}, u32[]{:S(2)}) collective-permute-start(bf16[512,512]{1,0:T(8,128)(2,1)S(1)} %broadcast_select_fusion.own), channel_id=1, source_target_pairs={{0,12},{12,0},{1,13},{13,1},{2,14},{14,2},{3,15},{15,3},{16,28},{2... | collective-permute-start | bytes 1572872 | tf_op jit(solution)/shard_map/ppermute | solution.py:439
  99.0 0.8 copy-done.9
  99.8 2.8 %copy-done.7 = bf16[1536,2048]{1,0:T(8,128)(2,1)S(1)} copy-done((bf16[1536,2048]{1,0:T(8,128)(2,1)S(1)}, bf16[1536,2048]{1,0:T(8,128)(2,1)}, u32[]{:S(2)}) %copy-start.7) | copy-done | bytes 6291480
  102.6 1.0 copy-done.10
  103.7 6.3 %project.2.query_ref.refs_0_.refs_2_.refs_3_ = bf16[1536,512]{1,0:T(8,128)(2,1)S(1)} custom-call(s32[2]{0:T(128)S(1)} %add_convert_fusion.ends_ref, bf16[1536,2048]{1,0:T(8,128)(2,1)S(1)} %copy-done.7, bf16[512,512]{1,0:T(8,128)(2,1)S(1)} %broadcast_select_fusion.3.own, bf16[512,512]{1,0:T(8,128)(2,1)} %collective-permute-done.1.before, ...), custom_call_target="tpu_custom_call" | custom-call | flops 3221225472 | bytes 9961472 | tf_op jit(solution)/shard_map/project/pallas_call | solution.py:236
  110.0 1.0 slice.28
  111.0 0.9 select_select_fusion
  111.9 0.8 copy-done.2
  112.8 3.6 %collective-permute-done.15.far = bf16[512,512]{1,0:T(8,128)(2,1)} collective-permute-done((bf16[512,512]{1,0:T(8,128)(2,1)S(1)}, bf16[512,512]{1,0:T(8,128)(2,1)}, u32[]{:S(2)}, u32[]{:S(2)}) %collective-permute-start.15) | collective-permute-done | bytes 524320 | tf_op jit(solution)/shard_map/ppermute | solution.py:439
  116.4 9.5 %collective-permute-done.14.across = bf16[512,512]{1,0:T(8,128)(2,1)} collective-permute-done((bf16[512,512]{1,0:T(8,128)(2,1)}, bf16[512,512]{1,0:T(8,128)(2,1)}, u32[]{:S(2)}, u32[]{:S(2)}) %collective-permute-start.14) | collective-permute-done | bytes 524320 | tf_op jit(solution)/shard_map/ppermute | solution.py:441
  125.9 1.0 copy-done.3
  126.9 2.8 %copy-done.8 = bf16[1536,2048]{1,0:T(8,128)(2,1)S(1)} copy-done((bf16[1536,2048]{1,0:T(8,128)(2,1)S(1)}, bf16[1536,2048]{1,0:T(8,128)(2,1)}, u32[]{:S(2)}) %copy-start.8) | copy-done | bytes 6291480
  129.7 6.5 %project.3.query_ref.refs_2_.refs_5_ = bf16[1536,512]{1,0:T(8,128)(2,1)S(1)} custom-call(s32[2]{0:T(128)S(1)} %add_convert_fusion.ends_ref, bf16[1536,2048]{1,0:T(8,128)(2,1)S(1)} %copy-done.8, bf16[512,512]{1,0:T(8,128)(2,1)S(1)} %broadcast_select_fusion.own, bf16[512,512]{1,0:T(8,128)(2,1)S(1)} %copy-done.3, ...), custom_call_target="tpu_custom_call" | custom-call | flops 3221225472 | bytes 9961472 | tf_op jit(solution)/shard_map/project/pallas_call | solution.py:236
  136.3 2.3 %collective-permute-start.16 = (bf16[1024,512]{1,0:T(8,128)(2,1)S(1)}, bf16[1024,512]{1,0:T(8,128)(2,1)S(1)}, u32[]{:S(2)}, u32[]{:S(2)}) collective-permute-start(bf16[1024,512]{1,0:T(8,128)(2,1)S(1)} %slice.29), channel_id=1, source_target_pairs={{0,16},{16,0},{1,17},{17,1},{2,18},{18,2},{3,19},{19,3},{4,20},{20... | collective-permute-start | bytes 3145736 | tf_op jit(solution)/shard_map/ppermute | solution.py:497
  138.6 4.8 %shard_map.73 = bf16[512,512]{1,0:T(8,128)(2,1)S(1)} custom-call(s32[1]{0:T(128)} %bitcast.seq_ref, s32[16]{0:T(128)S(1)} %copy-done.6, s32[16,16]{1,0:T(8,128)S(1)} %copy-done.5, bf16[1536,512]{1,0:T(8,128)(2,1)S(1)} %project.2.query_ref.refs_0_.refs_2_.refs_3_, bf16[1536,512]{1,0:T(8,128)(2,1)S(1)} %project.2.query_ref.refs_0_.refs_2_.refs_3_, ...), custom_call_target="tpu_custom_call" | custom-call | flops 1073741824 | bytes 3145728 | tf_op jit(solution)/shard_map/pallas_call | solution.py:353
  144.3 0.6 collective-permute-start.6
  145.4 5.5 %collective-permute-start.9 = (bf16[512,512]{1,0:T(8,128)(2,1)S(1)}, bf16[512,512]{1,0:T(8,128)(2,1)S(1)}, u32[]{:S(2)}, u32[]{:S(2)}) collective-permute-start(bf16[512,512]{1,0:T(8,128)(2,1)S(1)} %broadcast_select_fusion.2), channel_id=1, source_target_pairs={{0,12},{12,0},{1,13},{13,1},{2,14},{14,2},{3,15},{15,3},{16,28},{2... | collective-permute-start | bytes 1572872 | tf_op jit(solution)/shard_map/ppermute | solution.py:460
  150.9 6.9 %shard_map.74 = (f32[4,2,512]{2,1,0:T(2,128)S(1)}, f32[512,512]{1,0:T(8,128)S(1)}) custom-call(s32[1]{0:T(128)} %bitcast.seq_ref, s32[16]{0:T(128)S(1)} %copy-done.6, s32[16,16]{1,0:T(8,128)S(1)} %copy-done.5, bf16[1536,512]{1,0:T(8,128)(2,1)S(1)} %project.3.query_ref.refs_2_.refs_5_, bf16[1536,512]{1,0:T(8,128)(2,1)S(1)} %project.2.query_ref.refs_0_.refs_2_.refs_3_, ...), custom_call_target="tpu_custom_call" | custom-call | flops 1610612736 | bytes 4194304 | tf_op jit(solution)/shard_map/pallas_call | solution.py:353
  158.1 1.3 collective-permute-start.7
  159.3 15.4 %collective-permute-start.8 = (bf16[512,512]{1,0:T(8,128)(2,1)S(1)}, bf16[512,512]{1,0:T(8,128)(2,1)S(1)}, u32[]{:S(2)}, u32[]{:S(2)}) collective-permute-start(bf16[512,512]{1,0:T(8,128)(2,1)S(1)} %get-tuple-element.34), channel_id=1, source_target_pairs={{0,4},{4,8},{8,12},{1,5},{5,9},{9,13},{2,6},{6,10},{10,14},{3,7},{... | collective-permute-start | bytes 1572872 | tf_op jit(solution)/shard_map/ppermute | solution.py:462
  174.8 3.6 %shard_map.75 = bf16[512,512]{1,0:T(8,128)(2,1)S(1)} custom-call(s32[1]{0:T(128)} %bitcast.seq_ref, s32[16]{0:T(128)S(1)} %copy-done.6, s32[16,16]{1,0:T(8,128)S(1)} %copy-done.5, bf16[1536,512]{1,0:T(8,128)(2,1)S(1)} %project.3.query_ref.refs_2_.refs_5_, bf16[1024,512]{1,0:T(8,128)(2,1)S(1)} %collective-permute-done.16.refs_0_.refs_1_, ...), custom_call_target="tpu_custom_call" | custom-call | flops 536870912 | bytes 2097152 | tf_op jit(solution)/shard_map/pallas_call | solution.py:353
  178.4 0.4 convolution_convert_fusion.1
  179.3 2.0 collective-permute-start.17
  181.8 4.1 %collective-permute-start.20 = (bf16[512,512]{1,0:T(8,128)(2,1)S(1)}, bf16[512,512]{1,0:T(8,128)(2,1)S(1)}, u32[]{:S(2)}, u32[]{:S(2)}) collective-permute-start(bf16[512,512]{1,0:T(8,128)(2,1)S(1)} %broadcast_select_fusion.1), channel_id=1, source_target_pairs={{0,12},{12,0},{1,13},{13,1},{2,14},{14,2},{3,15},{15,3},{16,28},{2... | collective-permute-start | bytes 1572872 | tf_op jit(solution)/shard_map/ppermute | solution.py:460
  186.0 12.3 %collective-permute-done.17.refs_4_ = bf16[512,512]{1,0:T(8,128)(2,1)S(1)} collective-permute-done((bf16[512,512]{1,0:T(8,128)(2,1)S(1)}, bf16[512,512]{1,0:T(8,128)(2,1)S(1)}, u32[]{:S(2)}, u32[]{:S(2)}) %collective-permute-start.17) | collective-permute-done | bytes 524320 | tf_op jit(solution)/shard_map/ppermute | solution.py:458
  198.6 1.3 collective-permute-start.18
  199.9 11.3 %collective-permute-start.19 = (bf16[512,512]{1,0:T(8,128)(2,1)S(1)}, bf16[512,512]{1,0:T(8,128)(2,1)S(1)}, u32[]{:S(2)}, u32[]{:S(2)}) collective-permute-start(bf16[512,512]{1,0:T(8,128)(2,1)S(1)} %get-tuple-element.31), channel_id=1, source_target_pairs={{0,4},{4,8},{8,12},{1,5},{5,9},{9,13},{2,6},{6,10},{10,14},{3,7},{... | collective-permute-start | bytes 1572872 | tf_op jit(solution)/shard_map/ppermute | solution.py:462
  211.7 0.6 fusion.5.first_ref
  212.3 7.2 %collective-permute-done.18.refs_1_ = bf16[512,512]{1,0:T(8,128)(2,1)S(1)} collective-permute-done((bf16[512,512]{1,0:T(8,128)(2,1)S(1)}, bf16[512,512]{1,0:T(8,128)(2,1)S(1)}, u32[]{:S(2)}, u32[]{:S(2)}) %collective-permute-start.18) | collective-permute-done | bytes 524320 | tf_op jit(solution)/shard_map/ppermute | solution.py:461
  219.5 2.8 %place.1 = bf16[512,1024]{1,0:T(8,128)(2,1)} custom-call(s32[1]{0:T(128)} %bitcast.seq_ref, s32[16]{0:T(128)S(1)} %copy-done.6, s32[1]{0:T(128)} %bitcast.1.ends_ref, bf16[512,512]{1,0:T(8,128)(2,1)S(1)} %fusion.5.first_ref, bf16[512,512]{1,0:T(8,128)(2,1)S(1)} %convolution_convert_fusion.3.refs_0_, bf16[512,512]{1,0:T(8,128)(2,1)S(1)} %collective-permute-done.18.refs_1_, ...), custom_call_target="tpu_custom_call" | custom-call | flops 1048576 | bytes 3670016 | tf_op jit(solution)/shard_map/place/pallas_call | solution.py:411
  (47 shorter events, 3.7 us)
Async XLA Ops:
  0.0 50.8 %copy-start.6 = (s32[16]{0:T(128)S(1)}, s32[16]{0:T(128)}, u32[]{:S(2)}) copy-start(s32[16]{0:T(128)} %order_ref.11) | copy-start | bytes 196
  0.0 50.8 %copy-start = (bf16[512,1024]{1,0:T(8,128)(2,1)S(1)}, bf16[512,1024]{1,0:T(8,128)(2,1)}, u32[]{:S(2)}) copy-start(bf16[512,1024]{1,0:T(8,128)(2,1)} %refs_0_.3) | copy-start | bytes 3145732
  0.0 50.8 %copy-start.4 = (f32[27,512]{1,0:T(8,128)S(1)}, f32[27,512]{1,0:T(8,128)}, u32[]{:S(2)}) copy-start(f32[27,512]{1,0:T(8,128)} %refs_1_.3) | copy-start | bytes 165892
  12.0 17.5 %collective-permute-start = (bf16[512,512]{1,0:T(8,128)(2,1)}, bf16[512,512]{1,0:T(8,128)(2,1)S(1)}, u32[]{:S(2)}, u32[]{:S(2)}) collective-permute-start(bf16[512,512]{1,0:T(8,128)(2,1)} %get-tuple-element.21), channel_id=1, source_target_pairs={{0,16},{1,17},{2,18},{3,19},{4,20},{5,21},{6,22},{7,23},{8,24},{9,... | collective-permute-start | bytes 1572872 | tf_op jit(solution)/shard_map/ppermute | solution.py:478
  16.9 33.9 %collective-permute-start.10 = (bf16[512,1024]{1,0:T(8,128)(2,1)}, bf16[512,1024]{1,0:T(8,128)(2,1)S(1)}, u32[]{:S(2)}, u32[]{:S(2)}) collective-permute-start(bf16[512,1024]{1,0:T(8,128)(2,1)} %refs_0_.3), channel_id=1, source_target_pairs={{0,16},{1,17},{2,18},{3,19},{4,20},{5,21},{6,22},{7,23},{8,24},{9,... | collective-permute-start | bytes 3145736 | tf_op jit(solution)/shard_map/ppermute | solution.py:479
  30.6 39.0 %collective-permute-start.1 = (bf16[512,512]{1,0:T(8,128)(2,1)S(1)}, bf16[512,512]{1,0:T(8,128)(2,1)}, u32[]{:S(2)}, u32[]{:S(2)}) collective-permute-start(bf16[512,512]{1,0:T(8,128)(2,1)S(1)} %broadcast_select_fusion.3.own), channel_id=1, source_target_pairs={{0,4},{4,8},{8,12},{1,5},{5,9},{9,13},{2,6},{6,10},{10,14},{3,7},{... | collective-permute-start | bytes 1572872 | tf_op jit(solution)/shard_map/ppermute | solution.py:437
  34.9 34.6 %collective-permute-start.2 = (bf16[512,512]{1,0:T(8,128)(2,1)S(1)}, bf16[512,512]{1,0:T(8,128)(2,1)}, u32[]{:S(2)}, u32[]{:S(2)}) collective-permute-start(bf16[512,512]{1,0:T(8,128)(2,1)S(1)} %broadcast_select_fusion.3.own), channel_id=1, source_target_pairs={{4,0},{8,4},{12,8},{5,1},{9,5},{13,9},{6,2},{10,6},{14,10},{7,3},{... | collective-permute-start | bytes 1572872 | tf_op jit(solution)/shard_map/ppermute | solution.py:438
  50.8 1.6 copy-start.1
  62.7 14.9 %collective-permute-start.11 = (bf16[512,512]{1,0:T(8,128)(2,1)}, bf16[512,512]{1,0:T(8,128)(2,1)S(1)}, u32[]{:S(2)}, u32[]{:S(2)}) collective-permute-start(bf16[512,512]{1,0:T(8,128)(2,1)} %get-tuple-element.26), channel_id=1, source_target_pairs={{16,0},{17,1},{18,2},{19,3},{20,4},{21,5},{22,6},{23,7},{24,8},{25... | collective-permute-start | bytes 1572872 | tf_op jit(solution)/shard_map/ppermute | solution.py:486
  64.0 35.0 %collective-permute-start.4 = (bf16[512,512]{1,0:T(8,128)(2,1)S(1)}, bf16[512,512]{1,0:T(8,128)(2,1)S(1)}, u32[]{:S(2)}, u32[]{:S(2)}) collective-permute-start(bf16[512,512]{1,0:T(8,128)(2,1)S(1)} %broadcast_select_fusion.3.own), channel_id=1, source_target_pairs={{0,12},{12,0},{1,13},{13,1},{2,14},{14,2},{3,15},{15,3},{16,28},{2... | collective-permute-start | bytes 1572872 | tf_op jit(solution)/shard_map/ppermute | solution.py:439
  70.4 28.6 %collective-permute-start.3 = (bf16[512,512]{1,0:T(8,128)(2,1)}, bf16[512,512]{1,0:T(8,128)(2,1)S(1)}, u32[]{:S(2)}, u32[]{:S(2)}) collective-permute-start(bf16[512,512]{1,0:T(8,128)(2,1)} %select_select_fusion.1), channel_id=1, source_target_pairs={{4,0},{12,4},{8,12},{0,8},{5,1},{13,5},{9,13},{1,9},{6,2},{14,6},{... | collective-permute-start | bytes 1572872 | tf_op jit(solution)/shard_map/ppermute | solution.py:441
  77.7 33.3 %collective-permute-start.12 = (bf16[512,512]{1,0:T(8,128)(2,1)S(1)}, bf16[512,512]{1,0:T(8,128)(2,1)S(1)}, u32[]{:S(2)}, u32[]{:S(2)}) collective-permute-start(bf16[512,512]{1,0:T(8,128)(2,1)S(1)} %broadcast_select_fusion.own), channel_id=1, source_target_pairs={{0,4},{4,8},{8,12},{1,5},{5,9},{9,13},{2,6},{6,10},{10,14},{3,7},{... | collective-permute-start | bytes 1572872 | tf_op jit(solution)/shard_map/ppermute | solution.py:437
  81.2 29.8 %collective-permute-start.13 = (bf16[512,512]{1,0:T(8,128)(2,1)S(1)}, bf16[512,512]{1,0:T(8,128)(2,1)}, u32[]{:S(2)}, u32[]{:S(2)}) collective-permute-start(bf16[512,512]{1,0:T(8,128)(2,1)S(1)} %broadcast_select_fusion.own), channel_id=1, source_target_pairs={{4,0},{8,4},{12,8},{5,1},{9,5},{13,9},{6,2},{10,6},{14,10},{7,3},{... | collective-permute-start | bytes 1572872 | tf_op jit(solution)/shard_map/ppermute | solution.py:438
  91.7 24.7 %collective-permute-start.15 = (bf16[512,512]{1,0:T(8,128)(2,1)S(1)}, bf16[512,512]{1,0:T(8,128)(2,1)}, u32[]{:S(2)}, u32[]{:S(2)}) collective-permute-start(bf16[512,512]{1,0:T(8,128)(2,1)S(1)} %broadcast_select_fusion.own), channel_id=1, source_target_pairs={{0,12},{12,0},{1,13},{13,1},{2,14},{14,2},{3,15},{15,3},{16,28},{2... | collective-permute-start | bytes 1572872 | tf_op jit(solution)/shard_map/ppermute | solution.py:439
  99.0 0.8 copy-start.9
  99.8 2.8 %copy-start.7 = (bf16[1536,2048]{1,0:T(8,128)(2,1)S(1)}, bf16[1536,2048]{1,0:T(8,128)(2,1)}, u32[]{:S(2)}) copy-start(bf16[1536,2048]{1,0:T(8,128)(2,1)} %get-tuple-element.19.weight_ref) | copy-start | bytes 18874372
  102.6 1.0 copy-start.10
  111.0 27.6 %collective-permute-start.5 = (bf16[1024,512]{1,0:T(8,128)(2,1)}, bf16[1024,512]{1,0:T(8,128)(2,1)S(1)}, u32[]{:S(2)}, u32[]{:S(2)}) collective-permute-start(bf16[1024,512]{1,0:T(8,128)(2,1)} %slice.28), channel_id=1, source_target_pairs={{0,16},{16,0},{1,17},{17,1},{2,18},{18,2},{3,19},{19,3},{4,20},{20... | collective-permute-start | bytes 3145736 | tf_op jit(solution)/shard_map/ppermute | solution.py:492
  111.9 0.8 copy-start.2
  112.7 13.2 %collective-permute-start.14 = (bf16[512,512]{1,0:T(8,128)(2,1)}, bf16[512,512]{1,0:T(8,128)(2,1)}, u32[]{:S(2)}, u32[]{:S(2)}) collective-permute-start(bf16[512,512]{1,0:T(8,128)(2,1)} %select_select_fusion), channel_id=1, source_target_pairs={{4,0},{12,4},{8,12},{0,8},{5,1},{13,5},{9,13},{1,9},{6,2},{14,6},{... | collective-permute-start | bytes 1572872 | tf_op jit(solution)/shard_map/ppermute | solution.py:441
  125.9 1.0 copy-start.3
  126.9 2.8 %copy-start.8 = (bf16[1536,2048]{1,0:T(8,128)(2,1)S(1)}, bf16[1536,2048]{1,0:T(8,128)(2,1)}, u32[]{:S(2)}) copy-start(bf16[1536,2048]{1,0:T(8,128)(2,1)} %get-tuple-element.19.weight_ref) | copy-start | bytes 18874372
  136.2 2.4 %copy-start.5 = (s32[16,16]{1,0:T(8,128)S(1)}, s32[16,16]{1,0:T(8,128)}, u32[]{:S(2)}) copy-start(s32[16,16]{1,0:T(8,128)} %mask_ref.5) | copy-start | bytes 3076
  136.3 7.1 %copy-start.11 = (bf16[2048,512]{1,0:T(8,128)(2,1)S(1)}, bf16[2048,512]{1,0:T(8,128)(2,1)}, u32[]{:S(2)}) copy-start(bf16[2048,512]{1,0:T(8,128)(2,1)} %get-tuple-element.18) | copy-start | bytes 6291460
  136.3 38.5 %collective-permute-start.16 = (bf16[1024,512]{1,0:T(8,128)(2,1)S(1)}, bf16[1024,512]{1,0:T(8,128)(2,1)S(1)}, u32[]{:S(2)}, u32[]{:S(2)}) collective-permute-start(bf16[1024,512]{1,0:T(8,128)(2,1)S(1)} %slice.29), channel_id=1, source_target_pairs={{0,16},{16,0},{1,17},{17,1},{2,18},{18,2},{3,19},{19,3},{4,20},{20... | collective-permute-start | bytes 3145736 | tf_op jit(solution)/shard_map/ppermute | solution.py:497
  144.3 13.5 %collective-permute-start.6 = (bf16[512,512]{1,0:T(8,128)(2,1)S(1)}, bf16[512,512]{1,0:T(8,128)(2,1)S(1)}, u32[]{:S(2)}, u32[]{:S(2)}) collective-permute-start(bf16[512,512]{1,0:T(8,128)(2,1)S(1)} %convolution_convert_fusion.4), channel_id=1, source_target_pairs={{0,4},{4,12},{12,8},{8,0},{1,5},{5,13},{13,9},{9,1},{2,6},{6,14},{... | collective-permute-start | bytes 1572872 | tf_op jit(solution)/shard_map/ppermute | solution.py:458
  145.4 54.5 %collective-permute-start.9 = (bf16[512,512]{1,0:T(8,128)(2,1)S(1)}, bf16[512,512]{1,0:T(8,128)(2,1)S(1)}, u32[]{:S(2)}, u32[]{:S(2)}) collective-permute-start(bf16[512,512]{1,0:T(8,128)(2,1)S(1)} %broadcast_select_fusion.2), channel_id=1, source_target_pairs={{0,12},{12,0},{1,13},{13,1},{2,14},{14,2},{3,15},{15,3},{16,28},{2... | collective-permute-start | bytes 1572872 | tf_op jit(solution)/shard_map/ppermute | solution.py:460
  158.1 53.6 %collective-permute-start.7 = (bf16[512,512]{1,0:T(8,128)(2,1)S(1)}, bf16[512,512]{1,0:T(8,128)(2,1)S(1)}, u32[]{:S(2)}, u32[]{:S(2)}) collective-permute-start(bf16[512,512]{1,0:T(8,128)(2,1)S(1)} %get-tuple-element.33), channel_id=1, source_target_pairs={{4,0},{8,4},{12,8},{5,1},{9,5},{13,9},{6,2},{10,6},{14,10},{7,3},{... | collective-permute-start | bytes 1572872 | tf_op jit(solution)/shard_map/ppermute | solution.py:461
  159.3 52.3 %collective-permute-start.8 = (bf16[512,512]{1,0:T(8,128)(2,1)S(1)}, bf16[512,512]{1,0:T(8,128)(2,1)S(1)}, u32[]{:S(2)}, u32[]{:S(2)}) collective-permute-start(bf16[512,512]{1,0:T(8,128)(2,1)S(1)} %get-tuple-element.34), channel_id=1, source_target_pairs={{0,4},{4,8},{8,12},{1,5},{5,9},{9,13},{2,6},{6,10},{10,14},{3,7},{... | collective-permute-start | bytes 1572872 | tf_op jit(solution)/shard_map/ppermute | solution.py:462
  179.3 19.0 %collective-permute-start.17 = (bf16[512,512]{1,0:T(8,128)(2,1)S(1)}, bf16[512,512]{1,0:T(8,128)(2,1)S(1)}, u32[]{:S(2)}, u32[]{:S(2)}) collective-permute-start(bf16[512,512]{1,0:T(8,128)(2,1)S(1)} %convolution_convert_fusion), channel_id=1, source_target_pairs={{0,4},{4,12},{12,8},{8,0},{1,5},{5,13},{13,9},{9,1},{2,6},{6,14},{... | collective-permute-start | bytes 1572872 | tf_op jit(solution)/shard_map/ppermute | solution.py:458
  181.8 30.5 %collective-permute-start.20 = (bf16[512,512]{1,0:T(8,128)(2,1)S(1)}, bf16[512,512]{1,0:T(8,128)(2,1)S(1)}, u32[]{:S(2)}, u32[]{:S(2)}) collective-permute-start(bf16[512,512]{1,0:T(8,128)(2,1)S(1)} %broadcast_select_fusion.1), channel_id=1, source_target_pairs={{0,12},{12,0},{1,13},{13,1},{2,14},{14,2},{3,15},{15,3},{16,28},{2... | collective-permute-start | bytes 1572872 | tf_op jit(solution)/shard_map/ppermute | solution.py:460
  198.6 21.0 %collective-permute-start.18 = (bf16[512,512]{1,0:T(8,128)(2,1)S(1)}, bf16[512,512]{1,0:T(8,128)(2,1)S(1)}, u32[]{:S(2)}, u32[]{:S(2)}) collective-permute-start(bf16[512,512]{1,0:T(8,128)(2,1)S(1)} %get-tuple-element.32), channel_id=1, source_target_pairs={{4,0},{8,4},{12,8},{5,1},{9,5},{13,9},{6,2},{10,6},{14,10},{7,3},{... | collective-permute-start | bytes 1572872 | tf_op jit(solution)/shard_map/ppermute | solution.py:461
  199.9 19.7 %collective-permute-start.19 = (bf16[512,512]{1,0:T(8,128)(2,1)S(1)}, bf16[512,512]{1,0:T(8,128)(2,1)S(1)}, u32[]{:S(2)}, u32[]{:S(2)}) collective-permute-start(bf16[512,512]{1,0:T(8,128)(2,1)S(1)} %get-tuple-element.31), channel_id=1, source_target_pairs={{0,4},{4,8},{8,12},{1,5},{5,9},{9,13},{2,6},{6,10},{10,14},{3,7},{... | collective-permute-start | bytes 1572872 | tf_op jit(solution)/shard_map/ppermute | solution.py:462

commit v2 on v1

--- a/solution.py
+++ b/solution.py
@@ -22,6 +22,7 @@
 LOG2E = math.log2(math.e)
 
 VMEM_LIMIT = 20 * 1024 * 1024
+VMEM_MOST = 57 * 1024 * 1024
 VMEM_WHOLE = 60 * 1024 * 1024
 
 
@@ -40,6 +41,11 @@
     above = jnp.where(lane >= FW, pltpu.roll(rows[0], FW, 1), 0.0)
     below = jnp.where(lane < FRAME - FW, pltpu.roll(rows[2], FRAME - FW, 1), 0.0)
     return rows[1] + above + below
+
+
+def spread(taps, tap):
+    column = jnp.broadcast_to(taps[:, tap : tap + 1], (taps.shape[0], 128))
+    return jnp.concatenate([column] * (FRAME // 128), axis=1)
 
 
 def taps_applied(pairs, taps, lane):
@@ -49,7 +55,7 @@
         for time_off, shifts in pairs:
             for col_off in range(3):
                 tap = time_off * 9 + row_off * 3 + col_off
-                term = taps[:, tap : tap + 1] * shifts[col_off]
+                term = spread(taps, tap) * shifts[col_off]
                 total = term if total is None else total + term
         rows.append(total)
     return row_sum(rows, lane)
@@ -89,7 +95,7 @@
 
     taps_scr[:, :TAPS] = taps_ref[...].T
     group = 16
-    part = 8
+    part = 16
     lane = lax.broadcasted_iota(jnp.int32, (part, FRAME), 1)
 
     def frame_of(ref, rows, frame, piece):
@@ -125,7 +131,7 @@
             packed[rows, place] = joined.astype(jnp.bfloat16)
         return carry
 
-    lax.fori_loop(0, channels // group, advance, 0, unroll=2)
+    lax.fori_loop(0, channels // group, advance, 0)
     keep_ref[...] = packed[:, : tokens // 2]
     send_ref[...] = packed[:, tokens // 2 :]
 
@@ -162,7 +168,7 @@
         cost_estimate=pl.CostEstimate(
             flops=channels * count * TAPS, bytes_accessed=channels * count * 8, transcendentals=0
         ),
-        name="conv_before" if with_before else "conv_here",
+        name="conv",
     )(seq_here, stripe_order, tokens, conv_taps, *extra_args)
 
 
@@ -198,62 +204,67 @@
         cost_estimate=pl.CostEstimate(
             flops=kinds * cols * channels, bytes_accessed=16 * cols * channels, transcendentals=0
         ),
-        name="prepare_weights",
+        name="prepare",
     )(blocks, norm_gain[None, :], qkv_weight.reshape(kinds * cols, channels), out_weight)
 
 
-def project_body(query_steps, ends_ref, weight_ref, own, before, after, across, far, out_ref, tokens_ref, inverse_ref):
+def project_body(query_steps, weight_ref, own, before, after, across, query_ref, pair_ref, tokens_ref, inverse_ref):
     width = own.shape[0]
     step = pl.program_id(0)
 
     @pl.when(step == 0)
     def _():
-        at_start, at_stop = ends_ref[0] == 1, ends_ref[1] == 1
         squares = None
-        shards = (
-            own[...],
-            jnp.where(at_start, far[...], before[...]),
-            jnp.where(at_stop, far[...], after[...]),
-            across[...],
-        )
-        for index, shard in enumerate(shards):
-            tokens_ref[index * width : (index + 1) * width, :] = shard
-            wide = shard.astype(jnp.float32)
+        for index, shard in enumerate((own, before, after, across)):
+            block = shard[...]
+            tokens_ref[index * width : (index + 1) * width, :] = block
+            wide = block.astype(jnp.float32)
             term = jnp.sum(wide * wide, axis=0, keepdims=True)
             squares = term if squares is None else squares + term
-        inverse_ref[...] = lax.rsqrt(squares / (width * len(shards)) + EPSILON)
+        inverse_ref[...] = lax.rsqrt(squares / (4 * width) + EPSILON)
 
     total = jnp.dot(weight_ref[...], tokens_ref[...], preferred_element_type=jnp.float32)
-    scale = jnp.where(step < query_steps, LOG2E / math.sqrt(HEAD), 1.0)
-    out_ref[...] = (total * (inverse_ref[...] * scale)).astype(jnp.bfloat16)
-
-
-def project_call(ends, weights, shards):
+
+    @pl.when(step < query_steps)
+    def _():
+        query_ref[...] = (total * (inverse_ref[...] * (LOG2E / math.sqrt(HEAD)))).astype(jnp.bfloat16)
+
+    @pl.when(step >= query_steps)
+    def _():
+        pair_ref[...] = (total * inverse_ref[...]).astype(jnp.bfloat16)
+
+
+def project_call(weights, shards):
     rows, channels = weights.shape
     width, tokens = shards[0].shape
+    cols = rows // 3
     block = 256
-    whole = pl.BlockSpec((width, tokens), lambda i, *_: (0, 0))
+    query_steps = cols // block
+    whole = pl.BlockSpec((width, tokens), lambda i: (0, 0))
     return pl.pallas_call(
-        functools.partial(project_body, rows // 3 // block),
-        grid_spec=pltpu.PrefetchScalarGridSpec(
-            num_scalar_prefetch=1,
-            grid=(rows // block,),
-            in_specs=[pl.BlockSpec((block, channels), lambda i, *_: (i, 0))] + [whole] * len(shards),
-            out_specs=pl.BlockSpec((block, tokens), lambda i, *_: (i, 0)),
-            scratch_shapes=[
-                pltpu.VMEM((channels, tokens), jnp.bfloat16),
-                pltpu.VMEM((1, tokens), jnp.float32),
-            ],
-        ),
-        out_shape=jax.ShapeDtypeStruct((rows, tokens), jnp.bfloat16),
-        compiler_params=params(),
+        functools.partial(project_body, query_steps),
+        grid=(rows // block,),
+        in_specs=[pl.BlockSpec((block, channels), lambda i: (i, 0))] + [whole] * len(shards),
+        out_specs=[
+            pl.BlockSpec((block, tokens), lambda i: (jnp.minimum(i, query_steps - 1), 0)),
+            pl.BlockSpec((block, tokens), lambda i: (jnp.maximum(i - query_steps, 0), 0)),
+        ],
+        scratch_shapes=[
+            pltpu.VMEM((channels, tokens), jnp.bfloat16),
+            pltpu.VMEM((1, tokens), jnp.float32),
+        ],
+        out_shape=[
+            jax.ShapeDtypeStruct((cols, tokens), jnp.bfloat16),
+            jax.ShapeDtypeStruct((2 * cols, tokens), jnp.bfloat16),
+        ],
+        compiler_params=params(VMEM_MOST),
         cost_estimate=pl.CostEstimate(
             flops=2 * rows * channels * tokens,
             bytes_accessed=2 * (rows * channels + channels * tokens + rows * tokens),
             transcendentals=0,
         ),
         name="project",
-    )(ends, weights, *shards)
+    )(weights, *shards)
 
 
 def tile_lists(order_ref, ids_ref, seq_here, tiles_dev):
@@ -328,9 +339,9 @@
         new_weighted[...] = weighted
 
 
-def attend_call(chunk, tables, query_from, sources, state=None, ends=True):
-    rows, tokens = query_from.shape
-    heads = rows // 3 // HEAD
+def attend_call(chunk, tables, queries, sources, state=None, ends=True):
+    rows, tokens = queries.shape
+    heads = rows // HEAD
 
     def spec(start):
         return pl.BlockSpec((HEAD, tokens), lambda h, *_, start=start: (start + h, 0))
@@ -340,18 +351,16 @@
     state_specs = [stats_spec, spec(0)]
     state_shapes = [
         jax.ShapeDtypeStruct((heads, 2, tokens), jnp.float32),
-        jax.ShapeDtypeStruct((heads * HEAD, tokens), jnp.float32),
+        jax.ShapeDtypeStruct((rows, tokens), jnp.float32),
     ]
     goes_on = state is not None
-    in_specs = [spec(0)]
-    in_specs += [spec(first // HEAD) for _, first, _ in sources]
-    in_specs += [spec(first // HEAD + heads) for _, first, _ in sources]
-    arguments = [query_from] + [array for array, _, _ in sources] * 2
+    in_specs = [spec(0)] + [spec(0)] * count + [spec(heads)] * count
+    arguments = [queries] + [array for array, _ in sources] * 2
     if goes_on:
         in_specs += state_specs
         arguments += list(state)
     return pl.pallas_call(
-        functools.partial(attend_body, chunk, tuple(s for _, _, s in sources), goes_on, ends),
+        functools.partial(attend_body, chunk, tuple(s for _, s in sources), goes_on, ends),
         grid_spec=pltpu.PrefetchScalarGridSpec(
             num_scalar_prefetch=3,
             grid=(heads,),
@@ -362,18 +371,19 @@
                 pltpu.VMEM((count * tokens, tokens), jnp.float32),
             ],
         ),
-        out_shape=jax.ShapeDtypeStruct((heads * HEAD, tokens), jnp.bfloat16) if ends else state_shapes,
+        out_shape=jax.ShapeDtypeStruct((rows, tokens), jnp.bfloat16) if ends else state_shapes,
         compiler_params=params(),
         cost_estimate=pl.CostEstimate(
-            flops=4 * heads * HEAD * tokens * tokens * count,
-            bytes_accessed=2 * heads * HEAD * tokens * (2 + 2 * count),
+            flops=4 * rows * tokens * tokens * count,
+            bytes_accessed=2 * rows * tokens * (2 + 2 * count),
             transcendentals=heads * tokens * tokens * count,
         ),
+        name="attend",
     )(*tables, *arguments)
 
 
 def place_body(seq_ref, order_ref, ends_ref, first_ref, *refs):
-    parts, out_ref, second_ref = refs[:5], refs[5], refs[6]
+    parts, out_ref, second_ref = refs[:4], refs[4], refs[5]
     _, tokens = first_ref.shape
     tiles_dev = 2 * tokens // TILE
     seq_here = seq_ref[0]
@@ -382,8 +392,7 @@
         parts[0][...].astype(jnp.float32)
         + parts[1][...].astype(jnp.float32)
         + parts[2][...].astype(jnp.float32)
-        + parts[3][...].astype(jnp.float32)
-        + jnp.where(at_end, parts[4][...].astype(jnp.float32), 0.0)
+        + jnp.where(at_end, parts[3][...].astype(jnp.float32), 0.0)
     )
     second_ref[...] = total.astype(jnp.bfloat16)
     ranks = [jnp.int32(0), jnp.int32(0)]
@@ -413,7 +422,7 @@
         grid_spec=pltpu.PrefetchScalarGridSpec(
             num_scalar_prefetch=3,
             grid=(channels // block,),
-            in_specs=[slim] * 6,
+            in_specs=[slim] * 5,
             out_specs=pl.BlockSpec((block, 2 * tokens), lambda i, *_: (i, 0)),
             scratch_shapes=[pltpu.VMEM((block, tokens), jnp.bfloat16)],
         ),
@@ -426,20 +435,18 @@
     )(seq_here, stripe_order, at_end, first, *parts)
 
 
-UP = [(0, 1), (1, 2), (2, 3)]
-DOWN = [(1, 0), (2, 1), (3, 2)]
-ENDS = [(0, 3), (3, 0)]
+FORWARD = [(0, 1), (1, 2), (2, 3), (3, 0)]
+BACKWARD = [(1, 0), (2, 1), (3, 2), (0, 3)]
 FOLDED = [(0, 1), (1, 3), (3, 2), (2, 0)]
 UNFOLDED = [(1, 0), (3, 1), (2, 3), (0, 2)]
 
 
 def gather_blocks(block, here):
-    before = lax.ppermute(block, "tp", UP)
-    after = lax.ppermute(block, "tp", DOWN)
-    far = lax.ppermute(block, "tp", ENDS)
+    before = lax.ppermute(block, "tp", FORWARD)
+    after = lax.ppermute(block, "tp", BACKWARD)
     relay = jnp.where(here == 2, before, jnp.where(here == 1, after, block))
     across = lax.ppermute(relay, "tp", UNFOLDED)
-    return (block, before, after, across, far)
+    return (block, before, after, across)
 
 
 def plus(a, b, chosen):
@@ -457,10 +464,9 @@
     sent = partial(3)
     across = lax.ppermute(sent, "tp", FOLDED)
     down, up = lax.optimization_barrier((partial(1), partial(2)))
-    far = lax.ppermute(jnp.where(here == 0, down, up), "tp", ENDS)
-    back = lax.ppermute(plus(down, across, here == 2), "tp", DOWN)
-    onward = lax.ppermute(plus(up, across, here == 1), "tp", UP)
-    return (partial(0), back, onward, far, across)
+    back = lax.ppermute(plus(down, across, here == 2), "tp", BACKWARD)
+    onward = lax.ppermute(plus(up, across, here == 1), "tp", FORWARD)
+    return (partial(0), back, onward, across)
 
 
 def per_device_fast(
@@ -470,7 +476,6 @@
     here = lax.axis_index("tp")
     seq_here = seq.astype(jnp.int32)[None]
     at_end = ((here == 0) | (here == 3)).astype(jnp.int32)[None]
-    ends = jnp.stack([here == 0, here == 3]).astype(jnp.int32)
     blocks = jnp.stack([here, (here + 3) % 4, (here + 1) % 4, (here + 2) % 4]).astype(jnp.int32)
     tables = (seq_here, stripe_order, tile_mask)
 
@@ -486,21 +491,20 @@
     got_b = lax.ppermute(send_b, "seq", [(1, 0)])
     tokens_b = jnp.where(seq == 1, keep_b, got_b)
 
-    cols = weights.shape[0] // 3
     swap = [(0, 1), (1, 0)]
-    own_a = project_call(ends, weights, shards_a)
-    peer_a = lax.ppermute(own_a[cols:], "seq", swap)
+    query_a, pair_a = project_call(weights, shards_a)
+    peer_a = lax.ppermute(pair_a, "seq", swap)
     shards_b = gather_blocks(tokens_b, here)
-    out_a = attend_call(0, tables, own_a, [(own_a, cols, 0), (peer_a, 0, 1)])
+    out_a = attend_call(0, tables, query_a, [(pair_a, 0), (peer_a, 1)])
     parts_a = reduce_blocks(out_t, out_a, here)
-    own_b = project_call(ends, weights, shards_b)
-    peer_b = lax.ppermute(own_b[cols:], "seq", swap)
-    near = [(own_a, cols, 0), (peer_a, 0, 1), (own_b, cols, 2)]
-    state = attend_call(1, tables, own_b, near, ends=False)
-    out_b = attend_call(1, tables, own_b, [(peer_b, 0, 3)], state=state)
+    query_b, pair_b = project_call(weights, shards_b)
+    peer_b = lax.ppermute(pair_b, "seq", swap)
+    near = [(pair_a, 0), (peer_a, 1), (pair_b, 2)]
+    state = attend_call(1, tables, query_b, near, ends=False)
+    out_b = attend_call(1, tables, query_b, [(peer_b, 3)], state=state)
     parts_b = reduce_blocks(out_t, out_b, here)
-    first = sum(part.astype(jnp.float32) for part in parts_a[:4])
-    first = first + jnp.where(at_end == 1, parts_a[4].astype(jnp.float32), 0.0)
+    first = sum(part.astype(jnp.float32) for part in parts_a[:3])
+    first = first + jnp.where(at_end == 1, parts_a[3].astype(jnp.float32), 0.0)
     return place_call(seq_here, stripe_order, at_end, first.astype(jnp.bfloat16), parts_b)
 
 

time: 223 us -> 208 us (0.933)
  starting transfers between devices: 74.8 us -> 31.3 us
  waiting for transfers between devices: 65.6 us -> 102 us
  local copies, waits for them, and re-layouts: 12 us -> 3.24 us
    ppermute x14 -> x10, starting transfers between devices: 64.5 us -> 14.6 us  [the longest x2 4.83 us: reduce_blocks(): back = lax.ppermute(plus(down, across, here == 2), 'tp', BACKWARD)]
    ppermute x2, waiting for transfers between devices: 12.3 us -> 28 us  [reduce_blocks(): across = lax.ppermute(sent, 'tp', FOLDED)]
    ppermute x14 -> x10, waiting for transfers between devices: 10.8 us -> 25.3 us  [the longest x2 11.3 us: reduce_blocks(): back = lax.ppermute(plus(down, across, here == 2), 'tp', BACKWARD)]
    unnamed x24 -> x30, local copies, waits for them, and re-layouts: 10.8 us -> 3.24 us
    pallas_call x5, Pallas kernels: 28 us -> 32.3 us  [the longest x2 17.1 us: project_call(): pl.pallas_call(functools.partial(project_body, query_steps), grid=(rows /...]
    ppermute x2, starting transfers between devices: 0.15 us -> 4.02 us  [gather_blocks(): across = lax.ppermute(relay, 'tp', UNFOLDED)]
    pallas_call x2, Pallas kernels: 22.3 us -> 19.2 us  [conv_call(): pl.pallas_call(functools.partial(conv_body, with_before), grid_spec=pltpu...]
    ppermute x2, waiting for transfers between devices: 9.49 us -> 12.1 us  [gather_blocks(): across = lax.ppermute(relay, 'tp', UNFOLDED)]
  transfers between devices with their start and end apart: 21 -> 17, of which waited for: 7 -> 10; matrix products, arithmetic and copies ran while one was open for 4% -> 4% of each run, Pallas kernels for 21% -> 24%
where the time goes in v2:
time: 208 us; the launch traced here: 207 us
  waiting for transfers between devices  102 us (49%)
  Pallas kernels  62.7 us (30%)
  starting transfers between devices  31.3 us (15%)
  other arithmetic  4.42 us (2%)
  matrix products  3.62 us (2%)
  local copies, waits for them, and re-layouts  3.24 us (2%)
    ppermute x2, waiting for transfers between devices, reduce_blocks(): across = lax.ppermute(sent, 'tp', FOLDED)  28 us
    pallas_call x2, Pallas kernels, conv_call(): pl.pallas_call(functools.partial(conv_body, with_before), grid_spec=pltpu...  19.2 us
    pallas_call x2, Pallas kernels, project_call(): pl.pallas_call(functools.partial(project_body, query_steps), grid=(rows /...  17.1 us
    ppermute x1, waiting for transfers between devices, per_device_fast(): before = lax.ppermute(clip_tokens, 'seq', [(0, 1)])  15.6 us
    pallas_call x3, Pallas kernels, attend_call(): pl.pallas_call(functools.partial(attend_body, chunk, tuple((s for _, s in...  15.2 us
    ppermute x2, waiting for transfers between devices, gather_blocks(): across = lax.ppermute(relay, 'tp', UNFOLDED)  12.1 us
    ppermute x2, waiting for transfers between devices, reduce_blocks(): back = lax.ppermute(plus(down, across, here == 2), 'tp', BACKWARD)  11.3 us
    ppermute x1, waiting for transfers between devices, per_device_fast(): got_a = lax.ppermute(send_a, 'seq', [(0, 1)])  11.2 us
  transfers between devices with their start and end apart: 17, of which 10 were waited for; matrix products, arithmetic and copies ran while one was open for 4% of the time, Pallas kernels for 24%

profile of v2, /device:TPU:0, one launch (start us, length us, event | category | flops | bytes accessed | tf_op | source)
XLA Modules:
  0.0 207.3 jit_solution(13526802977182683860)
XLA Ops:
  0.0 10.7 %conv.2 = (f32[512,1024]{1,0:T(8,128)}, bf16[512,512]{1,0:T(8,128)(2,1)}, bf16[512,512]{1,0:T(8,128)(2,1)}) custom-call(s32[1]{0:T(128)} %bitcast.seq_ref, s32[16]{0:T(128)} %order_ref.11, bf16[512,1024]{1,0:T(8,128)(2,1)} %refs_0_.3, f32[27,512]{1,0:T(8,128)} %refs_1_.3), custom_call_target="tpu_custom_call" | custom-call | flops 14155776 | bytes 4194304 | tf_op jit(solution)/shard_map/conv/pallas_call | solution.py:153
  10.7 4.9 %collective-permute-start = (bf16[512,512]{1,0:T(8,128)(2,1)}, bf16[512,512]{1,0:T(8,128)(2,1)S(1)}, u32[]{:S(2)}, u32[]{:S(2)}) collective-permute-start(bf16[512,512]{1,0:T(8,128)(2,1)} %get-tuple-element.25), channel_id=1, source_target_pairs={{0,16},{1,17},{2,18},{3,19},{4,20},{5,21},{6,22},{7,23},{8,24},{9,... | collective-permute-start | bytes 1572872 | tf_op jit(solution)/shard_map/ppermute | solution.py:483
  15.6 1.4 collective-permute-start.8
  17.0 11.2 %collective-permute-done = bf16[512,512]{1,0:T(8,128)(2,1)S(1)} collective-permute-done((bf16[512,512]{1,0:T(8,128)(2,1)}, bf16[512,512]{1,0:T(8,128)(2,1)S(1)}, u32[]{:S(2)}, u32[]{:S(2)}) %collective-permute-start) | collective-permute-done | bytes 524320 | tf_op jit(solution)/shard_map/ppermute | solution.py:483
  28.2 1.9 broadcast_select_fusion.1.own
  30.1 1.6 collective-permute-start.1
  31.7 2.2 %collective-permute-start.2 = (bf16[512,512]{1,0:T(8,128)(2,1)}, bf16[512,512]{1,0:T(8,128)(2,1)}, u32[]{:S(2)}, u32[]{:S(2)}) collective-permute-start(bf16[512,512]{1,0:T(8,128)(2,1)} %broadcast_select_fusion.1.own), channel_id=1, source_target_pairs={{4,0},{8,4},{12,8},{0,12},{5,1},{9,5},{13,9},{1,13},{6,2},{10,6},{... | collective-permute-start | bytes 1572872 | tf_op jit(solution)/shard_map/ppermute | solution.py:446
  33.9 15.6 %collective-permute-done.8.refs_2_ = bf16[512,1024]{1,0:T(8,128)(2,1)S(1)} collective-permute-done((bf16[512,1024]{1,0:T(8,128)(2,1)}, bf16[512,1024]{1,0:T(8,128)(2,1)S(1)}, u32[]{:S(2)}, u32[]{:S(2)}) %collective-permute-start.8) | collective-permute-done | bytes 1048608 | tf_op jit(solution)/shard_map/ppermute | solution.py:484
  49.5 1.6 copy-done.4
  51.1 8.5 %conv.3 = (bf16[512,512]{1,0:T(8,128)(2,1)S(1)}, bf16[512,512]{1,0:T(8,128)(2,1)S(1)}) custom-call(s32[1]{0:T(128)} %bitcast.seq_ref, s32[16]{0:T(128)S(1)} %copy-done.8, bf16[512,1024]{1,0:T(8,128)(2,1)S(1)} %copy-done.1, f32[27,512]{1,0:T(8,128)S(1)} %copy-done.6, bf16[512,1024]{1,0:T(8,128)(2,1)S(1)} %collective-permute-done.8.refs_2_, ...), custom_call_target="tpu_custom_call" | custom-call | flops 14155776 | bytes 4194304 | tf_op jit(solution)/shard_map/conv/pallas_call | solution.py:153
  59.6 1.3 collective-permute-start.9
  60.9 1.1 select_select_fusion.1
  62.1 2.8 %collective-permute-start.3 = (bf16[512,512]{1,0:T(8,128)(2,1)S(1)}, bf16[512,512]{1,0:T(8,128)(2,1)S(1)}, u32[]{:S(2)}, u32[]{:S(2)}) collective-permute-start(bf16[512,512]{1,0:T(8,128)(2,1)S(1)} %select_select_fusion.1), channel_id=1, source_target_pairs={{4,0},{12,4},{8,12},{0,8},{5,1},{13,5},{9,13},{1,9},{6,2},{14,6},{... | collective-permute-start | bytes 1572872 | tf_op jit(solution)/shard_map/ppermute | solution.py:448
  64.9 9.6 %collective-permute-done.9 = bf16[512,512]{1,0:T(8,128)(2,1)S(1)} collective-permute-done((bf16[512,512]{1,0:T(8,128)(2,1)S(1)}, bf16[512,512]{1,0:T(8,128)(2,1)S(1)}, u32[]{:S(2)}, u32[]{:S(2)}) %collective-permute-start.9) | collective-permute-done | bytes 524320 | tf_op jit(solution)/shard_map/ppermute | solution.py:491
  74.5 1.6 collective-permute-start.10
  76.1 2.2 %collective-permute-start.11 = (bf16[512,512]{1,0:T(8,128)(2,1)S(1)}, bf16[512,512]{1,0:T(8,128)(2,1)S(1)}, u32[]{:S(2)}, u32[]{:S(2)}) collective-permute-start(bf16[512,512]{1,0:T(8,128)(2,1)S(1)} %broadcast_select_fusion.own), channel_id=1, source_target_pairs={{4,0},{8,4},{12,8},{0,12},{5,1},{9,5},{13,9},{1,13},{6,2},{10,6},{... | collective-permute-start | bytes 1572872 | tf_op jit(solution)/shard_map/ppermute | solution.py:446
  78.4 0.7 pad_add_fusion.blocks_ref
  79.1 8.5 %prepare.1 = (bf16[1536,2048]{1,0:T(8,128)(2,1)}, bf16[2048,512]{1,0:T(8,128)(2,1)}) custom-call(s32[4]{0:T(128)} %pad_add_fusion.blocks_ref, f32[1,2048]{1,0:T(1,128)} %bitcast.18, bf16[1536,2048]{1,0:T(8,128)(2,1)} %bitcast.17, bf16[512,2048]{1,0:T(8,128)(2,1)} %out_ref.1), custom_call_target="tpu_custom_call" | custom-call | flops 3145728 | bytes 16777216 | tf_op jit(solution)/shard_map/prepare/pallas_call | solution.py:184
  87.5 0.8 copy-done.13
  88.3 8.6 %project.2 = (bf16[512,512]{1,0:T(8,128)(2,1)}, bf16[1024,512]{1,0:T(8,128)(2,1)}) custom-call(bf16[1536,2048]{1,0:T(8,128)(2,1)} %get-tuple-element.23.weight_ref, bf16[512,512]{1,0:T(8,128)(2,1)} %broadcast_select_fusion.1.own, bf16[512,512]{1,0:T(8,128)(2,1)} %collective-permute-done.1.before, bf16[512,512]{1,0:T(8,128)(2,1)} %collective-permute-done.2.after, ...), custom_call_target="tpu_custom_call" | custom-call | flops 3221225472 | bytes 9961472 | tf_op jit(solution)/shard_map/project/pallas_call | solution.py:244
  96.9 2.3 %collective-permute-done.11.after = bf16[512,512]{1,0:T(8,128)(2,1)S(1)} collective-permute-done((bf16[512,512]{1,0:T(8,128)(2,1)S(1)}, bf16[512,512]{1,0:T(8,128)(2,1)S(1)}, u32[]{:S(2)}, u32[]{:S(2)}) %collective-permute-start.11) | collective-permute-done | bytes 524320 | tf_op jit(solution)/shard_map/ppermute | solution.py:446
  99.2 1.2 collective-permute-start.12
  100.5 12.1 %collective-permute-done.12.across = bf16[512,512]{1,0:T(8,128)(2,1)S(1)} collective-permute-done((bf16[512,512]{1,0:T(8,128)(2,1)S(1)}, bf16[512,512]{1,0:T(8,128)(2,1)S(1)}, u32[]{:S(2)}, u32[]{:S(2)}) %collective-permute-start.12) | collective-permute-done | bytes 524320 | tf_op jit(solution)/shard_map/ppermute | solution.py:448
  112.6 0.8 copy-done.14
  113.4 8.6 %project.3 = (bf16[512,512]{1,0:T(8,128)(2,1)}, bf16[1024,512]{1,0:T(8,128)(2,1)}) custom-call(bf16[1536,2048]{1,0:T(8,128)(2,1)} %get-tuple-element.23.weight_ref, bf16[512,512]{1,0:T(8,128)(2,1)} %copy-done.9, bf16[512,512]{1,0:T(8,128)(2,1)} %copy-done.10, bf16[512,512]{1,0:T(8,128)(2,1)} %copy-done.11, bf16[512,512]{1,0:T(8,128)(2,1)} %copy-done.14), custom_call_target="tpu_custom_call" | custom-call | flops 3221225472 | bytes 9961472 | tf_op jit(solution)/shard_map/project/pallas_call | solution.py:244
  122.0 2.1 collective-permute-start.13
  124.1 4.8 %attend.3 = bf16[512,512]{1,0:T(8,128)(2,1)S(1)} custom-call(s32[1]{0:T(128)} %bitcast.seq_ref, s32[16]{0:T(128)S(1)} %copy-done.8, s32[16,16]{1,0:T(8,128)S(1)} %copy-done.7, bf16[512,512]{1,0:T(8,128)(2,1)S(1)} %copy-done.5, bf16[1024,512]{1,0:T(8,128)(2,1)S(1)} %copy-done, bf16[1024,512]{1,0:T(8,128)(2,1)S(1)} %collective-permute-done.4.refs_1_.refs_3_.refs_4_, ...), custom_call_target="tpu_custom_call" | custom-call | flops 1073741824 | bytes 3145728 | tf_op jit(solution)/shard_map/attend/pallas_call | solution.py:362
  128.8 0.4 convolution_convert_fusion.4
  129.3 2.7 %collective-permute-start.5 = (bf16[512,512]{1,0:T(8,128)(2,1)S(1)}, bf16[512,512]{1,0:T(8,128)(2,1)S(1)}, u32[]{:S(2)}, u32[]{:S(2)}) collective-permute-start(bf16[512,512]{1,0:T(8,128)(2,1)S(1)} %convolution_convert_fusion.4), channel_id=1, source_target_pairs={{0,4},{4,12},{12,8},{8,0},{1,5},{5,13},{13,9},{9,1},{2,6},{6,14},{... | collective-permute-start | bytes 1572872 | tf_op jit(solution)/shard_map/ppermute | solution.py:465
  132.0 0.4 convolution_convert_fusion.5
  132.4 0.4 convolution_convert_fusion.6
  132.9 6.8 %attend.4 = (f32[4,2,512]{2,1,0:T(2,128)S(1)}, f32[512,512]{1,0:T(8,128)S(1)}) custom-call(s32[1]{0:T(128)} %bitcast.seq_ref, s32[16]{0:T(128)S(1)} %copy-done.8, s32[16,16]{1,0:T(8,128)S(1)} %copy-done.7, bf16[512,512]{1,0:T(8,128)(2,1)S(1)} %copy-done.3, bf16[1024,512]{1,0:T(8,128)(2,1)S(1)} %copy-done, ...), custom_call_target="tpu_custom_call" | custom-call | flops 1610612736 | bytes 4194304 | tf_op jit(solution)/shard_map/attend/pallas_call | solution.py:362
  139.7 3.5 %collective-permute-done.5 = bf16[512,512]{1,0:T(8,128)(2,1)S(1)} collective-permute-done((bf16[512,512]{1,0:T(8,128)(2,1)S(1)}, bf16[512,512]{1,0:T(8,128)(2,1)S(1)}, u32[]{:S(2)}, u32[]{:S(2)}) %collective-permute-start.5) | collective-permute-done | bytes 524320 | tf_op jit(solution)/shard_map/ppermute | solution.py:465
  143.5 2.1 %collective-permute-start.6 = (bf16[512,512]{1,0:T(8,128)(2,1)S(1)}, bf16[512,512]{1,0:T(8,128)(2,1)S(1)}, u32[]{:S(2)}, u32[]{:S(2)}) collective-permute-start(bf16[512,512]{1,0:T(8,128)(2,1)S(1)} %get-tuple-element.41), channel_id=1, source_target_pairs={{4,0},{8,4},{12,8},{0,12},{5,1},{9,5},{13,9},{1,13},{6,2},{10,6},{... | collective-permute-start | bytes 1572872 | tf_op jit(solution)/shard_map/ppermute | solution.py:467
  145.7 1.3 collective-permute-done.13.refs_0_.refs_1_
  147.0 3.6 %attend.5 = bf16[512,512]{1,0:T(8,128)(2,1)S(1)} custom-call(s32[1]{0:T(128)} %bitcast.seq_ref, s32[16]{0:T(128)S(1)} %copy-done.8, s32[16,16]{1,0:T(8,128)S(1)} %copy-done.7, bf16[512,512]{1,0:T(8,128)(2,1)S(1)} %copy-done.3, bf16[1024,512]{1,0:T(8,128)(2,1)S(1)} %collective-permute-done.13.refs_0_.refs_1_, ...), custom_call_target="tpu_custom_call" | custom-call | flops 536870912 | bytes 2097152 | tf_op jit(solution)/shard_map/attend/pallas_call | solution.py:362
  150.6 0.4 convolution_convert_fusion
  151.1 2.4 %collective-permute-start.14 = (bf16[512,512]{1,0:T(8,128)(2,1)S(1)}, bf16[512,512]{1,0:T(8,128)(2,1)S(1)}, u32[]{:S(2)}, u32[]{:S(2)}) collective-permute-start(bf16[512,512]{1,0:T(8,128)(2,1)S(1)} %convolution_convert_fusion), channel_id=1, source_target_pairs={{0,4},{4,12},{12,8},{8,0},{1,5},{5,13},{13,9},{9,1},{2,6},{6,14},{... | collective-permute-start | bytes 1572872 | tf_op jit(solution)/shard_map/ppermute | solution.py:465
  153.5 0.4 convolution_convert_fusion.1
  153.9 0.4 convolution_convert_fusion.2
  154.4 24.4 %collective-permute-done.14.refs_3_ = bf16[512,512]{1,0:T(8,128)(2,1)S(1)} collective-permute-done((bf16[512,512]{1,0:T(8,128)(2,1)S(1)}, bf16[512,512]{1,0:T(8,128)(2,1)S(1)}, u32[]{:S(2)}, u32[]{:S(2)}) %collective-permute-start.14) | collective-permute-done | bytes 524320 | tf_op jit(solution)/shard_map/ppermute | solution.py:465
  178.8 0.3 fusion.8
  179.1 2.7 %collective-permute-start.15 = (bf16[512,512]{1,0:T(8,128)(2,1)S(1)}, bf16[512,512]{1,0:T(8,128)(2,1)S(1)}, u32[]{:S(2)}, u32[]{:S(2)}) collective-permute-start(bf16[512,512]{1,0:T(8,128)(2,1)S(1)} %get-tuple-element.40), channel_id=1, source_target_pairs={{4,0},{8,4},{12,8},{0,12},{5,1},{9,5},{13,9},{1,13},{6,2},{10,6},{... | collective-permute-start | bytes 1572872 | tf_op jit(solution)/shard_map/ppermute | solution.py:467
  181.8 0.4 convolution_convert_fusion.3.refs_0_
  182.3 0.5 fusion.4.first_ref
  182.8 11.3 %collective-permute-done.15.refs_1_ = bf16[512,512]{1,0:T(8,128)(2,1)S(1)} collective-permute-done((bf16[512,512]{1,0:T(8,128)(2,1)S(1)}, bf16[512,512]{1,0:T(8,128)(2,1)S(1)}, u32[]{:S(2)}, u32[]{:S(2)}) %collective-permute-start.15) | collective-permute-done | bytes 524320 | tf_op jit(solution)/shard_map/ppermute | solution.py:467
  194.1 10.4 %collective-permute-done.16.refs_2_ = bf16[512,512]{1,0:T(8,128)(2,1)S(1)} collective-permute-done((bf16[512,512]{1,0:T(8,128)(2,1)S(1)}, bf16[512,512]{1,0:T(8,128)(2,1)S(1)}, u32[]{:S(2)}, u32[]{:S(2)}) %collective-permute-start.16) | collective-permute-done | bytes 524320 | tf_op jit(solution)/shard_map/ppermute | solution.py:468
  204.5 2.8 %place.1 = bf16[512,1024]{1,0:T(8,128)(2,1)} custom-call(s32[1]{0:T(128)} %bitcast.seq_ref, s32[16]{0:T(128)S(1)} %copy-done.8, s32[1]{0:T(128)} %bitcast.1.ends_ref, bf16[512,512]{1,0:T(8,128)(2,1)S(1)} %fusion.4.first_ref, bf16[512,512]{1,0:T(8,128)(2,1)S(1)} %convolution_convert_fusion.3.refs_0_, bf16[512,512]{1,0:T(8,128)(2,1)S(1)} %collective-permute-done.15.refs_1_, ...), custom_call_target="tpu_custom_call" | custom-call | flops 1048576 | bytes 3670016 | tf_op jit(solution)/shard_map/place/pallas_call | solution.py:420
  (40 shorter events, 0.5 us)
Async XLA Ops:
  0.0 49.5 %copy-start.8 = (s32[16]{0:T(128)S(1)}, s32[16]{0:T(128)}, u32[]{:S(2)}) copy-start(s32[16]{0:T(128)} %order_ref.11) | copy-start | bytes 196
  0.0 49.5 %copy-start.1 = (bf16[512,1024]{1,0:T(8,128)(2,1)S(1)}, bf16[512,1024]{1,0:T(8,128)(2,1)}, u32[]{:S(2)}) copy-start(bf16[512,1024]{1,0:T(8,128)(2,1)} %refs_0_.3) | copy-start | bytes 3145732
  0.0 49.5 %copy-start.6 = (f32[27,512]{1,0:T(8,128)S(1)}, f32[27,512]{1,0:T(8,128)}, u32[]{:S(2)}) copy-start(f32[27,512]{1,0:T(8,128)} %refs_1_.3) | copy-start | bytes 165892
  10.7 17.5 %collective-permute-start = (bf16[512,512]{1,0:T(8,128)(2,1)}, bf16[512,512]{1,0:T(8,128)(2,1)S(1)}, u32[]{:S(2)}, u32[]{:S(2)}) collective-permute-start(bf16[512,512]{1,0:T(8,128)(2,1)} %get-tuple-element.25), channel_id=1, source_target_pairs={{0,16},{1,17},{2,18},{3,19},{4,20},{5,21},{6,22},{7,23},{8,24},{9,... | collective-permute-start | bytes 1572872 | tf_op jit(solution)/shard_map/ppermute | solution.py:483
  15.6 33.9 %collective-permute-start.8 = (bf16[512,1024]{1,0:T(8,128)(2,1)}, bf16[512,1024]{1,0:T(8,128)(2,1)S(1)}, u32[]{:S(2)}, u32[]{:S(2)}) collective-permute-start(bf16[512,1024]{1,0:T(8,128)(2,1)} %refs_0_.3), channel_id=1, source_target_pairs={{0,16},{1,17},{2,18},{3,19},{4,20},{5,21},{6,22},{7,23},{8,24},{9,... | collective-permute-start | bytes 3145736 | tf_op jit(solution)/shard_map/ppermute | solution.py:484
  30.1 30.8 %collective-permute-start.1 = (bf16[512,512]{1,0:T(8,128)(2,1)}, bf16[512,512]{1,0:T(8,128)(2,1)}, u32[]{:S(2)}, u32[]{:S(2)}) collective-permute-start(bf16[512,512]{1,0:T(8,128)(2,1)} %broadcast_select_fusion.1.own), channel_id=1, source_target_pairs={{0,4},{4,8},{8,12},{12,0},{1,5},{5,9},{9,13},{13,1},{2,6},{6,10},{... | collective-permute-start | bytes 1572872 | tf_op jit(solution)/shard_map/ppermute | solution.py:445
  31.7 29.2 %collective-permute-start.2 = (bf16[512,512]{1,0:T(8,128)(2,1)}, bf16[512,512]{1,0:T(8,128)(2,1)}, u32[]{:S(2)}, u32[]{:S(2)}) collective-permute-start(bf16[512,512]{1,0:T(8,128)(2,1)} %broadcast_select_fusion.1.own), channel_id=1, source_target_pairs={{4,0},{8,4},{12,8},{0,12},{5,1},{9,5},{13,9},{1,13},{6,2},{10,6},{... | collective-permute-start | bytes 1572872 | tf_op jit(solution)/shard_map/ppermute | solution.py:446
  49.5 1.6 copy-start.4
  59.6 14.8 %collective-permute-start.9 = (bf16[512,512]{1,0:T(8,128)(2,1)S(1)}, bf16[512,512]{1,0:T(8,128)(2,1)S(1)}, u32[]{:S(2)}, u32[]{:S(2)}) collective-permute-start(bf16[512,512]{1,0:T(8,128)(2,1)S(1)} %get-tuple-element.32), channel_id=1, source_target_pairs={{16,0},{17,1},{18,2},{19,3},{20,4},{21,5},{22,6},{23,7},{24,8},{25... | collective-permute-start | bytes 1572872 | tf_op jit(solution)/shard_map/ppermute | solution.py:491
  62.1 25.5 %collective-permute-start.3 = (bf16[512,512]{1,0:T(8,128)(2,1)S(1)}, bf16[512,512]{1,0:T(8,128)(2,1)S(1)}, u32[]{:S(2)}, u32[]{:S(2)}) collective-permute-start(bf16[512,512]{1,0:T(8,128)(2,1)S(1)} %select_select_fusion.1), channel_id=1, source_target_pairs={{4,0},{12,4},{8,12},{0,8},{5,1},{13,5},{9,13},{1,9},{6,2},{14,6},{... | collective-permute-start | bytes 1572872 | tf_op jit(solution)/shard_map/ppermute | solution.py:448
  74.5 24.7 %copy-start.9 = (bf16[512,512]{1,0:T(8,128)(2,1)}, bf16[512,512]{1,0:T(8,128)(2,1)S(1)}, u32[]{:S(2)}) copy-start(bf16[512,512]{1,0:T(8,128)(2,1)S(1)} %broadcast_select_fusion.own) | copy-start | bytes 1572868
  74.5 22.4 %collective-permute-start.10 = (bf16[512,512]{1,0:T(8,128)(2,1)S(1)}, bf16[512,512]{1,0:T(8,128)(2,1)S(1)}, u32[]{:S(2)}, u32[]{:S(2)}) collective-permute-start(bf16[512,512]{1,0:T(8,128)(2,1)S(1)} %broadcast_select_fusion.own), channel_id=1, source_target_pairs={{0,4},{4,8},{8,12},{12,0},{1,5},{5,9},{9,13},{13,1},{2,6},{6,10},{... | collective-permute-start | bytes 1572872 | tf_op jit(solution)/shard_map/ppermute | solution.py:445
  76.1 23.0 %collective-permute-start.11 = (bf16[512,512]{1,0:T(8,128)(2,1)S(1)}, bf16[512,512]{1,0:T(8,128)(2,1)S(1)}, u32[]{:S(2)}, u32[]{:S(2)}) collective-permute-start(bf16[512,512]{1,0:T(8,128)(2,1)S(1)} %broadcast_select_fusion.own), channel_id=1, source_target_pairs={{4,0},{8,4},{12,8},{0,12},{5,1},{9,5},{13,9},{1,13},{6,2},{10,6},{... | collective-permute-start | bytes 1572872 | tf_op jit(solution)/shard_map/ppermute | solution.py:446
  87.5 0.8 copy-start.13
  96.9 27.2 %collective-permute-start.4 = (bf16[1024,512]{1,0:T(8,128)(2,1)}, bf16[1024,512]{1,0:T(8,128)(2,1)S(1)}, u32[]{:S(2)}, u32[]{:S(2)}) collective-permute-start(bf16[1024,512]{1,0:T(8,128)(2,1)} %get-tuple-element.27.refs_0_.refs_2_.refs_3_), channel_id=1, source_target_pairs={{0,16},{16,0},{1,17},{17,1},{2,18},{18,2},{3,19},{19,3},{4,20},{20... | collective-permute-start | bytes 3145736 | tf_op jit(solution)/shard_map/ppermute | solution.py:496
  96.9 15.7 %copy-start.10 = (bf16[512,512]{1,0:T(8,128)(2,1)}, bf16[512,512]{1,0:T(8,128)(2,1)S(1)}, u32[]{:S(2)}) copy-start(bf16[512,512]{1,0:T(8,128)(2,1)S(1)} %collective-permute-done.10.before) | copy-start | bytes 1572868
  99.2 13.4 %copy-start.11 = (bf16[512,512]{1,0:T(8,128)(2,1)}, bf16[512,512]{1,0:T(8,128)(2,1)S(1)}, u32[]{:S(2)}) copy-start(bf16[512,512]{1,0:T(8,128)(2,1)S(1)} %collective-permute-done.11.after) | copy-start | bytes 1572868
  99.2 13.3 %collective-permute-start.12 = (bf16[512,512]{1,0:T(8,128)(2,1)S(1)}, bf16[512,512]{1,0:T(8,128)(2,1)S(1)}, u32[]{:S(2)}, u32[]{:S(2)}) collective-permute-start(bf16[512,512]{1,0:T(8,128)(2,1)S(1)} %select_select_fusion), channel_id=1, source_target_pairs={{4,0},{12,4},{8,12},{0,8},{5,1},{13,5},{9,13},{1,9},{6,2},{14,6},{... | collective-permute-start | bytes 1572872 | tf_op jit(solution)/shard_map/ppermute | solution.py:448
  100.5 23.6 %copy-start = (bf16[1024,512]{1,0:T(8,128)(2,1)S(1)}, bf16[1024,512]{1,0:T(8,128)(2,1)}, u32[]{:S(2)}) copy-start(bf16[1024,512]{1,0:T(8,128)(2,1)} %get-tuple-element.27.refs_0_.refs_2_.refs_3_) | copy-start | bytes 3145732
  100.5 23.6 %copy-start.5 = (bf16[512,512]{1,0:T(8,128)(2,1)S(1)}, bf16[512,512]{1,0:T(8,128)(2,1)}, u32[]{:S(2)}) copy-start(bf16[512,512]{1,0:T(8,128)(2,1)} %get-tuple-element.26.query_ref) | copy-start | bytes 1572868
  100.5 23.6 %copy-start.7 = (s32[16,16]{1,0:T(8,128)S(1)}, s32[16,16]{1,0:T(8,128)}, u32[]{:S(2)}) copy-start(s32[16,16]{1,0:T(8,128)} %mask_ref.5) | copy-start | bytes 3076
  112.6 0.8 copy-start.14
  122.0 25.0 %collective-permute-start.13 = (bf16[1024,512]{1,0:T(8,128)(2,1)}, bf16[1024,512]{1,0:T(8,128)(2,1)S(1)}, u32[]{:S(2)}, u32[]{:S(2)}) collective-permute-start(bf16[1024,512]{1,0:T(8,128)(2,1)} %get-tuple-element.34.refs_2_.refs_5_), channel_id=1, source_target_pairs={{0,16},{16,0},{1,17},{17,1},{2,18},{18,2},{3,19},{19,3},{4,20},{20... | collective-permute-start | bytes 3145736 | tf_op jit(solution)/shard_map/ppermute | solution.py:501
  124.1 4.8 %copy-start.12 = (bf16[2048,512]{1,0:T(8,128)(2,1)S(1)}, bf16[2048,512]{1,0:T(8,128)(2,1)}, u32[]{:S(2)}) copy-start(bf16[2048,512]{1,0:T(8,128)(2,1)} %get-tuple-element.22) | copy-start | bytes 6291460
  129.3 3.6 %copy-start.2 = (bf16[1024,512]{1,0:T(8,128)(2,1)S(1)}, bf16[1024,512]{1,0:T(8,128)(2,1)}, u32[]{:S(2)}) copy-start(bf16[1024,512]{1,0:T(8,128)(2,1)} %get-tuple-element.34.refs_2_.refs_5_) | copy-start | bytes 3145732
  129.3 3.6 %copy-start.3 = (bf16[512,512]{1,0:T(8,128)(2,1)S(1)}, bf16[512,512]{1,0:T(8,128)(2,1)}, u32[]{:S(2)}) copy-start(bf16[512,512]{1,0:T(8,128)(2,1)} %get-tuple-element.33.query_ref) | copy-start | bytes 1572868
  129.3 13.9 %collective-permute-start.5 = (bf16[512,512]{1,0:T(8,128)(2,1)S(1)}, bf16[512,512]{1,0:T(8,128)(2,1)S(1)}, u32[]{:S(2)}, u32[]{:S(2)}) collective-permute-start(bf16[512,512]{1,0:T(8,128)(2,1)S(1)} %convolution_convert_fusion.4), channel_id=1, source_target_pairs={{0,4},{4,12},{12,8},{8,0},{1,5},{5,13},{13,9},{9,1},{2,6},{6,14},{... | collective-permute-start | bytes 1572872 | tf_op jit(solution)/shard_map/ppermute | solution.py:465
  143.5 38.7 %collective-permute-start.6 = (bf16[512,512]{1,0:T(8,128)(2,1)S(1)}, bf16[512,512]{1,0:T(8,128)(2,1)S(1)}, u32[]{:S(2)}, u32[]{:S(2)}) collective-permute-start(bf16[512,512]{1,0:T(8,128)(2,1)S(1)} %get-tuple-element.41), channel_id=1, source_target_pairs={{4,0},{8,4},{12,8},{0,12},{5,1},{9,5},{13,9},{1,13},{6,2},{10,6},{... | collective-permute-start | bytes 1572872 | tf_op jit(solution)/shard_map/ppermute | solution.py:467
  145.7 36.6 %collective-permute-start.7 = (bf16[512,512]{1,0:T(8,128)(2,1)S(1)}, bf16[512,512]{1,0:T(8,128)(2,1)S(1)}, u32[]{:S(2)}, u32[]{:S(2)}) collective-permute-start(bf16[512,512]{1,0:T(8,128)(2,1)S(1)} %get-tuple-element.42), channel_id=1, source_target_pairs={{0,4},{4,8},{8,12},{12,0},{1,5},{5,9},{9,13},{13,1},{2,6},{6,10},{... | collective-permute-start | bytes 1572872 | tf_op jit(solution)/shard_map/ppermute | solution.py:468
  151.1 27.7 %collective-permute-start.14 = (bf16[512,512]{1,0:T(8,128)(2,1)S(1)}, bf16[512,512]{1,0:T(8,128)(2,1)S(1)}, u32[]{:S(2)}, u32[]{:S(2)}) collective-permute-start(bf16[512,512]{1,0:T(8,128)(2,1)S(1)} %convolution_convert_fusion), channel_id=1, source_target_pairs={{0,4},{4,12},{12,8},{8,0},{1,5},{5,13},{13,9},{9,1},{2,6},{6,14},{... | collective-permute-start | bytes 1572872 | tf_op jit(solution)/shard_map/ppermute | solution.py:465
  179.1 15.0 %collective-permute-start.15 = (bf16[512,512]{1,0:T(8,128)(2,1)S(1)}, bf16[512,512]{1,0:T(8,128)(2,1)S(1)}, u32[]{:S(2)}, u32[]{:S(2)}) collective-permute-start(bf16[512,512]{1,0:T(8,128)(2,1)S(1)} %get-tuple-element.40), channel_id=1, source_target_pairs={{4,0},{8,4},{12,8},{0,12},{5,1},{9,5},{13,9},{1,13},{6,2},{10,6},{... | collective-permute-start | bytes 1572872 | tf_op jit(solution)/shard_map/ppermute | solution.py:467
  181.8 22.7 %collective-permute-start.16 = (bf16[512,512]{1,0:T(8,128)(2,1)S(1)}, bf16[512,512]{1,0:T(8,128)(2,1)S(1)}, u32[]{:S(2)}, u32[]{:S(2)}) collective-permute-start(bf16[512,512]{1,0:T(8,128)(2,1)S(1)} %get-tuple-element.39), channel_id=1, source_target_pairs={{0,4},{4,8},{8,12},{12,0},{1,5},{5,9},{9,13},{13,1},{2,6},{6,10},{... | collective-permute-start | bytes 1572872 | tf_op jit(solution)/shard_map/ppermute | solution.py:468

commit v3 on v2

--- a/solution.py
+++ b/solution.py
@@ -22,43 +22,56 @@
 LOG2E = math.log2(math.e)
 
 VMEM_LIMIT = 20 * 1024 * 1024
-VMEM_MOST = 57 * 1024 * 1024
 VMEM_WHOLE = 60 * 1024 * 1024
+
+
+def vmem_spec():
+    return pl.BlockSpec(memory_space=pltpu.VMEM)
+
+
+def smem_spec():
+    return pl.BlockSpec(memory_space=pltpu.SMEM)
 
 
 def params(limit=VMEM_LIMIT):
     return pltpu.CompilerParams(vmem_limit_bytes=limit)
 
 
-def column_shifts(frame, lane):
-    column = lane % FW
-    left = jnp.where(column > 0, pltpu.roll(frame, 1, 1), 0.0)
-    right = jnp.where(column < FW - 1, pltpu.roll(frame, FRAME - 1, 1), 0.0)
-    return (left, frame, right)
-
-
-def row_sum(rows, lane):
-    above = jnp.where(lane >= FW, pltpu.roll(rows[0], FW, 1), 0.0)
-    below = jnp.where(lane < FRAME - FW, pltpu.roll(rows[2], FRAME - FW, 1), 0.0)
-    return rows[1] + above + below
-
-
-def spread(taps, tap):
-    column = jnp.broadcast_to(taps[:, tap : tap + 1], (taps.shape[0], 128))
-    return jnp.concatenate([column] * (FRAME // 128), axis=1)
-
-
-def taps_applied(pairs, taps, lane):
-    rows = []
-    for row_off in range(3):
-        total = None
-        for time_off, shifts in pairs:
-            for col_off in range(3):
-                tap = time_off * 9 + row_off * 3 + col_off
-                term = spread(taps, tap) * shifts[col_off]
-                total = term if total is None else total + term
-        rows.append(total)
-    return row_sum(rows, lane)
+def shift_matrix(row_off, col_offs, rows):
+    shape = (rows, TILE * len(col_offs))
+    source = lax.broadcasted_iota(jnp.int32, shape, 0)
+    target = lax.broadcasted_iota(jnp.int32, shape, 1)
+    lane = target % TILE
+    col_off = jnp.zeros(shape, jnp.int32)
+    for index, offset in enumerate(col_offs):
+        col_off = jnp.where(target // TILE == index, offset, col_off)
+    base = TILE if row_off < 0 else 0
+    wanted = lane + row_off * FW + col_off + base
+    column = lane % FW + col_off
+    inside = (column >= 0) & (column < FW)
+    return jnp.where((source == wanted) & inside, 1.0, 0.0).astype(jnp.bfloat16)
+
+
+def shift_pieces(source_ref, shifted, matrices):
+    channels, tokens = source_ref.shape
+    pieces = tokens // TILE
+    per_frame = FRAME // TILE
+    nothing = jnp.zeros((channels, TILE), jnp.bfloat16)
+
+    def piece(index):
+        return source_ref[:, index * TILE : (index + 1) * TILE]
+
+    above, here, below = [], [], []
+    for index in range(pieces):
+        first, last = index % per_frame == 0, index % per_frame == per_frame - 1
+        now = piece(index)
+        here.append(now)
+        above.append(jnp.concatenate([nothing if first else piece(index - 1), now], axis=1))
+        below.append(jnp.concatenate([now, nothing if last else piece(index + 1)], axis=1))
+    for out, matrix, parts in zip(shifted, matrices, (above, here, below)):
+        out[...] = jnp.dot(
+            jnp.concatenate(parts, axis=0), matrix[...], preferred_element_type=jnp.float32
+        )
 
 
 def pack_slots(order_ref, slots_ref, seq_here, tiles_dev, positions):
@@ -81,54 +94,59 @@
 
 
 def conv_body(with_before, seq_ref, order_ref, *refs):
-    if with_before:
-        tokens_ref, taps_ref, before_ref, part_ref, keep_ref, send_ref, slots_ref, taps_scr, packed = refs
-    else:
-        tokens_ref, taps_ref, part_ref, keep_ref, send_ref, slots_ref, taps_scr, packed = refs
+    tokens_ref, taps_ref, part_ref, keep_ref, send_ref, *refs = refs
+    slots_ref, taps_scr, packed, *refs = refs
+    shifted, matrices = refs[:3], refs[3:]
     channels, tokens = tokens_ref.shape
     tiles_dev = tokens // TILE
+    per_frame = FRAME // TILE
     seq_here = seq_ref[0]
 
     @pl.when(pl.program_id(0) == 0)
     def _():
         pack_slots(order_ref, slots_ref, seq_here, tiles_dev, order_ref.shape[0])
+        matrices[0][...] = shift_matrix(-1, (-1, 0, 1), 2 * TILE)
+        matrices[1][...] = shift_matrix(0, (-1, 1), TILE)
+        matrices[2][...] = shift_matrix(1, (-1, 0, 1), 2 * TILE)
 
     taps_scr[:, :TAPS] = taps_ref[...].T
+    shift_pieces(tokens_ref, shifted, matrices)
     group = 16
-    part = 16
-    lane = lax.broadcasted_iota(jnp.int32, (part, FRAME), 1)
-
-    def frame_of(ref, rows, frame, piece):
-        wide = ref[rows, frame * FRAME : (frame + 1) * FRAME].astype(jnp.float32)
-        return column_shifts(wide[piece * part : (piece + 1) * part], lane)
+    reads = ((0, 0, 0), (0, 1, 1), (1, 1, 0)) if with_before else ((2, 0, 0), (2, 1, 1), (1, 0, 1))
 
     def advance(step, carry):
         start = pl.multiple_of(step * group, group)
         rows = pl.ds(start, group)
-        pieces = []
-        for piece in range(group // part):
-            inner = pl.ds(start + piece * part, part)
-            taps = taps_scr[inner, :]
-            if with_before:
-                old = [frame_of(before_ref, rows, f, piece) for f in range(2)]
-                sums = [
-                    part_ref[inner, :FRAME] + taps_applied([(0, old[0]), (1, old[1])], taps, lane),
-                    part_ref[inner, FRAME:] + taps_applied([(0, old[1])], taps, lane),
-                ]
-            else:
-                now = [frame_of(tokens_ref, rows, f, piece) for f in range(2)]
-                sums = [
-                    now[0][1] + taps_applied([(2, now[0])], taps, lane),
-                    now[1][1] + taps_applied([(1, now[0]), (2, now[1])], taps, lane),
-                ]
-                part_ref[inner, :FRAME] = sums[0]
-                part_ref[inner, FRAME:] = sums[1]
-            pieces.append(sums)
+        taps = taps_scr[rows, :]
+        centre = [
+            tokens_ref[rows, tile * TILE : (tile + 1) * TILE].astype(jnp.float32)
+            for tile in range(tiles_dev)
+        ]
+        if with_before:
+            sums = [part_ref[rows, tile * TILE : (tile + 1) * TILE] for tile in range(tiles_dev)]
+        else:
+            sums = list(centre)
+
+        def value(tile, row_off, col_off):
+            if row_off == 1 and col_off == 1:
+                return centre[tile]
+            column = col_off // 2 if row_off == 1 else col_off
+            lines = pl.ds(tile * channels + start, group)
+            return shifted[row_off][lines, column * TILE : (column + 1) * TILE]
+
+        for time_off, read, written in reads:
+            for row_off in range(3):
+                for col_off in range(3):
+                    tap = time_off * 9 + row_off * 3 + col_off
+                    weight = jnp.broadcast_to(taps[:, tap : tap + 1], (group, TILE))
+                    for spot in range(per_frame):
+                        out = written * per_frame + spot
+                        sums[out] = sums[out] + weight * value(read * per_frame + spot, row_off, col_off)
         for tile in range(tiles_dev):
-            frame, spot = divmod(tile * TILE, FRAME)
+            if not with_before:
+                part_ref[rows, tile * TILE : (tile + 1) * TILE] = sums[tile]
             place = pl.ds(pl.multiple_of(slots_ref[tile] * TILE, TILE), TILE)
-            joined = jnp.concatenate([sums[frame][:, spot : spot + TILE] for sums in pieces], axis=0)
-            packed[rows, place] = joined.astype(jnp.bfloat16)
+            packed[rows, place] = sums[tile].astype(jnp.bfloat16)
         return carry
 
     lax.fori_loop(0, channels // group, advance, 0)
@@ -136,31 +154,36 @@
     send_ref[...] = packed[:, tokens // 2 :]
 
 
-def conv_call(seq_here, stripe_order, tokens, conv_taps, before=None, part=None):
+def conv_call(seq_here, stripe_order, tokens, conv_taps, part=None):
     channels, count = tokens.shape
     block = 128
     wide = pl.BlockSpec((block, count), lambda i, *_: (i, 0))
     slim = pl.BlockSpec((block, count // 2), lambda i, *_: (i, 0))
     taps_spec = pl.BlockSpec((TAPS, block), lambda i, *_: (0, i))
     packed_shape = jax.ShapeDtypeStruct((channels, count // 2), jnp.bfloat16)
-    with_before = before is not None
-    extra_in, extra_args, out_specs, out_shape = [], [], [slim, slim], [packed_shape, packed_shape]
-    if with_before:
-        extra_in, extra_args = [wide, wide], [before, part]
-    else:
+    with_before = part is not None
+    out_specs, out_shape = [slim, slim], [packed_shape, packed_shape]
+    if not with_before:
         out_specs = [wide] + out_specs
         out_shape = [jax.ShapeDtypeStruct((channels, count), jnp.float32)] + out_shape
+    lines = block * (count // TILE)
     return pl.pallas_call(
         functools.partial(conv_body, with_before),
         grid_spec=pltpu.PrefetchScalarGridSpec(
             num_scalar_prefetch=2,
             grid=(channels // block,),
-            in_specs=[wide, taps_spec] + extra_in,
+            in_specs=[wide, taps_spec] + [wide] * with_before,
             out_specs=out_specs,
             scratch_shapes=[
                 pltpu.SMEM((count // TILE,), jnp.int32),
                 pltpu.VMEM((block, 128), jnp.float32),
                 pltpu.VMEM((block, count), jnp.bfloat16),
+                pltpu.VMEM((lines, 3 * TILE), jnp.float32),
+                pltpu.VMEM((lines, 2 * TILE), jnp.float32),
+                pltpu.VMEM((lines, 3 * TILE), jnp.float32),
+                pltpu.VMEM((2 * TILE, 3 * TILE), jnp.bfloat16),
+                pltpu.VMEM((TILE, 2 * TILE), jnp.bfloat16),
+                pltpu.VMEM((2 * TILE, 3 * TILE), jnp.bfloat16),
             ],
         ),
         out_shape=out_shape,
@@ -169,7 +192,7 @@
             flops=channels * count * TAPS, bytes_accessed=channels * count * 8, transcendentals=0
         ),
         name="conv",
-    )(seq_here, stripe_order, tokens, conv_taps, *extra_args)
+    )(seq_here, stripe_order, tokens, conv_taps, *([part] if with_before else []))
 
 
 def prepare_body(blocks_ref, gain_ref, qkv_ref, out_ref, qkv_out, out_out):
@@ -208,56 +231,62 @@
     )(blocks, norm_gain[None, :], qkv_weight.reshape(kinds * cols, channels), out_weight)
 
 
-def project_body(query_steps, weight_ref, own, before, after, across, query_ref, pair_ref, tokens_ref, inverse_ref):
+def fetches(source, target, semaphores):
+    block = target.shape[0] // semaphores.shape[0]
+    return [
+        pltpu.make_async_copy(
+            source.at[index * block : (index + 1) * block],
+            target.at[index * block : (index + 1) * block],
+            semaphores.at[index],
+        )
+        for index in range(semaphores.shape[0])
+    ]
+
+
+def project_body(weight_hbm, own, before, after, across, query_ref, pair_ref, weight_ref, tokens_ref, arrived):
+    copies = fetches(weight_hbm, weight_ref, arrived)
+    for copy in copies:
+        copy.start()
     width = own.shape[0]
-    step = pl.program_id(0)
-
-    @pl.when(step == 0)
-    def _():
-        squares = None
-        for index, shard in enumerate((own, before, after, across)):
-            block = shard[...]
-            tokens_ref[index * width : (index + 1) * width, :] = block
-            wide = block.astype(jnp.float32)
-            term = jnp.sum(wide * wide, axis=0, keepdims=True)
-            squares = term if squares is None else squares + term
-        inverse_ref[...] = lax.rsqrt(squares / (4 * width) + EPSILON)
-
-    total = jnp.dot(weight_ref[...], tokens_ref[...], preferred_element_type=jnp.float32)
-
-    @pl.when(step < query_steps)
-    def _():
-        query_ref[...] = (total * (inverse_ref[...] * (LOG2E / math.sqrt(HEAD)))).astype(jnp.bfloat16)
-
-    @pl.when(step >= query_steps)
-    def _():
-        pair_ref[...] = (total * inverse_ref[...]).astype(jnp.bfloat16)
+    cols = query_ref.shape[0]
+    squares = None
+    for index, shard in enumerate((own, before, after, across)):
+        block = shard[...]
+        tokens_ref[index * width : (index + 1) * width, :] = block
+        wide = block.astype(jnp.float32)
+        term = jnp.sum(wide * wide, axis=0, keepdims=True)
+        squares = term if squares is None else squares + term
+    inverse = lax.rsqrt(squares / (4 * width) + EPSILON)
+    rows = weight_ref.shape[0] // len(copies)
+    for index, copy in enumerate(copies):
+        copy.wait()
+        here = slice(index * rows, (index + 1) * rows)
+        total = jnp.dot(weight_ref[here, :], tokens_ref[...], preferred_element_type=jnp.float32)
+        if index * rows < cols:
+            query_ref[here, :] = (total * (inverse * (LOG2E / math.sqrt(HEAD)))).astype(jnp.bfloat16)
+        else:
+            there = slice(index * rows - cols, (index + 1) * rows - cols)
+            pair_ref[there, :] = (total * inverse).astype(jnp.bfloat16)
 
 
 def project_call(weights, shards):
     rows, channels = weights.shape
-    width, tokens = shards[0].shape
+    tokens = shards[0].shape[1]
     cols = rows // 3
-    block = 256
-    query_steps = cols // block
-    whole = pl.BlockSpec((width, tokens), lambda i: (0, 0))
     return pl.pallas_call(
-        functools.partial(project_body, query_steps),
-        grid=(rows // block,),
-        in_specs=[pl.BlockSpec((block, channels), lambda i: (i, 0))] + [whole] * len(shards),
-        out_specs=[
-            pl.BlockSpec((block, tokens), lambda i: (jnp.minimum(i, query_steps - 1), 0)),
-            pl.BlockSpec((block, tokens), lambda i: (jnp.maximum(i - query_steps, 0), 0)),
-        ],
+        project_body,
+        in_specs=[pl.BlockSpec(memory_space=pltpu.HBM)] + [vmem_spec()] * len(shards),
+        out_specs=[vmem_spec(), vmem_spec()],
         scratch_shapes=[
+            pltpu.VMEM((rows, channels), jnp.bfloat16),
             pltpu.VMEM((channels, tokens), jnp.bfloat16),
-            pltpu.VMEM((1, tokens), jnp.float32),
+            pltpu.SemaphoreType.DMA((6,)),
         ],
         out_shape=[
             jax.ShapeDtypeStruct((cols, tokens), jnp.bfloat16),
             jax.ShapeDtypeStruct((2 * cols, tokens), jnp.bfloat16),
         ],
-        compiler_params=params(VMEM_MOST),
+        compiler_params=params(),
         cost_estimate=pl.CostEstimate(
             flops=2 * rows * channels * tokens,
             bytes_accessed=2 * (rows * channels + channels * tokens + rows * tokens),
@@ -284,28 +313,23 @@
 
 def attend_body(chunk, sources, goes_on, ends, seq_ref, order_ref, mask_ref, query_ref, *refs):
     count = len(sources)
-    keys, values = refs[:count], refs[count : 2 * count]
-    refs = refs[2 * count :]
+    pairs, refs = refs[:count], refs[count:]
     if goes_on:
-        old_stats, old_weighted, refs = refs[0], refs[1], refs[2:]
+        old_stats, old_weighted, *refs = refs
     if ends:
-        out_ref, refs = refs[0], refs[1:]
+        weight_hbm, *refs = refs
+        partial_refs, refs = refs[:4], refs[4:]
+        ids_ref, bias_ref, scores_ref, heads_ref, weight_ref, arrived = refs
+        copies = fetches(weight_hbm, weight_ref, arrived)
+        for copy in copies:
+            copy.start()
     else:
-        new_stats, new_weighted, refs = refs[0], refs[1], refs[2:]
-    ids_ref, scores_ref = refs
-    tokens = query_ref.shape[1]
+        new_stats, new_weighted, ids_ref, bias_ref, scores_ref = refs
+    cols, tokens = query_ref.shape
     half = tokens // TILE
-
-    @pl.when(pl.program_id(0) == 0)
-    def _():
-        tile_lists(order_ref, ids_ref, seq_ref[0], 2 * half)
-
-    query = query_ref[...]
+    tile_lists(order_ref, ids_ref, seq_ref[0], 2 * half)
     lane_tile = lax.broadcasted_iota(jnp.int32, (1, tokens), 1) // TILE
-    old_top = old_stats[0, 0:1, :] if goes_on else None
-    top = old_top
     for index, source in enumerate(sources):
-        block = jnp.dot(keys[index][...].T, query, preferred_element_type=jnp.float32)
         for spot in range(half):
             key_tile = ids_ref[source * half + spot]
             bias = jnp.zeros((1, tokens), jnp.float32)
@@ -313,69 +337,95 @@
                 query_tile = ids_ref[2 * chunk * half + query_spot]
                 blocked = jnp.where(mask_ref[query_tile, key_tile] == 1, 0.0, MASKED_SCORE)
                 bias = jnp.where(lane_tile == query_spot, blocked, bias)
-            piece = block[spot * TILE : (spot + 1) * TILE, :] + bias
-            scores_ref[index * tokens + spot * TILE : index * tokens + (spot + 1) * TILE, :] = piece
-            best = jnp.max(piece, axis=0, keepdims=True)
-            top = best if top is None else jnp.maximum(top, best)
-    denom = None
-    weighted = None
-    if goes_on:
-        shrink = jnp.exp2(old_top - top)
-        denom = old_stats[0, 1:2, :] * shrink
-        weighted = old_weighted[...] * shrink
-    for index in range(count):
-        powers = jnp.exp2(scores_ref[index * tokens : (index + 1) * tokens, :] - top)
-        summed = jnp.sum(powers, axis=0, keepdims=True)
-        term = jnp.dot(
-            values[index][...], powers.astype(jnp.bfloat16), preferred_element_type=jnp.float32
-        )
-        denom = summed if denom is None else denom + summed
-        weighted = term if weighted is None else weighted + term
+            bias_ref[index * half + spot : index * half + spot + 1, :] = bias
+
+    def one_head(head, carry):
+        rows = pl.ds(pl.multiple_of(head * HEAD, HEAD), HEAD)
+        value_rows = pl.ds(pl.multiple_of(cols + head * HEAD, HEAD), HEAD)
+        query = query_ref[rows, :]
+        old_top = old_stats[head, 0:1, :] if goes_on else None
+        top = old_top
+        for index in range(count):
+            block = jnp.dot(pairs[index][rows, :].T, query, preferred_element_type=jnp.float32)
+            for spot in range(half):
+                line = index * half + spot
+                piece = block[spot * TILE : (spot + 1) * TILE, :] + bias_ref[line : line + 1, :]
+                scores_ref[line * TILE : (line + 1) * TILE, :] = piece
+                best = jnp.max(piece, axis=0, keepdims=True)
+                top = best if top is None else jnp.maximum(top, best)
+        denom = None
+        weighted = None
+        if goes_on:
+            shrink = jnp.exp2(old_top - top)
+            denom = old_stats[head, 1:2, :] * shrink
+            weighted = old_weighted[rows, :] * shrink
+        for index in range(count):
+            powers = jnp.exp2(scores_ref[index * tokens : (index + 1) * tokens, :] - top)
+            summed = jnp.sum(powers, axis=0, keepdims=True)
+            term = jnp.dot(
+                pairs[index][value_rows, :],
+                powers.astype(jnp.bfloat16),
+                preferred_element_type=jnp.float32,
+            )
+            denom = summed if denom is None else denom + summed
+            weighted = term if weighted is None else weighted + term
+        if ends:
+            heads_ref[rows, :] = (weighted / denom).astype(jnp.bfloat16)
+        else:
+            new_stats[head, 0:1, :] = top
+            new_stats[head, 1:2, :] = denom
+            new_weighted[rows, :] = weighted
+        return carry
+
+    lax.fori_loop(0, cols // HEAD, one_head, 0)
     if ends:
-        out_ref[...] = (weighted / denom).astype(jnp.bfloat16)
+        width = weight_ref.shape[0] // 4
+        for copy in copies:
+            copy.wait()
+        for index, out in enumerate(partial_refs):
+            block = weight_ref[index * width : (index + 1) * width, :]
+            out[...] = jnp.dot(
+                block, heads_ref[...], preferred_element_type=jnp.float32
+            ).astype(jnp.bfloat16)
+
+
+def attend_call(chunk, tables, queries, sources, state=None, out_t=None):
+    cols, tokens = queries.shape
+    heads = cols // HEAD
+    count = len(sources)
+    half = tokens // TILE
+    goes_on, ends = state is not None, out_t is not None
+    arguments = [queries] + [array for array, _ in sources] + (list(state) if goes_on else [])
+    in_specs = [vmem_spec()] * len(arguments)
+    scratch = [
+        pltpu.SMEM((4 * half,), jnp.int32),
+        pltpu.VMEM((count * half, tokens), jnp.float32),
+        pltpu.VMEM((count * tokens, tokens), jnp.float32),
+    ]
+    if ends:
+        in_specs += [pl.BlockSpec(memory_space=pltpu.HBM)]
+        arguments += [out_t]
+        shapes = [jax.ShapeDtypeStruct((out_t.shape[0] // 4, tokens), jnp.bfloat16)] * 4
+        scratch += [
+            pltpu.VMEM((cols, tokens), jnp.bfloat16),
+            pltpu.VMEM(out_t.shape, jnp.bfloat16),
+            pltpu.SemaphoreType.DMA((4,)),
+        ]
     else:
-        new_stats[0, 0:1, :] = top
-        new_stats[0, 1:2, :] = denom
-        new_weighted[...] = weighted
-
-
-def attend_call(chunk, tables, queries, sources, state=None, ends=True):
-    rows, tokens = queries.shape
-    heads = rows // HEAD
-
-    def spec(start):
-        return pl.BlockSpec((HEAD, tokens), lambda h, *_, start=start: (start + h, 0))
-
-    count = len(sources)
-    stats_spec = pl.BlockSpec((1, 2, tokens), lambda h, *_: (h, 0, 0))
-    state_specs = [stats_spec, spec(0)]
-    state_shapes = [
-        jax.ShapeDtypeStruct((heads, 2, tokens), jnp.float32),
-        jax.ShapeDtypeStruct((rows, tokens), jnp.float32),
-    ]
-    goes_on = state is not None
-    in_specs = [spec(0)] + [spec(0)] * count + [spec(heads)] * count
-    arguments = [queries] + [array for array, _ in sources] * 2
-    if goes_on:
-        in_specs += state_specs
-        arguments += list(state)
+        shapes = [
+            jax.ShapeDtypeStruct((heads, 2, tokens), jnp.float32),
+            jax.ShapeDtypeStruct((cols, tokens), jnp.float32),
+        ]
     return pl.pallas_call(
         functools.partial(attend_body, chunk, tuple(s for _, s in sources), goes_on, ends),
-        grid_spec=pltpu.PrefetchScalarGridSpec(
-            num_scalar_prefetch=3,
-            grid=(heads,),
-            in_specs=in_specs,
-            out_specs=spec(0) if ends else state_specs,
-            scratch_shapes=[
-                pltpu.SMEM((4 * tokens // TILE,), jnp.int32),
-                pltpu.VMEM((count * tokens, tokens), jnp.float32),
-            ],
-        ),
-        out_shape=jax.ShapeDtypeStruct((rows, tokens), jnp.bfloat16) if ends else state_shapes,
+        in_specs=[smem_spec()] * 3 + in_specs,
+        out_specs=[vmem_spec()] * len(shapes),
+        scratch_shapes=scratch,
+        out_shape=shapes,
         compiler_params=params(),
         cost_estimate=pl.CostEstimate(
-            flops=4 * rows * tokens * tokens * count,
-            bytes_accessed=2 * rows * tokens * (2 + 2 * count),
+            flops=4 * cols * tokens * tokens * count,
+            bytes_accessed=2 * cols * tokens * (2 + 2 * count),
             transcendentals=heads * tokens * tokens * count,
         ),
         name="attend",
@@ -454,19 +504,12 @@
     return summed.astype(jnp.bfloat16)
 
 
-def reduce_blocks(weights, heads_out, here):
-    width = weights.shape[0] // 4
-
-    def partial(index):
-        block = weights[index * width : (index + 1) * width]
-        return jnp.dot(block, heads_out, preferred_element_type=jnp.float32).astype(jnp.bfloat16)
-
-    sent = partial(3)
+def reduce_blocks(partials, here):
+    own, down, up, sent = partials
     across = lax.ppermute(sent, "tp", FOLDED)
-    down, up = lax.optimization_barrier((partial(1), partial(2)))
     back = lax.ppermute(plus(down, across, here == 2), "tp", BACKWARD)
     onward = lax.ppermute(plus(up, across, here == 1), "tp", FORWARD)
-    return (partial(0), back, onward, across)
+    return (own, back, onward, across)
 
 
 def per_device_fast(
@@ -487,7 +530,7 @@
     tokens_a = jnp.where(seq == 0, keep_a, got_a)
     shards_a = gather_blocks(tokens_a, here)
 
-    keep_b, send_b = conv_call(seq_here, stripe_order, clip_tokens, conv_taps, before, part)
+    keep_b, send_b = conv_call(seq_here, stripe_order, before, conv_taps, part)
     got_b = lax.ppermute(send_b, "seq", [(1, 0)])
     tokens_b = jnp.where(seq == 1, keep_b, got_b)
 
@@ -495,14 +538,14 @@
     query_a, pair_a = project_call(weights, shards_a)
     peer_a = lax.ppermute(pair_a, "seq", swap)
     shards_b = gather_blocks(tokens_b, here)
-    out_a = attend_call(0, tables, query_a, [(pair_a, 0), (peer_a, 1)])
-    parts_a = reduce_blocks(out_t, out_a, here)
+    partials_a = attend_call(0, tables, query_a, [(pair_a, 0), (peer_a, 1)], out_t=out_t)
+    parts_a = reduce_blocks(partials_a, here)
     query_b, pair_b = project_call(weights, shards_b)
     peer_b = lax.ppermute(pair_b, "seq", swap)
     near = [(pair_a, 0), (peer_a, 1), (pair_b, 2)]
-    state = attend_call(1, tables, query_b, near, ends=False)
-    out_b = attend_call(1, tables, query_b, [(peer_b, 3)], state=state)
-    parts_b = reduce_blocks(out_t, out_b, here)
+    state = attend_call(1, tables, query_b, near)
+    partials_b = attend_call(1, tables, query_b, [(peer_b, 3)], state=state, out_t=out_t)
+    parts_b = reduce_blocks(partials_b, here)
     first = sum(part.astype(jnp.float32) for part in parts_a[:3])
     first = first + jnp.where(at_end == 1, parts_a[3].astype(jnp.float32), 0.0)
     return place_call(seq_here, stripe_order, at_end, first.astype(jnp.bfloat16), parts_b)

time: 208 us -> 227 us (1.091)
  starting transfers between devices: 31.3 us -> 44 us
  waiting for transfers between devices: 102 us -> 109 us
  matrix products: 3.62 us -> 0 us
  other arithmetic: 4.42 us -> 7.52 us
  local copies, waits for them, and re-layouts: 3.24 us -> 5.88 us
  Pallas kernels: 62.7 us -> 60.1 us
    ppermute x2, waiting for transfers between devices: 28 us -> 10 us  [reduce_blocks(): across = lax.ppermute(sent, 'tp', FOLDED)]
    ppermute x1, waiting for transfers between devices: 0.01 us -> 17.9 us  [per_device_fast(): peer_a = lax.ppermute(pair_a, 'seq', swap)]
    ppermute x2, waiting for transfers between devices: 2.25 us -> 19.8 us  [gather_blocks(): after = lax.ppermute(block, 'tp', BACKWARD)]
    ppermute x2, starting transfers between devices: 4.83 us -> 17.2 us  [reduce_blocks(): back = lax.ppermute(plus(down, across, here == 2), 'tp', BACKWARD)]
    ppermute x2, waiting for transfers between devices: 12.1 us -> 0.01 us  [gather_blocks(): across = lax.ppermute(relay, 'tp', UNFOLDED)]
    ppermute x2, waiting for transfers between devices: 0.01 us -> 11.4 us  [gather_blocks(): before = lax.ppermute(block, 'tp', FORWARD)]
    ppermute x1, waiting for transfers between devices: 11.2 us -> 0.01 us  [per_device_fast(): got_a = lax.ppermute(send_a, 'seq', [(0, 1)])]
    ppermute x2, waiting for transfers between devices: 10.4 us -> 18.7 us  [reduce_blocks(): onward = lax.ppermute(plus(up, across, here == 1), 'tp', FORWARD)]
  transfers between devices with their start and end apart: 17 -> 17, of which waited for: 10 -> 12; matrix products, arithmetic and copies ran while one was open for 4% -> 3% of each run, Pallas kernels for 24% -> 25%
where the time goes in v3:
time: 227 us; the launch traced here: 226 us
  waiting for transfers between devices  109 us (48%)
  Pallas kernels  60.1 us (26%)
  starting transfers between devices  44 us (19%)
  other arithmetic  7.52 us (3%)
  local copies, waits for them, and re-layouts  5.88 us (3%)
    ppermute x2, waiting for transfers between devices, gather_blocks(): after = lax.ppermute(block, 'tp', BACKWARD)  19.8 us
    pallas_call x2, Pallas kernels, conv_call(): pl.pallas_call(functools.partial(conv_body, with_before), grid_spec=pltpu...  19.2 us
    ppermute x2, waiting for transfers between devices, reduce_blocks(): onward = lax.ppermute(plus(up, across, here == 1), 'tp', FORWARD)  18.7 us
    pallas_call x3, Pallas kernels, attend_call(): pl.pallas_call(functools.partial(attend_body, chunk, tuple((s for _, s in...  17.9 us
    ppermute x1, waiting for transfers between devices, per_device_fast(): peer_a = lax.ppermute(pair_a, 'seq', swap)  17.9 us
    ppermute x2, starting transfers between devices, reduce_blocks(): back = lax.ppermute(plus(down, across, here == 2), 'tp', BACKWARD)  17.2 us
    pallas_call x2, Pallas kernels, project_call(): pl.pallas_call(project_body, in_specs=[pl.BlockSpec(memory_space=pltpu.HB...  11.8 us
    ppermute x2, waiting for transfers between devices, gather_blocks(): before = lax.ppermute(block, 'tp', FORWARD)  11.4 us
  transfers between devices with their start and end apart: 17, of which 12 were waited for; matrix products, arithmetic and copies ran while one was open for 3% of the time, Pallas kernels for 25%

profile of v3, /device:TPU:0, one launch (start us, length us, event | category | flops | bytes accessed | tf_op | source)
XLA Modules:
  0.0 226.5 jit_solution(9169091646304227134)
XLA Ops:
  0.0 4.9 %collective-permute-start.8 = (bf16[512,1024]{1,0:T(8,128)(2,1)}, bf16[512,1024]{1,0:T(8,128)(2,1)S(1)}, u32[]{:S(2)}, u32[]{:S(2)}) collective-permute-start(bf16[512,1024]{1,0:T(8,128)(2,1)} %refs_0_.1), channel_id=1, source_target_pairs={{0,16},{1,17},{2,18},{3,19},{4,20},{5,21},{6,22},{7,23},{8,24},{9,... | collective-permute-start | bytes 3145736 | tf_op jit(solution)/shard_map/ppermute | solution.py:527
  4.9 10.5 %conv.2 = (f32[512,1024]{1,0:T(8,128)}, bf16[512,512]{1,0:T(8,128)(2,1)}, bf16[512,512]{1,0:T(8,128)(2,1)}) custom-call(s32[1]{0:T(128)} %bitcast.seq_ref, s32[16]{0:T(128)} %order_ref.11, bf16[512,1024]{1,0:T(8,128)(2,1)} %refs_0_.1, f32[27,512]{1,0:T(8,128)} %refs_1_.3), custom_call_target="tpu_custom_call" | custom-call | flops 14155776 | bytes 4194304 | tf_op jit(solution)/shard_map/conv/pallas_call | solution.py:170
  15.5 2.1 collective-permute-start
  17.5 11.2 %collective-permute-done.8.refs_0_ = bf16[512,1024]{1,0:T(8,128)(2,1)S(1)} collective-permute-done((bf16[512,1024]{1,0:T(8,128)(2,1)}, bf16[512,1024]{1,0:T(8,128)(2,1)S(1)}, u32[]{:S(2)}, u32[]{:S(2)}) %collective-permute-start.8) | collective-permute-done | bytes 1048608 | tf_op jit(solution)/shard_map/ppermute | solution.py:527
  28.7 1.6 copy-done.1
  30.3 0.8 copy-done.2
  31.1 0.7 copy-done.4
  31.8 8.6 %conv.3 = (bf16[512,512]{1,0:T(8,128)(2,1)S(1)}, bf16[512,512]{1,0:T(8,128)(2,1)S(1)}) custom-call(s32[1]{0:T(128)} %bitcast.seq_ref, s32[16]{0:T(128)S(1)} %copy-done.4, bf16[512,1024]{1,0:T(8,128)(2,1)S(1)} %collective-permute-done.8.refs_0_, f32[27,512]{1,0:T(8,128)S(1)} %copy-done.2, f32[512,1024]{1,0:T(8,128)S(1)} %copy-done.1), custom_call_target="tpu_custom_call" | custom-call | flops 14155776 | bytes 4194304 | tf_op jit(solution)/shard_map/conv/pallas_call | solution.py:170
  40.5 1.3 collective-permute-start.9
  41.8 1.1 broadcast_select_fusion.1.own
  42.9 1.6 collective-permute-start.1
  44.5 2.2 collective-permute-start.2
  46.8 7.3 %collective-permute-done.9 = bf16[512,512]{1,0:T(8,128)(2,1)S(1)} collective-permute-done((bf16[512,512]{1,0:T(8,128)(2,1)S(1)}, bf16[512,512]{1,0:T(8,128)(2,1)S(1)}, u32[]{:S(2)}, u32[]{:S(2)}) %collective-permute-start.9) | collective-permute-done | bytes 524320 | tf_op jit(solution)/shard_map/ppermute | solution.py:534
  54.1 1.6 collective-permute-start.10
  55.7 2.2 collective-permute-start.11
  58.0 1.6 collective-permute-done.1.before
  59.5 11.3 %collective-permute-done.2.after = bf16[512,512]{1,0:T(8,128)(2,1)S(1)} collective-permute-done((bf16[512,512]{1,0:T(8,128)(2,1)S(1)}, bf16[512,512]{1,0:T(8,128)(2,1)S(1)}, u32[]{:S(2)}, u32[]{:S(2)}) %collective-permute-start.2) | collective-permute-done | bytes 524320 | tf_op jit(solution)/shard_map/ppermute | solution.py:496
  70.8 0.9 select_select_fusion.1
  71.7 0.5 collective-permute-start.3
  72.2 9.9 %collective-permute-done.10.before = bf16[512,512]{1,0:T(8,128)(2,1)S(1)} collective-permute-done((bf16[512,512]{1,0:T(8,128)(2,1)S(1)}, bf16[512,512]{1,0:T(8,128)(2,1)S(1)}, u32[]{:S(2)}, u32[]{:S(2)}) %collective-permute-start.10) | collective-permute-done | bytes 524320 | tf_op jit(solution)/shard_map/ppermute | solution.py:495
  82.0 8.5 %collective-permute-done.11.after = bf16[512,512]{1,0:T(8,128)(2,1)S(1)} collective-permute-done((bf16[512,512]{1,0:T(8,128)(2,1)S(1)}, bf16[512,512]{1,0:T(8,128)(2,1)S(1)}, u32[]{:S(2)}, u32[]{:S(2)}) %collective-permute-start.11) | collective-permute-done | bytes 524320 | tf_op jit(solution)/shard_map/ppermute | solution.py:496
  90.6 0.9 select_select_fusion
  91.5 3.3 %collective-permute-start.12 = (bf16[512,512]{1,0:T(8,128)(2,1)}, bf16[512,512]{1,0:T(8,128)(2,1)}, u32[]{:S(2)}, u32[]{:S(2)}) collective-permute-start(bf16[512,512]{1,0:T(8,128)(2,1)} %select_select_fusion), channel_id=1, source_target_pairs={{4,0},{12,4},{8,12},{0,8},{5,1},{13,5},{9,13},{1,9},{6,2},{14,6},{... | collective-permute-start | bytes 1572872 | tf_op jit(solution)/shard_map/ppermute | solution.py:498
  94.7 0.6 pad_add_fusion.blocks_ref
  95.3 8.5 %prepare.1 = (bf16[1536,2048]{1,0:T(8,128)(2,1)}, bf16[2048,512]{1,0:T(8,128)(2,1)}) custom-call(s32[4]{0:T(128)} %pad_add_fusion.blocks_ref, f32[1,2048]{1,0:T(1,128)} %bitcast.10, bf16[1536,2048]{1,0:T(8,128)(2,1)} %bitcast.9, bf16[512,2048]{1,0:T(8,128)(2,1)} %out_ref.1), custom_call_target="tpu_custom_call" | custom-call | flops 3145728 | bytes 16777216 | tf_op jit(solution)/shard_map/prepare/pallas_call | solution.py:207
  103.8 2.8 %copy-done.6 = bf16[1536,2048]{1,0:T(8,128)(2,1)S(1)} copy-done((bf16[1536,2048]{1,0:T(8,128)(2,1)S(1)}, bf16[1536,2048]{1,0:T(8,128)(2,1)}, u32[]{:S(2)}) %copy-start.6) | copy-done | bytes 6291480
  106.6 5.9 %project.2 = (bf16[512,512]{1,0:T(8,128)(2,1)S(1)}, bf16[1024,512]{1,0:T(8,128)(2,1)S(1)}) custom-call(bf16[1536,2048]{1,0:T(8,128)(2,1)S(1)} %copy-done.6, bf16[512,512]{1,0:T(8,128)(2,1)S(1)} %broadcast_select_fusion.1.own, bf16[512,512]{1,0:T(8,128)(2,1)S(1)} %collective-permute-done.1.before, bf16[512,512]{1,0:T(8,128)(2,1)S(1)} %collective-permute-done.2.after, ...), custom_call_target="tpu_custom_call" | custom-call | flops 3221225472 | bytes 9961472 | tf_op jit(solution)/shard_map/project/pallas_call | solution.py:276
  112.5 2.7 %collective-permute-start.4 = (bf16[1024,512]{1,0:T(8,128)(2,1)S(1)}, bf16[1024,512]{1,0:T(8,128)(2,1)S(1)}, u32[]{:S(2)}, u32[]{:S(2)}) collective-permute-start(bf16[1024,512]{1,0:T(8,128)(2,1)S(1)} %get-tuple-element.30.refs_0_), channel_id=1, source_target_pairs={{0,16},{16,0},{1,17},{17,1},{2,18},{18,2},{3,19},{19,3},{4,20},{20... | collective-permute-start | bytes 3145736 | tf_op jit(solution)/shard_map/ppermute | solution.py:539
  115.3 5.9 %project.3 = (bf16[512,512]{1,0:T(8,128)(2,1)S(1)}, bf16[1024,512]{1,0:T(8,128)(2,1)S(1)}) custom-call(bf16[1536,2048]{1,0:T(8,128)(2,1)S(1)} %copy-done.6, bf16[512,512]{1,0:T(8,128)(2,1)S(1)} %broadcast_select_fusion.own, bf16[512,512]{1,0:T(8,128)(2,1)S(1)} %collective-permute-done.10.before, bf16[512,512]{1,0:T(8,128)(2,1)S(1)} %collective-permute-done.11.after, ...), custom_call_target="tpu_custom_call" | custom-call | flops 3221225472 | bytes 9961472 | tf_op jit(solution)/shard_map/project/pallas_call | solution.py:276
  121.2 0.2 collective-permute-start.13
  121.4 17.9 %collective-permute-done.4.refs_1_ = bf16[1024,512]{1,0:T(8,128)(2,1)S(1)} collective-permute-done((bf16[1024,512]{1,0:T(8,128)(2,1)S(1)}, bf16[1024,512]{1,0:T(8,128)(2,1)S(1)}, u32[]{:S(2)}, u32[]{:S(2)}) %collective-permute-start.4) | collective-permute-done | bytes 1048608 | tf_op jit(solution)/shard_map/ppermute | solution.py:539
  139.3 6.2 %attend.3 = (bf16[512,512]{1,0:T(8,128)(2,1)S(1)}, bf16[512,512]{1,0:T(8,128)(2,1)S(1)}, bf16[512,512]{1,0:T(8,128)(2,1)S(1)}, bf16[512,512]{1,0:T(8,128)(2,1)S(1)}) custom-call(s32[1]{0:T(128)} %bitcast.seq_ref, s32[16]{0:T(128)S(1)} %copy-done.5, s32[16,16]{1,0:T(8,128)S(1)} %copy-done.3, bf16[512,512]{1,0:T(8,128)(2,1)S(1)} %get-tuple-element.29.query_ref, ...), custom_call_target="tpu_custom_call" | custom-call | flops 1073741824 | bytes 3145728 | tf_op jit(solution)/shard_map/attend/pallas_call | solution.py:419
  145.5 1.6 collective-permute-start.5
  147.1 6.7 %attend.4 = (f32[4,2,512]{2,1,0:T(2,128)S(1)}, f32[512,512]{1,0:T(8,128)S(1)}) custom-call(s32[1]{0:T(128)} %bitcast.seq_ref, s32[16]{0:T(128)S(1)} %copy-done.5, s32[16,16]{1,0:T(8,128)S(1)} %copy-done.3, bf16[512,512]{1,0:T(8,128)(2,1)S(1)} %get-tuple-element.39.query_ref, bf16[1024,512]{1,0:T(8,128)(2,1)S(1)} %get-tuple-element.30.refs_0_, ...), custom_call_target="tpu_custom_call" | custom-call | flops 1610612736 | bytes 4194304 | tf_op jit(solution)/shard_map/attend/pallas_call | solution.py:419
  153.8 5.2 %collective-permute-done.13.refs_0_ = bf16[1024,512]{1,0:T(8,128)(2,1)S(1)} collective-permute-done((bf16[1024,512]{1,0:T(8,128)(2,1)S(1)}, bf16[1024,512]{1,0:T(8,128)(2,1)S(1)}, u32[]{:S(2)}, u32[]{:S(2)}) %collective-permute-start.13) | collective-permute-done | bytes 1048608 | tf_op jit(solution)/shard_map/ppermute | solution.py:544
  159.0 5.0 %attend.5 = (bf16[512,512]{1,0:T(8,128)(2,1)S(1)}, bf16[512,512]{1,0:T(8,128)(2,1)S(1)}, bf16[512,512]{1,0:T(8,128)(2,1)S(1)}, bf16[512,512]{1,0:T(8,128)(2,1)S(1)}) custom-call(s32[1]{0:T(128)} %bitcast.seq_ref, s32[16]{0:T(128)S(1)} %copy-done.5, s32[16,16]{1,0:T(8,128)S(1)} %copy-done.3, bf16[512,512]{1,0:T(8,128)(2,1)S(1)} %get-tuple-element.39.query_ref, ...), custom_call_target="tpu_custom_call" | custom-call | flops 536870912 | bytes 2097152 | tf_op jit(solution)/shard_map/attend/pallas_call | solution.py:419
  164.0 1.8 collective-permute-start.14
  165.9 1.3 fusion.5
  167.2 2.1 collective-permute-start.6
  169.3 0.5 collective-permute-start.7
  169.8 10.0 %collective-permute-done.14.refs_3_ = bf16[512,512]{1,0:T(8,128)(2,1)S(1)} collective-permute-done((bf16[512,512]{1,0:T(8,128)(2,1)S(1)}, bf16[512,512]{1,0:T(8,128)(2,1)S(1)}, u32[]{:S(2)}, u32[]{:S(2)}) %collective-permute-start.14) | collective-permute-done | bytes 524320 | tf_op jit(solution)/shard_map/ppermute | solution.py:509
  179.8 1.3 fusion.3
  181.1 15.1 %collective-permute-start.15 = (bf16[512,512]{1,0:T(8,128)(2,1)}, bf16[512,512]{1,0:T(8,128)(2,1)S(1)}, u32[]{:S(2)}, u32[]{:S(2)}) collective-permute-start(bf16[512,512]{1,0:T(8,128)(2,1)} %get-tuple-element.48), channel_id=1, source_target_pairs={{4,0},{8,4},{12,8},{0,12},{5,1},{9,5},{13,9},{1,13},{6,2},{10,6},{... | collective-permute-start | bytes 1572872 | tf_op jit(solution)/shard_map/ppermute | solution.py:510
  196.2 7.1 %collective-permute-done.7 = bf16[512,512]{1,0:T(8,128)(2,1)} collective-permute-done((bf16[512,512]{1,0:T(8,128)(2,1)}, bf16[512,512]{1,0:T(8,128)(2,1)}, u32[]{:S(2)}, u32[]{:S(2)}) %collective-permute-start.7) | collective-permute-done | bytes 524320 | tf_op jit(solution)/shard_map/ppermute | solution.py:511
  203.4 1.5 fusion.9.first_ref
  204.9 7.2 %collective-permute-done.15.refs_1_ = bf16[512,512]{1,0:T(8,128)(2,1)S(1)} collective-permute-done((bf16[512,512]{1,0:T(8,128)(2,1)}, bf16[512,512]{1,0:T(8,128)(2,1)S(1)}, u32[]{:S(2)}, u32[]{:S(2)}) %collective-permute-start.15) | collective-permute-done | bytes 524320 | tf_op jit(solution)/shard_map/ppermute | solution.py:510
  212.1 11.6 %collective-permute-done.16.refs_2_ = bf16[512,512]{1,0:T(8,128)(2,1)S(1)} collective-permute-done((bf16[512,512]{1,0:T(8,128)(2,1)}, bf16[512,512]{1,0:T(8,128)(2,1)S(1)}, u32[]{:S(2)}, u32[]{:S(2)}) %collective-permute-start.16) | collective-permute-done | bytes 524320 | tf_op jit(solution)/shard_map/ppermute | solution.py:511
  223.7 2.8 %place.1 = bf16[512,1024]{1,0:T(8,128)(2,1)} custom-call(s32[1]{0:T(128)} %bitcast.seq_ref, s32[16]{0:T(128)S(1)} %copy-done.5, s32[1]{0:T(128)} %bitcast.1.ends_ref, bf16[512,512]{1,0:T(8,128)(2,1)S(1)} %fusion.9.first_ref, bf16[512,512]{1,0:T(8,128)(2,1)S(1)} %get-tuple-element.43.refs_0_, bf16[512,512]{1,0:T(8,128)(2,1)S(1)} %collective-permute-done.15.refs_1_, ...), custom_call_target="tpu_custom_call" | custom-call | flops 1048576 | bytes 3670016 | tf_op jit(solution)/shard_map/place/pallas_call | solution.py:470
  (17 shorter events, 0.1 us)
Async XLA Ops:
  0.0 28.7 %collective-permute-start.8 = (bf16[512,1024]{1,0:T(8,128)(2,1)}, bf16[512,1024]{1,0:T(8,128)(2,1)S(1)}, u32[]{:S(2)}, u32[]{:S(2)}) collective-permute-start(bf16[512,1024]{1,0:T(8,128)(2,1)} %refs_0_.1), channel_id=1, source_target_pairs={{0,16},{1,17},{2,18},{3,19},{4,20},{5,21},{6,22},{7,23},{8,24},{9,... | collective-permute-start | bytes 3145736 | tf_op jit(solution)/shard_map/ppermute | solution.py:527
  15.5 26.3 %collective-permute-start = (bf16[512,512]{1,0:T(8,128)(2,1)}, bf16[512,512]{1,0:T(8,128)(2,1)}, u32[]{:S(2)}, u32[]{:S(2)}) collective-permute-start(bf16[512,512]{1,0:T(8,128)(2,1)} %get-tuple-element.28), channel_id=1, source_target_pairs={{0,16},{1,17},{2,18},{3,19},{4,20},{5,21},{6,22},{7,23},{8,24},{9,... | collective-permute-start | bytes 1572872 | tf_op jit(solution)/shard_map/ppermute | solution.py:526
  28.7 1.6 copy-start.1
  30.3 0.8 copy-start.2
  31.1 0.7 copy-start.4
  40.5 13.6 %collective-permute-start.9 = (bf16[512,512]{1,0:T(8,128)(2,1)S(1)}, bf16[512,512]{1,0:T(8,128)(2,1)S(1)}, u32[]{:S(2)}, u32[]{:S(2)}) collective-permute-start(bf16[512,512]{1,0:T(8,128)(2,1)S(1)} %get-tuple-element.38), channel_id=1, source_target_pairs={{16,0},{17,1},{18,2},{19,3},{20,4},{21,5},{22,6},{23,7},{24,8},{25... | collective-permute-start | bytes 1572872 | tf_op jit(solution)/shard_map/ppermute | solution.py:534
  42.9 16.7 %collective-permute-start.1 = (bf16[512,512]{1,0:T(8,128)(2,1)S(1)}, bf16[512,512]{1,0:T(8,128)(2,1)S(1)}, u32[]{:S(2)}, u32[]{:S(2)}) collective-permute-start(bf16[512,512]{1,0:T(8,128)(2,1)S(1)} %broadcast_select_fusion.1.own), channel_id=1, source_target_pairs={{0,4},{4,8},{8,12},{12,0},{1,5},{5,9},{9,13},{13,1},{2,6},{6,10},{... | collective-permute-start | bytes 1572872 | tf_op jit(solution)/shard_map/ppermute | solution.py:495
  44.5 26.3 %collective-permute-start.2 = (bf16[512,512]{1,0:T(8,128)(2,1)S(1)}, bf16[512,512]{1,0:T(8,128)(2,1)S(1)}, u32[]{:S(2)}, u32[]{:S(2)}) collective-permute-start(bf16[512,512]{1,0:T(8,128)(2,1)S(1)} %broadcast_select_fusion.1.own), channel_id=1, source_target_pairs={{4,0},{8,4},{12,8},{0,12},{5,1},{9,5},{13,9},{1,13},{6,2},{10,6},{... | collective-permute-start | bytes 1572872 | tf_op jit(solution)/shard_map/ppermute | solution.py:496
  54.1 27.9 %collective-permute-start.10 = (bf16[512,512]{1,0:T(8,128)(2,1)S(1)}, bf16[512,512]{1,0:T(8,128)(2,1)S(1)}, u32[]{:S(2)}, u32[]{:S(2)}) collective-permute-start(bf16[512,512]{1,0:T(8,128)(2,1)S(1)} %broadcast_select_fusion.own), channel_id=1, source_target_pairs={{0,4},{4,8},{8,12},{12,0},{1,5},{5,9},{9,13},{13,1},{2,6},{6,10},{... | collective-permute-start | bytes 1572872 | tf_op jit(solution)/shard_map/ppermute | solution.py:495
  55.7 34.9 %collective-permute-start.11 = (bf16[512,512]{1,0:T(8,128)(2,1)S(1)}, bf16[512,512]{1,0:T(8,128)(2,1)S(1)}, u32[]{:S(2)}, u32[]{:S(2)}) collective-permute-start(bf16[512,512]{1,0:T(8,128)(2,1)S(1)} %broadcast_select_fusion.own), channel_id=1, source_target_pairs={{4,0},{8,4},{12,8},{0,12},{5,1},{9,5},{13,9},{1,13},{6,2},{10,6},{... | collective-permute-start | bytes 1572872 | tf_op jit(solution)/shard_map/ppermute | solution.py:496
  71.7 32.1 %collective-permute-start.3 = (bf16[512,512]{1,0:T(8,128)(2,1)}, bf16[512,512]{1,0:T(8,128)(2,1)}, u32[]{:S(2)}, u32[]{:S(2)}) collective-permute-start(bf16[512,512]{1,0:T(8,128)(2,1)} %select_select_fusion.1), channel_id=1, source_target_pairs={{4,0},{12,4},{8,12},{0,8},{5,1},{13,5},{9,13},{1,9},{6,2},{14,6},{... | collective-permute-start | bytes 1572872 | tf_op jit(solution)/shard_map/ppermute | solution.py:498
  91.5 23.8 %collective-permute-start.12 = (bf16[512,512]{1,0:T(8,128)(2,1)}, bf16[512,512]{1,0:T(8,128)(2,1)}, u32[]{:S(2)}, u32[]{:S(2)}) collective-permute-start(bf16[512,512]{1,0:T(8,128)(2,1)} %select_select_fusion), channel_id=1, source_target_pairs={{4,0},{12,4},{8,12},{0,8},{5,1},{13,5},{9,13},{1,9},{6,2},{14,6},{... | collective-permute-start | bytes 1572872 | tf_op jit(solution)/shard_map/ppermute | solution.py:498
  103.8 2.8 %copy-start.6 = (bf16[1536,2048]{1,0:T(8,128)(2,1)S(1)}, bf16[1536,2048]{1,0:T(8,128)(2,1)}, u32[]{:S(2)}) copy-start(bf16[1536,2048]{1,0:T(8,128)(2,1)} %get-tuple-element.26.weight_hbm) | copy-start | bytes 18874372
  112.5 26.8 %copy-start = (bf16[2048,512]{1,0:T(8,128)(2,1)S(1)}, bf16[2048,512]{1,0:T(8,128)(2,1)}, u32[]{:S(2)}) copy-start(bf16[2048,512]{1,0:T(8,128)(2,1)} %get-tuple-element.31.refs_2_.refs_3_) | copy-start | bytes 6291460
  112.5 26.8 %copy-start.3 = (s32[16,16]{1,0:T(8,128)S(1)}, s32[16,16]{1,0:T(8,128)}, u32[]{:S(2)}) copy-start(s32[16,16]{1,0:T(8,128)} %mask_ref.5) | copy-start | bytes 3076
  112.5 26.8 %copy-start.5 = (s32[16]{0:T(128)S(1)}, s32[16]{0:T(128)}, u32[]{:S(2)}) copy-start(s32[16]{0:T(128)} %order_ref.11) | copy-start | bytes 196
  112.5 26.8 %collective-permute-start.4 = (bf16[1024,512]{1,0:T(8,128)(2,1)S(1)}, bf16[1024,512]{1,0:T(8,128)(2,1)S(1)}, u32[]{:S(2)}, u32[]{:S(2)}) collective-permute-start(bf16[1024,512]{1,0:T(8,128)(2,1)S(1)} %get-tuple-element.30.refs_0_), channel_id=1, source_target_pairs={{0,16},{16,0},{1,17},{17,1},{2,18},{18,2},{3,19},{19,3},{4,20},{20... | collective-permute-start | bytes 3145736 | tf_op jit(solution)/shard_map/ppermute | solution.py:539
  121.2 37.8 %collective-permute-start.13 = (bf16[1024,512]{1,0:T(8,128)(2,1)S(1)}, bf16[1024,512]{1,0:T(8,128)(2,1)S(1)}, u32[]{:S(2)}, u32[]{:S(2)}) collective-permute-start(bf16[1024,512]{1,0:T(8,128)(2,1)S(1)} %get-tuple-element.40.refs_2_), channel_id=1, source_target_pairs={{0,16},{16,0},{1,17},{17,1},{2,18},{18,2},{3,19},{19,3},{4,20},{20... | collective-permute-start | bytes 3145736 | tf_op jit(solution)/shard_map/ppermute | solution.py:544
  145.5 20.4 %collective-permute-start.5 = (bf16[512,512]{1,0:T(8,128)(2,1)S(1)}, bf16[512,512]{1,0:T(8,128)(2,1)S(1)}, u32[]{:S(2)}, u32[]{:S(2)}) collective-permute-start(bf16[512,512]{1,0:T(8,128)(2,1)S(1)} %get-tuple-element.34), channel_id=1, source_target_pairs={{0,4},{4,12},{12,8},{8,0},{1,5},{5,13},{13,9},{9,1},{2,6},{6,14},{... | collective-permute-start | bytes 1572872 | tf_op jit(solution)/shard_map/ppermute | solution.py:509
  164.0 15.8 %collective-permute-start.14 = (bf16[512,512]{1,0:T(8,128)(2,1)S(1)}, bf16[512,512]{1,0:T(8,128)(2,1)S(1)}, u32[]{:S(2)}, u32[]{:S(2)}) collective-permute-start(bf16[512,512]{1,0:T(8,128)(2,1)S(1)} %get-tuple-element.45), channel_id=1, source_target_pairs={{0,4},{4,12},{12,8},{8,0},{1,5},{5,13},{13,9},{9,1},{2,6},{6,14},{... | collective-permute-start | bytes 1572872 | tf_op jit(solution)/shard_map/ppermute | solution.py:509
  167.2 29.1 %collective-permute-start.6 = (bf16[512,512]{1,0:T(8,128)(2,1)}, bf16[512,512]{1,0:T(8,128)(2,1)}, u32[]{:S(2)}, u32[]{:S(2)}) collective-permute-start(bf16[512,512]{1,0:T(8,128)(2,1)} %get-tuple-element.49), channel_id=1, source_target_pairs={{4,0},{8,4},{12,8},{0,12},{5,1},{9,5},{13,9},{1,13},{6,2},{10,6},{... | collective-permute-start | bytes 1572872 | tf_op jit(solution)/shard_map/ppermute | solution.py:510
  169.3 34.1 %collective-permute-start.7 = (bf16[512,512]{1,0:T(8,128)(2,1)}, bf16[512,512]{1,0:T(8,128)(2,1)}, u32[]{:S(2)}, u32[]{:S(2)}) collective-permute-start(bf16[512,512]{1,0:T(8,128)(2,1)} %get-tuple-element.50), channel_id=1, source_target_pairs={{0,4},{4,8},{8,12},{12,0},{1,5},{5,9},{9,13},{13,1},{2,6},{6,10},{... | collective-permute-start | bytes 1572872 | tf_op jit(solution)/shard_map/ppermute | solution.py:511
  181.1 31.0 %collective-permute-start.15 = (bf16[512,512]{1,0:T(8,128)(2,1)}, bf16[512,512]{1,0:T(8,128)(2,1)S(1)}, u32[]{:S(2)}, u32[]{:S(2)}) collective-permute-start(bf16[512,512]{1,0:T(8,128)(2,1)} %get-tuple-element.48), channel_id=1, source_target_pairs={{4,0},{8,4},{12,8},{0,12},{5,1},{9,5},{13,9},{1,13},{6,2},{10,6},{... | collective-permute-start | bytes 1572872 | tf_op jit(solution)/shard_map/ppermute | solution.py:510
  196.2 27.5 %collective-permute-start.16 = (bf16[512,512]{1,0:T(8,128)(2,1)}, bf16[512,512]{1,0:T(8,128)(2,1)S(1)}, u32[]{:S(2)}, u32[]{:S(2)}) collective-permute-start(bf16[512,512]{1,0:T(8,128)(2,1)} %get-tuple-element.47), channel_id=1, source_target_pairs={{0,4},{4,8},{8,12},{12,0},{1,5},{5,9},{9,13},{13,1},{2,6},{6,10},{... | collective-permute-start | bytes 1572872 | tf_op jit(solution)/shard_map/ppermute | solution.py:511

commit v4 on v3

--- a/solution.py
+++ b/solution.py
@@ -22,7 +22,7 @@
 LOG2E = math.log2(math.e)
 
 VMEM_LIMIT = 20 * 1024 * 1024
-VMEM_WHOLE = 60 * 1024 * 1024
+VMEM_FIRST = 52 * 1024 * 1024
 
 
 def vmem_spec():
@@ -37,41 +37,35 @@
     return pltpu.CompilerParams(vmem_limit_bytes=limit)
 
 
-def shift_matrix(row_off, col_offs, rows):
-    shape = (rows, TILE * len(col_offs))
-    source = lax.broadcasted_iota(jnp.int32, shape, 0)
-    target = lax.broadcasted_iota(jnp.int32, shape, 1)
-    lane = target % TILE
-    col_off = jnp.zeros(shape, jnp.int32)
-    for index, offset in enumerate(col_offs):
-        col_off = jnp.where(target // TILE == index, offset, col_off)
-    base = TILE if row_off < 0 else 0
-    wanted = lane + row_off * FW + col_off + base
-    column = lane % FW + col_off
-    inside = (column >= 0) & (column < FW)
-    return jnp.where((source == wanted) & inside, 1.0, 0.0).astype(jnp.bfloat16)
-
-
-def shift_pieces(source_ref, shifted, matrices):
-    channels, tokens = source_ref.shape
-    pieces = tokens // TILE
-    per_frame = FRAME // TILE
-    nothing = jnp.zeros((channels, TILE), jnp.bfloat16)
-
-    def piece(index):
-        return source_ref[:, index * TILE : (index + 1) * TILE]
-
-    above, here, below = [], [], []
-    for index in range(pieces):
-        first, last = index % per_frame == 0, index % per_frame == per_frame - 1
-        now = piece(index)
-        here.append(now)
-        above.append(jnp.concatenate([nothing if first else piece(index - 1), now], axis=1))
-        below.append(jnp.concatenate([now, nothing if last else piece(index + 1)], axis=1))
-    for out, matrix, parts in zip(shifted, matrices, (above, here, below)):
-        out[...] = jnp.dot(
-            jnp.concatenate(parts, axis=0), matrix[...], preferred_element_type=jnp.float32
+def fetches(source, target, semaphores):
+    block = target.shape[0] // semaphores.shape[0]
+    return [
+        pltpu.make_async_copy(
+            source.at[index * block : (index + 1) * block],
+            target.at[index * block : (index + 1) * block],
+            semaphores.at[index],
         )
+        for index in range(semaphores.shape[0])
+    ]
+
+
+def column_shifts(pieces, column):
+    right = [jnp.where(column > 0, pltpu.roll(piece, 1, 1), 0.0) for piece in pieces]
+    left = [jnp.where(column < FW - 1, pltpu.roll(piece, TILE - 1, 1), 0.0) for piece in pieces]
+    return (right, pieces, left)
+
+
+def rows_joined(rows, lane):
+    down = [pltpu.roll(piece, FW, 1) for piece in rows[0]]
+    up = [pltpu.roll(piece, TILE - FW, 1) for piece in rows[2]]
+    joined = []
+    for spot, middle in enumerate(rows[1]):
+        before = down[spot - 1] if spot > 0 else 0.0
+        after = up[spot + 1] if spot + 1 < len(up) else 0.0
+        above = jnp.where(lane < FW, before, down[spot])
+        below = jnp.where(lane >= TILE - FW, after, up[spot])
+        joined.append(middle + (above + below))
+    return joined
 
 
 def pack_slots(order_ref, slots_ref, seq_here, tiles_dev, positions):
@@ -93,101 +87,113 @@
         sent = sent + jnp.where(stays, 0, step)
 
 
-def conv_body(with_before, seq_ref, order_ref, *refs):
-    tokens_ref, taps_ref, part_ref, keep_ref, send_ref, *refs = refs
-    slots_ref, taps_scr, packed, *refs = refs
-    shifted, matrices = refs[:3], refs[3:]
-    channels, tokens = tokens_ref.shape
+GROUP = 16
+CHUNKS = 4
+PIECES = 2
+
+
+def conv_body(with_before, first_row, seq_ref, order_ref, tokens_ref, taps_ref, part_ref, keep_ref, send_ref, *refs):
+    if with_before:
+        slots_ref, taps_scr, packed = refs
+        source_ref = tokens_ref
+    else:
+        source_ref, slots_ref, taps_scr, packed, arrived = refs
+    channels, tokens = packed.shape
     tiles_dev = tokens // TILE
     per_frame = FRAME // TILE
-    seq_here = seq_ref[0]
-
-    @pl.when(pl.program_id(0) == 0)
-    def _():
-        pack_slots(order_ref, slots_ref, seq_here, tiles_dev, order_ref.shape[0])
-        matrices[0][...] = shift_matrix(-1, (-1, 0, 1), 2 * TILE)
-        matrices[1][...] = shift_matrix(0, (-1, 1), TILE)
-        matrices[2][...] = shift_matrix(1, (-1, 0, 1), 2 * TILE)
-
-    taps_scr[:, :TAPS] = taps_ref[...].T
-    shift_pieces(tokens_ref, shifted, matrices)
-    group = 16
-    reads = ((0, 0, 0), (0, 1, 1), (1, 1, 0)) if with_before else ((2, 0, 0), (2, 1, 1), (1, 0, 1))
+    if not with_before:
+        copies = fetches(tokens_ref.at[first_row : first_row + channels], source_ref, arrived)
+        for copy in copies:
+            copy.start()
+    pack_slots(order_ref, slots_ref, seq_ref[0], tiles_dev, order_ref.shape[0])
+    for first in range(0, channels, TILE):
+        from_row = first_row + first
+        taps_scr[first : first + TILE, :TAPS] = taps_ref[:, from_row : from_row + TILE].T
+    lane = lax.broadcasted_iota(jnp.int32, (GROUP, TILE), 1)
+    column = lane % FW
+    if with_before:
+        reads = ([(0, 0), (1, 1)], [(0, 1)])
+    else:
+        reads = ([(2, 0)], [(1, 0), (2, 1)])
 
     def advance(step, carry):
-        start = pl.multiple_of(step * group, group)
-        rows = pl.ds(start, group)
+        rows = pl.ds(pl.multiple_of(step * GROUP, GROUP), GROUP)
         taps = taps_scr[rows, :]
-        centre = [
-            tokens_ref[rows, tile * TILE : (tile + 1) * TILE].astype(jnp.float32)
-            for tile in range(tiles_dev)
-        ]
-        if with_before:
-            sums = [part_ref[rows, tile * TILE : (tile + 1) * TILE] for tile in range(tiles_dev)]
-        else:
-            sums = list(centre)
-
-        def value(tile, row_off, col_off):
-            if row_off == 1 and col_off == 1:
-                return centre[tile]
-            column = col_off // 2 if row_off == 1 else col_off
-            lines = pl.ds(tile * channels + start, group)
-            return shifted[row_off][lines, column * TILE : (column + 1) * TILE]
-
-        for time_off, read, written in reads:
+        shifts = []
+        for frame in range(2):
+            pieces = []
+            for spot in range(per_frame):
+                tile = frame * per_frame + spot
+                pieces.append(source_ref[rows, tile * TILE : (tile + 1) * TILE].astype(jnp.float32))
+            shifts.append(column_shifts(pieces, column))
+        for frame in range(2):
+            sums = []
             for row_off in range(3):
-                for col_off in range(3):
-                    tap = time_off * 9 + row_off * 3 + col_off
-                    weight = jnp.broadcast_to(taps[:, tap : tap + 1], (group, TILE))
-                    for spot in range(per_frame):
-                        out = written * per_frame + spot
-                        sums[out] = sums[out] + weight * value(read * per_frame + spot, row_off, col_off)
-        for tile in range(tiles_dev):
-            if not with_before:
-                part_ref[rows, tile * TILE : (tile + 1) * TILE] = sums[tile]
-            place = pl.ds(pl.multiple_of(slots_ref[tile] * TILE, TILE), TILE)
-            packed[rows, place] = sums[tile].astype(jnp.bfloat16)
+                line = [None] * per_frame
+                for time_off, read in reads[frame]:
+                    for col_off in range(3):
+                        tap = time_off * 9 + row_off * 3 + col_off
+                        weight = jnp.broadcast_to(taps[:, tap : tap + 1], (GROUP, TILE))
+                        for spot in range(per_frame):
+                            term = weight * shifts[read][col_off][spot]
+                            line[spot] = term if line[spot] is None else line[spot] + term
+                sums.append(line)
+            for spot, value in enumerate(rows_joined(sums, lane)):
+                tile = frame * per_frame + spot
+                here = slice(tile * TILE, (tile + 1) * TILE)
+                if with_before:
+                    value = value + part_ref[rows, here]
+                else:
+                    value = value + shifts[frame][1][spot]
+                    part_ref[rows, here] = value
+                place = pl.ds(pl.multiple_of(slots_ref[tile] * TILE, TILE), TILE)
+                packed[rows, place] = value.astype(jnp.bfloat16)
+        keep_ref[rows, :] = packed[rows, : tokens // 2]
+        send_ref[rows, :] = packed[rows, tokens // 2 :]
         return carry
 
-    lax.fori_loop(0, channels // group, advance, 0)
-    keep_ref[...] = packed[:, : tokens // 2]
-    send_ref[...] = packed[:, tokens // 2 :]
-
-
-def conv_call(seq_here, stripe_order, tokens, conv_taps, part=None):
-    channels, count = tokens.shape
-    block = 128
-    wide = pl.BlockSpec((block, count), lambda i, *_: (i, 0))
-    slim = pl.BlockSpec((block, count // 2), lambda i, *_: (i, 0))
-    taps_spec = pl.BlockSpec((TAPS, block), lambda i, *_: (0, i))
+    steps = channels // GROUP
+    if with_before:
+        lax.fori_loop(0, steps, advance, 0)
+    else:
+        each = steps // CHUNKS
+
+        def chunk(index, carry):
+            begin = index * each * GROUP
+            pltpu.make_async_copy(
+                tokens_ref.at[pl.ds(first_row + begin, each * GROUP)],
+                source_ref.at[pl.ds(begin, each * GROUP)],
+                arrived.at[index],
+            ).wait()
+            return lax.fori_loop(index * each, (index + 1) * each, advance, carry)
+
+        lax.fori_loop(0, CHUNKS, chunk, 0)
+
+
+def conv_call(seq_here, stripe_order, tokens, conv_taps, piece, part=None):
+    count = tokens.shape[1]
+    channels = conv_taps.shape[1] // PIECES
     packed_shape = jax.ShapeDtypeStruct((channels, count // 2), jnp.bfloat16)
     with_before = part is not None
-    out_specs, out_shape = [slim, slim], [packed_shape, packed_shape]
+    out_shape = [packed_shape, packed_shape]
+    scratch = [
+        pltpu.SMEM((count // TILE,), jnp.int32),
+        pltpu.VMEM((channels, 128), jnp.float32),
+        pltpu.VMEM((channels, count), jnp.bfloat16),
+    ]
+    in_specs = [smem_spec(), smem_spec(), vmem_spec(), vmem_spec(), vmem_spec()]
     if not with_before:
-        out_specs = [wide] + out_specs
-        out_shape = [jax.ShapeDtypeStruct((channels, count), jnp.float32)] + out_shape
-    lines = block * (count // TILE)
+        in_specs = [smem_spec(), smem_spec(), pl.BlockSpec(memory_space=pl.ANY), vmem_spec()]
+        sum_shape = jax.ShapeDtypeStruct((channels, count), jnp.float32)
+        out_shape = [sum_shape] + out_shape + [jax.ShapeDtypeStruct((channels, count), jnp.bfloat16)]
+        scratch += [pltpu.SemaphoreType.DMA((CHUNKS,))]
     return pl.pallas_call(
-        functools.partial(conv_body, with_before),
-        grid_spec=pltpu.PrefetchScalarGridSpec(
-            num_scalar_prefetch=2,
-            grid=(channels // block,),
-            in_specs=[wide, taps_spec] + [wide] * with_before,
-            out_specs=out_specs,
-            scratch_shapes=[
-                pltpu.SMEM((count // TILE,), jnp.int32),
-                pltpu.VMEM((block, 128), jnp.float32),
-                pltpu.VMEM((block, count), jnp.bfloat16),
-                pltpu.VMEM((lines, 3 * TILE), jnp.float32),
-                pltpu.VMEM((lines, 2 * TILE), jnp.float32),
-                pltpu.VMEM((lines, 3 * TILE), jnp.float32),
-                pltpu.VMEM((2 * TILE, 3 * TILE), jnp.bfloat16),
-                pltpu.VMEM((TILE, 2 * TILE), jnp.bfloat16),
-                pltpu.VMEM((2 * TILE, 3 * TILE), jnp.bfloat16),
-            ],
-        ),
+        functools.partial(conv_body, with_before, piece * channels),
+        in_specs=in_specs,
+        out_specs=[vmem_spec()] * len(out_shape),
+        scratch_shapes=scratch,
         out_shape=out_shape,
-        compiler_params=params(VMEM_LIMIT if with_before else VMEM_WHOLE),
+        compiler_params=params(VMEM_LIMIT if with_before else VMEM_FIRST),
         cost_estimate=pl.CostEstimate(
             flops=channels * count * TAPS, bytes_accessed=channels * count * 8, transcendentals=0
         ),
@@ -223,7 +229,7 @@
             jax.ShapeDtypeStruct((kinds * cols, channels), jnp.bfloat16),
             jax.ShapeDtypeStruct((channels, cols), jnp.bfloat16),
         ],
-        compiler_params=params(VMEM_WHOLE),
+        compiler_params=params(),
         cost_estimate=pl.CostEstimate(
             flops=kinds * cols * channels, bytes_accessed=16 * cols * channels, transcendentals=0
         ),
@@ -231,35 +237,20 @@
     )(blocks, norm_gain[None, :], qkv_weight.reshape(kinds * cols, channels), out_weight)
 
 
-def fetches(source, target, semaphores):
-    block = target.shape[0] // semaphores.shape[0]
-    return [
-        pltpu.make_async_copy(
-            source.at[index * block : (index + 1) * block],
-            target.at[index * block : (index + 1) * block],
-            semaphores.at[index],
-        )
-        for index in range(semaphores.shape[0])
-    ]
-
-
-def project_body(weight_hbm, own, before, after, across, query_ref, pair_ref, weight_ref, tokens_ref, arrived):
-    copies = fetches(weight_hbm, weight_ref, arrived)
-    for copy in copies:
-        copy.start()
-    width = own.shape[0]
+def project_body(weight_ref, *refs):
+    shards, (query_ref, pair_ref, tokens_ref) = refs[:-3], refs[-3:]
+    width = shards[0].shape[0]
     cols = query_ref.shape[0]
     squares = None
-    for index, shard in enumerate((own, before, after, across)):
+    for index, shard in enumerate(shards):
         block = shard[...]
         tokens_ref[index * width : (index + 1) * width, :] = block
         wide = block.astype(jnp.float32)
         term = jnp.sum(wide * wide, axis=0, keepdims=True)
         squares = term if squares is None else squares + term
-    inverse = lax.rsqrt(squares / (4 * width) + EPSILON)
-    rows = weight_ref.shape[0] // len(copies)
-    for index, copy in enumerate(copies):
-        copy.wait()
+    inverse = lax.rsqrt(squares / (len(shards) * width) + EPSILON)
+    rows = 256
+    for index in range(weight_ref.shape[0] // rows):
         here = slice(index * rows, (index + 1) * rows)
         total = jnp.dot(weight_ref[here, :], tokens_ref[...], preferred_element_type=jnp.float32)
         if index * rows < cols:
@@ -275,13 +266,9 @@
     cols = rows // 3
     return pl.pallas_call(
         project_body,
-        in_specs=[pl.BlockSpec(memory_space=pltpu.HBM)] + [vmem_spec()] * len(shards),
+        in_specs=[vmem_spec()] * (1 + len(shards)),
         out_specs=[vmem_spec(), vmem_spec()],
-        scratch_shapes=[
-            pltpu.VMEM((rows, channels), jnp.bfloat16),
-            pltpu.VMEM((channels, tokens), jnp.bfloat16),
-            pltpu.SemaphoreType.DMA((6,)),
-        ],
+        scratch_shapes=[pltpu.VMEM((channels, tokens), jnp.bfloat16)],
         out_shape=[
             jax.ShapeDtypeStruct((cols, tokens), jnp.bfloat16),
             jax.ShapeDtypeStruct((2 * cols, tokens), jnp.bfloat16),
@@ -318,7 +305,7 @@
         old_stats, old_weighted, *refs = refs
     if ends:
         weight_hbm, *refs = refs
-        partial_refs, refs = refs[:4], refs[4:]
+        partial_refs, refs = refs[: 4 * PIECES], refs[4 * PIECES :]
         ids_ref, bias_ref, scores_ref, heads_ref, weight_ref, arrived = refs
         copies = fetches(weight_hbm, weight_ref, arrived)
         for copy in copies:
@@ -379,7 +366,7 @@
 
     lax.fori_loop(0, cols // HEAD, one_head, 0)
     if ends:
-        width = weight_ref.shape[0] // 4
+        width = weight_ref.shape[0] // (4 * PIECES)
         for copy in copies:
             copy.wait()
         for index, out in enumerate(partial_refs):
@@ -405,7 +392,8 @@
     if ends:
         in_specs += [pl.BlockSpec(memory_space=pltpu.HBM)]
         arguments += [out_t]
-        shapes = [jax.ShapeDtypeStruct((out_t.shape[0] // 4, tokens), jnp.bfloat16)] * 4
+        width = out_t.shape[0] // (4 * PIECES)
+        shapes = [jax.ShapeDtypeStruct((width, tokens), jnp.bfloat16)] * (4 * PIECES)
         scratch += [
             pltpu.VMEM((cols, tokens), jnp.bfloat16),
             pltpu.VMEM(out_t.shape, jnp.bfloat16),
@@ -432,28 +420,30 @@
     )(*tables, *arguments)
 
 
-def place_body(seq_ref, order_ref, ends_ref, first_ref, *refs):
-    parts, out_ref, second_ref = refs[:4], refs[4], refs[5]
-    _, tokens = first_ref.shape
+def summed(own, back, onward, across, at_end):
+    total = own.astype(jnp.float32) + back.astype(jnp.float32) + onward.astype(jnp.float32)
+    return (total + jnp.where(at_end, across.astype(jnp.float32), 0.0)).astype(jnp.bfloat16)
+
+
+def place_body(seq_ref, order_ref, ends_ref, *refs):
+    firsts, refs = refs[:PIECES], refs[PIECES:]
+    parts, (out_ref, second_ref) = refs[:-2], refs[-2:]
+    width, tokens = firsts[0].shape
     tiles_dev = 2 * tokens // TILE
-    seq_here = seq_ref[0]
     at_end = ends_ref[0] == 1
-    total = (
-        parts[0][...].astype(jnp.float32)
-        + parts[1][...].astype(jnp.float32)
-        + parts[2][...].astype(jnp.float32)
-        + jnp.where(at_end, parts[3][...].astype(jnp.float32), 0.0)
-    )
-    second_ref[...] = total.astype(jnp.bfloat16)
+    for piece in range(PIECES):
+        addends = [parts[4 * piece + index][...] for index in range(4)]
+        second_ref[piece * width : (piece + 1) * width, :] = summed(*addends, at_end)
     ranks = [jnp.int32(0), jnp.int32(0)]
     for position in range(tiles_dev):
-        late = order_ref[seq_here * tiles_dev + position] // tiles_dev
+        late = order_ref[seq_ref[0] * tiles_dev + position] // tiles_dev
         spot = pl.ds(pl.multiple_of(jnp.where(late == 0, ranks[0], ranks[1]) * TILE, TILE), TILE)
         here = slice(position * TILE, (position + 1) * TILE)
 
         @pl.when(late == 0)
         def _(spot=spot, here=here):
-            out_ref[:, here] = first_ref[:, spot]
+            for piece in range(PIECES):
+                out_ref[piece * width : (piece + 1) * width, here] = firsts[piece][:, spot]
 
         @pl.when(late == 1)
         def _(spot=spot, here=here):
@@ -463,26 +453,21 @@
         ranks[1] = ranks[1] + late
 
 
-def place_call(seq_here, stripe_order, at_end, first, parts):
-    channels, tokens = first.shape
-    block = 128
-    slim = pl.BlockSpec((block, tokens), lambda i, *_: (i, 0))
+def place_call(seq_here, stripe_order, at_end, firsts, parts):
+    width, tokens = firsts[0].shape
+    channels = width * PIECES
     return pl.pallas_call(
         place_body,
-        grid_spec=pltpu.PrefetchScalarGridSpec(
-            num_scalar_prefetch=3,
-            grid=(channels // block,),
-            in_specs=[slim] * 5,
-            out_specs=pl.BlockSpec((block, 2 * tokens), lambda i, *_: (i, 0)),
-            scratch_shapes=[pltpu.VMEM((block, tokens), jnp.bfloat16)],
-        ),
+        in_specs=[smem_spec()] * 3 + [vmem_spec()] * (5 * PIECES),
+        out_specs=vmem_spec(),
+        scratch_shapes=[pltpu.VMEM((channels, tokens), jnp.bfloat16)],
         out_shape=jax.ShapeDtypeStruct((channels, 2 * tokens), jnp.bfloat16),
         compiler_params=params(),
         cost_estimate=pl.CostEstimate(
             flops=4 * channels * tokens, bytes_accessed=14 * channels * tokens, transcendentals=0
         ),
         name="place",
-    )(seq_here, stripe_order, at_end, first, *parts)
+    )(seq_here, stripe_order, at_end, *firsts, *[part for piece in parts for part in piece])
 
 
 FORWARD = [(0, 1), (1, 2), (2, 3), (3, 0)]
@@ -521,34 +506,44 @@
     at_end = ((here == 0) | (here == 3)).astype(jnp.int32)[None]
     blocks = jnp.stack([here, (here + 3) % 4, (here + 1) % 4, (here + 2) % 4]).astype(jnp.int32)
     tables = (seq_here, stripe_order, tile_mask)
-
-    part, keep_a, send_a = conv_call(seq_here, stripe_order, clip_tokens, conv_taps)
-    got_a = lax.ppermute(send_a, "seq", [(0, 1)])
-    before = lax.ppermute(clip_tokens, "seq", [(0, 1)])
+    pieces = range(PIECES)
+
+    def gathered(blocks_here):
+        by_piece = [gather_blocks(block, here) for block in blocks_here]
+        return [by_piece[p][owner] for owner in range(4) for p in pieces]
+
+    def reduced(partials):
+        return [reduce_blocks(partials[p::PIECES], here) for p in pieces]
+
+    begun = [conv_call(seq_here, stripe_order, clip_tokens, conv_taps, p) for p in pieces]
+    tokens_a, before = [], []
+    for _, keep, send, tokens in begun:
+        got = lax.ppermute(send, "seq", [(0, 1)])
+        tokens_a.append(jnp.where(seq == 0, keep, got))
+        before.append(lax.ppermute(tokens, "seq", [(0, 1)]))
     weights, out_t = prepare_weights(blocks, norm_gain, qkv_weight, out_weight)
-
-    tokens_a = jnp.where(seq == 0, keep_a, got_a)
-    shards_a = gather_blocks(tokens_a, here)
-
-    keep_b, send_b = conv_call(seq_here, stripe_order, before, conv_taps, part)
-    got_b = lax.ppermute(send_b, "seq", [(1, 0)])
-    tokens_b = jnp.where(seq == 1, keep_b, got_b)
+    shards_a = gathered(tokens_a)
+
+    tokens_b = []
+    for p in pieces:
+        keep, send = conv_call(seq_here, stripe_order, before[p], conv_taps, p, begun[p][0])
+        got = lax.ppermute(send, "seq", [(1, 0)])
+        tokens_b.append(jnp.where(seq == 1, keep, got))
 
     swap = [(0, 1), (1, 0)]
     query_a, pair_a = project_call(weights, shards_a)
     peer_a = lax.ppermute(pair_a, "seq", swap)
-    shards_b = gather_blocks(tokens_b, here)
+    shards_b = gathered(tokens_b)
     partials_a = attend_call(0, tables, query_a, [(pair_a, 0), (peer_a, 1)], out_t=out_t)
-    parts_a = reduce_blocks(partials_a, here)
+    parts_a = reduced(partials_a)
     query_b, pair_b = project_call(weights, shards_b)
     peer_b = lax.ppermute(pair_b, "seq", swap)
     near = [(pair_a, 0), (peer_a, 1), (pair_b, 2)]
     state = attend_call(1, tables, query_b, near)
     partials_b = attend_call(1, tables, query_b, [(peer_b, 3)], state=state, out_t=out_t)
-    parts_b = reduce_blocks(partials_b, here)
-    first = sum(part.astype(jnp.float32) for part in parts_a[:3])
-    first = first + jnp.where(at_end == 1, parts_a[3].astype(jnp.float32), 0.0)
-    return place_call(seq_here, stripe_order, at_end, first.astype(jnp.bfloat16), parts_b)
+    parts_b = reduced(partials_b)
+    firsts = [summed(*part, at_end == 1) for part in parts_a]
+    return place_call(seq_here, stripe_order, at_end, firsts, parts_b)
 
 
 def passed_along(block, axis, distance):

time: 227 us -> 220 us (0.969)
  waiting for transfers between devices: 109 us -> 80.6 us
  starting transfers between devices: 44 us -> 62.2 us
  local copies, waits for them, and re-layouts: 5.88 us -> 13.8 us
  other arithmetic: 7.52 us -> 3.15 us
    ppermute x2 -> x4, waiting for transfers between devices: 18.7 us -> 6.37 us  [reduce_blocks(): onward = lax.ppermute(plus(up, across, here == 1), 'tp', FORWARD)]
    ppermute x2 -> x4, waiting for transfers between devices: 19.8 us -> 9.12 us  [gather_blocks(): after = lax.ppermute(block, 'tp', BACKWARD)]
    ppermute x2 -> x4, waiting for transfers between devices: 10 us -> 20 us  [reduce_blocks(): across = lax.ppermute(sent, 'tp', FOLDED)]
    ppermute x3 -> x6, waiting for transfers between devices: 18.5 us -> 9.61 us  [the longest x2 6.17 us: per_device_fast(): got = lax.ppermute(send, 'seq', [(1, 0)])]
    unnamed x14 -> x54, local copies, waits for them, and re-layouts: 5.88 us -> 13.8 us
    ppermute x2 -> x4, starting transfers between devices: 0.55 us -> 7.52 us  [reduce_blocks(): onward = lax.ppermute(plus(up, across, here == 1), 'tp', FORWARD)]
    ppermute x2 -> x4, starting transfers between devices: 17.2 us -> 10.8 us  [reduce_blocks(): back = lax.ppermute(plus(down, across, here == 2), 'tp', BACKWARD)]
    ppermute x3 -> x6, starting transfers between devices: 8.29 us -> 13.8 us  [the longest x2 7.01 us: per_device_fast(): got = lax.ppermute(send, 'seq', [(0, 1)])]
  transfers between devices with their start and end apart: 17 -> 32, of which waited for: 12 -> 14; matrix products, arithmetic and copies ran while one was open for 3% -> 1% of each run, Pallas kernels for 25% -> 23%
where the time goes in v4:
time: 220 us; the launch traced here: 219 us
  waiting for transfers between devices  80.6 us (37%)
  starting transfers between devices  62.2 us (28%)
  Pallas kernels  59 us (27%)
  local copies, waits for them, and re-layouts  13.8 us (6%)
  other arithmetic  3.15 us (1%)
    pallas_call x4, Pallas kernels, conv_call(): pl.pallas_call(functools.partial(conv_body, with_before, piece * channels...  23.4 us
    ppermute x4, waiting for transfers between devices, reduce_blocks(): across = lax.ppermute(sent, 'tp', FOLDED)  20 us
    pallas_call x3, Pallas kernels, attend_call(): pl.pallas_call(functools.partial(attend_body, chunk, tuple((s for _, s in...  19.9 us
    unnamed x54, local copies, waits for them, and re-layouts  13.8 us
    ppermute x1, waiting for transfers between devices, per_device_fast(): peer_a = lax.ppermute(pair_a, 'seq', swap)  13.6 us
    ppermute x4, starting transfers between devices, reduce_blocks(): back = lax.ppermute(plus(down, across, here == 2), 'tp', BACKWARD)  10.8 us
    ppermute x4, starting transfers between devices, gather_blocks(): after = lax.ppermute(block, 'tp', BACKWARD)  9.64 us
    ppermute x4, waiting for transfers between devices, gather_blocks(): after = lax.ppermute(block, 'tp', BACKWARD)  9.12 us
  transfers between devices with their start and end apart: 32, of which 14 were waited for; matrix products, arithmetic and copies ran while one was open for 1% of the time, Pallas kernels for 23%

profile of v4, /device:TPU:0, one launch (start us, length us, event | category | flops | bytes accessed | tf_op | source)
XLA Modules:
  0.0 219.1 jit_solution(16436285523308151462)
XLA Ops:
  1.5 6.6 %conv.4 = (f32[256,1024]{1,0:T(8,128)}, bf16[256,512]{1,0:T(8,128)(2,1)S(1)}, bf16[256,512]{1,0:T(8,128)(2,1)S(1)}, bf16[256,1024]{1,0:T(8,128)(2,1)}) custom-call(s32[1]{0:T(128)} %bitcast.seq_ref, s32[16]{0:T(128)S(1)} %copy-done.23, bf16[512,1024]{1,0:T(8,128)(2,1)} %tokens_ref.3, f32[27,512]{1,0:T(8,128)S(1)} %copy-done.2), custom_call_target="tpu_custom_call" | custom-call | flops 7077888 | bytes 2097152 | tf_op jit(solution)/shard_map/conv/pallas_call | solution.py:190
  8.2 5.0 %collective-permute-start = (bf16[256,512]{1,0:T(8,128)(2,1)S(1)}, bf16[256,512]{1,0:T(8,128)(2,1)S(1)}, u32[]{:S(2)}, u32[]{:S(2)}) collective-permute-start(bf16[256,512]{1,0:T(8,128)(2,1)S(1)} %get-tuple-element.43), channel_id=1, source_target_pairs={{0,16},{1,17},{2,18},{3,19},{4,20},{5,21},{6,22},{7,23},{8,24},{9,... | collective-permute-start | bytes 786440 | tf_op jit(solution)/shard_map/ppermute | solution.py:521
  13.2 6.7 %conv.5 = (f32[256,1024]{1,0:T(8,128)}, bf16[256,512]{1,0:T(8,128)(2,1)S(1)}, bf16[256,512]{1,0:T(8,128)(2,1)}, bf16[256,1024]{1,0:T(8,128)(2,1)}) custom-call(s32[1]{0:T(128)} %bitcast.seq_ref, s32[16]{0:T(128)S(1)} %copy-done.23, bf16[512,1024]{1,0:T(8,128)(2,1)} %tokens_ref.3, f32[27,512]{1,0:T(8,128)S(1)} %copy-done.2), custom_call_target="tpu_custom_call" | custom-call | flops 7077888 | bytes 2097152 | tf_op jit(solution)/shard_map/conv/pallas_call | solution.py:190
  20.7 2.1 collective-permute-start.17
  22.7 2.1 collective-permute-start.15
  24.8 2.0 collective-permute-start.1
  26.9 1.6 collective-permute-start.2
  28.5 2.2 %collective-permute-start.4 = (bf16[256,512]{1,0:T(8,128)(2,1)S(1)}, bf16[256,512]{1,0:T(8,128)(2,1)}, u32[]{:S(2)}, u32[]{:S(2)}) collective-permute-start(bf16[256,512]{1,0:T(8,128)(2,1)S(1)} %broadcast_select_fusion.3.refs_0_), channel_id=1, source_target_pairs={{4,0},{8,4},{12,8},{0,12},{5,1},{9,5},{13,9},{1,13},{6,2},{10,6},{... | collective-permute-start | bytes 786440 | tf_op jit(solution)/shard_map/ppermute | solution.py:481
  30.8 2.8 %copy-done = bf16[3,512,2048]{2,1,0:T(8,128)(2,1)S(1)} copy-done((bf16[3,512,2048]{2,1,0:T(8,128)(2,1)S(1)}, bf16[3,512,2048]{2,1,0:T(8,128)(2,1)}, u32[]{:S(2)}) %copy-start) | copy-done | bytes 6291480
  33.6 1.6 copy-done.1
  35.9 4.6 %prepare.1 = (bf16[1536,2048]{1,0:T(8,128)(2,1)S(1)}, bf16[2048,512]{1,0:T(8,128)(2,1)S(1)}) custom-call(s32[4]{0:T(128)S(1)} %pad_add_fusion.blocks_ref, f32[1,2048]{1,0:T(1,128)S(1)} %bitcast.10, bf16[1536,2048]{1,0:T(8,128)(2,1)S(1)} %bitcast.9, bf16[512,2048]{1,0:T(8,128)(2,1)S(1)} %copy-done.1), custom_call_target="tpu_custom_call" | custom-call | flops 3145728 | bytes 16777216 | tf_op jit(solution)/shard_map/prepare/pallas_call | solution.py:213
  40.6 5.0 %conv.7 = (bf16[256,512]{1,0:T(8,128)(2,1)S(1)}, bf16[256,512]{1,0:T(8,128)(2,1)S(1)}) custom-call(s32[1]{0:T(128)} %bitcast.seq_ref, s32[16]{0:T(128)S(1)} %copy-done.24, bf16[256,1024]{1,0:T(8,128)(2,1)} %collective-permute-done.17.tokens_ref, f32[27,512]{1,0:T(8,128)S(1)} %copy-done.3, f32[256,1024]{1,0:T(8,128)S(1)} %copy-done.5), custom_call_target="tpu_custom_call" | custom-call | flops 7077888 | bytes 2097152 | tf_op jit(solution)/shard_map/conv/pallas_call | solution.py:190
  45.6 1.3 collective-permute-start.18
  46.9 3.4 %collective-permute-done.1 = bf16[256,512]{1,0:T(8,128)(2,1)} collective-permute-done((bf16[256,512]{1,0:T(8,128)(2,1)}, bf16[256,512]{1,0:T(8,128)(2,1)}, u32[]{:S(2)}, u32[]{:S(2)}) %collective-permute-start.1) | collective-permute-done | bytes 262176 | tf_op jit(solution)/shard_map/ppermute | solution.py:521
  50.3 1.6 collective-permute-start.3
  52.0 2.2 %collective-permute-start.5 = (bf16[256,512]{1,0:T(8,128)(2,1)S(1)}, bf16[256,512]{1,0:T(8,128)(2,1)S(1)}, u32[]{:S(2)}, u32[]{:S(2)}) collective-permute-start(bf16[256,512]{1,0:T(8,128)(2,1)S(1)} %broadcast_select_fusion.2.refs_1_), channel_id=1, source_target_pairs={{4,0},{8,4},{12,8},{0,12},{5,1},{9,5},{13,9},{1,13},{6,2},{10,6},{... | collective-permute-start | bytes 786440 | tf_op jit(solution)/shard_map/ppermute | solution.py:481
  54.2 5.0 %conv.6 = (bf16[256,512]{1,0:T(8,128)(2,1)S(1)}, bf16[256,512]{1,0:T(8,128)(2,1)S(1)}) custom-call(s32[1]{0:T(128)} %bitcast.seq_ref, s32[16]{0:T(128)S(1)} %copy-done.24, bf16[256,1024]{1,0:T(8,128)(2,1)} %collective-permute-done.15.tokens_ref, f32[27,512]{1,0:T(8,128)S(1)} %copy-done.3, f32[256,1024]{1,0:T(8,128)S(1)} %copy-done.4), custom_call_target="tpu_custom_call" | custom-call | flops 7077888 | bytes 2097152 | tf_op jit(solution)/shard_map/conv/pallas_call | solution.py:190
  60.6 1.8 collective-permute-start.6
  62.8 6.2 %collective-permute-done.16 = bf16[256,512]{1,0:T(8,128)(2,1)S(1)} collective-permute-done((bf16[256,512]{1,0:T(8,128)(2,1)S(1)}, bf16[256,512]{1,0:T(8,128)(2,1)S(1)}, u32[]{:S(2)}, u32[]{:S(2)}) %collective-permute-start.16) | collective-permute-done | bytes 262176 | tf_op jit(solution)/shard_map/ppermute | solution.py:530
  68.9 1.7 collective-permute-start.22
  71.0 3.5 %collective-permute-start.21 = (bf16[256,512]{1,0:T(8,128)(2,1)S(1)}, bf16[256,512]{1,0:T(8,128)(2,1)S(1)}, u32[]{:S(2)}, u32[]{:S(2)}) collective-permute-start(bf16[256,512]{1,0:T(8,128)(2,1)S(1)} %broadcast_select_fusion.1.refs_0_), channel_id=1, source_target_pairs={{4,0},{8,4},{12,8},{0,12},{5,1},{9,5},{13,9},{1,13},{6,2},{10,6},{... | collective-permute-start | bytes 786440 | tf_op jit(solution)/shard_map/ppermute | solution.py:481
  74.6 3.8 %collective-permute-done.20.refs_3_ = bf16[256,512]{1,0:T(8,128)(2,1)S(1)} collective-permute-done((bf16[256,512]{1,0:T(8,128)(2,1)S(1)}, bf16[256,512]{1,0:T(8,128)(2,1)S(1)}, u32[]{:S(2)}, u32[]{:S(2)}) %collective-permute-start.20) | collective-permute-done | bytes 262176 | tf_op jit(solution)/shard_map/ppermute | solution.py:480
  78.5 5.5 %collective-permute-done.22.refs_5_ = bf16[256,512]{1,0:T(8,128)(2,1)S(1)} collective-permute-done((bf16[256,512]{1,0:T(8,128)(2,1)S(1)}, bf16[256,512]{1,0:T(8,128)(2,1)S(1)}, u32[]{:S(2)}, u32[]{:S(2)}) %collective-permute-start.22) | collective-permute-done | bytes 262176 | tf_op jit(solution)/shard_map/ppermute | solution.py:481
  84.6 5.0 %collective-permute-done.19.refs_2_ = bf16[256,512]{1,0:T(8,128)(2,1)S(1)} collective-permute-done((bf16[256,512]{1,0:T(8,128)(2,1)S(1)}, bf16[256,512]{1,0:T(8,128)(2,1)S(1)}, u32[]{:S(2)}, u32[]{:S(2)}) %collective-permute-start.19) | collective-permute-done | bytes 262176 | tf_op jit(solution)/shard_map/ppermute | solution.py:480
  89.6 3.7 %collective-permute-done.21.refs_4_ = bf16[256,512]{1,0:T(8,128)(2,1)S(1)} collective-permute-done((bf16[256,512]{1,0:T(8,128)(2,1)S(1)}, bf16[256,512]{1,0:T(8,128)(2,1)S(1)}, u32[]{:S(2)}, u32[]{:S(2)}) %collective-permute-start.21) | collective-permute-done | bytes 262176 | tf_op jit(solution)/shard_map/ppermute | solution.py:481
  93.3 2.8 %collective-permute-start.23 = (bf16[256,512]{1,0:T(8,128)(2,1)S(1)}, bf16[256,512]{1,0:T(8,128)(2,1)S(1)}, u32[]{:S(2)}, u32[]{:S(2)}) collective-permute-start(bf16[256,512]{1,0:T(8,128)(2,1)S(1)} %select_select_fusion.1), channel_id=1, source_target_pairs={{4,0},{12,4},{8,12},{0,8},{5,1},{13,5},{9,13},{1,9},{6,2},{14,6},{... | collective-permute-start | bytes 786440 | tf_op jit(solution)/shard_map/ppermute | solution.py:483
  96.0 2.8 %collective-permute-done.7.refs_7_ = bf16[256,512]{1,0:T(8,128)(2,1)S(1)} collective-permute-done((bf16[256,512]{1,0:T(8,128)(2,1)S(1)}, bf16[256,512]{1,0:T(8,128)(2,1)S(1)}, u32[]{:S(2)}, u32[]{:S(2)}) %collective-permute-start.7) | collective-permute-done | bytes 262176 | tf_op jit(solution)/shard_map/ppermute | solution.py:483
  98.9 4.5 %project.2 = (bf16[512,512]{1,0:T(8,128)(2,1)S(1)}, bf16[1024,512]{1,0:T(8,128)(2,1)S(1)}) custom-call(bf16[1536,2048]{1,0:T(8,128)(2,1)S(1)} %get-tuple-element.41.weight_ref, bf16[256,512]{1,0:T(8,128)(2,1)S(1)} %broadcast_select_fusion.3.refs_0_, bf16[256,512]{1,0:T(8,128)(2,1)S(1)} %broadcast_select_fusion.2.refs_1_, ...), custom_call_target="tpu_custom_call" | custom-call | flops 3221225472 | bytes 9961472 | tf_op jit(solution)/shard_map/project/pallas_call | solution.py:267
  103.4 3.5 %collective-permute-start.8 = (bf16[1024,512]{1,0:T(8,128)(2,1)S(1)}, bf16[1024,512]{1,0:T(8,128)(2,1)S(1)}, u32[]{:S(2)}, u32[]{:S(2)}) collective-permute-start(bf16[1024,512]{1,0:T(8,128)(2,1)S(1)} %get-tuple-element.47.refs_0_), channel_id=1, source_target_pairs={{0,16},{16,0},{1,17},{17,1},{2,18},{18,2},{3,19},{19,3},{4,20},{20... | collective-permute-start | bytes 3145736 | tf_op jit(solution)/shard_map/ppermute | solution.py:535
  106.9 2.5 %collective-permute-done.23.refs_6_ = bf16[256,512]{1,0:T(8,128)(2,1)S(1)} collective-permute-done((bf16[256,512]{1,0:T(8,128)(2,1)S(1)}, bf16[256,512]{1,0:T(8,128)(2,1)S(1)}, u32[]{:S(2)}, u32[]{:S(2)}) %collective-permute-start.23) | collective-permute-done | bytes 262176 | tf_op jit(solution)/shard_map/ppermute | solution.py:483
  109.4 4.5 %project.3 = (bf16[512,512]{1,0:T(8,128)(2,1)S(1)}, bf16[1024,512]{1,0:T(8,128)(2,1)}) custom-call(bf16[1536,2048]{1,0:T(8,128)(2,1)S(1)} %get-tuple-element.41.weight_ref, bf16[256,512]{1,0:T(8,128)(2,1)S(1)} %broadcast_select_fusion.1.refs_0_, bf16[256,512]{1,0:T(8,128)(2,1)S(1)} %broadcast_select_fusion.refs_1_, ...), custom_call_target="tpu_custom_call" | custom-call | flops 3221225472 | bytes 9961472 | tf_op jit(solution)/shard_map/project/pallas_call | solution.py:267
  113.9 3.4 %collective-permute-start.25 = (bf16[1024,512]{1,0:T(8,128)(2,1)}, bf16[1024,512]{1,0:T(8,128)(2,1)}, u32[]{:S(2)}, u32[]{:S(2)}) collective-permute-start(bf16[1024,512]{1,0:T(8,128)(2,1)} %get-tuple-element.66.refs_2_), channel_id=1, source_target_pairs={{0,16},{16,0},{1,17},{17,1},{2,18},{18,2},{3,19},{19,3},{4,20},{20... | collective-permute-start | bytes 3145736 | tf_op jit(solution)/shard_map/ppermute | solution.py:540
  117.3 13.6 %collective-permute-done.8.refs_1_ = bf16[1024,512]{1,0:T(8,128)(2,1)S(1)} collective-permute-done((bf16[1024,512]{1,0:T(8,128)(2,1)S(1)}, bf16[1024,512]{1,0:T(8,128)(2,1)S(1)}, u32[]{:S(2)}, u32[]{:S(2)}) %collective-permute-start.8) | collective-permute-done | bytes 1048608 | tf_op jit(solution)/shard_map/ppermute | solution.py:535
  130.9 6.9 %attend.3 = (bf16[256,512]{1,0:T(8,128)(2,1)S(1)}, bf16[256,512]{1,0:T(8,128)(2,1)S(1)}, bf16[256,512]{1,0:T(8,128)(2,1)S(1)}, bf16[256,512]{1,0:T(8,128)(2,1)S(...) custom-call(s32[1]{0:T(128)} %bitcast.seq_ref, ...), custom_call_target="tpu_custom_call" | custom-call | flops 1073741824 | bytes 3145728 | tf_op jit(solution)/shard_map/attend/pallas_call | solution.py:407
  142.1 2.5 %collective-permute-start.12 = (bf16[256,512]{1,0:T(8,128)(2,1)}, bf16[256,512]{1,0:T(8,128)(2,1)}, u32[]{:S(2)}, u32[]{:S(2)}) collective-permute-start(bf16[256,512]{1,0:T(8,128)(2,1)} %get-tuple-element.55), channel_id=1, source_target_pairs={{0,4},{4,12},{12,8},{8,0},{1,5},{5,13},{13,9},{9,1},{2,6},{6,14},{... | collective-permute-start | bytes 786440 | tf_op jit(solution)/shard_map/ppermute | solution.py:494
  146.9 7.3 %attend.4 = (f32[4,2,512]{2,1,0:T(2,128)S(1)}, f32[512,512]{1,0:T(8,128)S(1)}) custom-call(s32[1]{0:T(128)} %bitcast.seq_ref, s32[16]{0:T(128)S(1)} %copy-done.24, s32[16,16]{1,0:T(8,128)S(1)} %copy-done.22, bf16[512,512]{1,0:T(8,128)(2,1)S(1)} %copy-done.9, bf16[1024,512]{1,0:T(8,128)(2,1)S(1)} %copy-done.7, ...), custom_call_target="tpu_custom_call" | custom-call | flops 1610612736 | bytes 4194304 | tf_op jit(solution)/shard_map/attend/pallas_call | solution.py:407
  154.3 5.6 %attend.5 = (bf16[256,512]{1,0:T(8,128)(2,1)S(1)}, bf16[256,512]{1,0:T(8,128)(2,1)S(1)}, bf16[256,512]{1,0:T(8,128)(2,1)S(1)}, bf16[256,512]{1,0:T(8,128)(2,1)S(...) custom-call(s32[1]{0:T(128)} %bitcast.seq_ref, ...), custom_call_target="tpu_custom_call" | custom-call | flops 536870912 | bytes 2097152 | tf_op jit(solution)/shard_map/attend/pallas_call | solution.py:407
  159.9 1.6 collective-permute-start.29
  162.7 2.8 %collective-permute-start.13 = (bf16[256,512]{1,0:T(8,128)(2,1)S(1)}, bf16[256,512]{1,0:T(8,128)(2,1)S(1)}, u32[]{:S(2)}, u32[]{:S(2)}) collective-permute-start(bf16[256,512]{1,0:T(8,128)(2,1)S(1)} %get-tuple-element.81), channel_id=1, source_target_pairs={{4,0},{8,4},{12,8},{0,12},{5,1},{9,5},{13,9},{1,13},{6,2},{10,6},{... | collective-permute-start | bytes 786440 | tf_op jit(solution)/shard_map/ppermute | solution.py:495
  165.7 3.8 %collective-permute-start.10 = (bf16[256,512]{1,0:T(8,128)(2,1)S(1)}, bf16[256,512]{1,0:T(8,128)(2,1)S(1)}, u32[]{:S(2)}, u32[]{:S(2)}) collective-permute-start(bf16[256,512]{1,0:T(8,128)(2,1)S(1)} %get-tuple-element.83), channel_id=1, source_target_pairs={{4,0},{8,4},{12,8},{0,12},{5,1},{9,5},{13,9},{1,13},{6,2},{10,6},{... | collective-permute-start | bytes 786440 | tf_op jit(solution)/shard_map/ppermute | solution.py:495
  169.6 3.3 %collective-permute-done.29.refs_9_ = bf16[256,512]{1,0:T(8,128)(2,1)S(1)} collective-permute-done((bf16[256,512]{1,0:T(8,128)(2,1)S(1)}, bf16[256,512]{1,0:T(8,128)(2,1)S(1)}, u32[]{:S(2)}, u32[]{:S(2)}) %collective-permute-start.29) | collective-permute-done | bytes 262176 | tf_op jit(solution)/shard_map/ppermute | solution.py:494
  173.0 16.7 %collective-permute-done.26.refs_5_ = bf16[256,512]{1,0:T(8,128)(2,1)S(1)} collective-permute-done((bf16[256,512]{1,0:T(8,128)(2,1)S(1)}, bf16[256,512]{1,0:T(8,128)(2,1)S(1)}, u32[]{:S(2)}, u32[]{:S(2)}) %collective-permute-start.26) | collective-permute-done | bytes 262176 | tf_op jit(solution)/shard_map/ppermute | solution.py:494
  192.0 3.0 %collective-permute-start.27 = (bf16[256,512]{1,0:T(8,128)(2,1)S(1)}, bf16[256,512]{1,0:T(8,128)(2,1)S(1)}, u32[]{:S(2)}, u32[]{:S(2)}) collective-permute-start(bf16[256,512]{1,0:T(8,128)(2,1)S(1)} %get-tuple-element.80), channel_id=1, source_target_pairs={{4,0},{8,4},{12,8},{0,12},{5,1},{9,5},{13,9},{1,13},{6,2},{10,6},{... | collective-permute-start | bytes 786440 | tf_op jit(solution)/shard_map/ppermute | solution.py:495
  194.9 6.6 %collective-permute-start.28 = (bf16[256,512]{1,0:T(8,128)(2,1)S(1)}, bf16[256,512]{1,0:T(8,128)(2,1)S(1)}, u32[]{:S(2)}, u32[]{:S(2)}) collective-permute-start(bf16[256,512]{1,0:T(8,128)(2,1)S(1)} %get-tuple-element.79), channel_id=1, source_target_pairs={{0,4},{4,8},{8,12},{12,0},{1,5},{5,9},{9,13},{13,1},{2,6},{6,10},{... | collective-permute-start | bytes 786440 | tf_op jit(solution)/shard_map/ppermute | solution.py:496
  202.8 1.8 collective-permute-done.30.refs_7_
  204.6 6.4 %collective-permute-done.31.refs_8_ = bf16[256,512]{1,0:T(8,128)(2,1)S(1)} collective-permute-done((bf16[256,512]{1,0:T(8,128)(2,1)S(1)}, bf16[256,512]{1,0:T(8,128)(2,1)S(1)}, u32[]{:S(2)}, u32[]{:S(2)}) %collective-permute-start.31) | collective-permute-done | bytes 262176 | tf_op jit(solution)/shard_map/ppermute | solution.py:496
  211.0 6.0 %collective-permute-done.27.refs_3_ = bf16[256,512]{1,0:T(8,128)(2,1)S(1)} collective-permute-done((bf16[256,512]{1,0:T(8,128)(2,1)S(1)}, bf16[256,512]{1,0:T(8,128)(2,1)S(1)}, u32[]{:S(2)}, u32[]{:S(2)}) %collective-permute-start.27) | collective-permute-done | bytes 262176 | tf_op jit(solution)/shard_map/ppermute | solution.py:495
  216.9 2.2 %place.1 = bf16[512,1024]{1,0:T(8,128)(2,1)} custom-call(s32[1]{0:T(128)} %bitcast.seq_ref, s32[16]{0:T(128)S(1)} %copy-done.24, s32[1]{0:T(128)} %bitcast.1.ends_ref, bf16[256,512]{1,0:T(8,128)(2,1)S(1)} %fusion.13.refs_0_, bf16[256,512]{1,0:T(8,128)(2,1)S(1)} %fusion.19.refs_1_, bf16[256,512]{1,0:T(8,128)(2,1)S(1)} %get-tuple-element.69.refs_2_, ...), custom_call_target="tpu_custom_call" | custom-call | flops 1048576 | bytes 3670016 | tf_op jit(solution)/shard_map/place/pallas_call | solution.py:459
  (96 shorter events, 17.6 us)
Async XLA Ops:
  0.0 40.5 %copy-start.24 = (s32[16]{0:T(128)S(1)}, s32[16]{0:T(128)}, u32[]{:S(2)}) copy-start(s32[16]{0:T(128)} %order_ref.15) | copy-start | bytes 196
  1.5 39.0 %copy-start.3 = (f32[27,512]{1,0:T(8,128)S(1)}, f32[27,512]{1,0:T(8,128)}, u32[]{:S(2)}) copy-start(f32[27,512]{1,0:T(8,128)} %taps_ref.7) | copy-start | bytes 165892
  8.2 46.1 %copy-start.4 = (f32[256,1024]{1,0:T(8,128)S(1)}, f32[256,1024]{1,0:T(8,128)}, u32[]{:S(2)}) copy-start(f32[256,1024]{1,0:T(8,128)} %get-tuple-element.58.part_ref) | copy-start | bytes 3145732
  8.2 18.7 %collective-permute-start = (bf16[256,512]{1,0:T(8,128)(2,1)S(1)}, bf16[256,512]{1,0:T(8,128)(2,1)S(1)}, u32[]{:S(2)}, u32[]{:S(2)}) collective-permute-start(bf16[256,512]{1,0:T(8,128)(2,1)S(1)} %get-tuple-element.43), channel_id=1, source_target_pairs={{0,16},{1,17},{2,18},{3,19},{4,20},{5,21},{6,22},{7,23},{8,24},{9,... | collective-permute-start | bytes 786440 | tf_op jit(solution)/shard_map/ppermute | solution.py:521
  20.7 19.9 %collective-permute-start.17 = (bf16[256,1024]{1,0:T(8,128)(2,1)}, bf16[256,1024]{1,0:T(8,128)(2,1)}, u32[]{:S(2)}, u32[]{:S(2)}) collective-permute-start(bf16[256,1024]{1,0:T(8,128)(2,1)} %get-tuple-element.61), channel_id=1, source_target_pairs={{0,16},{1,17},{2,18},{3,19},{4,20},{5,21},{6,22},{7,23},{8,24},{9,... | collective-permute-start | bytes 1572872 | tf_op jit(solution)/shard_map/ppermute | solution.py:523
  22.7 29.2 %collective-permute-start.15 = (bf16[256,1024]{1,0:T(8,128)(2,1)}, bf16[256,1024]{1,0:T(8,128)(2,1)}, u32[]{:S(2)}, u32[]{:S(2)}) collective-permute-start(bf16[256,1024]{1,0:T(8,128)(2,1)} %get-tuple-element.57), channel_id=1, source_target_pairs={{0,16},{1,17},{2,18},{3,19},{4,20},{5,21},{6,22},{7,23},{8,24},{9,... | collective-permute-start | bytes 1572872 | tf_op jit(solution)/shard_map/ppermute | solution.py:523
  24.8 25.5 %collective-permute-start.1 = (bf16[256,512]{1,0:T(8,128)(2,1)}, bf16[256,512]{1,0:T(8,128)(2,1)}, u32[]{:S(2)}, u32[]{:S(2)}) collective-permute-start(bf16[256,512]{1,0:T(8,128)(2,1)} %get-tuple-element.45), channel_id=1, source_target_pairs={{0,16},{1,17},{2,18},{3,19},{4,20},{5,21},{6,22},{7,23},{8,24},{9,... | collective-permute-start | bytes 786440 | tf_op jit(solution)/shard_map/ppermute | solution.py:521
  26.9 32.3 %collective-permute-start.2 = (bf16[256,512]{1,0:T(8,128)(2,1)S(1)}, bf16[256,512]{1,0:T(8,128)(2,1)}, u32[]{:S(2)}, u32[]{:S(2)}) collective-permute-start(bf16[256,512]{1,0:T(8,128)(2,1)S(1)} %broadcast_select_fusion.3.refs_0_), channel_id=1, source_target_pairs={{0,4},{4,8},{8,12},{12,0},{1,5},{5,9},{9,13},{13,1},{2,6},{6,10},{... | collective-permute-start | bytes 786440 | tf_op jit(solution)/shard_map/ppermute | solution.py:480
  28.5 32.0 %collective-permute-start.4 = (bf16[256,512]{1,0:T(8,128)(2,1)S(1)}, bf16[256,512]{1,0:T(8,128)(2,1)}, u32[]{:S(2)}, u32[]{:S(2)}) collective-permute-start(bf16[256,512]{1,0:T(8,128)(2,1)S(1)} %broadcast_select_fusion.3.refs_0_), channel_id=1, source_target_pairs={{4,0},{8,4},{12,8},{0,12},{5,1},{9,5},{13,9},{1,13},{6,2},{10,6},{... | collective-permute-start | bytes 786440 | tf_op jit(solution)/shard_map/ppermute | solution.py:481
  30.8 2.8 %copy-start = (bf16[3,512,2048]{2,1,0:T(8,128)(2,1)S(1)}, bf16[3,512,2048]{2,1,0:T(8,128)(2,1)}, u32[]{:S(2)}) copy-start(bf16[3,512,2048]{2,1,0:T(8,128)(2,1)} %param.10) | copy-start | bytes 18874372
  33.6 1.6 copy-start.1
  35.9 4.6 %copy-start.5 = (f32[256,1024]{1,0:T(8,128)S(1)}, f32[256,1024]{1,0:T(8,128)}, u32[]{:S(2)}) copy-start(f32[256,1024]{1,0:T(8,128)} %get-tuple-element.62.part_ref) | copy-start | bytes 3145732
  35.9 14.4 %copy-start.13 = (bf16[256,512]{1,0:T(8,128)(2,1)S(1)}, bf16[256,512]{1,0:T(8,128)(2,1)}, u32[]{:S(2)}) copy-start(bf16[256,512]{1,0:T(8,128)(2,1)} %copy-done.12) | copy-start | bytes 786436
  45.6 16.8 %collective-permute-start.18 = (bf16[256,512]{1,0:T(8,128)(2,1)S(1)}, bf16[256,512]{1,0:T(8,128)(2,1)S(1)}, u32[]{:S(2)}, u32[]{:S(2)}) collective-permute-start(bf16[256,512]{1,0:T(8,128)(2,1)S(1)} %get-tuple-element.64), channel_id=1, source_target_pairs={{16,0},{17,1},{18,2},{19,3},{20,4},{21,5},{22,6},{23,7},{24,8},{25... | collective-permute-start | bytes 786440 | tf_op jit(solution)/shard_map/ppermute | solution.py:530
  50.3 20.3 %collective-permute-start.3 = (bf16[256,512]{1,0:T(8,128)(2,1)S(1)}, bf16[256,512]{1,0:T(8,128)(2,1)S(1)}, u32[]{:S(2)}, u32[]{:S(2)}) collective-permute-start(bf16[256,512]{1,0:T(8,128)(2,1)S(1)} %broadcast_select_fusion.2.refs_1_), channel_id=1, source_target_pairs={{0,4},{4,8},{8,12},{12,0},{1,5},{5,9},{9,13},{13,1},{2,6},{6,10},{... | collective-permute-start | bytes 786440 | tf_op jit(solution)/shard_map/ppermute | solution.py:480
  52.0 19.1 %collective-permute-start.5 = (bf16[256,512]{1,0:T(8,128)(2,1)S(1)}, bf16[256,512]{1,0:T(8,128)(2,1)S(1)}, u32[]{:S(2)}, u32[]{:S(2)}) collective-permute-start(bf16[256,512]{1,0:T(8,128)(2,1)S(1)} %broadcast_select_fusion.2.refs_1_), channel_id=1, source_target_pairs={{4,0},{8,4},{12,8},{0,12},{5,1},{9,5},{13,9},{1,13},{6,2},{10,6},{... | collective-permute-start | bytes 786440 | tf_op jit(solution)/shard_map/ppermute | solution.py:481
  59.2 9.7 %collective-permute-start.16 = (bf16[256,512]{1,0:T(8,128)(2,1)S(1)}, bf16[256,512]{1,0:T(8,128)(2,1)S(1)}, u32[]{:S(2)}, u32[]{:S(2)}) collective-permute-start(bf16[256,512]{1,0:T(8,128)(2,1)S(1)} %get-tuple-element.60), channel_id=1, source_target_pairs={{16,0},{17,1},{18,2},{19,3},{20,4},{21,5},{22,6},{23,7},{24,8},{25... | collective-permute-start | bytes 786440 | tf_op jit(solution)/shard_map/ppermute | solution.py:530
  60.6 35.5 %collective-permute-start.6 = (bf16[256,512]{1,0:T(8,128)(2,1)S(1)}, bf16[256,512]{1,0:T(8,128)(2,1)S(1)}, u32[]{:S(2)}, u32[]{:S(2)}) collective-permute-start(bf16[256,512]{1,0:T(8,128)(2,1)S(1)} %select_select_fusion.3), channel_id=1, source_target_pairs={{4,0},{12,4},{8,12},{0,8},{5,1},{13,5},{9,13},{1,9},{6,2},{14,6},{... | collective-permute-start | bytes 786440 | tf_op jit(solution)/shard_map/ppermute | solution.py:483
  62.4 15.9 %collective-permute-start.20 = (bf16[256,512]{1,0:T(8,128)(2,1)S(1)}, bf16[256,512]{1,0:T(8,128)(2,1)S(1)}, u32[]{:S(2)}, u32[]{:S(2)}) collective-permute-start(bf16[256,512]{1,0:T(8,128)(2,1)S(1)} %broadcast_select_fusion.refs_1_), channel_id=1, source_target_pairs={{0,4},{4,8},{8,12},{12,0},{1,5},{5,9},{9,13},{13,1},{2,6},{6,10},{... | collective-permute-start | bytes 786440 | tf_op jit(solution)/shard_map/ppermute | solution.py:480
  68.9 15.0 %collective-permute-start.22 = (bf16[256,512]{1,0:T(8,128)(2,1)S(1)}, bf16[256,512]{1,0:T(8,128)(2,1)S(1)}, u32[]{:S(2)}, u32[]{:S(2)}) collective-permute-start(bf16[256,512]{1,0:T(8,128)(2,1)S(1)} %broadcast_select_fusion.refs_1_), channel_id=1, source_target_pairs={{4,0},{8,4},{12,8},{0,12},{5,1},{9,5},{13,9},{1,13},{6,2},{10,6},{... | collective-permute-start | bytes 786440 | tf_op jit(solution)/shard_map/ppermute | solution.py:481
  70.6 19.0 %collective-permute-start.19 = (bf16[256,512]{1,0:T(8,128)(2,1)S(1)}, bf16[256,512]{1,0:T(8,128)(2,1)S(1)}, u32[]{:S(2)}, u32[]{:S(2)}) collective-permute-start(bf16[256,512]{1,0:T(8,128)(2,1)S(1)} %broadcast_select_fusion.1.refs_0_), channel_id=1, source_target_pairs={{0,4},{4,8},{8,12},{12,0},{1,5},{5,9},{9,13},{13,1},{2,6},{6,10},{... | collective-permute-start | bytes 786440 | tf_op jit(solution)/shard_map/ppermute | solution.py:480
  71.0 22.2 %collective-permute-start.21 = (bf16[256,512]{1,0:T(8,128)(2,1)S(1)}, bf16[256,512]{1,0:T(8,128)(2,1)S(1)}, u32[]{:S(2)}, u32[]{:S(2)}) collective-permute-start(bf16[256,512]{1,0:T(8,128)(2,1)S(1)} %broadcast_select_fusion.1.refs_0_), channel_id=1, source_target_pairs={{4,0},{8,4},{12,8},{0,12},{5,1},{9,5},{13,9},{1,13},{6,2},{10,6},{... | collective-permute-start | bytes 786440 | tf_op jit(solution)/shard_map/ppermute | solution.py:481
  78.3 20.6 %collective-permute-start.7 = (bf16[256,512]{1,0:T(8,128)(2,1)S(1)}, bf16[256,512]{1,0:T(8,128)(2,1)S(1)}, u32[]{:S(2)}, u32[]{:S(2)}) collective-permute-start(bf16[256,512]{1,0:T(8,128)(2,1)S(1)} %select_select_fusion.2), channel_id=1, source_target_pairs={{4,0},{12,4},{8,12},{0,8},{5,1},{13,5},{9,13},{1,9},{6,2},{14,6},{... | collective-permute-start | bytes 786440 | tf_op jit(solution)/shard_map/ppermute | solution.py:483
  84.0 22.9 %collective-permute-start.24 = (bf16[256,512]{1,0:T(8,128)(2,1)S(1)}, bf16[256,512]{1,0:T(8,128)(2,1)S(1)}, u32[]{:S(2)}, u32[]{:S(2)}) collective-permute-start(bf16[256,512]{1,0:T(8,128)(2,1)S(1)} %select_select_fusion), channel_id=1, source_target_pairs={{4,0},{12,4},{8,12},{0,8},{5,1},{13,5},{9,13},{1,9},{6,2},{14,6},{... | collective-permute-start | bytes 786440 | tf_op jit(solution)/shard_map/ppermute | solution.py:483
  93.3 16.2 %collective-permute-start.23 = (bf16[256,512]{1,0:T(8,128)(2,1)S(1)}, bf16[256,512]{1,0:T(8,128)(2,1)S(1)}, u32[]{:S(2)}, u32[]{:S(2)}) collective-permute-start(bf16[256,512]{1,0:T(8,128)(2,1)S(1)} %select_select_fusion.1), channel_id=1, source_target_pairs={{4,0},{12,4},{8,12},{0,8},{5,1},{13,5},{9,13},{1,9},{6,2},{14,6},{... | collective-permute-start | bytes 786440 | tf_op jit(solution)/shard_map/ppermute | solution.py:483
  103.4 34.5 %copy-start.6 = (bf16[1024,512]{1,0:T(8,128)(2,1)}, bf16[1024,512]{1,0:T(8,128)(2,1)S(1)}, u32[]{:S(2)}) copy-start(bf16[1024,512]{1,0:T(8,128)(2,1)S(1)} %get-tuple-element.47.refs_0_) | copy-start | bytes 3145732
  103.4 27.5 %copy-start.22 = (s32[16,16]{1,0:T(8,128)S(1)}, s32[16,16]{1,0:T(8,128)}, u32[]{:S(2)}) copy-start(s32[16,16]{1,0:T(8,128)} %mask_ref.5) | copy-start | bytes 3076
  103.4 27.5 %collective-permute-start.8 = (bf16[1024,512]{1,0:T(8,128)(2,1)S(1)}, bf16[1024,512]{1,0:T(8,128)(2,1)S(1)}, u32[]{:S(2)}, u32[]{:S(2)}) collective-permute-start(bf16[1024,512]{1,0:T(8,128)(2,1)S(1)} %get-tuple-element.47.refs_0_), channel_id=1, source_target_pairs={{0,16},{16,0},{1,17},{17,1},{2,18},{18,2},{3,19},{19,3},{4,20},{20... | collective-permute-start | bytes 3145736 | tf_op jit(solution)/shard_map/ppermute | solution.py:535
  113.9 27.5 %copy-start.8 = (bf16[512,512]{1,0:T(8,128)(2,1)}, bf16[512,512]{1,0:T(8,128)(2,1)S(1)}, u32[]{:S(2)}) copy-start(bf16[512,512]{1,0:T(8,128)(2,1)S(1)} %get-tuple-element.65.query_ref) | copy-start | bytes 1572868
  113.9 40.4 %collective-permute-start.25 = (bf16[1024,512]{1,0:T(8,128)(2,1)}, bf16[1024,512]{1,0:T(8,128)(2,1)}, u32[]{:S(2)}, u32[]{:S(2)}) collective-permute-start(bf16[1024,512]{1,0:T(8,128)(2,1)} %get-tuple-element.66.refs_2_), channel_id=1, source_target_pairs={{0,16},{16,0},{1,17},{17,1},{2,18},{18,2},{3,19},{19,3},{4,20},{20... | collective-permute-start | bytes 3145736 | tf_op jit(solution)/shard_map/ppermute | solution.py:540
  142.1 19.5 %collective-permute-start.12 = (bf16[256,512]{1,0:T(8,128)(2,1)}, bf16[256,512]{1,0:T(8,128)(2,1)}, u32[]{:S(2)}, u32[]{:S(2)}) collective-permute-start(bf16[256,512]{1,0:T(8,128)(2,1)} %get-tuple-element.55), channel_id=1, source_target_pairs={{0,4},{4,12},{12,8},{8,0},{1,5},{5,13},{13,9},{9,1},{2,6},{6,14},{... | collective-permute-start | bytes 786440 | tf_op jit(solution)/shard_map/ppermute | solution.py:494
  144.6 20.9 %collective-permute-start.9 = (bf16[256,512]{1,0:T(8,128)(2,1)}, bf16[256,512]{1,0:T(8,128)(2,1)S(1)}, u32[]{:S(2)}, u32[]{:S(2)}) collective-permute-start(bf16[256,512]{1,0:T(8,128)(2,1)} %copy-done.26), channel_id=1, source_target_pairs={{0,4},{4,12},{12,8},{8,0},{1,5},{5,13},{13,9},{9,1},{2,6},{6,14},{... | collective-permute-start | bytes 786440 | tf_op jit(solution)/shard_map/ppermute | solution.py:494
  144.6 1.2 copy-start.7
  146.9 14.6 %copy-start.19 = (bf16[256,512]{1,0:T(8,128)(2,1)S(1)}, bf16[256,512]{1,0:T(8,128)(2,1)}, u32[]{:S(2)}) copy-start(bf16[256,512]{1,0:T(8,128)(2,1)} %copy-done.18) | copy-start | bytes 786436
  146.9 14.6 %copy-start.21 = (bf16[256,512]{1,0:T(8,128)(2,1)S(1)}, bf16[256,512]{1,0:T(8,128)(2,1)}, u32[]{:S(2)}) copy-start(bf16[256,512]{1,0:T(8,128)(2,1)} %copy-done.20) | copy-start | bytes 786436
  146.9 18.7 %copy-start.15 = (bf16[256,512]{1,0:T(8,128)(2,1)S(1)}, bf16[256,512]{1,0:T(8,128)(2,1)}, u32[]{:S(2)}) copy-start(bf16[256,512]{1,0:T(8,128)(2,1)} %copy-done.14) | copy-start | bytes 786436
  146.9 18.7 %copy-start.17 = (bf16[256,512]{1,0:T(8,128)(2,1)S(1)}, bf16[256,512]{1,0:T(8,128)(2,1)}, u32[]{:S(2)}) copy-start(bf16[256,512]{1,0:T(8,128)(2,1)} %copy-done.16) | copy-start | bytes 786436
  154.3 47.2 %copy-start.11 = (bf16[256,512]{1,0:T(8,128)(2,1)S(1)}, bf16[256,512]{1,0:T(8,128)(2,1)}, u32[]{:S(2)}) copy-start(bf16[256,512]{1,0:T(8,128)(2,1)} %copy-done.10) | copy-start | bytes 786436
  159.9 12.9 %collective-permute-start.29 = (bf16[256,512]{1,0:T(8,128)(2,1)S(1)}, bf16[256,512]{1,0:T(8,128)(2,1)S(1)}, u32[]{:S(2)}, u32[]{:S(2)}) collective-permute-start(bf16[256,512]{1,0:T(8,128)(2,1)S(1)} %get-tuple-element.75), channel_id=1, source_target_pairs={{0,4},{4,12},{12,8},{8,0},{1,5},{5,13},{13,9},{9,1},{2,6},{6,14},{... | collective-permute-start | bytes 786440 | tf_op jit(solution)/shard_map/ppermute | solution.py:494
  162.7 28.4 %collective-permute-start.13 = (bf16[256,512]{1,0:T(8,128)(2,1)S(1)}, bf16[256,512]{1,0:T(8,128)(2,1)S(1)}, u32[]{:S(2)}, u32[]{:S(2)}) collective-permute-start(bf16[256,512]{1,0:T(8,128)(2,1)S(1)} %get-tuple-element.81), channel_id=1, source_target_pairs={{4,0},{8,4},{12,8},{0,12},{5,1},{9,5},{13,9},{1,13},{6,2},{10,6},{... | collective-permute-start | bytes 786440 | tf_op jit(solution)/shard_map/ppermute | solution.py:495
  165.5 26.5 %collective-permute-start.14 = (bf16[256,512]{1,0:T(8,128)(2,1)S(1)}, bf16[256,512]{1,0:T(8,128)(2,1)S(1)}, u32[]{:S(2)}, u32[]{:S(2)}) collective-permute-start(bf16[256,512]{1,0:T(8,128)(2,1)S(1)} %get-tuple-element.82), channel_id=1, source_target_pairs={{0,4},{4,8},{8,12},{12,0},{1,5},{5,9},{9,13},{13,1},{2,6},{6,10},{... | collective-permute-start | bytes 786440 | tf_op jit(solution)/shard_map/ppermute | solution.py:496
  165.5 24.2 %collective-permute-start.26 = (bf16[256,512]{1,0:T(8,128)(2,1)S(1)}, bf16[256,512]{1,0:T(8,128)(2,1)S(1)}, u32[]{:S(2)}, u32[]{:S(2)}) collective-permute-start(bf16[256,512]{1,0:T(8,128)(2,1)S(1)} %get-tuple-element.71), channel_id=1, source_target_pairs={{0,4},{4,12},{12,8},{8,0},{1,5},{5,13},{13,9},{9,1},{2,6},{6,14},{... | collective-permute-start | bytes 786440 | tf_op jit(solution)/shard_map/ppermute | solution.py:494
  165.7 29.2 %collective-permute-start.10 = (bf16[256,512]{1,0:T(8,128)(2,1)S(1)}, bf16[256,512]{1,0:T(8,128)(2,1)S(1)}, u32[]{:S(2)}, u32[]{:S(2)}) collective-permute-start(bf16[256,512]{1,0:T(8,128)(2,1)S(1)} %get-tuple-element.83), channel_id=1, source_target_pairs={{4,0},{8,4},{12,8},{0,12},{5,1},{9,5},{13,9},{1,13},{6,2},{10,6},{... | collective-permute-start | bytes 786440 | tf_op jit(solution)/shard_map/ppermute | solution.py:495
  172.9 29.8 %collective-permute-start.11 = (bf16[256,512]{1,0:T(8,128)(2,1)S(1)}, bf16[256,512]{1,0:T(8,128)(2,1)S(1)}, u32[]{:S(2)}, u32[]{:S(2)}) collective-permute-start(bf16[256,512]{1,0:T(8,128)(2,1)S(1)} %get-tuple-element.84), channel_id=1, source_target_pairs={{0,4},{4,8},{8,12},{12,0},{1,5},{5,9},{9,13},{13,1},{2,6},{6,10},{... | collective-permute-start | bytes 786440 | tf_op jit(solution)/shard_map/ppermute | solution.py:496
  189.7 14.9 %collective-permute-start.30 = (bf16[256,512]{1,0:T(8,128)(2,1)S(1)}, bf16[256,512]{1,0:T(8,128)(2,1)S(1)}, u32[]{:S(2)}, u32[]{:S(2)}) collective-permute-start(bf16[256,512]{1,0:T(8,128)(2,1)S(1)} %get-tuple-element.78), channel_id=1, source_target_pairs={{4,0},{8,4},{12,8},{0,12},{5,1},{9,5},{13,9},{1,13},{6,2},{10,6},{... | collective-permute-start | bytes 786440 | tf_op jit(solution)/shard_map/ppermute | solution.py:495
  191.0 19.9 %collective-permute-start.31 = (bf16[256,512]{1,0:T(8,128)(2,1)S(1)}, bf16[256,512]{1,0:T(8,128)(2,1)S(1)}, u32[]{:S(2)}, u32[]{:S(2)}) collective-permute-start(bf16[256,512]{1,0:T(8,128)(2,1)S(1)} %get-tuple-element.77), channel_id=1, source_target_pairs={{0,4},{4,8},{8,12},{12,0},{1,5},{5,9},{9,13},{13,1},{2,6},{6,10},{... | collective-permute-start | bytes 786440 | tf_op jit(solution)/shard_map/ppermute | solution.py:496
  192.0 25.0 %collective-permute-start.27 = (bf16[256,512]{1,0:T(8,128)(2,1)S(1)}, bf16[256,512]{1,0:T(8,128)(2,1)S(1)}, u32[]{:S(2)}, u32[]{:S(2)}) collective-permute-start(bf16[256,512]{1,0:T(8,128)(2,1)S(1)} %get-tuple-element.80), channel_id=1, source_target_pairs={{4,0},{8,4},{12,8},{0,12},{5,1},{9,5},{13,9},{1,13},{6,2},{10,6},{... | collective-permute-start | bytes 786440 | tf_op jit(solution)/shard_map/ppermute | solution.py:495
  194.9 22.0 %collective-permute-start.28 = (bf16[256,512]{1,0:T(8,128)(2,1)S(1)}, bf16[256,512]{1,0:T(8,128)(2,1)S(1)}, u32[]{:S(2)}, u32[]{:S(2)}) collective-permute-start(bf16[256,512]{1,0:T(8,128)(2,1)S(1)} %get-tuple-element.79), channel_id=1, source_target_pairs={{0,4},{4,8},{8,12},{12,0},{1,5},{5,9},{9,13},{13,1},{2,6},{6,10},{... | collective-permute-start | bytes 786440 | tf_op jit(solution)/shard_map/ppermute | solution.py:496
  (11 other events, 8.2 us)

commit v5 on v4

--- a/solution.py
+++ b/solution.py
@@ -116,8 +116,8 @@
     else:
         reads = ([(2, 0)], [(1, 0), (2, 1)])
 
-    def advance(step, carry):
-        rows = pl.ds(pl.multiple_of(step * GROUP, GROUP), GROUP)
+    def advance(step, carry, base=0):
+        rows = pl.ds(pl.multiple_of(base + step * GROUP, GROUP), GROUP)
         taps = taps_scr[rows, :]
         shifts = []
         for frame in range(2):
@@ -148,13 +148,11 @@
                     part_ref[rows, here] = value
                 place = pl.ds(pl.multiple_of(slots_ref[tile] * TILE, TILE), TILE)
                 packed[rows, place] = value.astype(jnp.bfloat16)
-        keep_ref[rows, :] = packed[rows, : tokens // 2]
-        send_ref[rows, :] = packed[rows, tokens // 2 :]
         return carry
 
     steps = channels // GROUP
     if with_before:
-        lax.fori_loop(0, steps, advance, 0)
+        lax.fori_loop(0, steps, advance, 0, unroll=2)
     else:
         each = steps // CHUNKS
 
@@ -165,9 +163,12 @@
                 source_ref.at[pl.ds(begin, each * GROUP)],
                 arrived.at[index],
             ).wait()
-            return lax.fori_loop(index * each, (index + 1) * each, advance, carry)
+            later = functools.partial(advance, base=begin)
+            return lax.fori_loop(0, each, later, carry, unroll=2)
 
         lax.fori_loop(0, CHUNKS, chunk, 0)
+    keep_ref[...] = packed[:, : tokens // 2]
+    send_ref[...] = packed[:, tokens // 2 :]
 
 
 def conv_call(seq_here, stripe_order, tokens, conv_taps, piece, part=None):
@@ -201,13 +202,12 @@
     )(seq_here, stripe_order, tokens, conv_taps, *([part] if with_before else []))
 
 
-def prepare_body(blocks_ref, gain_ref, qkv_ref, out_ref, qkv_out, out_out):
-    qkv_out[...] = (qkv_ref[...].astype(jnp.float32) * gain_ref[...]).astype(jnp.bfloat16)
+def prepare_body(blocks_ref, out_ref, out_out):
     out_out[...] = out_ref[...].T
 
 
-def prepare_weights(blocks, norm_gain, qkv_weight, out_weight):
-    kinds, cols, channels = qkv_weight.shape
+def prepare_out(blocks, out_weight):
+    cols, channels = out_weight.shape
     count = blocks.shape[0]
     width = channels // count
     return pl.pallas_call(
@@ -215,39 +215,33 @@
         grid_spec=pltpu.PrefetchScalarGridSpec(
             num_scalar_prefetch=1,
             grid=(count,),
-            in_specs=[
-                pl.BlockSpec((1, width), lambda j, b: (0, b[j])),
-                pl.BlockSpec((kinds * cols, width), lambda j, b: (0, b[j])),
-                pl.BlockSpec((cols, width), lambda j, b: (0, b[j])),
-            ],
-            out_specs=[
-                pl.BlockSpec((kinds * cols, width), lambda j, b: (0, j)),
-                pl.BlockSpec((width, cols), lambda j, b: (j, 0)),
-            ],
+            in_specs=[pl.BlockSpec((cols, width), lambda j, b: (0, b[j]))],
+            out_specs=pl.BlockSpec((width, cols), lambda j, b: (j, 0)),
         ),
-        out_shape=[
-            jax.ShapeDtypeStruct((kinds * cols, channels), jnp.bfloat16),
-            jax.ShapeDtypeStruct((channels, cols), jnp.bfloat16),
-        ],
+        out_shape=jax.ShapeDtypeStruct((channels, cols), jnp.bfloat16),
         compiler_params=params(),
         cost_estimate=pl.CostEstimate(
-            flops=kinds * cols * channels, bytes_accessed=16 * cols * channels, transcendentals=0
+            flops=cols * channels, bytes_accessed=4 * cols * channels, transcendentals=0
         ),
         name="prepare",
-    )(blocks, norm_gain[None, :], qkv_weight.reshape(kinds * cols, channels), out_weight)
-
-
-def project_body(weight_ref, *refs):
+    )(blocks, out_weight)
+
+
+def project_body(blocks_ref, weight_ref, gains_ref, *refs):
     shards, (query_ref, pair_ref, tokens_ref) = refs[:-3], refs[-3:]
-    width = shards[0].shape[0]
+    width, tokens = shards[0].shape
     cols = query_ref.shape[0]
-    squares = None
+    lines = 128
+    squares = jnp.zeros((1, tokens), jnp.float32)
     for index, shard in enumerate(shards):
-        block = shard[...]
-        tokens_ref[index * width : (index + 1) * width, :] = block
-        wide = block.astype(jnp.float32)
-        term = jnp.sum(wide * wide, axis=0, keepdims=True)
-        squares = term if squares is None else squares + term
+        owner, piece = divmod(index, PIECES)
+        start = (blocks_ref[owner] * PIECES + piece) * width
+        for first in range(0, width, lines):
+            there = pl.ds(pl.multiple_of(start + first, lines), lines)
+            wide = shard[first : first + lines, :].astype(jnp.float32)
+            squares = squares + jnp.sum(wide * wide, axis=0, keepdims=True)
+            gain = jnp.concatenate([gains_ref[there, :]] * (tokens // 128), axis=1)
+            tokens_ref[there, :] = (wide * gain).astype(jnp.bfloat16)
     inverse = lax.rsqrt(squares / (len(shards) * width) + EPSILON)
     rows = 256
     for index in range(weight_ref.shape[0] // rows):
@@ -260,13 +254,13 @@
             pair_ref[there, :] = (total * inverse).astype(jnp.bfloat16)
 
 
-def project_call(weights, shards):
+def project_call(blocks, weights, gains, shards):
     rows, channels = weights.shape
     tokens = shards[0].shape[1]
     cols = rows // 3
     return pl.pallas_call(
         project_body,
-        in_specs=[vmem_spec()] * (1 + len(shards)),
+        in_specs=[smem_spec()] + [vmem_spec()] * (2 + len(shards)),
         out_specs=[vmem_spec(), vmem_spec()],
         scratch_shapes=[pltpu.VMEM((channels, tokens), jnp.bfloat16)],
         out_shape=[
@@ -280,7 +274,7 @@
             transcendentals=0,
         ),
         name="project",
-    )(weights, *shards)
+    )(blocks, weights, gains, *shards)
 
 
 def tile_lists(order_ref, ids_ref, seq_here, tiles_dev):
@@ -521,7 +515,10 @@
         got = lax.ppermute(send, "seq", [(0, 1)])
         tokens_a.append(jnp.where(seq == 0, keep, got))
         before.append(lax.ppermute(tokens, "seq", [(0, 1)]))
-    weights, out_t = prepare_weights(blocks, norm_gain, qkv_weight, out_weight)
+    kinds, cols, channels = qkv_weight.shape
+    weights = qkv_weight.reshape(kinds * cols, channels)
+    gains = jnp.broadcast_to(norm_gain[:, None], (channels, 128))
+    out_t = prepare_out(blocks, out_weight)
     shards_a = gathered(tokens_a)
 
     tokens_b = []
@@ -531,12 +528,12 @@
         tokens_b.append(jnp.where(seq == 1, keep, got))
 
     swap = [(0, 1), (1, 0)]
-    query_a, pair_a = project_call(weights, shards_a)
+    query_a, pair_a = project_call(blocks, weights, gains, shards_a)
     peer_a = lax.ppermute(pair_a, "seq", swap)
     shards_b = gathered(tokens_b)
     partials_a = attend_call(0, tables, query_a, [(pair_a, 0), (peer_a, 1)], out_t=out_t)
     parts_a = reduced(partials_a)
-    query_b, pair_b = project_call(weights, shards_b)
+    query_b, pair_b = project_call(blocks, weights, gains, shards_b)
     peer_b = lax.ppermute(pair_b, "seq", swap)
     near = [(pair_a, 0), (peer_a, 1), (pair_b, 2)]
     state = attend_call(1, tables, query_b, near)

time: 220 us -> 216 us (0.982)
  local copies, waits for them, and re-layouts: 13.8 us -> 9.01 us
  Pallas kernels: 59 us -> 54.3 us
  waiting for transfers between devices: 80.6 us -> 85.3 us
    ppermute x2, waiting for transfers between devices: 3.43 us -> 10.4 us  [per_device_fast(): got = lax.ppermute(send, 'seq', [(0, 1)])]
    unnamed x54, local copies, waits for them, and re-layouts: 13.8 us -> 8.69 us
    ppermute x4, starting transfers between devices: 10.8 us -> 7.91 us  [reduce_blocks(): back = lax.ppermute(plus(down, across, here == 2), 'tp', BACKWARD)]
    pallas_call x4, Pallas kernels: 23.4 us -> 20.6 us  [conv_call(): pl.pallas_call(functools.partial(conv_body, with_before, piece * channels...]
    ppermute x4, starting transfers between devices: 7.52 us -> 9.84 us  [reduce_blocks(): onward = lax.ppermute(plus(up, across, here == 1), 'tp', FORWARD)]
  transfers between devices with their start and end apart: 32 -> 32, of which waited for: 14 -> 15; matrix products, arithmetic and copies ran while one was open for 1% -> 2% of each run, Pallas kernels for 23% -> 21%
where the time goes in v5:
time: 216 us; the launch traced here: 215 us
  waiting for transfers between devices  85.3 us (39%)
  starting transfers between devices  61.4 us (28%)
  Pallas kernels  54.3 us (25%)
  local copies, waits for them, and re-layouts  9.01 us (4%)
  other arithmetic  5.04 us (2%)
    pallas_call x4, Pallas kernels, conv_call(): pl.pallas_call(functools.partial(conv_body, with_before, piece * channels...  20.6 us
    ppermute x4, waiting for transfers between devices, reduce_blocks(): across = lax.ppermute(sent, 'tp', FOLDED)  20.1 us
    pallas_call x3, Pallas kernels, attend_call(): pl.pallas_call(functools.partial(attend_body, chunk, tuple((s for _, s in...  19.8 us
    ppermute x1, waiting for transfers between devices, per_device_fast(): peer_a = lax.ppermute(pair_a, 'seq', swap)  11.8 us
    ppermute x4, waiting for transfers between devices, gather_blocks(): before = lax.ppermute(block, 'tp', FORWARD)  10.7 us
    ppermute x2, waiting for transfers between devices, per_device_fast(): got = lax.ppermute(send, 'seq', [(0, 1)])  10.4 us
    pallas_call x2, Pallas kernels, project_call(): pl.pallas_call(project_body, in_specs=[smem_spec()] + [vmem_spec()] * (2...  10.2 us
    ppermute x4, starting transfers between devices, reduce_blocks(): onward = lax.ppermute(plus(up, across, here == 1), 'tp', FORWARD)  9.84 us
  transfers between devices with their start and end apart: 32, of which 15 were waited for; matrix products, arithmetic and copies ran while one was open for 2% of the time, Pallas kernels for 21%

profile of v5, /device:TPU:0, one launch (start us, length us, event | category | flops | bytes accessed | tf_op | source)
XLA Modules:
  0.0 215.5 jit_solution(12362470166472760512)
XLA Ops:
  1.5 6.3 %conv.5 = (f32[256,1024]{1,0:T(8,128)}, bf16[256,512]{1,0:T(8,128)(2,1)S(1)}, bf16[256,512]{1,0:T(8,128)(2,1)S(1)}, bf16[256,1024]{1,0:T(8,128)(2,1)}) custom-call(s32[1]{0:T(128)} %bitcast.seq_ref, s32[16]{0:T(128)S(1)} %copy-done.22, bf16[512,1024]{1,0:T(8,128)(2,1)} %tokens_ref.3, f32[27,512]{1,0:T(8,128)S(1)} %copy-done.1), custom_call_target="tpu_custom_call" | custom-call | flops 7077888 | bytes 2097152 | tf_op jit(solution)/shard_map/conv/pallas_call | solution.py:191
  7.8 5.7 %collective-permute-start.1 = (bf16[256,512]{1,0:T(8,128)(2,1)S(1)}, bf16[256,512]{1,0:T(8,128)(2,1)}, u32[]{:S(2)}, u32[]{:S(2)}) collective-permute-start(bf16[256,512]{1,0:T(8,128)(2,1)S(1)} %get-tuple-element.42), channel_id=1, source_target_pairs={{0,16},{1,17},{2,18},{3,19},{4,20},{5,21},{6,22},{7,23},{8,24},{9,... | collective-permute-start | bytes 786440 | tf_op jit(solution)/shard_map/ppermute | solution.py:515
  13.6 1.3 collective-permute-start.17
  14.9 6.3 %conv.4 = (f32[256,1024]{1,0:T(8,128)}, bf16[256,512]{1,0:T(8,128)(2,1)S(1)}, bf16[256,512]{1,0:T(8,128)(2,1)}, bf16[256,1024]{1,0:T(8,128)(2,1)}) custom-call(s32[1]{0:T(128)} %bitcast.seq_ref, s32[16]{0:T(128)S(1)} %copy-done.22, bf16[512,1024]{1,0:T(8,128)(2,1)} %tokens_ref.3, f32[27,512]{1,0:T(8,128)S(1)} %copy-done.1), custom_call_target="tpu_custom_call" | custom-call | flops 7077888 | bytes 2097152 | tf_op jit(solution)/shard_map/conv/pallas_call | solution.py:191
  21.9 1.4 collective-permute-start.15
  23.4 2.0 collective-permute-start
  26.4 1.6 collective-permute-start.3
  28.0 2.2 %collective-permute-start.5 = (bf16[256,512]{1,0:T(8,128)(2,1)S(1)}, bf16[256,512]{1,0:T(8,128)(2,1)}, u32[]{:S(2)}, u32[]{:S(2)}) collective-permute-start(bf16[256,512]{1,0:T(8,128)(2,1)S(1)} %broadcast_select_fusion.2.refs_1_), channel_id=1, source_target_pairs={{4,0},{8,4},{12,8},{0,12},{5,1},{9,5},{13,9},{1,13},{6,2},{10,6},{... | collective-permute-start | bytes 786440 | tf_op jit(solution)/shard_map/ppermute | solution.py:475
  30.9 4.0 %conv.7 = (bf16[256,512]{1,0:T(8,128)(2,1)S(1)}, bf16[256,512]{1,0:T(8,128)(2,1)S(1)}) custom-call(s32[1]{0:T(128)} %bitcast.seq_ref, s32[16]{0:T(128)S(1)} %copy-done.23, bf16[256,1024]{1,0:T(8,128)(2,1)S(1)} %collective-permute-done.17.tokens_ref, f32[27,512]{1,0:T(8,128)S(1)} %copy-done.2, f32[256,1024]{1,0:T(8,128)S(1)} %copy-done.4), custom_call_target="tpu_custom_call" | custom-call | flops 7077888 | bytes 2097152 | tf_op jit(solution)/shard_map/conv/pallas_call | solution.py:191
  34.8 1.3 collective-permute-start.18
  36.1 10.4 %collective-permute-done = bf16[256,512]{1,0:T(8,128)(2,1)} collective-permute-done((bf16[256,512]{1,0:T(8,128)(2,1)}, bf16[256,512]{1,0:T(8,128)(2,1)}, u32[]{:S(2)}, u32[]{:S(2)}) %collective-permute-start) | collective-permute-done | bytes 262176 | tf_op jit(solution)/shard_map/ppermute | solution.py:515
  47.6 1.6 collective-permute-start.2
  49.2 2.2 %collective-permute-start.4 = (bf16[256,512]{1,0:T(8,128)(2,1)S(1)}, bf16[256,512]{1,0:T(8,128)(2,1)S(1)}, u32[]{:S(2)}, u32[]{:S(2)}) collective-permute-start(bf16[256,512]{1,0:T(8,128)(2,1)S(1)} %broadcast_select_fusion.3.refs_0_), channel_id=1, source_target_pairs={{4,0},{8,4},{12,8},{0,12},{5,1},{9,5},{13,9},{1,13},{6,2},{10,6},{... | collective-permute-start | bytes 786440 | tf_op jit(solution)/shard_map/ppermute | solution.py:475
  51.5 4.0 %conv.6 = (bf16[256,512]{1,0:T(8,128)(2,1)S(1)}, bf16[256,512]{1,0:T(8,128)(2,1)S(1)}) custom-call(s32[1]{0:T(128)} %bitcast.seq_ref, s32[16]{0:T(128)S(1)} %copy-done.23, bf16[256,1024]{1,0:T(8,128)(2,1)S(1)} %collective-permute-done.15.tokens_ref, f32[27,512]{1,0:T(8,128)S(1)} %copy-done.2, f32[256,1024]{1,0:T(8,128)S(1)} %copy-done.3), custom_call_target="tpu_custom_call" | custom-call | flops 7077888 | bytes 2097152 | tf_op jit(solution)/shard_map/conv/pallas_call | solution.py:191
  56.8 1.9 collective-permute-start.7
  59.0 5.2 %collective-permute-done.16 = bf16[256,512]{1,0:T(8,128)(2,1)S(1)} collective-permute-done((bf16[256,512]{1,0:T(8,128)(2,1)S(1)}, bf16[256,512]{1,0:T(8,128)(2,1)S(1)}, u32[]{:S(2)}, u32[]{:S(2)}) %collective-permute-start.16) | collective-permute-done | bytes 262176 | tf_op jit(solution)/shard_map/ppermute | solution.py:527
  64.2 1.7 collective-permute-start.22
  66.3 3.5 %collective-permute-start.21 = (bf16[256,512]{1,0:T(8,128)(2,1)S(1)}, bf16[256,512]{1,0:T(8,128)(2,1)S(1)}, u32[]{:S(2)}, u32[]{:S(2)}) collective-permute-start(bf16[256,512]{1,0:T(8,128)(2,1)S(1)} %broadcast_select_fusion.1.refs_0_), channel_id=1, source_target_pairs={{4,0},{8,4},{12,8},{0,12},{5,1},{9,5},{13,9},{1,13},{6,2},{10,6},{... | collective-permute-start | bytes 786440 | tf_op jit(solution)/shard_map/ppermute | solution.py:475
  69.9 5.7 %collective-permute-done.20.refs_3_ = bf16[256,512]{1,0:T(8,128)(2,1)S(1)} collective-permute-done((bf16[256,512]{1,0:T(8,128)(2,1)S(1)}, bf16[256,512]{1,0:T(8,128)(2,1)S(1)}, u32[]{:S(2)}, u32[]{:S(2)}) %collective-permute-start.20) | collective-permute-done | bytes 262176 | tf_op jit(solution)/shard_map/ppermute | solution.py:474
  75.5 2.0 collective-permute-start.6
  77.5 3.6 %collective-permute-done.22.refs_5_ = bf16[256,512]{1,0:T(8,128)(2,1)S(1)} collective-permute-done((bf16[256,512]{1,0:T(8,128)(2,1)S(1)}, bf16[256,512]{1,0:T(8,128)(2,1)S(1)}, u32[]{:S(2)}, u32[]{:S(2)}) %collective-permute-start.22) | collective-permute-done | bytes 262176 | tf_op jit(solution)/shard_map/ppermute | solution.py:475
  81.8 5.0 %collective-permute-done.19.refs_2_ = bf16[256,512]{1,0:T(8,128)(2,1)S(1)} collective-permute-done((bf16[256,512]{1,0:T(8,128)(2,1)S(1)}, bf16[256,512]{1,0:T(8,128)(2,1)S(1)}, u32[]{:S(2)}, u32[]{:S(2)}) %collective-permute-start.19) | collective-permute-done | bytes 262176 | tf_op jit(solution)/shard_map/ppermute | solution.py:474
  86.8 3.7 %collective-permute-done.21.refs_4_ = bf16[256,512]{1,0:T(8,128)(2,1)S(1)} collective-permute-done((bf16[256,512]{1,0:T(8,128)(2,1)S(1)}, bf16[256,512]{1,0:T(8,128)(2,1)S(1)}, u32[]{:S(2)}, u32[]{:S(2)}) %collective-permute-start.21) | collective-permute-done | bytes 262176 | tf_op jit(solution)/shard_map/ppermute | solution.py:475
  90.5 2.8 %collective-permute-start.23 = (bf16[256,512]{1,0:T(8,128)(2,1)S(1)}, bf16[256,512]{1,0:T(8,128)(2,1)S(1)}, u32[]{:S(2)}, u32[]{:S(2)}) collective-permute-start(bf16[256,512]{1,0:T(8,128)(2,1)S(1)} %select_select_fusion.1), channel_id=1, source_target_pairs={{4,0},{12,4},{8,12},{0,8},{5,1},{13,5},{9,13},{1,9},{6,2},{14,6},{... | collective-permute-start | bytes 786440 | tf_op jit(solution)/shard_map/ppermute | solution.py:477
  93.3 2.8 %collective-permute-done.6.refs_6_ = bf16[256,512]{1,0:T(8,128)(2,1)S(1)} collective-permute-done((bf16[256,512]{1,0:T(8,128)(2,1)S(1)}, bf16[256,512]{1,0:T(8,128)(2,1)S(1)}, u32[]{:S(2)}, u32[]{:S(2)}) %collective-permute-start.6) | collective-permute-done | bytes 262176 | tf_op jit(solution)/shard_map/ppermute | solution.py:477
  96.4 4.9 %project.2 = (bf16[512,512]{1,0:T(8,128)(2,1)S(1)}, bf16[1024,512]{1,0:T(8,128)(2,1)S(1)}) custom-call(s32[4]{0:T(128)S(1)} %pad_add_fusion.blocks_ref, bf16[1536,2048]{1,0:T(8,128)(2,1)S(1)} %bitcast.8, f32[2048,128]{1,0:T(8,128)S(1)} %broadcast_in_dim.42.gains_ref, bf16[256,512]{1,0:T(8,128)(2,1)S(1)} %broadcast_select_fusion.3.refs_0_, ...), custom_call_target="tpu_custom_call" | custom-call | flops 3221225472 | bytes 9961472 | tf_op jit(solution)/shard_map/project/pallas_call | solution.py:261
  101.3 2.5 %collective-permute-start.8 = (bf16[1024,512]{1,0:T(8,128)(2,1)S(1)}, bf16[1024,512]{1,0:T(8,128)(2,1)S(1)}, u32[]{:S(2)}, u32[]{:S(2)}) collective-permute-start(bf16[1024,512]{1,0:T(8,128)(2,1)S(1)} %get-tuple-element.44.refs_0_), channel_id=1, source_target_pairs={{0,16},{16,0},{1,17},{17,1},{2,18},{18,2},{3,19},{19,3},{4,20},{20... | collective-permute-start | bytes 3145736 | tf_op jit(solution)/shard_map/ppermute | solution.py:532
  103.9 2.8 %collective-permute-done.23.refs_6_ = bf16[256,512]{1,0:T(8,128)(2,1)S(1)} collective-permute-done((bf16[256,512]{1,0:T(8,128)(2,1)S(1)}, bf16[256,512]{1,0:T(8,128)(2,1)S(1)}, u32[]{:S(2)}, u32[]{:S(2)}) %collective-permute-start.23) | collective-permute-done | bytes 262176 | tf_op jit(solution)/shard_map/ppermute | solution.py:477
  106.7 5.4 %project.3 = (bf16[512,512]{1,0:T(8,128)(2,1)S(1)}, bf16[1024,512]{1,0:T(8,128)(2,1)}) custom-call(s32[4]{0:T(128)S(1)} %pad_add_fusion.blocks_ref, bf16[1536,2048]{1,0:T(8,128)(2,1)S(1)} %bitcast.9, f32[2048,128]{1,0:T(8,128)S(1)} %broadcast_in_dim.42.gains_ref, bf16[256,512]{1,0:T(8,128)(2,1)S(1)} %broadcast_select_fusion.1.refs_0_, ...), custom_call_target="tpu_custom_call" | custom-call | flops 3221225472 | bytes 9961472 | tf_op jit(solution)/shard_map/project/pallas_call | solution.py:261
  112.0 2.5 %collective-permute-start.25 = (bf16[1024,512]{1,0:T(8,128)(2,1)}, bf16[1024,512]{1,0:T(8,128)(2,1)}, u32[]{:S(2)}, u32[]{:S(2)}) collective-permute-start(bf16[1024,512]{1,0:T(8,128)(2,1)} %get-tuple-element.62.refs_2_), channel_id=1, source_target_pairs={{0,16},{16,0},{1,17},{17,1},{2,18},{18,2},{3,19},{19,3},{4,20},{20... | collective-permute-start | bytes 3145736 | tf_op jit(solution)/shard_map/ppermute | solution.py:537
  114.5 1.5 prepare.1.refs_2_.refs_3_
  116.1 11.8 %collective-permute-done.8.refs_1_ = bf16[1024,512]{1,0:T(8,128)(2,1)S(1)} collective-permute-done((bf16[1024,512]{1,0:T(8,128)(2,1)S(1)}, bf16[1024,512]{1,0:T(8,128)(2,1)S(1)}, u32[]{:S(2)}, u32[]{:S(2)}) %collective-permute-start.8) | collective-permute-done | bytes 1048608 | tf_op jit(solution)/shard_map/ppermute | solution.py:532
  127.9 6.9 %attend.3 = (bf16[256,512]{1,0:T(8,128)(2,1)S(1)}, bf16[256,512]{1,0:T(8,128)(2,1)S(1)}, bf16[256,512]{1,0:T(8,128)(2,1)S(1)}, bf16[256,512]{1,0:T(8,128)(2,1)S(...) custom-call(s32[1]{0:T(128)} %bitcast.seq_ref, ...), custom_call_target="tpu_custom_call" | custom-call | flops 1073741824 | bytes 3145728 | tf_op jit(solution)/shard_map/attend/pallas_call | solution.py:401
  139.0 2.5 %collective-permute-start.12 = (bf16[256,512]{1,0:T(8,128)(2,1)}, bf16[256,512]{1,0:T(8,128)(2,1)}, u32[]{:S(2)}, u32[]{:S(2)}) collective-permute-start(bf16[256,512]{1,0:T(8,128)(2,1)} %get-tuple-element.51), channel_id=1, source_target_pairs={{0,4},{4,12},{12,8},{8,0},{1,5},{5,13},{13,9},{9,1},{2,6},{6,14},{... | collective-permute-start | bytes 786440 | tf_op jit(solution)/shard_map/ppermute | solution.py:488
  143.9 7.3 %attend.4 = (f32[4,2,512]{2,1,0:T(2,128)S(1)}, f32[512,512]{1,0:T(8,128)S(1)}) custom-call(s32[1]{0:T(128)} %bitcast.seq_ref, s32[16]{0:T(128)S(1)} %copy-done.23, s32[16,16]{1,0:T(8,128)S(1)} %copy-done.21, bf16[512,512]{1,0:T(8,128)(2,1)S(1)} %copy-done.8, bf16[1024,512]{1,0:T(8,128)(2,1)S(1)} %get-tuple-element.44.refs_0_, ...), custom_call_target="tpu_custom_call" | custom-call | flops 1610612736 | bytes 4194304 | tf_op jit(solution)/shard_map/attend/pallas_call | solution.py:401
  151.2 5.7 %attend.5 = (bf16[256,512]{1,0:T(8,128)(2,1)S(1)}, bf16[256,512]{1,0:T(8,128)(2,1)S(1)}, bf16[256,512]{1,0:T(8,128)(2,1)S(1)}, bf16[256,512]{1,0:T(8,128)(2,1)S(...) custom-call(s32[1]{0:T(128)} %bitcast.seq_ref, ...), custom_call_target="tpu_custom_call" | custom-call | flops 536870912 | bytes 2097152 | tf_op jit(solution)/shard_map/attend/pallas_call | solution.py:401
  156.9 2.1 collective-permute-start.29
  160.1 2.3 %collective-permute-start.13 = (bf16[256,512]{1,0:T(8,128)(2,1)S(1)}, bf16[256,512]{1,0:T(8,128)(2,1)S(1)}, u32[]{:S(2)}, u32[]{:S(2)}) collective-permute-start(bf16[256,512]{1,0:T(8,128)(2,1)S(1)} %get-tuple-element.77), channel_id=1, source_target_pairs={{4,0},{8,4},{12,8},{0,12},{5,1},{9,5},{13,9},{1,13},{6,2},{10,6},{... | collective-permute-start | bytes 786440 | tf_op jit(solution)/shard_map/ppermute | solution.py:489
  162.6 3.8 %collective-permute-start.10 = (bf16[256,512]{1,0:T(8,128)(2,1)S(1)}, bf16[256,512]{1,0:T(8,128)(2,1)S(1)}, u32[]{:S(2)}, u32[]{:S(2)}) collective-permute-start(bf16[256,512]{1,0:T(8,128)(2,1)S(1)} %get-tuple-element.79), channel_id=1, source_target_pairs={{4,0},{8,4},{12,8},{0,12},{5,1},{9,5},{13,9},{1,13},{6,2},{10,6},{... | collective-permute-start | bytes 786440 | tf_op jit(solution)/shard_map/ppermute | solution.py:489
  166.4 3.4 %collective-permute-done.29.refs_9_ = bf16[256,512]{1,0:T(8,128)(2,1)S(1)} collective-permute-done((bf16[256,512]{1,0:T(8,128)(2,1)S(1)}, bf16[256,512]{1,0:T(8,128)(2,1)S(1)}, u32[]{:S(2)}, u32[]{:S(2)}) %collective-permute-start.29) | collective-permute-done | bytes 262176 | tf_op jit(solution)/shard_map/ppermute | solution.py:488
  170.0 16.7 %collective-permute-done.26.refs_5_ = bf16[256,512]{1,0:T(8,128)(2,1)S(1)} collective-permute-done((bf16[256,512]{1,0:T(8,128)(2,1)S(1)}, bf16[256,512]{1,0:T(8,128)(2,1)S(1)}, u32[]{:S(2)}, u32[]{:S(2)}) %collective-permute-start.26) | collective-permute-done | bytes 262176 | tf_op jit(solution)/shard_map/ppermute | solution.py:488
  186.9 2.1 collective-permute-start.31
  188.9 1.8 collective-permute-start.27
  190.8 7.8 %collective-permute-start.28 = (bf16[256,512]{1,0:T(8,128)(2,1)S(1)}, bf16[256,512]{1,0:T(8,128)(2,1)S(1)}, u32[]{:S(2)}, u32[]{:S(2)}) collective-permute-start(bf16[256,512]{1,0:T(8,128)(2,1)S(1)} %get-tuple-element.75), channel_id=1, source_target_pairs={{0,4},{4,8},{8,12},{12,0},{1,5},{5,9},{9,13},{13,1},{2,6},{6,10},{... | collective-permute-start | bytes 786440 | tf_op jit(solution)/shard_map/ppermute | solution.py:490
  199.8 1.9 collective-permute-done.30.refs_7_
  201.6 5.7 %collective-permute-done.31.refs_8_ = bf16[256,512]{1,0:T(8,128)(2,1)S(1)} collective-permute-done((bf16[256,512]{1,0:T(8,128)(2,1)S(1)}, bf16[256,512]{1,0:T(8,128)(2,1)S(1)}, u32[]{:S(2)}, u32[]{:S(2)}) %collective-permute-start.31) | collective-permute-done | bytes 262176 | tf_op jit(solution)/shard_map/ppermute | solution.py:490
  207.4 5.9 %collective-permute-done.27.refs_3_ = bf16[256,512]{1,0:T(8,128)(2,1)S(1)} collective-permute-done((bf16[256,512]{1,0:T(8,128)(2,1)S(1)}, bf16[256,512]{1,0:T(8,128)(2,1)S(1)}, u32[]{:S(2)}, u32[]{:S(2)}) %collective-permute-start.27) | collective-permute-done | bytes 262176 | tf_op jit(solution)/shard_map/ppermute | solution.py:489
  213.3 2.2 %place.1 = bf16[512,1024]{1,0:T(8,128)(2,1)} custom-call(s32[1]{0:T(128)} %bitcast.seq_ref, s32[16]{0:T(128)S(1)} %copy-done.23, s32[1]{0:T(128)} %bitcast.1.ends_ref, bf16[256,512]{1,0:T(8,128)(2,1)S(1)} %fusion.13.refs_0_, bf16[256,512]{1,0:T(8,128)(2,1)S(1)} %fusion.19.refs_1_, bf16[256,512]{1,0:T(8,128)(2,1)S(1)} %get-tuple-element.65.refs_2_, ...), custom_call_target="tpu_custom_call" | custom-call | flops 1048576 | bytes 3670016 | tf_op jit(solution)/shard_map/place/pallas_call | solution.py:453
  (97 shorter events, 17.4 us)
Async XLA Ops:
  0.0 30.9 %copy-start.23 = (s32[16]{0:T(128)S(1)}, s32[16]{0:T(128)}, u32[]{:S(2)}) copy-start(s32[16]{0:T(128)} %order_ref.15) | copy-start | bytes 196
  1.5 29.4 %copy-start.2 = (f32[27,512]{1,0:T(8,128)S(1)}, f32[27,512]{1,0:T(8,128)}, u32[]{:S(2)}) copy-start(f32[27,512]{1,0:T(8,128)} %taps_ref.7) | copy-start | bytes 165892
  7.8 13.4 %copy-start.12 = (bf16[256,512]{1,0:T(8,128)(2,1)}, bf16[256,512]{1,0:T(8,128)(2,1)S(1)}, u32[]{:S(2)}) copy-start(bf16[256,512]{1,0:T(8,128)(2,1)S(1)} %get-tuple-element.41) | copy-start | bytes 786436
  7.8 23.0 %copy-start.4 = (f32[256,1024]{1,0:T(8,128)S(1)}, f32[256,1024]{1,0:T(8,128)}, u32[]{:S(2)}) copy-start(f32[256,1024]{1,0:T(8,128)} %get-tuple-element.58.part_ref) | copy-start | bytes 3145732
  7.8 17.5 %collective-permute-start.1 = (bf16[256,512]{1,0:T(8,128)(2,1)S(1)}, bf16[256,512]{1,0:T(8,128)(2,1)}, u32[]{:S(2)}, u32[]{:S(2)}) collective-permute-start(bf16[256,512]{1,0:T(8,128)(2,1)S(1)} %get-tuple-element.42), channel_id=1, source_target_pairs={{0,16},{1,17},{2,18},{3,19},{4,20},{5,21},{6,22},{7,23},{8,24},{9,... | collective-permute-start | bytes 786440 | tf_op jit(solution)/shard_map/ppermute | solution.py:515
  13.6 17.3 %collective-permute-start.17 = (bf16[256,1024]{1,0:T(8,128)(2,1)}, bf16[256,1024]{1,0:T(8,128)(2,1)S(1)}, u32[]{:S(2)}, u32[]{:S(2)}) collective-permute-start(bf16[256,1024]{1,0:T(8,128)(2,1)} %get-tuple-element.57), channel_id=1, source_target_pairs={{0,16},{1,17},{2,18},{3,19},{4,20},{5,21},{6,22},{7,23},{8,24},{9,... | collective-permute-start | bytes 1572872 | tf_op jit(solution)/shard_map/ppermute | solution.py:517
  21.9 29.5 %copy-start.3 = (f32[256,1024]{1,0:T(8,128)S(1)}, f32[256,1024]{1,0:T(8,128)}, u32[]{:S(2)}) copy-start(f32[256,1024]{1,0:T(8,128)} %get-tuple-element.54.part_ref) | copy-start | bytes 3145732
  21.9 27.3 %collective-permute-start.15 = (bf16[256,1024]{1,0:T(8,128)(2,1)}, bf16[256,1024]{1,0:T(8,128)(2,1)S(1)}, u32[]{:S(2)}, u32[]{:S(2)}) collective-permute-start(bf16[256,1024]{1,0:T(8,128)(2,1)} %get-tuple-element.53), channel_id=1, source_target_pairs={{0,16},{1,17},{2,18},{3,19},{4,20},{5,21},{6,22},{7,23},{8,24},{9,... | collective-permute-start | bytes 1572872 | tf_op jit(solution)/shard_map/ppermute | solution.py:517
  23.4 23.2 %collective-permute-start = (bf16[256,512]{1,0:T(8,128)(2,1)}, bf16[256,512]{1,0:T(8,128)(2,1)}, u32[]{:S(2)}, u32[]{:S(2)}) collective-permute-start(bf16[256,512]{1,0:T(8,128)(2,1)} %get-tuple-element.40), channel_id=1, source_target_pairs={{0,16},{1,17},{2,18},{3,19},{4,20},{5,21},{6,22},{7,23},{8,24},{9,... | collective-permute-start | bytes 786440 | tf_op jit(solution)/shard_map/ppermute | solution.py:515
  26.4 29.1 %collective-permute-start.3 = (bf16[256,512]{1,0:T(8,128)(2,1)S(1)}, bf16[256,512]{1,0:T(8,128)(2,1)}, u32[]{:S(2)}, u32[]{:S(2)}) collective-permute-start(bf16[256,512]{1,0:T(8,128)(2,1)S(1)} %broadcast_select_fusion.2.refs_1_), channel_id=1, source_target_pairs={{0,4},{4,8},{8,12},{12,0},{1,5},{5,9},{9,13},{13,1},{2,6},{6,10},{... | collective-permute-start | bytes 786440 | tf_op jit(solution)/shard_map/ppermute | solution.py:474
  28.0 28.8 %collective-permute-start.5 = (bf16[256,512]{1,0:T(8,128)(2,1)S(1)}, bf16[256,512]{1,0:T(8,128)(2,1)}, u32[]{:S(2)}, u32[]{:S(2)}) collective-permute-start(bf16[256,512]{1,0:T(8,128)(2,1)S(1)} %broadcast_select_fusion.2.refs_1_), channel_id=1, source_target_pairs={{4,0},{8,4},{12,8},{0,12},{5,1},{9,5},{13,9},{1,13},{6,2},{10,6},{... | collective-permute-start | bytes 786440 | tf_op jit(solution)/shard_map/ppermute | solution.py:475
  34.8 23.9 %collective-permute-start.18 = (bf16[256,512]{1,0:T(8,128)(2,1)S(1)}, bf16[256,512]{1,0:T(8,128)(2,1)S(1)}, u32[]{:S(2)}, u32[]{:S(2)}) collective-permute-start(bf16[256,512]{1,0:T(8,128)(2,1)S(1)} %get-tuple-element.60), channel_id=1, source_target_pairs={{16,0},{17,1},{18,2},{19,3},{20,4},{21,5},{22,6},{23,7},{24,8},{25... | collective-permute-start | bytes 786440 | tf_op jit(solution)/shard_map/ppermute | solution.py:527
  47.6 18.4 %collective-permute-start.2 = (bf16[256,512]{1,0:T(8,128)(2,1)S(1)}, bf16[256,512]{1,0:T(8,128)(2,1)S(1)}, u32[]{:S(2)}, u32[]{:S(2)}) collective-permute-start(bf16[256,512]{1,0:T(8,128)(2,1)S(1)} %broadcast_select_fusion.3.refs_0_), channel_id=1, source_target_pairs={{0,4},{4,8},{8,12},{12,0},{1,5},{5,9},{9,13},{13,1},{2,6},{6,10},{... | collective-permute-start | bytes 786440 | tf_op jit(solution)/shard_map/ppermute | solution.py:474
  49.2 17.1 %collective-permute-start.4 = (bf16[256,512]{1,0:T(8,128)(2,1)S(1)}, bf16[256,512]{1,0:T(8,128)(2,1)S(1)}, u32[]{:S(2)}, u32[]{:S(2)}) collective-permute-start(bf16[256,512]{1,0:T(8,128)(2,1)S(1)} %broadcast_select_fusion.3.refs_0_), channel_id=1, source_target_pairs={{4,0},{8,4},{12,8},{0,12},{5,1},{9,5},{13,9},{1,13},{6,2},{10,6},{... | collective-permute-start | bytes 786440 | tf_op jit(solution)/shard_map/ppermute | solution.py:475
  55.4 8.8 %collective-permute-start.16 = (bf16[256,512]{1,0:T(8,128)(2,1)S(1)}, bf16[256,512]{1,0:T(8,128)(2,1)S(1)}, u32[]{:S(2)}, u32[]{:S(2)}) collective-permute-start(bf16[256,512]{1,0:T(8,128)(2,1)S(1)} %get-tuple-element.56), channel_id=1, source_target_pairs={{16,0},{17,1},{18,2},{19,3},{20,4},{21,5},{22,6},{23,7},{24,8},{25... | collective-permute-start | bytes 786440 | tf_op jit(solution)/shard_map/ppermute | solution.py:527
  56.7 39.4 %copy-start.26 = (f32[2048]{0:T(1024)S(1)}, f32[2048]{0:T(1024)}, u32[]{:S(2)}) copy-start(f32[2048]{0:T(1024)} %param.9) | copy-start | bytes 24580
  56.8 39.7 %copy-start.24 = (bf16[3,512,2048]{2,1,0:T(8,128)(2,1)S(1)}, bf16[3,512,2048]{2,1,0:T(8,128)(2,1)}, u32[]{:S(2)}) copy-start(bf16[3,512,2048]{2,1,0:T(8,128)(2,1)} %param.10) | copy-start | bytes 18874372
  56.8 36.4 %collective-permute-start.7 = (bf16[256,512]{1,0:T(8,128)(2,1)S(1)}, bf16[256,512]{1,0:T(8,128)(2,1)S(1)}, u32[]{:S(2)}, u32[]{:S(2)}) collective-permute-start(bf16[256,512]{1,0:T(8,128)(2,1)S(1)} %select_select_fusion.2), channel_id=1, source_target_pairs={{4,0},{12,4},{8,12},{0,8},{5,1},{13,5},{9,13},{1,9},{6,2},{14,6},{... | collective-permute-start | bytes 786440 | tf_op jit(solution)/shard_map/ppermute | solution.py:477
  58.8 16.7 %collective-permute-start.20 = (bf16[256,512]{1,0:T(8,128)(2,1)S(1)}, bf16[256,512]{1,0:T(8,128)(2,1)S(1)}, u32[]{:S(2)}, u32[]{:S(2)}) collective-permute-start(bf16[256,512]{1,0:T(8,128)(2,1)S(1)} %broadcast_select_fusion.refs_1_), channel_id=1, source_target_pairs={{0,4},{4,8},{8,12},{12,0},{1,5},{5,9},{9,13},{13,1},{2,6},{6,10},{... | collective-permute-start | bytes 786440 | tf_op jit(solution)/shard_map/ppermute | solution.py:474
  64.2 17.0 %collective-permute-start.22 = (bf16[256,512]{1,0:T(8,128)(2,1)S(1)}, bf16[256,512]{1,0:T(8,128)(2,1)S(1)}, u32[]{:S(2)}, u32[]{:S(2)}) collective-permute-start(bf16[256,512]{1,0:T(8,128)(2,1)S(1)} %broadcast_select_fusion.refs_1_), channel_id=1, source_target_pairs={{4,0},{8,4},{12,8},{0,12},{5,1},{9,5},{13,9},{1,13},{6,2},{10,6},{... | collective-permute-start | bytes 786440 | tf_op jit(solution)/shard_map/ppermute | solution.py:475
  65.9 20.9 %collective-permute-start.19 = (bf16[256,512]{1,0:T(8,128)(2,1)S(1)}, bf16[256,512]{1,0:T(8,128)(2,1)S(1)}, u32[]{:S(2)}, u32[]{:S(2)}) collective-permute-start(bf16[256,512]{1,0:T(8,128)(2,1)S(1)} %broadcast_select_fusion.1.refs_0_), channel_id=1, source_target_pairs={{0,4},{4,8},{8,12},{12,0},{1,5},{5,9},{9,13},{13,1},{2,6},{6,10},{... | collective-permute-start | bytes 786440 | tf_op jit(solution)/shard_map/ppermute | solution.py:474
  66.3 24.1 %collective-permute-start.21 = (bf16[256,512]{1,0:T(8,128)(2,1)S(1)}, bf16[256,512]{1,0:T(8,128)(2,1)S(1)}, u32[]{:S(2)}, u32[]{:S(2)}) collective-permute-start(bf16[256,512]{1,0:T(8,128)(2,1)S(1)} %broadcast_select_fusion.1.refs_0_), channel_id=1, source_target_pairs={{4,0},{8,4},{12,8},{0,12},{5,1},{9,5},{13,9},{1,13},{6,2},{10,6},{... | collective-permute-start | bytes 786440 | tf_op jit(solution)/shard_map/ppermute | solution.py:475
  75.5 20.6 %collective-permute-start.6 = (bf16[256,512]{1,0:T(8,128)(2,1)S(1)}, bf16[256,512]{1,0:T(8,128)(2,1)S(1)}, u32[]{:S(2)}, u32[]{:S(2)}) collective-permute-start(bf16[256,512]{1,0:T(8,128)(2,1)S(1)} %select_select_fusion.3), channel_id=1, source_target_pairs={{4,0},{12,4},{8,12},{0,8},{5,1},{13,5},{9,13},{1,9},{6,2},{14,6},{... | collective-permute-start | bytes 786440 | tf_op jit(solution)/shard_map/ppermute | solution.py:477
  81.2 22.7 %collective-permute-start.24 = (bf16[256,512]{1,0:T(8,128)(2,1)S(1)}, bf16[256,512]{1,0:T(8,128)(2,1)S(1)}, u32[]{:S(2)}, u32[]{:S(2)}) collective-permute-start(bf16[256,512]{1,0:T(8,128)(2,1)S(1)} %select_select_fusion), channel_id=1, source_target_pairs={{4,0},{12,4},{8,12},{0,8},{5,1},{13,5},{9,13},{1,9},{6,2},{14,6},{... | collective-permute-start | bytes 786440 | tf_op jit(solution)/shard_map/ppermute | solution.py:477
  90.5 16.2 %collective-permute-start.23 = (bf16[256,512]{1,0:T(8,128)(2,1)S(1)}, bf16[256,512]{1,0:T(8,128)(2,1)S(1)}, u32[]{:S(2)}, u32[]{:S(2)}) collective-permute-start(bf16[256,512]{1,0:T(8,128)(2,1)S(1)} %select_select_fusion.1), channel_id=1, source_target_pairs={{4,0},{12,4},{8,12},{0,8},{5,1},{13,5},{9,13},{1,9},{6,2},{14,6},{... | collective-permute-start | bytes 786440 | tf_op jit(solution)/shard_map/ppermute | solution.py:477
  101.3 13.2 %copy-start = (bf16[512,2048]{1,0:T(8,128)(2,1)S(1)}, bf16[512,2048]{1,0:T(8,128)(2,1)}, u32[]{:S(2)}) copy-start(bf16[512,2048]{1,0:T(8,128)(2,1)} %out_ref.1) | copy-start | bytes 6291460
  101.3 26.6 %collective-permute-start.8 = (bf16[1024,512]{1,0:T(8,128)(2,1)S(1)}, bf16[1024,512]{1,0:T(8,128)(2,1)S(1)}, u32[]{:S(2)}, u32[]{:S(2)}) collective-permute-start(bf16[1024,512]{1,0:T(8,128)(2,1)S(1)} %get-tuple-element.44.refs_0_), channel_id=1, source_target_pairs={{0,16},{16,0},{1,17},{17,1},{2,18},{18,2},{3,19},{19,3},{4,20},{20... | collective-permute-start | bytes 3145736 | tf_op jit(solution)/shard_map/ppermute | solution.py:532
  112.0 4.0 %copy-start.7 = (bf16[512,512]{1,0:T(8,128)(2,1)}, bf16[512,512]{1,0:T(8,128)(2,1)S(1)}, u32[]{:S(2)}) copy-start(bf16[512,512]{1,0:T(8,128)(2,1)S(1)} %get-tuple-element.61.query_ref) | copy-start | bytes 1572868
  112.0 15.9 %copy-start.21 = (s32[16,16]{1,0:T(8,128)S(1)}, s32[16,16]{1,0:T(8,128)}, u32[]{:S(2)}) copy-start(s32[16,16]{1,0:T(8,128)} %mask_ref.5) | copy-start | bytes 3076
  112.0 39.2 %collective-permute-start.25 = (bf16[1024,512]{1,0:T(8,128)(2,1)}, bf16[1024,512]{1,0:T(8,128)(2,1)}, u32[]{:S(2)}, u32[]{:S(2)}) collective-permute-start(bf16[1024,512]{1,0:T(8,128)(2,1)} %get-tuple-element.62.refs_2_), channel_id=1, source_target_pairs={{0,16},{16,0},{1,17},{17,1},{2,18},{18,2},{3,19},{19,3},{4,20},{20... | collective-permute-start | bytes 3145736 | tf_op jit(solution)/shard_map/ppermute | solution.py:537
  127.9 6.9 %copy-start.5 = (bf16[1024,512]{1,0:T(8,128)(2,1)}, bf16[1024,512]{1,0:T(8,128)(2,1)S(1)}, u32[]{:S(2)}) copy-start(bf16[1024,512]{1,0:T(8,128)(2,1)S(1)} %collective-permute-done.8.refs_1_) | copy-start | bytes 3145732
  139.0 20.0 %collective-permute-start.12 = (bf16[256,512]{1,0:T(8,128)(2,1)}, bf16[256,512]{1,0:T(8,128)(2,1)}, u32[]{:S(2)}, u32[]{:S(2)}) collective-permute-start(bf16[256,512]{1,0:T(8,128)(2,1)} %get-tuple-element.51), channel_id=1, source_target_pairs={{0,4},{4,12},{12,8},{8,0},{1,5},{5,13},{13,9},{9,1},{2,6},{6,14},{... | collective-permute-start | bytes 786440 | tf_op jit(solution)/shard_map/ppermute | solution.py:488
  141.5 20.9 %collective-permute-start.9 = (bf16[256,512]{1,0:T(8,128)(2,1)}, bf16[256,512]{1,0:T(8,128)(2,1)S(1)}, u32[]{:S(2)}, u32[]{:S(2)}) collective-permute-start(bf16[256,512]{1,0:T(8,128)(2,1)} %copy-done.25), channel_id=1, source_target_pairs={{0,4},{4,12},{12,8},{8,0},{1,5},{5,13},{13,9},{9,1},{2,6},{6,14},{... | collective-permute-start | bytes 786440 | tf_op jit(solution)/shard_map/ppermute | solution.py:488
  151.2 7.8 %copy-start.18 = (bf16[256,512]{1,0:T(8,128)(2,1)S(1)}, bf16[256,512]{1,0:T(8,128)(2,1)}, u32[]{:S(2)}) copy-start(bf16[256,512]{1,0:T(8,128)(2,1)} %copy-done.17) | copy-start | bytes 786436
  151.2 7.8 %copy-start.20 = (bf16[256,512]{1,0:T(8,128)(2,1)S(1)}, bf16[256,512]{1,0:T(8,128)(2,1)}, u32[]{:S(2)}) copy-start(bf16[256,512]{1,0:T(8,128)(2,1)} %copy-done.19) | copy-start | bytes 786436
  151.2 11.3 %copy-start.14 = (bf16[256,512]{1,0:T(8,128)(2,1)S(1)}, bf16[256,512]{1,0:T(8,128)(2,1)}, u32[]{:S(2)}) copy-start(bf16[256,512]{1,0:T(8,128)(2,1)} %copy-done.13) | copy-start | bytes 786436
  151.2 11.3 %copy-start.16 = (bf16[256,512]{1,0:T(8,128)(2,1)S(1)}, bf16[256,512]{1,0:T(8,128)(2,1)}, u32[]{:S(2)}) copy-start(bf16[256,512]{1,0:T(8,128)(2,1)} %copy-done.15) | copy-start | bytes 786436
  156.9 12.9 %collective-permute-start.29 = (bf16[256,512]{1,0:T(8,128)(2,1)S(1)}, bf16[256,512]{1,0:T(8,128)(2,1)S(1)}, u32[]{:S(2)}, u32[]{:S(2)}) collective-permute-start(bf16[256,512]{1,0:T(8,128)(2,1)S(1)} %get-tuple-element.71), channel_id=1, source_target_pairs={{0,4},{4,12},{12,8},{8,0},{1,5},{5,13},{13,9},{9,1},{2,6},{6,14},{... | collective-permute-start | bytes 786440 | tf_op jit(solution)/shard_map/ppermute | solution.py:488
  160.1 38.4 %copy-start.10 = (bf16[256,512]{1,0:T(8,128)(2,1)S(1)}, bf16[256,512]{1,0:T(8,128)(2,1)}, u32[]{:S(2)}) copy-start(bf16[256,512]{1,0:T(8,128)(2,1)} %copy-done.9) | copy-start | bytes 786436
  160.1 26.8 %collective-permute-start.13 = (bf16[256,512]{1,0:T(8,128)(2,1)S(1)}, bf16[256,512]{1,0:T(8,128)(2,1)S(1)}, u32[]{:S(2)}, u32[]{:S(2)}) collective-permute-start(bf16[256,512]{1,0:T(8,128)(2,1)S(1)} %get-tuple-element.77), channel_id=1, source_target_pairs={{4,0},{8,4},{12,8},{0,12},{5,1},{9,5},{13,9},{1,13},{6,2},{10,6},{... | collective-permute-start | bytes 786440 | tf_op jit(solution)/shard_map/ppermute | solution.py:489
  162.4 26.5 %collective-permute-start.14 = (bf16[256,512]{1,0:T(8,128)(2,1)S(1)}, bf16[256,512]{1,0:T(8,128)(2,1)S(1)}, u32[]{:S(2)}, u32[]{:S(2)}) collective-permute-start(bf16[256,512]{1,0:T(8,128)(2,1)S(1)} %get-tuple-element.78), channel_id=1, source_target_pairs={{0,4},{4,8},{8,12},{12,0},{1,5},{5,9},{9,13},{13,1},{2,6},{6,10},{... | collective-permute-start | bytes 786440 | tf_op jit(solution)/shard_map/ppermute | solution.py:490
  162.4 24.3 %collective-permute-start.26 = (bf16[256,512]{1,0:T(8,128)(2,1)S(1)}, bf16[256,512]{1,0:T(8,128)(2,1)S(1)}, u32[]{:S(2)}, u32[]{:S(2)}) collective-permute-start(bf16[256,512]{1,0:T(8,128)(2,1)S(1)} %get-tuple-element.67), channel_id=1, source_target_pairs={{0,4},{4,12},{12,8},{8,0},{1,5},{5,13},{13,9},{9,1},{2,6},{6,14},{... | collective-permute-start | bytes 786440 | tf_op jit(solution)/shard_map/ppermute | solution.py:488
  162.6 28.1 %collective-permute-start.10 = (bf16[256,512]{1,0:T(8,128)(2,1)S(1)}, bf16[256,512]{1,0:T(8,128)(2,1)S(1)}, u32[]{:S(2)}, u32[]{:S(2)}) collective-permute-start(bf16[256,512]{1,0:T(8,128)(2,1)S(1)} %get-tuple-element.79), channel_id=1, source_target_pairs={{4,0},{8,4},{12,8},{0,12},{5,1},{9,5},{13,9},{1,13},{6,2},{10,6},{... | collective-permute-start | bytes 786440 | tf_op jit(solution)/shard_map/ppermute | solution.py:489
  169.9 29.8 %collective-permute-start.11 = (bf16[256,512]{1,0:T(8,128)(2,1)S(1)}, bf16[256,512]{1,0:T(8,128)(2,1)S(1)}, u32[]{:S(2)}, u32[]{:S(2)}) collective-permute-start(bf16[256,512]{1,0:T(8,128)(2,1)S(1)} %get-tuple-element.80), channel_id=1, source_target_pairs={{0,4},{4,8},{8,12},{12,0},{1,5},{5,9},{9,13},{13,1},{2,6},{6,10},{... | collective-permute-start | bytes 786440 | tf_op jit(solution)/shard_map/ppermute | solution.py:490
  186.7 14.9 %collective-permute-start.30 = (bf16[256,512]{1,0:T(8,128)(2,1)S(1)}, bf16[256,512]{1,0:T(8,128)(2,1)S(1)}, u32[]{:S(2)}, u32[]{:S(2)}) collective-permute-start(bf16[256,512]{1,0:T(8,128)(2,1)S(1)} %get-tuple-element.74), channel_id=1, source_target_pairs={{4,0},{8,4},{12,8},{0,12},{5,1},{9,5},{13,9},{1,13},{6,2},{10,6},{... | collective-permute-start | bytes 786440 | tf_op jit(solution)/shard_map/ppermute | solution.py:489
  186.9 20.5 %collective-permute-start.31 = (bf16[256,512]{1,0:T(8,128)(2,1)S(1)}, bf16[256,512]{1,0:T(8,128)(2,1)S(1)}, u32[]{:S(2)}, u32[]{:S(2)}) collective-permute-start(bf16[256,512]{1,0:T(8,128)(2,1)S(1)} %get-tuple-element.73), channel_id=1, source_target_pairs={{0,4},{4,8},{8,12},{12,0},{1,5},{5,9},{9,13},{13,1},{2,6},{6,10},{... | collective-permute-start | bytes 786440 | tf_op jit(solution)/shard_map/ppermute | solution.py:490
  188.9 24.3 %collective-permute-start.27 = (bf16[256,512]{1,0:T(8,128)(2,1)S(1)}, bf16[256,512]{1,0:T(8,128)(2,1)S(1)}, u32[]{:S(2)}, u32[]{:S(2)}) collective-permute-start(bf16[256,512]{1,0:T(8,128)(2,1)S(1)} %get-tuple-element.76), channel_id=1, source_target_pairs={{4,0},{8,4},{12,8},{0,12},{5,1},{9,5},{13,9},{1,13},{6,2},{10,6},{... | collective-permute-start | bytes 786440 | tf_op jit(solution)/shard_map/ppermute | solution.py:489
  190.8 22.5 %collective-permute-start.28 = (bf16[256,512]{1,0:T(8,128)(2,1)S(1)}, bf16[256,512]{1,0:T(8,128)(2,1)S(1)}, u32[]{:S(2)}, u32[]{:S(2)}) collective-permute-start(bf16[256,512]{1,0:T(8,128)(2,1)S(1)} %get-tuple-element.75), channel_id=1, source_target_pairs={{0,4},{4,8},{8,12},{12,0},{1,5},{5,9},{9,13},{13,1},{2,6},{6,10},{... | collective-permute-start | bytes 786440 | tf_op jit(solution)/shard_map/ppermute | solution.py:490
  (11 other events, 8.6 us)

commit v6 on v5

--- a/solution.py
+++ b/solution.py
@@ -23,6 +23,7 @@
 
 VMEM_LIMIT = 20 * 1024 * 1024
 VMEM_FIRST = 52 * 1024 * 1024
+VMEM_PROJECT = 55 * 1024 * 1024
 
 
 def vmem_spec():
@@ -227,8 +228,11 @@
     )(blocks, out_weight)
 
 
-def project_body(blocks_ref, weight_ref, gains_ref, *refs):
-    shards, (query_ref, pair_ref, tokens_ref) = refs[:-3], refs[-3:]
+def project_body(blocks_ref, weight_hbm, gains_ref, *refs):
+    shards, (query_ref, pair_ref, weight_ref, tokens_ref, arrived) = refs[:-5], refs[-5:]
+    copies = fetches(weight_hbm, weight_ref, arrived)
+    for copy in copies:
+        copy.start()
     width, tokens = shards[0].shape
     cols = query_ref.shape[0]
     lines = 128
@@ -243,8 +247,9 @@
             gain = jnp.concatenate([gains_ref[there, :]] * (tokens // 128), axis=1)
             tokens_ref[there, :] = (wide * gain).astype(jnp.bfloat16)
     inverse = lax.rsqrt(squares / (len(shards) * width) + EPSILON)
-    rows = 256
-    for index in range(weight_ref.shape[0] // rows):
+    rows = weight_ref.shape[0] // len(copies)
+    for index, copy in enumerate(copies):
+        copy.wait()
         here = slice(index * rows, (index + 1) * rows)
         total = jnp.dot(weight_ref[here, :], tokens_ref[...], preferred_element_type=jnp.float32)
         if index * rows < cols:
@@ -260,14 +265,18 @@
     cols = rows // 3
     return pl.pallas_call(
         project_body,
-        in_specs=[smem_spec()] + [vmem_spec()] * (2 + len(shards)),
+        in_specs=[smem_spec(), pl.BlockSpec(memory_space=pl.ANY)] + [vmem_spec()] * (1 + len(shards)),
         out_specs=[vmem_spec(), vmem_spec()],
-        scratch_shapes=[pltpu.VMEM((channels, tokens), jnp.bfloat16)],
+        scratch_shapes=[
+            pltpu.VMEM((rows, channels), jnp.bfloat16),
+            pltpu.VMEM((channels, tokens), jnp.bfloat16),
+            pltpu.SemaphoreType.DMA((6,)),
+        ],
         out_shape=[
             jax.ShapeDtypeStruct((cols, tokens), jnp.bfloat16),
             jax.ShapeDtypeStruct((2 * cols, tokens), jnp.bfloat16),
         ],
-        compiler_params=params(),
+        compiler_params=params(VMEM_PROJECT),
         cost_estimate=pl.CostEstimate(
             flops=2 * rows * channels * tokens,
             bytes_accessed=2 * (rows * channels + channels * tokens + rows * tokens),

time: 216 us -> 222 us (1.028)
  Pallas kernels: 54.3 us -> 61.1 us
  waiting for transfers between devices: 85.3 us -> 81.4 us
  local copies, waits for them, and re-layouts: 9.01 us -> 12 us
    pallas_call x2, Pallas kernels: 10.2 us -> 17.3 us  [project_call(): pl.pallas_call(project_body, in_specs=[smem_spec(), pl.BlockSpec(memory_s...]
    ppermute x4, waiting for transfers between devices: 5.61 us -> 2.83 us  [gather_blocks(): across = lax.ppermute(relay, 'tp', UNFOLDED)]
    ppermute x1, starting transfers between devices: 2.48 us -> 0.09 us  [per_device_fast(): peer_b = lax.ppermute(pair_b, 'seq', swap)]
    unnamed x54 -> x82, local copies, waits for them, and re-layouts: 8.69 us -> 10.7 us
  transfers between devices with their start and end apart: 32 -> 32, of which waited for: 15 -> 14; matrix products, arithmetic and copies ran while one was open for 2% -> 3% of each run, Pallas kernels for 21% -> 24%
where the time goes in v6:
time: 222 us
  waiting for transfers between devices  81.4 us (37%)
  Pallas kernels  61.1 us (28%)
  starting transfers between devices  60.2 us (27%)
  local copies, waits for them, and re-layouts  12 us (5%)
  other arithmetic  6.36 us (3%)
    pallas_call x4, Pallas kernels, conv_call(): pl.pallas_call(functools.partial(conv_body, with_before, piece * channels...  20.7 us
    ppermute x4, waiting for transfers between devices, reduce_blocks(): across = lax.ppermute(sent, 'tp', FOLDED)  20.2 us
    pallas_call x3, Pallas kernels, attend_call(): pl.pallas_call(functools.partial(attend_body, chunk, tuple((s for _, s in...  19.4 us
    pallas_call x2, Pallas kernels, project_call(): pl.pallas_call(project_body, in_specs=[smem_spec(), pl.BlockSpec(memory_s...  17.3 us
    ppermute x1, waiting for transfers between devices, per_device_fast(): peer_a = lax.ppermute(pair_a, 'seq', swap)  12.5 us
    unnamed x82, local copies, waits for them, and re-layouts  10.7 us
    ppermute x2, waiting for transfers between devices, per_device_fast(): got = lax.ppermute(send, 'seq', [(0, 1)])  10.4 us
    ppermute x4, waiting for transfers between devices, gather_blocks(): before = lax.ppermute(block, 'tp', FORWARD)  9.69 us
  transfers between devices with their start and end apart: 32, of which 14 were waited for; matrix products, arithmetic and copies ran while one was open for 3% of the time, Pallas kernels for 24%

profile of v6, /device:TPU:0, one launch (start us, length us, event | category | flops | bytes accessed | tf_op | source)
XLA Modules:
  0.0 221.7 jit_solution(17337340160091157128)
XLA Ops:
  1.5 6.4 %conv.5 = (f32[256,1024]{1,0:T(8,128)}, bf16[256,512]{1,0:T(8,128)(2,1)S(1)}, bf16[256,512]{1,0:T(8,128)(2,1)}, bf16[256,1024]{1,0:T(8,128)(2,1)}) custom-call(s32[1]{0:T(128)} %bitcast.seq_ref, s32[16]{0:T(128)S(1)} %copy-done.22, bf16[512,1024]{1,0:T(8,128)(2,1)} %tokens_ref.3, f32[27,512]{1,0:T(8,128)S(1)} %copy-done.1), custom_call_target="tpu_custom_call" | custom-call | flops 7077888 | bytes 2097152 | tf_op jit(solution)/shard_map/conv/pallas_call | solution.py:192
  7.9 5.7 %collective-permute-start.1 = (bf16[256,512]{1,0:T(8,128)(2,1)}, bf16[256,512]{1,0:T(8,128)(2,1)}, u32[]{:S(2)}, u32[]{:S(2)}) collective-permute-start(bf16[256,512]{1,0:T(8,128)(2,1)} %get-tuple-element.42), channel_id=1, source_target_pairs={{0,16},{1,17},{2,18},{3,19},{4,20},{5,21},{6,22},{7,23},{8,24},{9,... | collective-permute-start | bytes 786440 | tf_op jit(solution)/shard_map/ppermute | solution.py:524
  13.7 1.3 collective-permute-start.17
  15.0 6.3 %conv.4 = (f32[256,1024]{1,0:T(8,128)}, bf16[256,512]{1,0:T(8,128)(2,1)S(1)}, bf16[256,512]{1,0:T(8,128)(2,1)}, bf16[256,1024]{1,0:T(8,128)(2,1)}) custom-call(s32[1]{0:T(128)} %bitcast.seq_ref, s32[16]{0:T(128)S(1)} %copy-done.22, bf16[512,1024]{1,0:T(8,128)(2,1)} %tokens_ref.3, f32[27,512]{1,0:T(8,128)S(1)} %copy-done.1), custom_call_target="tpu_custom_call" | custom-call | flops 7077888 | bytes 2097152 | tf_op jit(solution)/shard_map/conv/pallas_call | solution.py:192
  21.4 1.5 collective-permute-start.15
  22.8 2.0 collective-permute-start
  24.8 1.7 broadcast_select_fusion.2.refs_1_
  26.5 1.6 collective-permute-start.3
  28.1 2.2 %collective-permute-start.5 = (bf16[256,512]{1,0:T(8,128)(2,1)}, bf16[256,512]{1,0:T(8,128)(2,1)}, u32[]{:S(2)}, u32[]{:S(2)}) collective-permute-start(bf16[256,512]{1,0:T(8,128)(2,1)} %broadcast_select_fusion.2.refs_1_), channel_id=1, source_target_pairs={{4,0},{8,4},{12,8},{0,12},{5,1},{9,5},{13,9},{1,13},{6,2},{10,6},{... | collective-permute-start | bytes 786440 | tf_op jit(solution)/shard_map/ppermute | solution.py:484
  31.2 4.0 %conv.7 = (bf16[256,512]{1,0:T(8,128)(2,1)S(1)}, bf16[256,512]{1,0:T(8,128)(2,1)S(1)}) custom-call(s32[1]{0:T(128)} %bitcast.seq_ref, s32[16]{0:T(128)S(1)} %copy-done.23, bf16[256,1024]{1,0:T(8,128)(2,1)S(1)} %collective-permute-done.17.tokens_ref, f32[27,512]{1,0:T(8,128)S(1)} %copy-done.2, f32[256,1024]{1,0:T(8,128)S(1)} %copy-done.4), custom_call_target="tpu_custom_call" | custom-call | flops 7077888 | bytes 2097152 | tf_op jit(solution)/shard_map/conv/pallas_call | solution.py:192
  35.2 1.3 collective-permute-start.18
  36.5 10.4 %collective-permute-done = bf16[256,512]{1,0:T(8,128)(2,1)} collective-permute-done((bf16[256,512]{1,0:T(8,128)(2,1)}, bf16[256,512]{1,0:T(8,128)(2,1)}, u32[]{:S(2)}, u32[]{:S(2)}) %collective-permute-start) | collective-permute-done | bytes 262176 | tf_op jit(solution)/shard_map/ppermute | solution.py:524
  46.9 1.6 collective-permute-start.2
  48.6 2.2 %collective-permute-start.4 = (bf16[256,512]{1,0:T(8,128)(2,1)S(1)}, bf16[256,512]{1,0:T(8,128)(2,1)S(1)}, u32[]{:S(2)}, u32[]{:S(2)}) collective-permute-start(bf16[256,512]{1,0:T(8,128)(2,1)S(1)} %broadcast_select_fusion.3.refs_0_), channel_id=1, source_target_pairs={{4,0},{8,4},{12,8},{0,12},{5,1},{9,5},{13,9},{1,13},{6,2},{10,6},{... | collective-permute-start | bytes 786440 | tf_op jit(solution)/shard_map/ppermute | solution.py:484
  50.8 4.0 %conv.6 = (bf16[256,512]{1,0:T(8,128)(2,1)S(1)}, bf16[256,512]{1,0:T(8,128)(2,1)S(1)}) custom-call(s32[1]{0:T(128)} %bitcast.seq_ref, s32[16]{0:T(128)S(1)} %copy-done.23, bf16[256,1024]{1,0:T(8,128)(2,1)S(1)} %collective-permute-done.15.tokens_ref, f32[27,512]{1,0:T(8,128)S(1)} %copy-done.2, f32[256,1024]{1,0:T(8,128)S(1)} %copy-done.3), custom_call_target="tpu_custom_call" | custom-call | flops 7077888 | bytes 2097152 | tf_op jit(solution)/shard_map/conv/pallas_call | solution.py:192
  54.8 1.3 collective-permute-start.16
  59.3 5.2 %collective-permute-done.16 = bf16[256,512]{1,0:T(8,128)(2,1)S(1)} collective-permute-done((bf16[256,512]{1,0:T(8,128)(2,1)S(1)}, bf16[256,512]{1,0:T(8,128)(2,1)S(1)}, u32[]{:S(2)}, u32[]{:S(2)}) %collective-permute-start.16) | collective-permute-done | bytes 262176 | tf_op jit(solution)/shard_map/ppermute | solution.py:536
  64.6 1.7 collective-permute-start.22
  66.7 3.5 %collective-permute-start.21 = (bf16[256,512]{1,0:T(8,128)(2,1)S(1)}, bf16[256,512]{1,0:T(8,128)(2,1)S(1)}, u32[]{:S(2)}, u32[]{:S(2)}) collective-permute-start(bf16[256,512]{1,0:T(8,128)(2,1)S(1)} %broadcast_select_fusion.1.refs_0_), channel_id=1, source_target_pairs={{4,0},{8,4},{12,8},{0,12},{5,1},{9,5},{13,9},{1,13},{6,2},{10,6},{... | collective-permute-start | bytes 786440 | tf_op jit(solution)/shard_map/ppermute | solution.py:484
  70.2 4.7 %collective-permute-done.20.refs_3_ = bf16[256,512]{1,0:T(8,128)(2,1)S(1)} collective-permute-done((bf16[256,512]{1,0:T(8,128)(2,1)S(1)}, bf16[256,512]{1,0:T(8,128)(2,1)S(1)}, u32[]{:S(2)}, u32[]{:S(2)}) %collective-permute-start.20) | collective-permute-done | bytes 262176 | tf_op jit(solution)/shard_map/ppermute | solution.py:483
  74.9 2.1 collective-permute-start.6
  77.0 3.5 %collective-permute-done.22.refs_5_ = bf16[256,512]{1,0:T(8,128)(2,1)S(1)} collective-permute-done((bf16[256,512]{1,0:T(8,128)(2,1)S(1)}, bf16[256,512]{1,0:T(8,128)(2,1)S(1)}, u32[]{:S(2)}, u32[]{:S(2)}) %collective-permute-start.22) | collective-permute-done | bytes 262176 | tf_op jit(solution)/shard_map/ppermute | solution.py:484
  81.2 5.0 %collective-permute-done.19.refs_2_ = bf16[256,512]{1,0:T(8,128)(2,1)S(1)} collective-permute-done((bf16[256,512]{1,0:T(8,128)(2,1)S(1)}, bf16[256,512]{1,0:T(8,128)(2,1)S(1)}, u32[]{:S(2)}, u32[]{:S(2)}) %collective-permute-start.19) | collective-permute-done | bytes 262176 | tf_op jit(solution)/shard_map/ppermute | solution.py:483
  86.2 3.7 %collective-permute-done.21.refs_4_ = bf16[256,512]{1,0:T(8,128)(2,1)S(1)} collective-permute-done((bf16[256,512]{1,0:T(8,128)(2,1)S(1)}, bf16[256,512]{1,0:T(8,128)(2,1)S(1)}, u32[]{:S(2)}, u32[]{:S(2)}) %collective-permute-start.21) | collective-permute-done | bytes 262176 | tf_op jit(solution)/shard_map/ppermute | solution.py:484
  89.9 2.7 %collective-permute-start.23 = (bf16[256,512]{1,0:T(8,128)(2,1)S(1)}, bf16[256,512]{1,0:T(8,128)(2,1)S(1)}, u32[]{:S(2)}, u32[]{:S(2)}) collective-permute-start(bf16[256,512]{1,0:T(8,128)(2,1)S(1)} %select_select_fusion.1), channel_id=1, source_target_pairs={{4,0},{12,4},{8,12},{0,8},{5,1},{13,5},{9,13},{1,9},{6,2},{14,6},{... | collective-permute-start | bytes 786440 | tf_op jit(solution)/shard_map/ppermute | solution.py:486
  92.7 2.8 %collective-permute-done.6.refs_6_ = bf16[256,512]{1,0:T(8,128)(2,1)S(1)} collective-permute-done((bf16[256,512]{1,0:T(8,128)(2,1)S(1)}, bf16[256,512]{1,0:T(8,128)(2,1)S(1)}, u32[]{:S(2)}, u32[]{:S(2)}) %collective-permute-start.6) | collective-permute-done | bytes 262176 | tf_op jit(solution)/shard_map/ppermute | solution.py:486
  95.5 1.3 broadcast_in_dim.42.gains_ref
  96.8 8.7 %project.2 = (bf16[512,512]{1,0:T(8,128)(2,1)}, bf16[1024,512]{1,0:T(8,128)(2,1)}) custom-call(s32[4]{0:T(128)} %pad_add_fusion.blocks_ref, bf16[1536,2048]{1,0:T(8,128)(2,1)} %bitcast.8, f32[2048,128]{1,0:T(8,128)} %broadcast_in_dim.42.gains_ref, bf16[256,512]{1,0:T(8,128)(2,1)} %copy-done.27, bf16[256,512]{1,0:T(8,128)(2,1)} %broadcast_select_fusion.2.refs_1_, ...), custom_call_target="tpu_custom_call" | custom-call | flops 3221225472 | bytes 9961472 | tf_op jit(solution)/shard_map/project/pallas_call | solution.py:266
  105.5 3.5 %collective-permute-start.8 = (bf16[1024,512]{1,0:T(8,128)(2,1)}, bf16[1024,512]{1,0:T(8,128)(2,1)S(1)}, u32[]{:S(2)}, u32[]{:S(2)}) collective-permute-start(bf16[1024,512]{1,0:T(8,128)(2,1)} %get-tuple-element.44.refs_0_), channel_id=1, source_target_pairs={{0,16},{16,0},{1,17},{17,1},{2,18},{18,2},{3,19},{19,3},{4,20},{20... | collective-permute-start | bytes 3145736 | tf_op jit(solution)/shard_map/ppermute | solution.py:541
  110.4 8.6 %project.3 = (bf16[512,512]{1,0:T(8,128)(2,1)}, bf16[1024,512]{1,0:T(8,128)(2,1)}) custom-call(s32[4]{0:T(128)} %pad_add_fusion.blocks_ref, bf16[1536,2048]{1,0:T(8,128)(2,1)} %bitcast.9, f32[2048,128]{1,0:T(8,128)} %broadcast_in_dim.42.gains_ref, bf16[256,512]{1,0:T(8,128)(2,1)} %copy-done.29, bf16[256,512]{1,0:T(8,128)(2,1)} %copy-done.28, ...), custom_call_target="tpu_custom_call" | custom-call | flops 3221225472 | bytes 9961472 | tf_op jit(solution)/shard_map/project/pallas_call | solution.py:266
  119.2 1.5 prepare.1.refs_2_.refs_3_
  120.8 12.5 %collective-permute-done.8.refs_1_ = bf16[1024,512]{1,0:T(8,128)(2,1)S(1)} collective-permute-done((bf16[1024,512]{1,0:T(8,128)(2,1)}, bf16[1024,512]{1,0:T(8,128)(2,1)S(1)}, u32[]{:S(2)}, u32[]{:S(2)}) %collective-permute-start.8) | collective-permute-done | bytes 1048608 | tf_op jit(solution)/shard_map/ppermute | solution.py:541
  133.3 7.0 %attend.3 = (bf16[256,512]{1,0:T(8,128)(2,1)S(1)}, bf16[256,512]{1,0:T(8,128)(2,1)S(1)}, bf16[256,512]{1,0:T(8,128)(2,1)S(1)}, bf16[256,512]{1,0:T(8,128)(2,1)S(...) custom-call(s32[1]{0:T(128)} %bitcast.seq_ref, ...), custom_call_target="tpu_custom_call" | custom-call | flops 1073741824 | bytes 3145728 | tf_op jit(solution)/shard_map/attend/pallas_call | solution.py:410
  144.5 2.5 %collective-permute-start.12 = (bf16[256,512]{1,0:T(8,128)(2,1)}, bf16[256,512]{1,0:T(8,128)(2,1)}, u32[]{:S(2)}, u32[]{:S(2)}) collective-permute-start(bf16[256,512]{1,0:T(8,128)(2,1)} %get-tuple-element.51), channel_id=1, source_target_pairs={{0,4},{4,12},{12,8},{8,0},{1,5},{5,13},{13,9},{9,1},{2,6},{6,14},{... | collective-permute-start | bytes 786440 | tf_op jit(solution)/shard_map/ppermute | solution.py:497
  150.7 6.8 %attend.4 = (f32[4,2,512]{2,1,0:T(2,128)S(1)}, f32[512,512]{1,0:T(8,128)S(1)}) custom-call(s32[1]{0:T(128)} %bitcast.seq_ref, s32[16]{0:T(128)S(1)} %copy-done.23, s32[16,16]{1,0:T(8,128)S(1)} %copy-done.21, bf16[512,512]{1,0:T(8,128)(2,1)S(1)} %copy-done.8, bf16[1024,512]{1,0:T(8,128)(2,1)S(1)} %copy-done.5, bf16[1024,512]{1,0:T(8,128)(2,1)S(1)} %copy-done.7, ...), custom_call_target="tpu_custom_call" | custom-call | flops 1610612736 | bytes 4194304 | tf_op jit(solution)/shard_map/attend/pallas_call | solution.py:410
  157.6 5.7 %attend.5 = (bf16[256,512]{1,0:T(8,128)(2,1)S(1)}, bf16[256,512]{1,0:T(8,128)(2,1)S(1)}, bf16[256,512]{1,0:T(8,128)(2,1)S(1)}, bf16[256,512]{1,0:T(8,128)(2,1)S(...) custom-call(s32[1]{0:T(128)} %bitcast.seq_ref, ...), custom_call_target="tpu_custom_call" | custom-call | flops 536870912 | bytes 2097152 | tf_op jit(solution)/shard_map/attend/pallas_call | solution.py:410
  163.2 2.2 %collective-permute-start.29 = (bf16[256,512]{1,0:T(8,128)(2,1)S(1)}, bf16[256,512]{1,0:T(8,128)(2,1)S(1)}, u32[]{:S(2)}, u32[]{:S(2)}) collective-permute-start(bf16[256,512]{1,0:T(8,128)(2,1)S(1)} %get-tuple-element.71), channel_id=1, source_target_pairs={{0,4},{4,12},{12,8},{8,0},{1,5},{5,13},{13,9},{9,1},{2,6},{6,14},{... | collective-permute-start | bytes 786440 | tf_op jit(solution)/shard_map/ppermute | solution.py:497
  166.6 2.3 %collective-permute-start.13 = (bf16[256,512]{1,0:T(8,128)(2,1)S(1)}, bf16[256,512]{1,0:T(8,128)(2,1)S(1)}, u32[]{:S(2)}, u32[]{:S(2)}) collective-permute-start(bf16[256,512]{1,0:T(8,128)(2,1)S(1)} %get-tuple-element.77), channel_id=1, source_target_pairs={{4,0},{8,4},{12,8},{0,12},{5,1},{9,5},{13,9},{1,13},{6,2},{10,6},{... | collective-permute-start | bytes 786440 | tf_op jit(solution)/shard_map/ppermute | solution.py:498
  169.1 3.8 %collective-permute-start.10 = (bf16[256,512]{1,0:T(8,128)(2,1)S(1)}, bf16[256,512]{1,0:T(8,128)(2,1)S(1)}, u32[]{:S(2)}, u32[]{:S(2)}) collective-permute-start(bf16[256,512]{1,0:T(8,128)(2,1)S(1)} %get-tuple-element.79), channel_id=1, source_target_pairs={{4,0},{8,4},{12,8},{0,12},{5,1},{9,5},{13,9},{1,13},{6,2},{10,6},{... | collective-permute-start | bytes 786440 | tf_op jit(solution)/shard_map/ppermute | solution.py:498
  172.9 3.5 %collective-permute-done.29.refs_9_ = bf16[256,512]{1,0:T(8,128)(2,1)S(1)} collective-permute-done((bf16[256,512]{1,0:T(8,128)(2,1)S(1)}, bf16[256,512]{1,0:T(8,128)(2,1)S(1)}, u32[]{:S(2)}, u32[]{:S(2)}) %collective-permute-start.29) | collective-permute-done | bytes 262176 | tf_op jit(solution)/shard_map/ppermute | solution.py:497
  176.5 16.7 %collective-permute-done.26.refs_5_ = bf16[256,512]{1,0:T(8,128)(2,1)S(1)} collective-permute-done((bf16[256,512]{1,0:T(8,128)(2,1)S(1)}, bf16[256,512]{1,0:T(8,128)(2,1)S(1)}, u32[]{:S(2)}, u32[]{:S(2)}) %collective-permute-start.26) | collective-permute-done | bytes 262176 | tf_op jit(solution)/shard_map/ppermute | solution.py:497
  193.5 2.0 collective-permute-start.31
  195.5 1.9 collective-permute-start.27
  197.4 7.7 %collective-permute-start.28 = (bf16[256,512]{1,0:T(8,128)(2,1)S(1)}, bf16[256,512]{1,0:T(8,128)(2,1)S(1)}, u32[]{:S(2)}, u32[]{:S(2)}) collective-permute-start(bf16[256,512]{1,0:T(8,128)(2,1)S(1)} %get-tuple-element.75), channel_id=1, source_target_pairs={{0,4},{4,8},{8,12},{12,0},{1,5},{5,9},{9,13},{13,1},{2,6},{6,10},{... | collective-permute-start | bytes 786440 | tf_op jit(solution)/shard_map/ppermute | solution.py:499
  206.3 2.1 collective-permute-done.30.refs_7_
  208.4 5.2 %collective-permute-done.31.refs_8_ = bf16[256,512]{1,0:T(8,128)(2,1)S(1)} collective-permute-done((bf16[256,512]{1,0:T(8,128)(2,1)S(1)}, bf16[256,512]{1,0:T(8,128)(2,1)S(1)}, u32[]{:S(2)}, u32[]{:S(2)}) %collective-permute-start.31) | collective-permute-done | bytes 262176 | tf_op jit(solution)/shard_map/ppermute | solution.py:499
  213.6 5.9 %collective-permute-done.27.refs_3_ = bf16[256,512]{1,0:T(8,128)(2,1)S(1)} collective-permute-done((bf16[256,512]{1,0:T(8,128)(2,1)S(1)}, bf16[256,512]{1,0:T(8,128)(2,1)S(1)}, u32[]{:S(2)}, u32[]{:S(2)}) %collective-permute-start.27) | collective-permute-done | bytes 262176 | tf_op jit(solution)/shard_map/ppermute | solution.py:498
  219.5 2.2 place.1
  (125 shorter events, 19.2 us)
Async XLA Ops:
  0.0 31.2 %copy-start.23 = (s32[16]{0:T(128)S(1)}, s32[16]{0:T(128)}, u32[]{:S(2)}) copy-start(s32[16]{0:T(128)} %order_ref.15) | copy-start | bytes 196
  1.5 29.7 %copy-start.2 = (f32[27,512]{1,0:T(8,128)S(1)}, f32[27,512]{1,0:T(8,128)}, u32[]{:S(2)}) copy-start(f32[27,512]{1,0:T(8,128)} %taps_ref.7) | copy-start | bytes 165892
  7.9 23.3 %copy-start.4 = (f32[256,1024]{1,0:T(8,128)S(1)}, f32[256,1024]{1,0:T(8,128)}, u32[]{:S(2)}) copy-start(f32[256,1024]{1,0:T(8,128)} %get-tuple-element.58.part_ref) | copy-start | bytes 3145732
  7.9 16.9 %collective-permute-start.1 = (bf16[256,512]{1,0:T(8,128)(2,1)}, bf16[256,512]{1,0:T(8,128)(2,1)}, u32[]{:S(2)}, u32[]{:S(2)}) collective-permute-start(bf16[256,512]{1,0:T(8,128)(2,1)} %get-tuple-element.42), channel_id=1, source_target_pairs={{0,16},{1,17},{2,18},{3,19},{4,20},{5,21},{6,22},{7,23},{8,24},{9,... | collective-permute-start | bytes 786440 | tf_op jit(solution)/shard_map/ppermute | solution.py:524
  13.7 17.5 %collective-permute-start.17 = (bf16[256,1024]{1,0:T(8,128)(2,1)}, bf16[256,1024]{1,0:T(8,128)(2,1)S(1)}, u32[]{:S(2)}, u32[]{:S(2)}) collective-permute-start(bf16[256,1024]{1,0:T(8,128)(2,1)} %get-tuple-element.57), channel_id=1, source_target_pairs={{0,16},{1,17},{2,18},{3,19},{4,20},{5,21},{6,22},{7,23},{8,24},{9,... | collective-permute-start | bytes 1572872 | tf_op jit(solution)/shard_map/ppermute | solution.py:526
  21.3 29.5 %copy-start.3 = (f32[256,1024]{1,0:T(8,128)S(1)}, f32[256,1024]{1,0:T(8,128)}, u32[]{:S(2)}) copy-start(f32[256,1024]{1,0:T(8,128)} %get-tuple-element.54.part_ref) | copy-start | bytes 3145732
  21.4 27.2 %collective-permute-start.15 = (bf16[256,1024]{1,0:T(8,128)(2,1)}, bf16[256,1024]{1,0:T(8,128)(2,1)S(1)}, u32[]{:S(2)}, u32[]{:S(2)}) collective-permute-start(bf16[256,1024]{1,0:T(8,128)(2,1)} %get-tuple-element.53), channel_id=1, source_target_pairs={{0,16},{1,17},{2,18},{3,19},{4,20},{5,21},{6,22},{7,23},{8,24},{9,... | collective-permute-start | bytes 1572872 | tf_op jit(solution)/shard_map/ppermute | solution.py:526
  22.8 24.1 %collective-permute-start = (bf16[256,512]{1,0:T(8,128)(2,1)}, bf16[256,512]{1,0:T(8,128)(2,1)}, u32[]{:S(2)}, u32[]{:S(2)}) collective-permute-start(bf16[256,512]{1,0:T(8,128)(2,1)} %get-tuple-element.40), channel_id=1, source_target_pairs={{0,16},{1,17},{2,18},{3,19},{4,20},{5,21},{6,22},{7,23},{8,24},{9,... | collective-permute-start | bytes 786440 | tf_op jit(solution)/shard_map/ppermute | solution.py:524
  26.5 28.3 %collective-permute-start.3 = (bf16[256,512]{1,0:T(8,128)(2,1)}, bf16[256,512]{1,0:T(8,128)(2,1)}, u32[]{:S(2)}, u32[]{:S(2)}) collective-permute-start(bf16[256,512]{1,0:T(8,128)(2,1)} %broadcast_select_fusion.2.refs_1_), channel_id=1, source_target_pairs={{0,4},{4,8},{8,12},{12,0},{1,5},{5,9},{9,13},{13,1},{2,6},{6,10},{... | collective-permute-start | bytes 786440 | tf_op jit(solution)/shard_map/ppermute | solution.py:483
  28.1 28.0 %collective-permute-start.5 = (bf16[256,512]{1,0:T(8,128)(2,1)}, bf16[256,512]{1,0:T(8,128)(2,1)}, u32[]{:S(2)}, u32[]{:S(2)}) collective-permute-start(bf16[256,512]{1,0:T(8,128)(2,1)} %broadcast_select_fusion.2.refs_1_), channel_id=1, source_target_pairs={{4,0},{8,4},{12,8},{0,12},{5,1},{9,5},{13,9},{1,13},{6,2},{10,6},{... | collective-permute-start | bytes 786440 | tf_op jit(solution)/shard_map/ppermute | solution.py:484
  35.2 22.9 %collective-permute-start.18 = (bf16[256,512]{1,0:T(8,128)(2,1)S(1)}, bf16[256,512]{1,0:T(8,128)(2,1)S(1)}, u32[]{:S(2)}, u32[]{:S(2)}) collective-permute-start(bf16[256,512]{1,0:T(8,128)(2,1)S(1)} %get-tuple-element.60), channel_id=1, source_target_pairs={{16,0},{17,1},{18,2},{19,3},{20,4},{21,5},{22,6},{23,7},{24,8},{25... | collective-permute-start | bytes 786440 | tf_op jit(solution)/shard_map/ppermute | solution.py:536
  46.9 23.2 %copy-start.27 = (bf16[256,512]{1,0:T(8,128)(2,1)}, bf16[256,512]{1,0:T(8,128)(2,1)S(1)}, u32[]{:S(2)}) copy-start(bf16[256,512]{1,0:T(8,128)(2,1)S(1)} %broadcast_select_fusion.3.refs_0_) | copy-start | bytes 786436
  46.9 19.3 %collective-permute-start.2 = (bf16[256,512]{1,0:T(8,128)(2,1)S(1)}, bf16[256,512]{1,0:T(8,128)(2,1)S(1)}, u32[]{:S(2)}, u32[]{:S(2)}) collective-permute-start(bf16[256,512]{1,0:T(8,128)(2,1)S(1)} %broadcast_select_fusion.3.refs_0_), channel_id=1, source_target_pairs={{0,4},{4,8},{8,12},{12,0},{1,5},{5,9},{9,13},{13,1},{2,6},{6,10},{... | collective-permute-start | bytes 786440 | tf_op jit(solution)/shard_map/ppermute | solution.py:483
  48.6 18.1 %collective-permute-start.4 = (bf16[256,512]{1,0:T(8,128)(2,1)S(1)}, bf16[256,512]{1,0:T(8,128)(2,1)S(1)}, u32[]{:S(2)}, u32[]{:S(2)}) collective-permute-start(bf16[256,512]{1,0:T(8,128)(2,1)S(1)} %broadcast_select_fusion.3.refs_0_), channel_id=1, source_target_pairs={{4,0},{8,4},{12,8},{0,12},{5,1},{9,5},{13,9},{1,13},{6,2},{10,6},{... | collective-permute-start | bytes 786440 | tf_op jit(solution)/shard_map/ppermute | solution.py:484
  54.8 9.7 %collective-permute-start.16 = (bf16[256,512]{1,0:T(8,128)(2,1)S(1)}, bf16[256,512]{1,0:T(8,128)(2,1)S(1)}, u32[]{:S(2)}, u32[]{:S(2)}) collective-permute-start(bf16[256,512]{1,0:T(8,128)(2,1)S(1)} %get-tuple-element.56), channel_id=1, source_target_pairs={{16,0},{17,1},{18,2},{19,3},{20,4},{21,5},{22,6},{23,7},{24,8},{25... | collective-permute-start | bytes 786440 | tf_op jit(solution)/shard_map/ppermute | solution.py:536
  57.1 35.5 %collective-permute-start.7 = (bf16[256,512]{1,0:T(8,128)(2,1)S(1)}, bf16[256,512]{1,0:T(8,128)(2,1)S(1)}, u32[]{:S(2)}, u32[]{:S(2)}) collective-permute-start(bf16[256,512]{1,0:T(8,128)(2,1)S(1)} %select_select_fusion.2), channel_id=1, source_target_pairs={{4,0},{12,4},{8,12},{0,8},{5,1},{13,5},{9,13},{1,9},{6,2},{14,6},{... | collective-permute-start | bytes 786440 | tf_op jit(solution)/shard_map/ppermute | solution.py:486
  58.1 38.7 %copy-start.28 = (bf16[256,512]{1,0:T(8,128)(2,1)}, bf16[256,512]{1,0:T(8,128)(2,1)S(1)}, u32[]{:S(2)}) copy-start(bf16[256,512]{1,0:T(8,128)(2,1)S(1)} %broadcast_select_fusion.refs_1_) | copy-start | bytes 786436
  58.1 37.4 %copy-start.36 = (f32[2048]{0:T(1024)S(1)}, f32[2048]{0:T(1024)}, u32[]{:S(2)}) copy-start(f32[2048]{0:T(1024)} %param.9) | copy-start | bytes 24580
  58.1 16.8 %collective-permute-start.20 = (bf16[256,512]{1,0:T(8,128)(2,1)S(1)}, bf16[256,512]{1,0:T(8,128)(2,1)S(1)}, u32[]{:S(2)}, u32[]{:S(2)}) collective-permute-start(bf16[256,512]{1,0:T(8,128)(2,1)S(1)} %broadcast_select_fusion.refs_1_), channel_id=1, source_target_pairs={{0,4},{4,8},{8,12},{12,0},{1,5},{5,9},{9,13},{13,1},{2,6},{6,10},{... | collective-permute-start | bytes 786440 | tf_op jit(solution)/shard_map/ppermute | solution.py:483
  64.6 16.0 %collective-permute-start.22 = (bf16[256,512]{1,0:T(8,128)(2,1)S(1)}, bf16[256,512]{1,0:T(8,128)(2,1)S(1)}, u32[]{:S(2)}, u32[]{:S(2)}) collective-permute-start(bf16[256,512]{1,0:T(8,128)(2,1)S(1)} %broadcast_select_fusion.refs_1_), channel_id=1, source_target_pairs={{4,0},{8,4},{12,8},{0,12},{5,1},{9,5},{13,9},{1,13},{6,2},{10,6},{... | collective-permute-start | bytes 786440 | tf_op jit(solution)/shard_map/ppermute | solution.py:484
  66.3 30.5 %copy-start.29 = (bf16[256,512]{1,0:T(8,128)(2,1)}, bf16[256,512]{1,0:T(8,128)(2,1)S(1)}, u32[]{:S(2)}) copy-start(bf16[256,512]{1,0:T(8,128)(2,1)S(1)} %broadcast_select_fusion.1.refs_0_) | copy-start | bytes 786436
  66.3 30.5 %copy-start.30 = (bf16[256,512]{1,0:T(8,128)(2,1)}, bf16[256,512]{1,0:T(8,128)(2,1)S(1)}, u32[]{:S(2)}) copy-start(bf16[256,512]{1,0:T(8,128)(2,1)S(1)} %collective-permute-done.2.refs_2_) | copy-start | bytes 786436
  66.3 19.9 %collective-permute-start.19 = (bf16[256,512]{1,0:T(8,128)(2,1)S(1)}, bf16[256,512]{1,0:T(8,128)(2,1)S(1)}, u32[]{:S(2)}, u32[]{:S(2)}) collective-permute-start(bf16[256,512]{1,0:T(8,128)(2,1)S(1)} %broadcast_select_fusion.1.refs_0_), channel_id=1, source_target_pairs={{0,4},{4,8},{8,12},{12,0},{1,5},{5,9},{9,13},{13,1},{2,6},{6,10},{... | collective-permute-start | bytes 786440 | tf_op jit(solution)/shard_map/ppermute | solution.py:483
  66.7 30.1 %copy-start.31 = (bf16[256,512]{1,0:T(8,128)(2,1)}, bf16[256,512]{1,0:T(8,128)(2,1)S(1)}, u32[]{:S(2)}) copy-start(bf16[256,512]{1,0:T(8,128)(2,1)S(1)} %collective-permute-done.4.refs_4_) | copy-start | bytes 786436
  66.7 23.2 %collective-permute-start.21 = (bf16[256,512]{1,0:T(8,128)(2,1)S(1)}, bf16[256,512]{1,0:T(8,128)(2,1)S(1)}, u32[]{:S(2)}, u32[]{:S(2)}) collective-permute-start(bf16[256,512]{1,0:T(8,128)(2,1)S(1)} %broadcast_select_fusion.1.refs_0_), channel_id=1, source_target_pairs={{4,0},{8,4},{12,8},{0,12},{5,1},{9,5},{13,9},{1,13},{6,2},{10,6},{... | collective-permute-start | bytes 786440 | tf_op jit(solution)/shard_map/ppermute | solution.py:484
  74.9 30.6 %copy-start.32 = (bf16[256,512]{1,0:T(8,128)(2,1)}, bf16[256,512]{1,0:T(8,128)(2,1)S(1)}, u32[]{:S(2)}) copy-start(bf16[256,512]{1,0:T(8,128)(2,1)S(1)} %collective-permute-done.20.refs_3_) | copy-start | bytes 786436
  74.9 20.6 %collective-permute-start.6 = (bf16[256,512]{1,0:T(8,128)(2,1)S(1)}, bf16[256,512]{1,0:T(8,128)(2,1)S(1)}, u32[]{:S(2)}, u32[]{:S(2)}) collective-permute-start(bf16[256,512]{1,0:T(8,128)(2,1)S(1)} %select_select_fusion.3), channel_id=1, source_target_pairs={{4,0},{12,4},{8,12},{0,8},{5,1},{13,5},{9,13},{1,9},{6,2},{14,6},{... | collective-permute-start | bytes 786440 | tf_op jit(solution)/shard_map/ppermute | solution.py:486
  80.5 25.0 %copy-start.33 = (bf16[256,512]{1,0:T(8,128)(2,1)}, bf16[256,512]{1,0:T(8,128)(2,1)S(1)}, u32[]{:S(2)}) copy-start(bf16[256,512]{1,0:T(8,128)(2,1)S(1)} %collective-permute-done.22.refs_5_) | copy-start | bytes 786436
  80.6 28.5 %collective-permute-start.24 = (bf16[256,512]{1,0:T(8,128)(2,1)S(1)}, bf16[256,512]{1,0:T(8,128)(2,1)S(1)}, u32[]{:S(2)}, u32[]{:S(2)}) collective-permute-start(bf16[256,512]{1,0:T(8,128)(2,1)S(1)} %select_select_fusion), channel_id=1, source_target_pairs={{4,0},{12,4},{8,12},{0,8},{5,1},{13,5},{9,13},{1,9},{6,2},{14,6},{... | collective-permute-start | bytes 786440 | tf_op jit(solution)/shard_map/ppermute | solution.py:486
  86.2 19.3 %copy-start.34 = (bf16[256,512]{1,0:T(8,128)(2,1)}, bf16[256,512]{1,0:T(8,128)(2,1)S(1)}, u32[]{:S(2)}) copy-start(bf16[256,512]{1,0:T(8,128)(2,1)S(1)} %collective-permute-done.19.refs_2_) | copy-start | bytes 786436
  89.9 15.7 %copy-start.35 = (bf16[256,512]{1,0:T(8,128)(2,1)}, bf16[256,512]{1,0:T(8,128)(2,1)S(1)}, u32[]{:S(2)}) copy-start(bf16[256,512]{1,0:T(8,128)(2,1)S(1)} %collective-permute-done.21.refs_4_) | copy-start | bytes 786436
  89.9 19.2 %collective-permute-start.23 = (bf16[256,512]{1,0:T(8,128)(2,1)S(1)}, bf16[256,512]{1,0:T(8,128)(2,1)S(1)}, u32[]{:S(2)}, u32[]{:S(2)}) collective-permute-start(bf16[256,512]{1,0:T(8,128)(2,1)S(1)} %select_select_fusion.1), channel_id=1, source_target_pairs={{4,0},{12,4},{8,12},{0,8},{5,1},{13,5},{9,13},{1,9},{6,2},{14,6},{... | collective-permute-start | bytes 786440 | tf_op jit(solution)/shard_map/ppermute | solution.py:486
  105.5 27.7 %collective-permute-start.8 = (bf16[1024,512]{1,0:T(8,128)(2,1)}, bf16[1024,512]{1,0:T(8,128)(2,1)S(1)}, u32[]{:S(2)}, u32[]{:S(2)}) collective-permute-start(bf16[1024,512]{1,0:T(8,128)(2,1)} %get-tuple-element.44.refs_0_), channel_id=1, source_target_pairs={{0,16},{16,0},{1,17},{17,1},{2,18},{18,2},{3,19},{19,3},{4,20},{20... | collective-permute-start | bytes 3145736 | tf_op jit(solution)/shard_map/ppermute | solution.py:541
  119.1 14.2 %copy-start.5 = (bf16[1024,512]{1,0:T(8,128)(2,1)S(1)}, bf16[1024,512]{1,0:T(8,128)(2,1)}, u32[]{:S(2)}) copy-start(bf16[1024,512]{1,0:T(8,128)(2,1)} %get-tuple-element.44.refs_0_) | copy-start | bytes 3145732
  119.1 38.4 %collective-permute-start.25 = (bf16[1024,512]{1,0:T(8,128)(2,1)}, bf16[1024,512]{1,0:T(8,128)(2,1)}, u32[]{:S(2)}, u32[]{:S(2)}) collective-permute-start(bf16[1024,512]{1,0:T(8,128)(2,1)} %get-tuple-element.62.refs_2_), channel_id=1, source_target_pairs={{0,16},{16,0},{1,17},{17,1},{2,18},{18,2},{3,19},{19,3},{4,20},{20... | collective-permute-start | bytes 3145736 | tf_op jit(solution)/shard_map/ppermute | solution.py:546
  144.5 21.0 %collective-permute-start.12 = (bf16[256,512]{1,0:T(8,128)(2,1)}, bf16[256,512]{1,0:T(8,128)(2,1)}, u32[]{:S(2)}, u32[]{:S(2)}) collective-permute-start(bf16[256,512]{1,0:T(8,128)(2,1)} %get-tuple-element.51), channel_id=1, source_target_pairs={{0,4},{4,12},{12,8},{8,0},{1,5},{5,13},{13,9},{9,1},{2,6},{6,14},{... | collective-permute-start | bytes 786440 | tf_op jit(solution)/shard_map/ppermute | solution.py:497
  147.0 21.9 %collective-permute-start.9 = (bf16[256,512]{1,0:T(8,128)(2,1)}, bf16[256,512]{1,0:T(8,128)(2,1)S(1)}, u32[]{:S(2)}, u32[]{:S(2)}) collective-permute-start(bf16[256,512]{1,0:T(8,128)(2,1)} %copy-done.26), channel_id=1, source_target_pairs={{0,4},{4,12},{12,8},{8,0},{1,5},{5,13},{13,9},{9,1},{2,6},{6,14},{... | collective-permute-start | bytes 786440 | tf_op jit(solution)/shard_map/ppermute | solution.py:497
  163.2 13.2 %collective-permute-start.29 = (bf16[256,512]{1,0:T(8,128)(2,1)S(1)}, bf16[256,512]{1,0:T(8,128)(2,1)S(1)}, u32[]{:S(2)}, u32[]{:S(2)}) collective-permute-start(bf16[256,512]{1,0:T(8,128)(2,1)S(1)} %get-tuple-element.71), channel_id=1, source_target_pairs={{0,4},{4,12},{12,8},{8,0},{1,5},{5,13},{13,9},{9,1},{2,6},{6,14},{... | collective-permute-start | bytes 786440 | tf_op jit(solution)/shard_map/ppermute | solution.py:497
  166.6 38.5 %copy-start.11 = (bf16[256,512]{1,0:T(8,128)(2,1)S(1)}, bf16[256,512]{1,0:T(8,128)(2,1)}, u32[]{:S(2)}) copy-start(bf16[256,512]{1,0:T(8,128)(2,1)} %copy-done.10) | copy-start | bytes 786436
  166.6 26.9 %collective-permute-start.13 = (bf16[256,512]{1,0:T(8,128)(2,1)S(1)}, bf16[256,512]{1,0:T(8,128)(2,1)S(1)}, u32[]{:S(2)}, u32[]{:S(2)}) collective-permute-start(bf16[256,512]{1,0:T(8,128)(2,1)S(1)} %get-tuple-element.77), channel_id=1, source_target_pairs={{4,0},{8,4},{12,8},{0,12},{5,1},{9,5},{13,9},{1,13},{6,2},{10,6},{... | collective-permute-start | bytes 786440 | tf_op jit(solution)/shard_map/ppermute | solution.py:498
  168.9 26.6 %collective-permute-start.14 = (bf16[256,512]{1,0:T(8,128)(2,1)S(1)}, bf16[256,512]{1,0:T(8,128)(2,1)S(1)}, u32[]{:S(2)}, u32[]{:S(2)}) collective-permute-start(bf16[256,512]{1,0:T(8,128)(2,1)S(1)} %get-tuple-element.78), channel_id=1, source_target_pairs={{0,4},{4,8},{8,12},{12,0},{1,5},{5,9},{9,13},{13,1},{2,6},{6,10},{... | collective-permute-start | bytes 786440 | tf_op jit(solution)/shard_map/ppermute | solution.py:499
  168.9 24.4 %collective-permute-start.26 = (bf16[256,512]{1,0:T(8,128)(2,1)S(1)}, bf16[256,512]{1,0:T(8,128)(2,1)S(1)}, u32[]{:S(2)}, u32[]{:S(2)}) collective-permute-start(bf16[256,512]{1,0:T(8,128)(2,1)S(1)} %get-tuple-element.67), channel_id=1, source_target_pairs={{0,4},{4,12},{12,8},{8,0},{1,5},{5,13},{13,9},{9,1},{2,6},{6,14},{... | collective-permute-start | bytes 786440 | tf_op jit(solution)/shard_map/ppermute | solution.py:497
  169.1 28.3 %collective-permute-start.10 = (bf16[256,512]{1,0:T(8,128)(2,1)S(1)}, bf16[256,512]{1,0:T(8,128)(2,1)S(1)}, u32[]{:S(2)}, u32[]{:S(2)}) collective-permute-start(bf16[256,512]{1,0:T(8,128)(2,1)S(1)} %get-tuple-element.79), channel_id=1, source_target_pairs={{4,0},{8,4},{12,8},{0,12},{5,1},{9,5},{13,9},{1,13},{6,2},{10,6},{... | collective-permute-start | bytes 786440 | tf_op jit(solution)/shard_map/ppermute | solution.py:498
  176.4 29.8 %collective-permute-start.11 = (bf16[256,512]{1,0:T(8,128)(2,1)S(1)}, bf16[256,512]{1,0:T(8,128)(2,1)S(1)}, u32[]{:S(2)}, u32[]{:S(2)}) collective-permute-start(bf16[256,512]{1,0:T(8,128)(2,1)S(1)} %get-tuple-element.80), channel_id=1, source_target_pairs={{0,4},{4,8},{8,12},{12,0},{1,5},{5,9},{9,13},{13,1},{2,6},{6,10},{... | collective-permute-start | bytes 786440 | tf_op jit(solution)/shard_map/ppermute | solution.py:499
  193.2 15.2 %collective-permute-start.30 = (bf16[256,512]{1,0:T(8,128)(2,1)S(1)}, bf16[256,512]{1,0:T(8,128)(2,1)S(1)}, u32[]{:S(2)}, u32[]{:S(2)}) collective-permute-start(bf16[256,512]{1,0:T(8,128)(2,1)S(1)} %get-tuple-element.74), channel_id=1, source_target_pairs={{4,0},{8,4},{12,8},{0,12},{5,1},{9,5},{13,9},{1,13},{6,2},{10,6},{... | collective-permute-start | bytes 786440 | tf_op jit(solution)/shard_map/ppermute | solution.py:498
  193.5 20.1 %collective-permute-start.31 = (bf16[256,512]{1,0:T(8,128)(2,1)S(1)}, bf16[256,512]{1,0:T(8,128)(2,1)S(1)}, u32[]{:S(2)}, u32[]{:S(2)}) collective-permute-start(bf16[256,512]{1,0:T(8,128)(2,1)S(1)} %get-tuple-element.73), channel_id=1, source_target_pairs={{0,4},{4,8},{8,12},{12,0},{1,5},{5,9},{9,13},{13,1},{2,6},{6,10},{... | collective-permute-start | bytes 786440 | tf_op jit(solution)/shard_map/ppermute | solution.py:499
  195.5 24.0 %collective-permute-start.27 = (bf16[256,512]{1,0:T(8,128)(2,1)S(1)}, bf16[256,512]{1,0:T(8,128)(2,1)S(1)}, u32[]{:S(2)}, u32[]{:S(2)}) collective-permute-start(bf16[256,512]{1,0:T(8,128)(2,1)S(1)} %get-tuple-element.76), channel_id=1, source_target_pairs={{4,0},{8,4},{12,8},{0,12},{5,1},{9,5},{13,9},{1,13},{6,2},{10,6},{... | collective-permute-start | bytes 786440 | tf_op jit(solution)/shard_map/ppermute | solution.py:498
  197.4 22.1 %collective-permute-start.28 = (bf16[256,512]{1,0:T(8,128)(2,1)S(1)}, bf16[256,512]{1,0:T(8,128)(2,1)S(1)}, u32[]{:S(2)}, u32[]{:S(2)}) collective-permute-start(bf16[256,512]{1,0:T(8,128)(2,1)S(1)} %get-tuple-element.75), channel_id=1, source_target_pairs={{0,4},{4,8},{8,12},{12,0},{1,5},{5,9},{9,13},{13,1},{2,6},{6,10},{... | collective-permute-start | bytes 786440 | tf_op jit(solution)/shard_map/ppermute | solution.py:499
  (25 other events, 130.9 us)

commit v7 on v6

--- a/solution.py
+++ b/solution.py
@@ -21,13 +21,19 @@
 MASKED_SCORE = -1e30
 LOG2E = math.log2(math.e)
 
-VMEM_LIMIT = 20 * 1024 * 1024
-VMEM_FIRST = 52 * 1024 * 1024
-VMEM_PROJECT = 55 * 1024 * 1024
+VMEM_LIMIT = 14 * 1024 * 1024
 
 
 def vmem_spec():
     return pl.BlockSpec(memory_space=pltpu.VMEM)
+
+
+def off_chip_spec():
+    return pl.BlockSpec(memory_space=pltpu.HBM)
+
+
+def off_chip(array):
+    return pltpu.with_memory_space_constraint(array, pltpu.HBM)
 
 
 def smem_spec():
@@ -98,18 +104,24 @@
         slots_ref, taps_scr, packed = refs
         source_ref = tokens_ref
     else:
-        source_ref, slots_ref, taps_scr, packed, arrived = refs
+        source_ref, slots_ref, taps_scr, packed, arrived, taps_in, taps_arrived = refs
     channels, tokens = packed.shape
     tiles_dev = tokens // TILE
     per_frame = FRAME // TILE
     if not with_before:
+        taps_copy = pltpu.make_async_copy(
+            taps_ref.at[:, first_row : first_row + channels], taps_in, taps_arrived
+        )
+        taps_copy.start()
         copies = fetches(tokens_ref.at[first_row : first_row + channels], source_ref, arrived)
         for copy in copies:
             copy.start()
     pack_slots(order_ref, slots_ref, seq_ref[0], tiles_dev, order_ref.shape[0])
+    if not with_before:
+        taps_copy.wait()
     for first in range(0, channels, TILE):
-        from_row = first_row + first
-        taps_scr[first : first + TILE, :TAPS] = taps_ref[:, from_row : from_row + TILE].T
+        wide = taps_ref[:, first_row + first : first_row + first + TILE] if with_before else taps_in[:, first : first + TILE]
+        taps_scr[first : first + TILE, :TAPS] = wide.T
     lane = lax.broadcasted_iota(jnp.int32, (GROUP, TILE), 1)
     column = lane % FW
     if with_before:
@@ -185,17 +197,22 @@
     ]
     in_specs = [smem_spec(), smem_spec(), vmem_spec(), vmem_spec(), vmem_spec()]
     if not with_before:
-        in_specs = [smem_spec(), smem_spec(), pl.BlockSpec(memory_space=pl.ANY), vmem_spec()]
+        in_specs = [smem_spec(), smem_spec(), off_chip_spec(), off_chip_spec()]
+        tokens, conv_taps, stripe_order = (off_chip(a) for a in (tokens, conv_taps, stripe_order))
         sum_shape = jax.ShapeDtypeStruct((channels, count), jnp.float32)
         out_shape = [sum_shape] + out_shape + [jax.ShapeDtypeStruct((channels, count), jnp.bfloat16)]
-        scratch += [pltpu.SemaphoreType.DMA((CHUNKS,))]
+        scratch += [
+            pltpu.SemaphoreType.DMA((CHUNKS,)),
+            pltpu.VMEM((TAPS, channels), jnp.float32),
+            pltpu.SemaphoreType.DMA,
+        ]
     return pl.pallas_call(
         functools.partial(conv_body, with_before, piece * channels),
         in_specs=in_specs,
         out_specs=[vmem_spec()] * len(out_shape),
         scratch_shapes=scratch,
         out_shape=out_shape,
-        compiler_params=params(VMEM_LIMIT if with_before else VMEM_FIRST),
+        compiler_params=params(),
         cost_estimate=pl.CostEstimate(
             flops=channels * count * TAPS, bytes_accessed=channels * count * 8, transcendentals=0
         ),
@@ -231,7 +248,7 @@
 def project_body(blocks_ref, weight_hbm, gains_ref, *refs):
     shards, (query_ref, pair_ref, weight_ref, tokens_ref, arrived) = refs[:-5], refs[-5:]
     copies = fetches(weight_hbm, weight_ref, arrived)
-    for copy in copies:
+    for copy in copies[:2]:
         copy.start()
     width, tokens = shards[0].shape
     cols = query_ref.shape[0]
@@ -250,6 +267,8 @@
     rows = weight_ref.shape[0] // len(copies)
     for index, copy in enumerate(copies):
         copy.wait()
+        if index + 2 < len(copies):
+            copies[index + 2].start()
         here = slice(index * rows, (index + 1) * rows)
         total = jnp.dot(weight_ref[here, :], tokens_ref[...], preferred_element_type=jnp.float32)
         if index * rows < cols:
@@ -265,7 +284,7 @@
     cols = rows // 3
     return pl.pallas_call(
         project_body,
-        in_specs=[smem_spec(), pl.BlockSpec(memory_space=pl.ANY)] + [vmem_spec()] * (1 + len(shards)),
+        in_specs=[smem_spec(), off_chip_spec()] + [vmem_spec()] * (1 + len(shards)),
         out_specs=[vmem_spec(), vmem_spec()],
         scratch_shapes=[
             pltpu.VMEM((rows, channels), jnp.bfloat16),
@@ -276,14 +295,14 @@
             jax.ShapeDtypeStruct((cols, tokens), jnp.bfloat16),
             jax.ShapeDtypeStruct((2 * cols, tokens), jnp.bfloat16),
         ],
-        compiler_params=params(VMEM_PROJECT),
+        compiler_params=params(),
         cost_estimate=pl.CostEstimate(
             flops=2 * rows * channels * tokens,
             bytes_accessed=2 * (rows * channels + channels * tokens + rows * tokens),
             transcendentals=0,
         ),
         name="project",
-    )(blocks, weights, gains, *shards)
+    )(blocks, off_chip(weights), gains, *shards)
 
 
 def tile_lists(order_ref, ids_ref, seq_here, tiles_dev):
@@ -393,7 +412,7 @@
         pltpu.VMEM((count * tokens, tokens), jnp.float32),
     ]
     if ends:
-        in_specs += [pl.BlockSpec(memory_space=pltpu.HBM)]
+        in_specs += [off_chip_spec()]
         arguments += [out_t]
         width = out_t.shape[0] // (4 * PIECES)
         shapes = [jax.ShapeDtypeStruct((width, tokens), jnp.bfloat16)] * (4 * PIECES)

time: 222 us -> 217 us (0.977)
  local copies, waits for them, and re-layouts: 12 us -> 8.27 us
  Pallas kernels: 61.1 us -> 58.5 us
    pallas_call x2, Pallas kernels: 17.3 us -> 14.4 us  [project_call(): pl.pallas_call(project_body, in_specs=[smem_spec(), off_chip_spec()] + [v...]
    unnamed x82 -> x44, local copies, waits for them, and re-layouts: 10.7 us -> 7.94 us
    ppermute x1, starting transfers between devices: 0.09 us -> 2.55 us  [per_device_fast(): peer_b = lax.ppermute(pair_b, 'seq', swap)]
  transfers between devices with their start and end apart: 32 -> 32, of which waited for: 14 -> 15; matrix products, arithmetic and copies ran while one was open for 3% -> 2% of each run, Pallas kernels for 24% -> 23%
where the time goes in v7:
time: 217 us
  waiting for transfers between devices  83.2 us (38%)
  starting transfers between devices  61.2 us (28%)
  Pallas kernels  58.5 us (27%)
  local copies, waits for them, and re-layouts  8.27 us (4%)
  other arithmetic  5.04 us (2%)
    pallas_call x4, Pallas kernels, conv_call(): pl.pallas_call(functools.partial(conv_body, with_before, piece * channels...  20.5 us
    ppermute x4, waiting for transfers between devices, reduce_blocks(): across = lax.ppermute(sent, 'tp', FOLDED)  20.1 us
    pallas_call x3, Pallas kernels, attend_call(): pl.pallas_call(functools.partial(attend_body, chunk, tuple((s for _, s in...  19.8 us
    pallas_call x2, Pallas kernels, project_call(): pl.pallas_call(project_body, in_specs=[smem_spec(), off_chip_spec()] + [v...  14.4 us
    ppermute x1, waiting for transfers between devices, per_device_fast(): peer_a = lax.ppermute(pair_a, 'seq', swap)  11.7 us
    ppermute x4, waiting for transfers between devices, gather_blocks(): before = lax.ppermute(block, 'tp', FORWARD)  10.7 us
    ppermute x2, waiting for transfers between devices, per_device_fast(): got = lax.ppermute(send, 'seq', [(0, 1)])  10.4 us
    ppermute x4, starting transfers between devices, reduce_blocks(): onward = lax.ppermute(plus(up, across, here == 1), 'tp', FORWARD)  9.84 us
  transfers between devices with their start and end apart: 32, of which 15 were waited for; matrix products, arithmetic and copies ran while one was open for 2% of the time, Pallas kernels for 23%

profile of v7, /device:TPU:0, one launch (start us, length us, event | category | flops | bytes accessed | tf_op | source)
XLA Modules:
  0.0 216.6 jit_solution(13623738590053279854)
XLA Ops:
  0.0 6.3 %conv.5 = (f32[256,1024]{1,0:T(8,128)S(1)}, bf16[256,512]{1,0:T(8,128)(2,1)S(1)}, bf16[256,512]{1,0:T(8,128)(2,1)S(1)}, bf16[256,1024]{1,0:T(8,128)(2,1)}) custom-call(s32[1]{0:T(128)} %bitcast.seq_ref, s32[16]{0:T(128)} %order_ref.15, bf16[512,1024]{1,0:T(8,128)(2,1)} %tokens_ref.3, f32[27,512]{1,0:T(8,128)} %taps_ref.7), custom_call_target="tpu_custom_call" | custom-call | flops 7077888 | bytes 2097152 | tf_op jit(solution)/shard_map/conv/pallas_call | solution.py:209
  7.0 5.6 %collective-permute-start.1 = (bf16[256,512]{1,0:T(8,128)(2,1)S(1)}, bf16[256,512]{1,0:T(8,128)(2,1)}, u32[]{:S(2)}, u32[]{:S(2)}) collective-permute-start(bf16[256,512]{1,0:T(8,128)(2,1)S(1)} %get-tuple-element.42), channel_id=1, source_target_pairs={{0,16},{1,17},{2,18},{3,19},{4,20},{5,21},{6,22},{7,23},{8,24},{9,... | collective-permute-start | bytes 786440 | tf_op jit(solution)/shard_map/ppermute | solution.py:543
  12.6 1.3 collective-permute-start.17
  13.9 6.2 %conv.4 = (f32[256,1024]{1,0:T(8,128)S(1)}, bf16[256,512]{1,0:T(8,128)(2,1)S(1)}, bf16[256,512]{1,0:T(8,128)(2,1)}, bf16[256,1024]{1,0:T(8,128)(2,1)}) custom-call(s32[1]{0:T(128)} %bitcast.seq_ref, s32[16]{0:T(128)} %order_ref.15, bf16[512,1024]{1,0:T(8,128)(2,1)} %tokens_ref.3, f32[27,512]{1,0:T(8,128)} %taps_ref.7), custom_call_target="tpu_custom_call" | custom-call | flops 7077888 | bytes 2097152 | tf_op jit(solution)/shard_map/conv/pallas_call | solution.py:209
  20.9 1.3 collective-permute-start.15
  22.2 2.0 collective-permute-start
  25.2 1.6 collective-permute-start.3
  26.8 2.2 %collective-permute-start.5 = (bf16[256,512]{1,0:T(8,128)(2,1)S(1)}, bf16[256,512]{1,0:T(8,128)(2,1)}, u32[]{:S(2)}, u32[]{:S(2)}) collective-permute-start(bf16[256,512]{1,0:T(8,128)(2,1)S(1)} %broadcast_select_fusion.2.refs_1_), channel_id=1, source_target_pairs={{4,0},{8,4},{12,8},{0,12},{5,1},{9,5},{13,9},{1,13},{6,2},{10,6},{... | collective-permute-start | bytes 786440 | tf_op jit(solution)/shard_map/ppermute | solution.py:503
  29.9 4.0 %conv.7 = (bf16[256,512]{1,0:T(8,128)(2,1)S(1)}, bf16[256,512]{1,0:T(8,128)(2,1)S(1)}) custom-call(s32[1]{0:T(128)} %bitcast.seq_ref, s32[16]{0:T(128)S(1)} %copy-done.19, bf16[256,1024]{1,0:T(8,128)(2,1)S(1)} %collective-permute-done.17.tokens_ref, f32[27,512]{1,0:T(8,128)S(1)} %copy-done.1, f32[256,1024]{1,0:T(8,128)S(1)} %get-tuple-element.58.part_ref), custom_call_target="tpu_custom_call" | custom-call | flops 7077888 | bytes 2097152 | tf_op jit(solution)/shard_map/conv/pallas_call | solution.py:209
  33.9 1.3 collective-permute-start.18
  35.2 10.4 %collective-permute-done = bf16[256,512]{1,0:T(8,128)(2,1)} collective-permute-done((bf16[256,512]{1,0:T(8,128)(2,1)}, bf16[256,512]{1,0:T(8,128)(2,1)}, u32[]{:S(2)}, u32[]{:S(2)}) %collective-permute-start) | collective-permute-done | bytes 262176 | tf_op jit(solution)/shard_map/ppermute | solution.py:543
  46.6 1.6 collective-permute-start.2
  48.2 2.2 %collective-permute-start.4 = (bf16[256,512]{1,0:T(8,128)(2,1)S(1)}, bf16[256,512]{1,0:T(8,128)(2,1)S(1)}, u32[]{:S(2)}, u32[]{:S(2)}) collective-permute-start(bf16[256,512]{1,0:T(8,128)(2,1)S(1)} %broadcast_select_fusion.3.refs_0_), channel_id=1, source_target_pairs={{4,0},{8,4},{12,8},{0,12},{5,1},{9,5},{13,9},{1,13},{6,2},{10,6},{... | collective-permute-start | bytes 786440 | tf_op jit(solution)/shard_map/ppermute | solution.py:503
  50.5 4.0 %conv.6 = (bf16[256,512]{1,0:T(8,128)(2,1)S(1)}, bf16[256,512]{1,0:T(8,128)(2,1)S(1)}) custom-call(s32[1]{0:T(128)} %bitcast.seq_ref, s32[16]{0:T(128)S(1)} %copy-done.19, bf16[256,1024]{1,0:T(8,128)(2,1)S(1)} %collective-permute-done.15.tokens_ref, f32[27,512]{1,0:T(8,128)S(1)} %copy-done.1, f32[256,1024]{1,0:T(8,128)S(1)} %get-tuple-element.54.part_ref), custom_call_target="tpu_custom_call" | custom-call | flops 7077888 | bytes 2097152 | tf_op jit(solution)/shard_map/conv/pallas_call | solution.py:209
  54.5 1.3 collective-permute-start.16
  55.8 1.8 collective-permute-start.7
  58.0 5.2 %collective-permute-done.16 = bf16[256,512]{1,0:T(8,128)(2,1)S(1)} collective-permute-done((bf16[256,512]{1,0:T(8,128)(2,1)S(1)}, bf16[256,512]{1,0:T(8,128)(2,1)S(1)}, u32[]{:S(2)}, u32[]{:S(2)}) %collective-permute-start.16) | collective-permute-done | bytes 262176 | tf_op jit(solution)/shard_map/ppermute | solution.py:555
  63.2 1.7 collective-permute-start.22
  65.4 3.5 %collective-permute-start.21 = (bf16[256,512]{1,0:T(8,128)(2,1)S(1)}, bf16[256,512]{1,0:T(8,128)(2,1)S(1)}, u32[]{:S(2)}, u32[]{:S(2)}) collective-permute-start(bf16[256,512]{1,0:T(8,128)(2,1)S(1)} %broadcast_select_fusion.1.refs_0_), channel_id=1, source_target_pairs={{4,0},{8,4},{12,8},{0,12},{5,1},{9,5},{13,9},{1,13},{6,2},{10,6},{... | collective-permute-start | bytes 786440 | tf_op jit(solution)/shard_map/ppermute | solution.py:503
  68.9 5.7 %collective-permute-done.20.refs_3_ = bf16[256,512]{1,0:T(8,128)(2,1)S(1)} collective-permute-done((bf16[256,512]{1,0:T(8,128)(2,1)S(1)}, bf16[256,512]{1,0:T(8,128)(2,1)S(1)}, u32[]{:S(2)}, u32[]{:S(2)}) %collective-permute-start.20) | collective-permute-done | bytes 262176 | tf_op jit(solution)/shard_map/ppermute | solution.py:502
  74.6 2.0 collective-permute-start.6
  76.6 3.6 %collective-permute-done.22.refs_5_ = bf16[256,512]{1,0:T(8,128)(2,1)S(1)} collective-permute-done((bf16[256,512]{1,0:T(8,128)(2,1)S(1)}, bf16[256,512]{1,0:T(8,128)(2,1)S(1)}, u32[]{:S(2)}, u32[]{:S(2)}) %collective-permute-start.22) | collective-permute-done | bytes 262176 | tf_op jit(solution)/shard_map/ppermute | solution.py:503
  80.9 5.0 %collective-permute-done.19.refs_2_ = bf16[256,512]{1,0:T(8,128)(2,1)S(1)} collective-permute-done((bf16[256,512]{1,0:T(8,128)(2,1)S(1)}, bf16[256,512]{1,0:T(8,128)(2,1)S(1)}, u32[]{:S(2)}, u32[]{:S(2)}) %collective-permute-start.19) | collective-permute-done | bytes 262176 | tf_op jit(solution)/shard_map/ppermute | solution.py:502
  85.9 3.7 %collective-permute-done.21.refs_4_ = bf16[256,512]{1,0:T(8,128)(2,1)S(1)} collective-permute-done((bf16[256,512]{1,0:T(8,128)(2,1)S(1)}, bf16[256,512]{1,0:T(8,128)(2,1)S(1)}, u32[]{:S(2)}, u32[]{:S(2)}) %collective-permute-start.21) | collective-permute-done | bytes 262176 | tf_op jit(solution)/shard_map/ppermute | solution.py:503
  89.6 2.8 %collective-permute-start.23 = (bf16[256,512]{1,0:T(8,128)(2,1)S(1)}, bf16[256,512]{1,0:T(8,128)(2,1)S(1)}, u32[]{:S(2)}, u32[]{:S(2)}) collective-permute-start(bf16[256,512]{1,0:T(8,128)(2,1)S(1)} %select_select_fusion.1), channel_id=1, source_target_pairs={{4,0},{12,4},{8,12},{0,8},{5,1},{13,5},{9,13},{1,9},{6,2},{14,6},{... | collective-permute-start | bytes 786440 | tf_op jit(solution)/shard_map/ppermute | solution.py:505
  92.3 2.8 %collective-permute-done.6.refs_6_ = bf16[256,512]{1,0:T(8,128)(2,1)S(1)} collective-permute-done((bf16[256,512]{1,0:T(8,128)(2,1)S(1)}, bf16[256,512]{1,0:T(8,128)(2,1)S(1)}, u32[]{:S(2)}, u32[]{:S(2)}) %collective-permute-start.6) | collective-permute-done | bytes 262176 | tf_op jit(solution)/shard_map/ppermute | solution.py:505
  95.5 7.0 %project.2 = (bf16[512,512]{1,0:T(8,128)(2,1)S(1)}, bf16[1024,512]{1,0:T(8,128)(2,1)S(1)}) custom-call(s32[4]{0:T(128)S(1)} %pad_add_fusion.blocks_ref, bf16[1536,2048]{1,0:T(8,128)(2,1)} %bitcast.8, f32[2048,128]{1,0:T(8,128)S(1)} %broadcast_in_dim.42.gains_ref, bf16[256,512]{1,0:T(8,128)(2,1)S(1)} %broadcast_select_fusion.3.refs_0_, ...), custom_call_target="tpu_custom_call" | custom-call | flops 3221225472 | bytes 9961472 | tf_op jit(solution)/shard_map/project/pallas_call | solution.py:285
  102.5 2.5 %collective-permute-start.8 = (bf16[1024,512]{1,0:T(8,128)(2,1)S(1)}, bf16[1024,512]{1,0:T(8,128)(2,1)S(1)}, u32[]{:S(2)}, u32[]{:S(2)}) collective-permute-start(bf16[1024,512]{1,0:T(8,128)(2,1)S(1)} %get-tuple-element.44.refs_0_), channel_id=1, source_target_pairs={{0,16},{16,0},{1,17},{17,1},{2,18},{18,2},{3,19},{19,3},{4,20},{20... | collective-permute-start | bytes 3145736 | tf_op jit(solution)/shard_map/ppermute | solution.py:560
  105.7 7.5 %project.3 = (bf16[512,512]{1,0:T(8,128)(2,1)S(1)}, bf16[1024,512]{1,0:T(8,128)(2,1)}) custom-call(s32[4]{0:T(128)S(1)} %pad_add_fusion.blocks_ref, bf16[1536,2048]{1,0:T(8,128)(2,1)} %bitcast.9, f32[2048,128]{1,0:T(8,128)S(1)} %broadcast_in_dim.42.gains_ref, bf16[256,512]{1,0:T(8,128)(2,1)S(1)} %broadcast_select_fusion.1.refs_0_, ...), custom_call_target="tpu_custom_call" | custom-call | flops 3221225472 | bytes 9961472 | tf_op jit(solution)/shard_map/project/pallas_call | solution.py:285
  113.2 2.5 %collective-permute-start.25 = (bf16[1024,512]{1,0:T(8,128)(2,1)}, bf16[1024,512]{1,0:T(8,128)(2,1)}, u32[]{:S(2)}, u32[]{:S(2)}) collective-permute-start(bf16[1024,512]{1,0:T(8,128)(2,1)} %get-tuple-element.62.refs_2_), channel_id=1, source_target_pairs={{0,16},{16,0},{1,17},{17,1},{2,18},{18,2},{3,19},{19,3},{4,20},{20... | collective-permute-start | bytes 3145736 | tf_op jit(solution)/shard_map/ppermute | solution.py:565
  115.8 1.5 prepare.1.refs_2_.refs_3_
  117.3 11.7 %collective-permute-done.8.refs_1_ = bf16[1024,512]{1,0:T(8,128)(2,1)S(1)} collective-permute-done((bf16[1024,512]{1,0:T(8,128)(2,1)S(1)}, bf16[1024,512]{1,0:T(8,128)(2,1)S(1)}, u32[]{:S(2)}, u32[]{:S(2)}) %collective-permute-start.8) | collective-permute-done | bytes 1048608 | tf_op jit(solution)/shard_map/ppermute | solution.py:560
  129.0 6.9 %attend.3 = (bf16[256,512]{1,0:T(8,128)(2,1)S(1)}, bf16[256,512]{1,0:T(8,128)(2,1)S(1)}, bf16[256,512]{1,0:T(8,128)(2,1)S(1)}, bf16[256,512]{1,0:T(8,128)(2,1)S(...) custom-call(s32[1]{0:T(128)} %bitcast.seq_ref, ...), custom_call_target="tpu_custom_call" | custom-call | flops 1073741824 | bytes 3145728 | tf_op jit(solution)/shard_map/attend/pallas_call | solution.py:429
  140.2 2.5 %collective-permute-start.12 = (bf16[256,512]{1,0:T(8,128)(2,1)}, bf16[256,512]{1,0:T(8,128)(2,1)}, u32[]{:S(2)}, u32[]{:S(2)}) collective-permute-start(bf16[256,512]{1,0:T(8,128)(2,1)} %get-tuple-element.51), channel_id=1, source_target_pairs={{0,4},{4,12},{12,8},{8,0},{1,5},{5,13},{13,9},{9,1},{2,6},{6,14},{... | collective-permute-start | bytes 786440 | tf_op jit(solution)/shard_map/ppermute | solution.py:516
  145.2 7.3 %attend.4 = (f32[4,2,512]{2,1,0:T(2,128)S(1)}, f32[512,512]{1,0:T(8,128)S(1)}) custom-call(s32[1]{0:T(128)} %bitcast.seq_ref, s32[16]{0:T(128)S(1)} %copy-done.19, s32[16,16]{1,0:T(8,128)S(1)} %copy-done.18, bf16[512,512]{1,0:T(8,128)(2,1)S(1)} %copy-done.5, bf16[1024,512]{1,0:T(8,128)(2,1)S(1)} %get-tuple-element.44.refs_0_, ...), custom_call_target="tpu_custom_call" | custom-call | flops 1610612736 | bytes 4194304 | tf_op jit(solution)/shard_map/attend/pallas_call | solution.py:429
  152.5 5.7 %attend.5 = (bf16[256,512]{1,0:T(8,128)(2,1)S(1)}, bf16[256,512]{1,0:T(8,128)(2,1)S(1)}, bf16[256,512]{1,0:T(8,128)(2,1)S(1)}, bf16[256,512]{1,0:T(8,128)(2,1)S(...) custom-call(s32[1]{0:T(128)} %bitcast.seq_ref, ...), custom_call_target="tpu_custom_call" | custom-call | flops 536870912 | bytes 2097152 | tf_op jit(solution)/shard_map/attend/pallas_call | solution.py:429
  158.2 2.1 collective-permute-start.29
  161.3 2.3 %collective-permute-start.13 = (bf16[256,512]{1,0:T(8,128)(2,1)S(1)}, bf16[256,512]{1,0:T(8,128)(2,1)S(1)}, u32[]{:S(2)}, u32[]{:S(2)}) collective-permute-start(bf16[256,512]{1,0:T(8,128)(2,1)S(1)} %get-tuple-element.77), channel_id=1, source_target_pairs={{4,0},{8,4},{12,8},{0,12},{5,1},{9,5},{13,9},{1,13},{6,2},{10,6},{... | collective-permute-start | bytes 786440 | tf_op jit(solution)/shard_map/ppermute | solution.py:517
  163.8 3.8 %collective-permute-start.10 = (bf16[256,512]{1,0:T(8,128)(2,1)S(1)}, bf16[256,512]{1,0:T(8,128)(2,1)S(1)}, u32[]{:S(2)}, u32[]{:S(2)}) collective-permute-start(bf16[256,512]{1,0:T(8,128)(2,1)S(1)} %get-tuple-element.79), channel_id=1, source_target_pairs={{4,0},{8,4},{12,8},{0,12},{5,1},{9,5},{13,9},{1,13},{6,2},{10,6},{... | collective-permute-start | bytes 786440 | tf_op jit(solution)/shard_map/ppermute | solution.py:517
  167.7 3.4 %collective-permute-done.29.refs_9_ = bf16[256,512]{1,0:T(8,128)(2,1)S(1)} collective-permute-done((bf16[256,512]{1,0:T(8,128)(2,1)S(1)}, bf16[256,512]{1,0:T(8,128)(2,1)S(1)}, u32[]{:S(2)}, u32[]{:S(2)}) %collective-permute-start.29) | collective-permute-done | bytes 262176 | tf_op jit(solution)/shard_map/ppermute | solution.py:516
  171.3 16.7 %collective-permute-done.26.refs_5_ = bf16[256,512]{1,0:T(8,128)(2,1)S(1)} collective-permute-done((bf16[256,512]{1,0:T(8,128)(2,1)S(1)}, bf16[256,512]{1,0:T(8,128)(2,1)S(1)}, u32[]{:S(2)}, u32[]{:S(2)}) %collective-permute-start.26) | collective-permute-done | bytes 262176 | tf_op jit(solution)/shard_map/ppermute | solution.py:516
  188.1 2.1 collective-permute-start.31
  190.2 1.8 collective-permute-start.27
  192.0 7.8 %collective-permute-start.28 = (bf16[256,512]{1,0:T(8,128)(2,1)S(1)}, bf16[256,512]{1,0:T(8,128)(2,1)S(1)}, u32[]{:S(2)}, u32[]{:S(2)}) collective-permute-start(bf16[256,512]{1,0:T(8,128)(2,1)S(1)} %get-tuple-element.75), channel_id=1, source_target_pairs={{0,4},{4,8},{8,12},{12,0},{1,5},{5,9},{9,13},{13,1},{2,6},{6,10},{... | collective-permute-start | bytes 786440 | tf_op jit(solution)/shard_map/ppermute | solution.py:518
  201.0 2.0 collective-permute-done.30.refs_7_
  203.0 5.5 %collective-permute-done.31.refs_8_ = bf16[256,512]{1,0:T(8,128)(2,1)S(1)} collective-permute-done((bf16[256,512]{1,0:T(8,128)(2,1)S(1)}, bf16[256,512]{1,0:T(8,128)(2,1)S(1)}, u32[]{:S(2)}, u32[]{:S(2)}) %collective-permute-start.31) | collective-permute-done | bytes 262176 | tf_op jit(solution)/shard_map/ppermute | solution.py:518
  208.5 5.9 %collective-permute-done.27.refs_3_ = bf16[256,512]{1,0:T(8,128)(2,1)S(1)} collective-permute-done((bf16[256,512]{1,0:T(8,128)(2,1)S(1)}, bf16[256,512]{1,0:T(8,128)(2,1)S(1)}, u32[]{:S(2)}, u32[]{:S(2)}) %collective-permute-start.27) | collective-permute-done | bytes 262176 | tf_op jit(solution)/shard_map/ppermute | solution.py:517
  214.4 2.2 %place.1 = bf16[512,1024]{1,0:T(8,128)(2,1)} custom-call(s32[1]{0:T(128)} %bitcast.seq_ref, s32[16]{0:T(128)S(1)} %copy-done.19, s32[1]{0:T(128)} %bitcast.1.ends_ref, bf16[256,512]{1,0:T(8,128)(2,1)S(1)} %fusion.13.refs_0_, bf16[256,512]{1,0:T(8,128)(2,1)S(1)} %fusion.19.refs_1_, bf16[256,512]{1,0:T(8,128)(2,1)S(1)} %get-tuple-element.65.refs_2_, ...), custom_call_target="tpu_custom_call" | custom-call | flops 1048576 | bytes 3670016 | tf_op jit(solution)/shard_map/place/pallas_call | solution.py:481
  (87 shorter events, 16.4 us)
Async XLA Ops:
  0.0 29.9 %copy-start.19 = (s32[16]{0:T(128)S(1)}, s32[16]{0:T(128)}, u32[]{:S(2)}) copy-start(s32[16]{0:T(128)} %order_ref.15) | copy-start | bytes 196
  0.0 29.9 %copy-start.1 = (f32[27,512]{1,0:T(8,128)S(1)}, f32[27,512]{1,0:T(8,128)}, u32[]{:S(2)}) copy-start(f32[27,512]{1,0:T(8,128)} %taps_ref.7) | copy-start | bytes 165892
  6.3 0.7 copy-start.9
  7.0 17.2 %collective-permute-start.1 = (bf16[256,512]{1,0:T(8,128)(2,1)S(1)}, bf16[256,512]{1,0:T(8,128)(2,1)}, u32[]{:S(2)}, u32[]{:S(2)}) collective-permute-start(bf16[256,512]{1,0:T(8,128)(2,1)S(1)} %get-tuple-element.42), channel_id=1, source_target_pairs={{0,16},{1,17},{2,18},{3,19},{4,20},{5,21},{6,22},{7,23},{8,24},{9,... | collective-permute-start | bytes 786440 | tf_op jit(solution)/shard_map/ppermute | solution.py:543
  12.6 17.3 %collective-permute-start.17 = (bf16[256,1024]{1,0:T(8,128)(2,1)}, bf16[256,1024]{1,0:T(8,128)(2,1)S(1)}, u32[]{:S(2)}, u32[]{:S(2)}) collective-permute-start(bf16[256,1024]{1,0:T(8,128)(2,1)} %get-tuple-element.57), channel_id=1, source_target_pairs={{0,16},{1,17},{2,18},{3,19},{4,20},{5,21},{6,22},{7,23},{8,24},{9,... | collective-permute-start | bytes 1572872 | tf_op jit(solution)/shard_map/ppermute | solution.py:545
  20.9 27.4 %collective-permute-start.15 = (bf16[256,1024]{1,0:T(8,128)(2,1)}, bf16[256,1024]{1,0:T(8,128)(2,1)S(1)}, u32[]{:S(2)}, u32[]{:S(2)}) collective-permute-start(bf16[256,1024]{1,0:T(8,128)(2,1)} %get-tuple-element.53), channel_id=1, source_target_pairs={{0,16},{1,17},{2,18},{3,19},{4,20},{5,21},{6,22},{7,23},{8,24},{9,... | collective-permute-start | bytes 1572872 | tf_op jit(solution)/shard_map/ppermute | solution.py:545
  22.2 23.4 %collective-permute-start = (bf16[256,512]{1,0:T(8,128)(2,1)}, bf16[256,512]{1,0:T(8,128)(2,1)}, u32[]{:S(2)}, u32[]{:S(2)}) collective-permute-start(bf16[256,512]{1,0:T(8,128)(2,1)} %get-tuple-element.40), channel_id=1, source_target_pairs={{0,16},{1,17},{2,18},{3,19},{4,20},{5,21},{6,22},{7,23},{8,24},{9,... | collective-permute-start | bytes 786440 | tf_op jit(solution)/shard_map/ppermute | solution.py:543
  25.2 29.3 %collective-permute-start.3 = (bf16[256,512]{1,0:T(8,128)(2,1)S(1)}, bf16[256,512]{1,0:T(8,128)(2,1)}, u32[]{:S(2)}, u32[]{:S(2)}) collective-permute-start(bf16[256,512]{1,0:T(8,128)(2,1)S(1)} %broadcast_select_fusion.2.refs_1_), channel_id=1, source_target_pairs={{0,4},{4,8},{8,12},{12,0},{1,5},{5,9},{9,13},{13,1},{2,6},{6,10},{... | collective-permute-start | bytes 786440 | tf_op jit(solution)/shard_map/ppermute | solution.py:502
  26.8 29.0 %collective-permute-start.5 = (bf16[256,512]{1,0:T(8,128)(2,1)S(1)}, bf16[256,512]{1,0:T(8,128)(2,1)}, u32[]{:S(2)}, u32[]{:S(2)}) collective-permute-start(bf16[256,512]{1,0:T(8,128)(2,1)S(1)} %broadcast_select_fusion.2.refs_1_), channel_id=1, source_target_pairs={{4,0},{8,4},{12,8},{0,12},{5,1},{9,5},{13,9},{1,13},{6,2},{10,6},{... | collective-permute-start | bytes 786440 | tf_op jit(solution)/shard_map/ppermute | solution.py:503
  33.9 23.8 %collective-permute-start.18 = (bf16[256,512]{1,0:T(8,128)(2,1)S(1)}, bf16[256,512]{1,0:T(8,128)(2,1)S(1)}, u32[]{:S(2)}, u32[]{:S(2)}) collective-permute-start(bf16[256,512]{1,0:T(8,128)(2,1)S(1)} %get-tuple-element.60), channel_id=1, source_target_pairs={{16,0},{17,1},{18,2},{19,3},{20,4},{21,5},{22,6},{23,7},{24,8},{25... | collective-permute-start | bytes 786440 | tf_op jit(solution)/shard_map/ppermute | solution.py:555
  46.6 18.4 %collective-permute-start.2 = (bf16[256,512]{1,0:T(8,128)(2,1)S(1)}, bf16[256,512]{1,0:T(8,128)(2,1)S(1)}, u32[]{:S(2)}, u32[]{:S(2)}) collective-permute-start(bf16[256,512]{1,0:T(8,128)(2,1)S(1)} %broadcast_select_fusion.3.refs_0_), channel_id=1, source_target_pairs={{0,4},{4,8},{8,12},{12,0},{1,5},{5,9},{9,13},{13,1},{2,6},{6,10},{... | collective-permute-start | bytes 786440 | tf_op jit(solution)/shard_map/ppermute | solution.py:502
  48.2 17.1 %collective-permute-start.4 = (bf16[256,512]{1,0:T(8,128)(2,1)S(1)}, bf16[256,512]{1,0:T(8,128)(2,1)S(1)}, u32[]{:S(2)}, u32[]{:S(2)}) collective-permute-start(bf16[256,512]{1,0:T(8,128)(2,1)S(1)} %broadcast_select_fusion.3.refs_0_), channel_id=1, source_target_pairs={{4,0},{8,4},{12,8},{0,12},{5,1},{9,5},{13,9},{1,13},{6,2},{10,6},{... | collective-permute-start | bytes 786440 | tf_op jit(solution)/shard_map/ppermute | solution.py:503
  54.5 8.8 %collective-permute-start.16 = (bf16[256,512]{1,0:T(8,128)(2,1)S(1)}, bf16[256,512]{1,0:T(8,128)(2,1)S(1)}, u32[]{:S(2)}, u32[]{:S(2)}) collective-permute-start(bf16[256,512]{1,0:T(8,128)(2,1)S(1)} %get-tuple-element.56), channel_id=1, source_target_pairs={{16,0},{17,1},{18,2},{19,3},{20,4},{21,5},{22,6},{23,7},{24,8},{25... | collective-permute-start | bytes 786440 | tf_op jit(solution)/shard_map/ppermute | solution.py:555
  55.8 36.5 %collective-permute-start.7 = (bf16[256,512]{1,0:T(8,128)(2,1)S(1)}, bf16[256,512]{1,0:T(8,128)(2,1)S(1)}, u32[]{:S(2)}, u32[]{:S(2)}) collective-permute-start(bf16[256,512]{1,0:T(8,128)(2,1)S(1)} %select_select_fusion.2), channel_id=1, source_target_pairs={{4,0},{12,4},{8,12},{0,8},{5,1},{13,5},{9,13},{1,9},{6,2},{14,6},{... | collective-permute-start | bytes 786440 | tf_op jit(solution)/shard_map/ppermute | solution.py:505
  57.7 37.5 %copy-start.21 = (f32[2048]{0:T(1024)S(1)}, f32[2048]{0:T(1024)}, u32[]{:S(2)}) copy-start(f32[2048]{0:T(1024)} %param.9) | copy-start | bytes 24580
  57.7 16.9 %collective-permute-start.20 = (bf16[256,512]{1,0:T(8,128)(2,1)S(1)}, bf16[256,512]{1,0:T(8,128)(2,1)S(1)}, u32[]{:S(2)}, u32[]{:S(2)}) collective-permute-start(bf16[256,512]{1,0:T(8,128)(2,1)S(1)} %broadcast_select_fusion.refs_1_), channel_id=1, source_target_pairs={{0,4},{4,8},{8,12},{12,0},{1,5},{5,9},{9,13},{13,1},{2,6},{6,10},{... | collective-permute-start | bytes 786440 | tf_op jit(solution)/shard_map/ppermute | solution.py:502
  63.2 17.0 %collective-permute-start.22 = (bf16[256,512]{1,0:T(8,128)(2,1)S(1)}, bf16[256,512]{1,0:T(8,128)(2,1)S(1)}, u32[]{:S(2)}, u32[]{:S(2)}) collective-permute-start(bf16[256,512]{1,0:T(8,128)(2,1)S(1)} %broadcast_select_fusion.refs_1_), channel_id=1, source_target_pairs={{4,0},{8,4},{12,8},{0,12},{5,1},{9,5},{13,9},{1,13},{6,2},{10,6},{... | collective-permute-start | bytes 786440 | tf_op jit(solution)/shard_map/ppermute | solution.py:503
  65.0 20.9 %collective-permute-start.19 = (bf16[256,512]{1,0:T(8,128)(2,1)S(1)}, bf16[256,512]{1,0:T(8,128)(2,1)S(1)}, u32[]{:S(2)}, u32[]{:S(2)}) collective-permute-start(bf16[256,512]{1,0:T(8,128)(2,1)S(1)} %broadcast_select_fusion.1.refs_0_), channel_id=1, source_target_pairs={{0,4},{4,8},{8,12},{12,0},{1,5},{5,9},{9,13},{13,1},{2,6},{6,10},{... | collective-permute-start | bytes 786440 | tf_op jit(solution)/shard_map/ppermute | solution.py:502
  65.4 24.1 %collective-permute-start.21 = (bf16[256,512]{1,0:T(8,128)(2,1)S(1)}, bf16[256,512]{1,0:T(8,128)(2,1)S(1)}, u32[]{:S(2)}, u32[]{:S(2)}) collective-permute-start(bf16[256,512]{1,0:T(8,128)(2,1)S(1)} %broadcast_select_fusion.1.refs_0_), channel_id=1, source_target_pairs={{4,0},{8,4},{12,8},{0,12},{5,1},{9,5},{13,9},{1,13},{6,2},{10,6},{... | collective-permute-start | bytes 786440 | tf_op jit(solution)/shard_map/ppermute | solution.py:503
  74.6 20.6 %collective-permute-start.6 = (bf16[256,512]{1,0:T(8,128)(2,1)S(1)}, bf16[256,512]{1,0:T(8,128)(2,1)S(1)}, u32[]{:S(2)}, u32[]{:S(2)}) collective-permute-start(bf16[256,512]{1,0:T(8,128)(2,1)S(1)} %select_select_fusion.3), channel_id=1, source_target_pairs={{4,0},{12,4},{8,12},{0,8},{5,1},{13,5},{9,13},{1,9},{6,2},{14,6},{... | collective-permute-start | bytes 786440 | tf_op jit(solution)/shard_map/ppermute | solution.py:505
  80.3 24.8 %collective-permute-start.24 = (bf16[256,512]{1,0:T(8,128)(2,1)S(1)}, bf16[256,512]{1,0:T(8,128)(2,1)S(1)}, u32[]{:S(2)}, u32[]{:S(2)}) collective-permute-start(bf16[256,512]{1,0:T(8,128)(2,1)S(1)} %select_select_fusion), channel_id=1, source_target_pairs={{4,0},{12,4},{8,12},{0,8},{5,1},{13,5},{9,13},{1,9},{6,2},{14,6},{... | collective-permute-start | bytes 786440 | tf_op jit(solution)/shard_map/ppermute | solution.py:505
  89.6 16.2 %collective-permute-start.23 = (bf16[256,512]{1,0:T(8,128)(2,1)S(1)}, bf16[256,512]{1,0:T(8,128)(2,1)S(1)}, u32[]{:S(2)}, u32[]{:S(2)}) collective-permute-start(bf16[256,512]{1,0:T(8,128)(2,1)S(1)} %select_select_fusion.1), channel_id=1, source_target_pairs={{4,0},{12,4},{8,12},{0,8},{5,1},{13,5},{9,13},{1,9},{6,2},{14,6},{... | collective-permute-start | bytes 786440 | tf_op jit(solution)/shard_map/ppermute | solution.py:505
  102.5 13.3 %copy-start = (bf16[512,2048]{1,0:T(8,128)(2,1)S(1)}, bf16[512,2048]{1,0:T(8,128)(2,1)}, u32[]{:S(2)}) copy-start(bf16[512,2048]{1,0:T(8,128)(2,1)} %out_ref.1) | copy-start | bytes 6291460
  102.5 26.6 %collective-permute-start.8 = (bf16[1024,512]{1,0:T(8,128)(2,1)S(1)}, bf16[1024,512]{1,0:T(8,128)(2,1)S(1)}, u32[]{:S(2)}, u32[]{:S(2)}) collective-permute-start(bf16[1024,512]{1,0:T(8,128)(2,1)S(1)} %get-tuple-element.44.refs_0_), channel_id=1, source_target_pairs={{0,16},{16,0},{1,17},{17,1},{2,18},{18,2},{3,19},{19,3},{4,20},{20... | collective-permute-start | bytes 3145736 | tf_op jit(solution)/shard_map/ppermute | solution.py:560
  113.2 4.1 %copy-start.4 = (bf16[512,512]{1,0:T(8,128)(2,1)}, bf16[512,512]{1,0:T(8,128)(2,1)S(1)}, u32[]{:S(2)}) copy-start(bf16[512,512]{1,0:T(8,128)(2,1)S(1)} %get-tuple-element.61.query_ref) | copy-start | bytes 1572868
  113.2 15.9 %copy-start.18 = (s32[16,16]{1,0:T(8,128)S(1)}, s32[16,16]{1,0:T(8,128)}, u32[]{:S(2)}) copy-start(s32[16,16]{1,0:T(8,128)} %mask_ref.5) | copy-start | bytes 3076
  113.2 39.2 %collective-permute-start.25 = (bf16[1024,512]{1,0:T(8,128)(2,1)}, bf16[1024,512]{1,0:T(8,128)(2,1)}, u32[]{:S(2)}, u32[]{:S(2)}) collective-permute-start(bf16[1024,512]{1,0:T(8,128)(2,1)} %get-tuple-element.62.refs_2_), channel_id=1, source_target_pairs={{0,16},{16,0},{1,17},{17,1},{2,18},{18,2},{3,19},{19,3},{4,20},{20... | collective-permute-start | bytes 3145736 | tf_op jit(solution)/shard_map/ppermute | solution.py:565
  129.0 6.9 %copy-start.2 = (bf16[1024,512]{1,0:T(8,128)(2,1)}, bf16[1024,512]{1,0:T(8,128)(2,1)S(1)}, u32[]{:S(2)}) copy-start(bf16[1024,512]{1,0:T(8,128)(2,1)S(1)} %collective-permute-done.8.refs_1_) | copy-start | bytes 3145732
  138.8 0.7 copy-start.16
  140.2 20.0 %collective-permute-start.12 = (bf16[256,512]{1,0:T(8,128)(2,1)}, bf16[256,512]{1,0:T(8,128)(2,1)}, u32[]{:S(2)}, u32[]{:S(2)}) collective-permute-start(bf16[256,512]{1,0:T(8,128)(2,1)} %get-tuple-element.51), channel_id=1, source_target_pairs={{0,4},{4,12},{12,8},{8,0},{1,5},{5,13},{13,9},{9,1},{2,6},{6,14},{... | collective-permute-start | bytes 786440 | tf_op jit(solution)/shard_map/ppermute | solution.py:516
  142.8 20.9 %collective-permute-start.9 = (bf16[256,512]{1,0:T(8,128)(2,1)}, bf16[256,512]{1,0:T(8,128)(2,1)S(1)}, u32[]{:S(2)}, u32[]{:S(2)}) collective-permute-start(bf16[256,512]{1,0:T(8,128)(2,1)} %copy-done.20), channel_id=1, source_target_pairs={{0,4},{4,12},{12,8},{8,0},{1,5},{5,13},{13,9},{9,1},{2,6},{6,14},{... | collective-permute-start | bytes 786440 | tf_op jit(solution)/shard_map/ppermute | solution.py:516
  142.9 1.2 copy-start.3
  144.1 1.0 copy-start.5
  152.5 7.8 %copy-start.15 = (bf16[256,512]{1,0:T(8,128)(2,1)S(1)}, bf16[256,512]{1,0:T(8,128)(2,1)}, u32[]{:S(2)}) copy-start(bf16[256,512]{1,0:T(8,128)(2,1)} %copy-done.14) | copy-start | bytes 786436
  152.5 7.8 %copy-start.17 = (bf16[256,512]{1,0:T(8,128)(2,1)S(1)}, bf16[256,512]{1,0:T(8,128)(2,1)}, u32[]{:S(2)}) copy-start(bf16[256,512]{1,0:T(8,128)(2,1)} %copy-done.16) | copy-start | bytes 786436
  152.5 11.2 %copy-start.11 = (bf16[256,512]{1,0:T(8,128)(2,1)S(1)}, bf16[256,512]{1,0:T(8,128)(2,1)}, u32[]{:S(2)}) copy-start(bf16[256,512]{1,0:T(8,128)(2,1)} %copy-done.10) | copy-start | bytes 786436
  152.5 11.2 %copy-start.13 = (bf16[256,512]{1,0:T(8,128)(2,1)S(1)}, bf16[256,512]{1,0:T(8,128)(2,1)}, u32[]{:S(2)}) copy-start(bf16[256,512]{1,0:T(8,128)(2,1)} %copy-done.12) | copy-start | bytes 786436
  158.2 12.9 %collective-permute-start.29 = (bf16[256,512]{1,0:T(8,128)(2,1)S(1)}, bf16[256,512]{1,0:T(8,128)(2,1)S(1)}, u32[]{:S(2)}, u32[]{:S(2)}) collective-permute-start(bf16[256,512]{1,0:T(8,128)(2,1)S(1)} %get-tuple-element.71), channel_id=1, source_target_pairs={{0,4},{4,12},{12,8},{8,0},{1,5},{5,13},{13,9},{9,1},{2,6},{6,14},{... | collective-permute-start | bytes 786440 | tf_op jit(solution)/shard_map/ppermute | solution.py:516
  161.3 38.4 %copy-start.7 = (bf16[256,512]{1,0:T(8,128)(2,1)S(1)}, bf16[256,512]{1,0:T(8,128)(2,1)}, u32[]{:S(2)}) copy-start(bf16[256,512]{1,0:T(8,128)(2,1)} %copy-done.6) | copy-start | bytes 786436
  161.3 26.8 %collective-permute-start.13 = (bf16[256,512]{1,0:T(8,128)(2,1)S(1)}, bf16[256,512]{1,0:T(8,128)(2,1)S(1)}, u32[]{:S(2)}, u32[]{:S(2)}) collective-permute-start(bf16[256,512]{1,0:T(8,128)(2,1)S(1)} %get-tuple-element.77), channel_id=1, source_target_pairs={{4,0},{8,4},{12,8},{0,12},{5,1},{9,5},{13,9},{1,13},{6,2},{10,6},{... | collective-permute-start | bytes 786440 | tf_op jit(solution)/shard_map/ppermute | solution.py:517
  163.6 26.6 %collective-permute-start.14 = (bf16[256,512]{1,0:T(8,128)(2,1)S(1)}, bf16[256,512]{1,0:T(8,128)(2,1)S(1)}, u32[]{:S(2)}, u32[]{:S(2)}) collective-permute-start(bf16[256,512]{1,0:T(8,128)(2,1)S(1)} %get-tuple-element.78), channel_id=1, source_target_pairs={{0,4},{4,8},{8,12},{12,0},{1,5},{5,9},{9,13},{13,1},{2,6},{6,10},{... | collective-permute-start | bytes 786440 | tf_op jit(solution)/shard_map/ppermute | solution.py:518
  163.6 24.3 %collective-permute-start.26 = (bf16[256,512]{1,0:T(8,128)(2,1)S(1)}, bf16[256,512]{1,0:T(8,128)(2,1)S(1)}, u32[]{:S(2)}, u32[]{:S(2)}) collective-permute-start(bf16[256,512]{1,0:T(8,128)(2,1)S(1)} %get-tuple-element.67), channel_id=1, source_target_pairs={{0,4},{4,12},{12,8},{8,0},{1,5},{5,13},{13,9},{9,1},{2,6},{6,14},{... | collective-permute-start | bytes 786440 | tf_op jit(solution)/shard_map/ppermute | solution.py:516
  163.8 28.2 %collective-permute-start.10 = (bf16[256,512]{1,0:T(8,128)(2,1)S(1)}, bf16[256,512]{1,0:T(8,128)(2,1)S(1)}, u32[]{:S(2)}, u32[]{:S(2)}) collective-permute-start(bf16[256,512]{1,0:T(8,128)(2,1)S(1)} %get-tuple-element.79), channel_id=1, source_target_pairs={{4,0},{8,4},{12,8},{0,12},{5,1},{9,5},{13,9},{1,13},{6,2},{10,6},{... | collective-permute-start | bytes 786440 | tf_op jit(solution)/shard_map/ppermute | solution.py:517
  171.1 29.8 %collective-permute-start.11 = (bf16[256,512]{1,0:T(8,128)(2,1)S(1)}, bf16[256,512]{1,0:T(8,128)(2,1)S(1)}, u32[]{:S(2)}, u32[]{:S(2)}) collective-permute-start(bf16[256,512]{1,0:T(8,128)(2,1)S(1)} %get-tuple-element.80), channel_id=1, source_target_pairs={{0,4},{4,8},{8,12},{12,0},{1,5},{5,9},{9,13},{13,1},{2,6},{6,10},{... | collective-permute-start | bytes 786440 | tf_op jit(solution)/shard_map/ppermute | solution.py:518
  188.0 15.0 %collective-permute-start.30 = (bf16[256,512]{1,0:T(8,128)(2,1)S(1)}, bf16[256,512]{1,0:T(8,128)(2,1)S(1)}, u32[]{:S(2)}, u32[]{:S(2)}) collective-permute-start(bf16[256,512]{1,0:T(8,128)(2,1)S(1)} %get-tuple-element.74), channel_id=1, source_target_pairs={{4,0},{8,4},{12,8},{0,12},{5,1},{9,5},{13,9},{1,13},{6,2},{10,6},{... | collective-permute-start | bytes 786440 | tf_op jit(solution)/shard_map/ppermute | solution.py:517
  188.1 20.4 %collective-permute-start.31 = (bf16[256,512]{1,0:T(8,128)(2,1)S(1)}, bf16[256,512]{1,0:T(8,128)(2,1)S(1)}, u32[]{:S(2)}, u32[]{:S(2)}) collective-permute-start(bf16[256,512]{1,0:T(8,128)(2,1)S(1)} %get-tuple-element.73), channel_id=1, source_target_pairs={{0,4},{4,8},{8,12},{12,0},{1,5},{5,9},{9,13},{13,1},{2,6},{6,10},{... | collective-permute-start | bytes 786440 | tf_op jit(solution)/shard_map/ppermute | solution.py:518
  190.2 24.2 %collective-permute-start.27 = (bf16[256,512]{1,0:T(8,128)(2,1)S(1)}, bf16[256,512]{1,0:T(8,128)(2,1)S(1)}, u32[]{:S(2)}, u32[]{:S(2)}) collective-permute-start(bf16[256,512]{1,0:T(8,128)(2,1)S(1)} %get-tuple-element.76), channel_id=1, source_target_pairs={{4,0},{8,4},{12,8},{0,12},{5,1},{9,5},{13,9},{1,13},{6,2},{10,6},{... | collective-permute-start | bytes 786440 | tf_op jit(solution)/shard_map/ppermute | solution.py:517
  192.0 22.4 %collective-permute-start.28 = (bf16[256,512]{1,0:T(8,128)(2,1)S(1)}, bf16[256,512]{1,0:T(8,128)(2,1)S(1)}, u32[]{:S(2)}, u32[]{:S(2)}) collective-permute-start(bf16[256,512]{1,0:T(8,128)(2,1)S(1)} %get-tuple-element.75), channel_id=1, source_target_pairs={{0,4},{4,8},{8,12},{12,0},{1,5},{5,9},{9,13},{13,1},{2,6},{6,10},{... | collective-permute-start | bytes 786440 | tf_op jit(solution)/shard_map/ppermute | solution.py:518
  (6 other events, 4.2 us)

commit v8 on v7

--- a/solution.py
+++ b/solution.py
@@ -104,7 +104,7 @@
         slots_ref, taps_scr, packed = refs
         source_ref = tokens_ref
     else:
-        source_ref, slots_ref, taps_scr, packed, arrived, taps_in, taps_arrived = refs
+        copy_ref, slots_ref, taps_scr, packed, source_ref, arrived, taps_in, taps_arrived, left = refs
     channels, tokens = packed.shape
     tiles_dev = tokens // TILE
     per_frame = FRAME // TILE
@@ -169,6 +169,10 @@
     else:
         each = steps // CHUNKS
 
+        def leaving(begin, index):
+            block = pl.ds(begin, each * GROUP)
+            return pltpu.make_async_copy(source_ref.at[block], copy_ref.at[block], left.at[index])
+
         def chunk(index, carry):
             begin = index * each * GROUP
             pltpu.make_async_copy(
@@ -176,10 +180,13 @@
                 source_ref.at[pl.ds(begin, each * GROUP)],
                 arrived.at[index],
             ).wait()
+            leaving(begin, index).start()
             later = functools.partial(advance, base=begin)
             return lax.fori_loop(0, each, later, carry, unroll=2)
 
         lax.fori_loop(0, CHUNKS, chunk, 0)
+        for index in range(CHUNKS):
+            leaving(index * each * GROUP, index).wait()
     keep_ref[...] = packed[:, : tokens // 2]
     send_ref[...] = packed[:, tokens // 2 :]
 
@@ -190,6 +197,7 @@
     packed_shape = jax.ShapeDtypeStruct((channels, count // 2), jnp.bfloat16)
     with_before = part is not None
     out_shape = [packed_shape, packed_shape]
+    out_specs = [vmem_spec()] * 2
     scratch = [
         pltpu.SMEM((count // TILE,), jnp.int32),
         pltpu.VMEM((channels, 128), jnp.float32),
@@ -198,18 +206,21 @@
     in_specs = [smem_spec(), smem_spec(), vmem_spec(), vmem_spec(), vmem_spec()]
     if not with_before:
         in_specs = [smem_spec(), smem_spec(), off_chip_spec(), off_chip_spec()]
-        tokens, conv_taps, stripe_order = (off_chip(a) for a in (tokens, conv_taps, stripe_order))
+        tokens = off_chip(tokens)
         sum_shape = jax.ShapeDtypeStruct((channels, count), jnp.float32)
-        out_shape = [sum_shape] + out_shape + [jax.ShapeDtypeStruct((channels, count), jnp.bfloat16)]
+        out_shape = [sum_shape] + out_shape + [pltpu.HBM((channels, count), jnp.bfloat16)]
+        out_specs = [vmem_spec()] * 3 + [off_chip_spec()]
         scratch += [
+            pltpu.VMEM((channels, count), jnp.bfloat16),
             pltpu.SemaphoreType.DMA((CHUNKS,)),
             pltpu.VMEM((TAPS, channels), jnp.float32),
             pltpu.SemaphoreType.DMA,
+            pltpu.SemaphoreType.DMA((CHUNKS,)),
         ]
     return pl.pallas_call(
         functools.partial(conv_body, with_before, piece * channels),
         in_specs=in_specs,
-        out_specs=[vmem_spec()] * len(out_shape),
+        out_specs=out_specs,
         scratch_shapes=scratch,
         out_shape=out_shape,
         compiler_params=params(),
@@ -248,7 +259,8 @@
 def project_body(blocks_ref, weight_hbm, gains_ref, *refs):
     shards, (query_ref, pair_ref, weight_ref, tokens_ref, arrived) = refs[:-5], refs[-5:]
     copies = fetches(weight_hbm, weight_ref, arrived)
-    for copy in copies[:2]:
+    ahead, behind = copies[: len(copies) // 2], copies[len(copies) // 2 :]
+    for copy in ahead:
         copy.start()
     width, tokens = shards[0].shape
     cols = query_ref.shape[0]
@@ -264,17 +276,23 @@
             gain = jnp.concatenate([gains_ref[there, :]] * (tokens // 128), axis=1)
             tokens_ref[there, :] = (wide * gain).astype(jnp.bfloat16)
     inverse = lax.rsqrt(squares / (len(shards) * width) + EPSILON)
-    rows = weight_ref.shape[0] // len(copies)
-    for index, copy in enumerate(copies):
-        copy.wait()
-        if index + 2 < len(copies):
-            copies[index + 2].start()
-        here = slice(index * rows, (index + 1) * rows)
+    rows = 256
+    halfway = weight_ref.shape[0] // 2
+    for first in range(0, weight_ref.shape[0], rows):
+        if first == 0:
+            for copy in ahead:
+                copy.wait()
+            for copy in behind:
+                copy.start()
+        if first == halfway:
+            for copy in behind:
+                copy.wait()
+        here = slice(first, first + rows)
         total = jnp.dot(weight_ref[here, :], tokens_ref[...], preferred_element_type=jnp.float32)
-        if index * rows < cols:
+        if first < cols:
             query_ref[here, :] = (total * (inverse * (LOG2E / math.sqrt(HEAD)))).astype(jnp.bfloat16)
         else:
-            there = slice(index * rows - cols, (index + 1) * rows - cols)
+            there = slice(first - cols, first - cols + rows)
             pair_ref[there, :] = (total * inverse).astype(jnp.bfloat16)
 
 
@@ -522,6 +540,8 @@
 def per_device_fast(
     clip_tokens, conv_taps, norm_gain, qkv_weight, out_weight, tile_mask, stripe_order
 ):
+    tables = (conv_taps, stripe_order, tile_mask)
+    conv_taps, stripe_order, tile_mask = (off_chip(table) for table in tables)
     seq = lax.axis_index("seq")
     here = lax.axis_index("tp")
     seq_here = seq.astype(jnp.int32)[None]

time: 217 us -> 217 us (level)
    unnamed x44 -> x38, local copies, waits for them, and re-layouts: 7.94 us -> 7.25 us
where the time goes in v8:
time: 217 us; the launch traced here: 216 us
  waiting for transfers between devices  83.4 us (38%)
  starting transfers between devices  61.2 us (28%)
  Pallas kernels  58.4 us (27%)
  local copies, waits for them, and re-layouts  7.57 us (3%)
  other arithmetic  5.05 us (2%)
    pallas_call x4, Pallas kernels, conv_call(): pl.pallas_call(functools.partial(conv_body, with_before, piece * channels...  20.1 us
    ppermute x4, waiting for transfers between devices, reduce_blocks(): across = lax.ppermute(sent, 'tp', FOLDED)  20 us
    pallas_call x3, Pallas kernels, attend_call(): pl.pallas_call(functools.partial(attend_body, chunk, tuple((s for _, s in...  19.9 us
    pallas_call x2, Pallas kernels, project_call(): pl.pallas_call(project_body, in_specs=[smem_spec(), off_chip_spec()] + [v...  14.5 us
    ppermute x1, waiting for transfers between devices, per_device_fast(): peer_a = lax.ppermute(pair_a, 'seq', swap)  11.8 us
    ppermute x4, waiting for transfers between devices, gather_blocks(): before = lax.ppermute(block, 'tp', FORWARD)  10.4 us
    ppermute x2, waiting for transfers between devices, per_device_fast(): got = lax.ppermute(send, 'seq', [(0, 1)])  10.1 us
    ppermute x4, starting transfers between devices, gather_blocks(): after = lax.ppermute(block, 'tp', BACKWARD)  9.64 us
  transfers between devices with their start and end apart: 32, of which 15 were waited for; matrix products, arithmetic and copies ran while one was open for 2% of the time, Pallas kernels for 23%

profile of v8, /device:TPU:0, one launch (start us, length us, event | category | flops | bytes accessed | tf_op | source)
XLA Modules:
  0.0 216.0 jit_solution(17114843848591224026)
XLA Ops:
  0.0 5.5 %conv.5 = (f32[256,1024]{1,0:T(8,128)S(1)}, bf16[256,512]{1,0:T(8,128)(2,1)S(1)}, bf16[256,512]{1,0:T(8,128)(2,1)S(1)}, bf16[256,1024]{1,0:T(8,128)(2,1)}) custom-call(s32[1]{0:T(128)} %bitcast.seq_ref, s32[16]{0:T(128)} %order_ref.15, bf16[512,1024]{1,0:T(8,128)(2,1)} %tokens_ref.3, f32[27,512]{1,0:T(8,128)} %taps_ref.7), custom_call_target="tpu_custom_call" | custom-call | flops 7077888 | bytes 2097152 | tf_op jit(solution)/shard_map/conv/pallas_call | solution.py:220
  5.5 5.6 %collective-permute-start.1 = (bf16[256,512]{1,0:T(8,128)(2,1)S(1)}, bf16[256,512]{1,0:T(8,128)(2,1)}, u32[]{:S(2)}, u32[]{:S(2)}) collective-permute-start(bf16[256,512]{1,0:T(8,128)(2,1)S(1)} %get-tuple-element.42), channel_id=1, source_target_pairs={{0,16},{1,17},{2,18},{3,19},{4,20},{5,21},{6,22},{7,23},{8,24},{9,... | collective-permute-start | bytes 786440 | tf_op jit(solution)/shard_map/ppermute | solution.py:563
  11.1 1.3 collective-permute-start.17
  12.4 6.1 %conv.4 = (f32[256,1024]{1,0:T(8,128)S(1)}, bf16[256,512]{1,0:T(8,128)(2,1)S(1)}, bf16[256,512]{1,0:T(8,128)(2,1)}, bf16[256,1024]{1,0:T(8,128)(2,1)}) custom-call(s32[1]{0:T(128)} %bitcast.seq_ref, s32[16]{0:T(128)} %order_ref.15, bf16[512,1024]{1,0:T(8,128)(2,1)} %tokens_ref.3, f32[27,512]{1,0:T(8,128)} %taps_ref.7), custom_call_target="tpu_custom_call" | custom-call | flops 7077888 | bytes 2097152 | tf_op jit(solution)/shard_map/conv/pallas_call | solution.py:220
  19.2 1.3 collective-permute-start.15
  20.6 2.0 collective-permute-start
  23.6 1.6 collective-permute-start.3
  25.2 2.2 %collective-permute-start.5 = (bf16[256,512]{1,0:T(8,128)(2,1)S(1)}, bf16[256,512]{1,0:T(8,128)(2,1)}, u32[]{:S(2)}, u32[]{:S(2)}) collective-permute-start(bf16[256,512]{1,0:T(8,128)(2,1)S(1)} %broadcast_select_fusion.2.refs_1_), channel_id=1, source_target_pairs={{4,0},{8,4},{12,8},{0,12},{5,1},{9,5},{13,9},{1,13},{6,2},{10,6},{... | collective-permute-start | bytes 786440 | tf_op jit(solution)/shard_map/ppermute | solution.py:521
  28.4 4.3 %conv.7 = (bf16[256,512]{1,0:T(8,128)(2,1)S(1)}, bf16[256,512]{1,0:T(8,128)(2,1)S(1)}) custom-call(s32[1]{0:T(128)} %bitcast.seq_ref, s32[16]{0:T(128)} %order_ref.15, bf16[256,1024]{1,0:T(8,128)(2,1)S(1)} %collective-permute-done.17.tokens_ref, f32[27,512]{1,0:T(8,128)} %taps_ref.7, f32[256,1024]{1,0:T(8,128)S(1)} %get-tuple-element.58.part_ref), custom_call_target="tpu_custom_call" | custom-call | flops 7077888 | bytes 2097152 | tf_op jit(solution)/shard_map/conv/pallas_call | solution.py:220
  32.6 1.3 collective-permute-start.18
  33.9 10.1 %collective-permute-done = bf16[256,512]{1,0:T(8,128)(2,1)} collective-permute-done((bf16[256,512]{1,0:T(8,128)(2,1)}, bf16[256,512]{1,0:T(8,128)(2,1)}, u32[]{:S(2)}, u32[]{:S(2)}) %collective-permute-start) | collective-permute-done | bytes 262176 | tf_op jit(solution)/shard_map/ppermute | solution.py:563
  45.1 1.6 collective-permute-start.2
  46.7 2.2 %collective-permute-start.4 = (bf16[256,512]{1,0:T(8,128)(2,1)S(1)}, bf16[256,512]{1,0:T(8,128)(2,1)S(1)}, u32[]{:S(2)}, u32[]{:S(2)}) collective-permute-start(bf16[256,512]{1,0:T(8,128)(2,1)S(1)} %broadcast_select_fusion.3.refs_0_), channel_id=1, source_target_pairs={{4,0},{8,4},{12,8},{0,12},{5,1},{9,5},{13,9},{1,13},{6,2},{10,6},{... | collective-permute-start | bytes 786440 | tf_op jit(solution)/shard_map/ppermute | solution.py:521
  49.0 4.3 %conv.6 = (bf16[256,512]{1,0:T(8,128)(2,1)S(1)}, bf16[256,512]{1,0:T(8,128)(2,1)S(1)}) custom-call(s32[1]{0:T(128)} %bitcast.seq_ref, s32[16]{0:T(128)} %order_ref.15, bf16[256,1024]{1,0:T(8,128)(2,1)S(1)} %collective-permute-done.15.tokens_ref, f32[27,512]{1,0:T(8,128)} %taps_ref.7, f32[256,1024]{1,0:T(8,128)S(1)} %get-tuple-element.54.part_ref), custom_call_target="tpu_custom_call" | custom-call | flops 7077888 | bytes 2097152 | tf_op jit(solution)/shard_map/conv/pallas_call | solution.py:220
  53.2 1.3 collective-permute-start.16
  54.6 1.8 collective-permute-start.7
  56.8 5.2 %collective-permute-done.16 = bf16[256,512]{1,0:T(8,128)(2,1)S(1)} collective-permute-done((bf16[256,512]{1,0:T(8,128)(2,1)S(1)}, bf16[256,512]{1,0:T(8,128)(2,1)S(1)}, u32[]{:S(2)}, u32[]{:S(2)}) %collective-permute-start.16) | collective-permute-done | bytes 262176 | tf_op jit(solution)/shard_map/ppermute | solution.py:575
  62.0 1.7 collective-permute-start.22
  64.2 3.5 %collective-permute-start.21 = (bf16[256,512]{1,0:T(8,128)(2,1)S(1)}, bf16[256,512]{1,0:T(8,128)(2,1)S(1)}, u32[]{:S(2)}, u32[]{:S(2)}) collective-permute-start(bf16[256,512]{1,0:T(8,128)(2,1)S(1)} %broadcast_select_fusion.1.refs_0_), channel_id=1, source_target_pairs={{4,0},{8,4},{12,8},{0,12},{5,1},{9,5},{13,9},{1,13},{6,2},{10,6},{... | collective-permute-start | bytes 786440 | tf_op jit(solution)/shard_map/ppermute | solution.py:521
  67.7 5.4 %collective-permute-done.20.refs_3_ = bf16[256,512]{1,0:T(8,128)(2,1)S(1)} collective-permute-done((bf16[256,512]{1,0:T(8,128)(2,1)S(1)}, bf16[256,512]{1,0:T(8,128)(2,1)S(1)}, u32[]{:S(2)}, u32[]{:S(2)}) %collective-permute-start.20) | collective-permute-done | bytes 262176 | tf_op jit(solution)/shard_map/ppermute | solution.py:520
  73.0 1.7 collective-permute-start.6
  74.8 3.9 %collective-permute-done.22.refs_5_ = bf16[256,512]{1,0:T(8,128)(2,1)S(1)} collective-permute-done((bf16[256,512]{1,0:T(8,128)(2,1)S(1)}, bf16[256,512]{1,0:T(8,128)(2,1)S(1)}, u32[]{:S(2)}, u32[]{:S(2)}) %collective-permute-start.22) | collective-permute-done | bytes 262176 | tf_op jit(solution)/shard_map/ppermute | solution.py:521
  79.3 5.0 %collective-permute-done.19.refs_2_ = bf16[256,512]{1,0:T(8,128)(2,1)S(1)} collective-permute-done((bf16[256,512]{1,0:T(8,128)(2,1)S(1)}, bf16[256,512]{1,0:T(8,128)(2,1)S(1)}, u32[]{:S(2)}, u32[]{:S(2)}) %collective-permute-start.19) | collective-permute-done | bytes 262176 | tf_op jit(solution)/shard_map/ppermute | solution.py:520
  84.3 3.7 %collective-permute-done.21.refs_4_ = bf16[256,512]{1,0:T(8,128)(2,1)S(1)} collective-permute-done((bf16[256,512]{1,0:T(8,128)(2,1)S(1)}, bf16[256,512]{1,0:T(8,128)(2,1)S(1)}, u32[]{:S(2)}, u32[]{:S(2)}) %collective-permute-start.21) | collective-permute-done | bytes 262176 | tf_op jit(solution)/shard_map/ppermute | solution.py:521
  88.0 2.8 %collective-permute-start.23 = (bf16[256,512]{1,0:T(8,128)(2,1)S(1)}, bf16[256,512]{1,0:T(8,128)(2,1)S(1)}, u32[]{:S(2)}, u32[]{:S(2)}) collective-permute-start(bf16[256,512]{1,0:T(8,128)(2,1)S(1)} %select_select_fusion.1), channel_id=1, source_target_pairs={{4,0},{12,4},{8,12},{0,8},{5,1},{13,5},{9,13},{1,9},{6,2},{14,6},{... | collective-permute-start | bytes 786440 | tf_op jit(solution)/shard_map/ppermute | solution.py:523
  90.8 2.8 %collective-permute-done.6.refs_6_ = bf16[256,512]{1,0:T(8,128)(2,1)S(1)} collective-permute-done((bf16[256,512]{1,0:T(8,128)(2,1)S(1)}, bf16[256,512]{1,0:T(8,128)(2,1)S(1)}, u32[]{:S(2)}, u32[]{:S(2)}) %collective-permute-start.6) | collective-permute-done | bytes 262176 | tf_op jit(solution)/shard_map/ppermute | solution.py:523
  93.9 7.0 %project.2 = (bf16[512,512]{1,0:T(8,128)(2,1)S(1)}, bf16[1024,512]{1,0:T(8,128)(2,1)S(1)}) custom-call(s32[4]{0:T(128)S(1)} %pad_add_fusion.blocks_ref, bf16[1536,2048]{1,0:T(8,128)(2,1)} %bitcast.8, f32[2048,128]{1,0:T(8,128)S(1)} %broadcast_in_dim.42.gains_ref, bf16[256,512]{1,0:T(8,128)(2,1)S(1)} %broadcast_select_fusion.3.refs_0_, ...), custom_call_target="tpu_custom_call" | custom-call | flops 3221225472 | bytes 9961472 | tf_op jit(solution)/shard_map/project/pallas_call | solution.py:303
  101.0 2.5 %collective-permute-start.8 = (bf16[1024,512]{1,0:T(8,128)(2,1)S(1)}, bf16[1024,512]{1,0:T(8,128)(2,1)S(1)}, u32[]{:S(2)}, u32[]{:S(2)}) collective-permute-start(bf16[1024,512]{1,0:T(8,128)(2,1)S(1)} %get-tuple-element.44.refs_0_), channel_id=1, source_target_pairs={{0,16},{16,0},{1,17},{17,1},{2,18},{18,2},{3,19},{19,3},{4,20},{20... | collective-permute-start | bytes 3145736 | tf_op jit(solution)/shard_map/ppermute | solution.py:580
  104.2 7.5 %project.3 = (bf16[512,512]{1,0:T(8,128)(2,1)S(1)}, bf16[1024,512]{1,0:T(8,128)(2,1)}) custom-call(s32[4]{0:T(128)S(1)} %pad_add_fusion.blocks_ref, bf16[1536,2048]{1,0:T(8,128)(2,1)} %bitcast.9, f32[2048,128]{1,0:T(8,128)S(1)} %broadcast_in_dim.42.gains_ref, bf16[256,512]{1,0:T(8,128)(2,1)S(1)} %broadcast_select_fusion.1.refs_0_, ...), custom_call_target="tpu_custom_call" | custom-call | flops 3221225472 | bytes 9961472 | tf_op jit(solution)/shard_map/project/pallas_call | solution.py:303
  111.7 2.5 %collective-permute-start.25 = (bf16[1024,512]{1,0:T(8,128)(2,1)}, bf16[1024,512]{1,0:T(8,128)(2,1)}, u32[]{:S(2)}, u32[]{:S(2)}) collective-permute-start(bf16[1024,512]{1,0:T(8,128)(2,1)} %get-tuple-element.62.refs_2_), channel_id=1, source_target_pairs={{0,16},{16,0},{1,17},{17,1},{2,18},{18,2},{3,19},{19,3},{4,20},{20... | collective-permute-start | bytes 3145736 | tf_op jit(solution)/shard_map/ppermute | solution.py:585
  114.2 1.5 prepare.1.refs_2_.refs_3_
  115.8 11.8 %collective-permute-done.8.refs_1_ = bf16[1024,512]{1,0:T(8,128)(2,1)S(1)} collective-permute-done((bf16[1024,512]{1,0:T(8,128)(2,1)S(1)}, bf16[1024,512]{1,0:T(8,128)(2,1)S(1)}, u32[]{:S(2)}, u32[]{:S(2)}) %collective-permute-start.8) | collective-permute-done | bytes 1048608 | tf_op jit(solution)/shard_map/ppermute | solution.py:580
  127.5 7.0 %attend.3 = (bf16[256,512]{1,0:T(8,128)(2,1)S(1)}, bf16[256,512]{1,0:T(8,128)(2,1)S(1)}, bf16[256,512]{1,0:T(8,128)(2,1)S(1)}, bf16[256,512]{1,0:T(8,128)(2,1)S(...) custom-call(s32[1]{0:T(128)} %bitcast.seq_ref, ...), custom_call_target="tpu_custom_call" | custom-call | flops 1073741824 | bytes 3145728 | tf_op jit(solution)/shard_map/attend/pallas_call | solution.py:447
  138.8 2.5 %collective-permute-start.12 = (bf16[256,512]{1,0:T(8,128)(2,1)}, bf16[256,512]{1,0:T(8,128)(2,1)}, u32[]{:S(2)}, u32[]{:S(2)}) collective-permute-start(bf16[256,512]{1,0:T(8,128)(2,1)} %get-tuple-element.51), channel_id=1, source_target_pairs={{0,4},{4,12},{12,8},{8,0},{1,5},{5,13},{13,9},{9,1},{2,6},{6,14},{... | collective-permute-start | bytes 786440 | tf_op jit(solution)/shard_map/ppermute | solution.py:534
  143.6 7.3 %attend.4 = (f32[4,2,512]{2,1,0:T(2,128)S(1)}, f32[512,512]{1,0:T(8,128)S(1)}) custom-call(s32[1]{0:T(128)} %bitcast.seq_ref, s32[16]{0:T(128)} %order_ref.15, s32[16,16]{1,0:T(8,128)} %mask_ref.5, bf16[512,512]{1,0:T(8,128)(2,1)S(1)} %copy-done.4, bf16[1024,512]{1,0:T(8,128)(2,1)S(1)} %get-tuple-element.44.refs_0_, bf16[1024,512]{1,0:T(8,128)(2,1)S(1)} %copy-done.2, ...), custom_call_target="tpu_custom_call" | custom-call | flops 1610612736 | bytes 4194304 | tf_op jit(solution)/shard_map/attend/pallas_call | solution.py:447
  150.9 5.7 %attend.5 = (bf16[256,512]{1,0:T(8,128)(2,1)S(1)}, bf16[256,512]{1,0:T(8,128)(2,1)S(1)}, bf16[256,512]{1,0:T(8,128)(2,1)S(1)}, bf16[256,512]{1,0:T(8,128)(2,1)S(...) custom-call(s32[1]{0:T(128)} %bitcast.seq_ref, ...), custom_call_target="tpu_custom_call" | custom-call | flops 536870912 | bytes 2097152 | tf_op jit(solution)/shard_map/attend/pallas_call | solution.py:447
  156.6 2.4 %collective-permute-start.29 = (bf16[256,512]{1,0:T(8,128)(2,1)S(1)}, bf16[256,512]{1,0:T(8,128)(2,1)S(1)}, u32[]{:S(2)}, u32[]{:S(2)}) collective-permute-start(bf16[256,512]{1,0:T(8,128)(2,1)S(1)} %get-tuple-element.71), channel_id=1, source_target_pairs={{0,4},{4,12},{12,8},{8,0},{1,5},{5,13},{13,9},{9,1},{2,6},{6,14},{... | collective-permute-start | bytes 786440 | tf_op jit(solution)/shard_map/ppermute | solution.py:534
  160.1 2.3 %collective-permute-start.13 = (bf16[256,512]{1,0:T(8,128)(2,1)S(1)}, bf16[256,512]{1,0:T(8,128)(2,1)S(1)}, u32[]{:S(2)}, u32[]{:S(2)}) collective-permute-start(bf16[256,512]{1,0:T(8,128)(2,1)S(1)} %get-tuple-element.77), channel_id=1, source_target_pairs={{4,0},{8,4},{12,8},{0,12},{5,1},{9,5},{13,9},{1,13},{6,2},{10,6},{... | collective-permute-start | bytes 786440 | tf_op jit(solution)/shard_map/ppermute | solution.py:535
  162.7 3.8 %collective-permute-start.10 = (bf16[256,512]{1,0:T(8,128)(2,1)S(1)}, bf16[256,512]{1,0:T(8,128)(2,1)S(1)}, u32[]{:S(2)}, u32[]{:S(2)}) collective-permute-start(bf16[256,512]{1,0:T(8,128)(2,1)S(1)} %get-tuple-element.79), channel_id=1, source_target_pairs={{4,0},{8,4},{12,8},{0,12},{5,1},{9,5},{13,9},{1,13},{6,2},{10,6},{... | collective-permute-start | bytes 786440 | tf_op jit(solution)/shard_map/ppermute | solution.py:535
  166.5 3.3 %collective-permute-done.29.refs_9_ = bf16[256,512]{1,0:T(8,128)(2,1)S(1)} collective-permute-done((bf16[256,512]{1,0:T(8,128)(2,1)S(1)}, bf16[256,512]{1,0:T(8,128)(2,1)S(1)}, u32[]{:S(2)}, u32[]{:S(2)}) %collective-permute-start.29) | collective-permute-done | bytes 262176 | tf_op jit(solution)/shard_map/ppermute | solution.py:534
  169.9 16.7 %collective-permute-done.26.refs_5_ = bf16[256,512]{1,0:T(8,128)(2,1)S(1)} collective-permute-done((bf16[256,512]{1,0:T(8,128)(2,1)S(1)}, bf16[256,512]{1,0:T(8,128)(2,1)S(1)}, u32[]{:S(2)}, u32[]{:S(2)}) %collective-permute-start.26) | collective-permute-done | bytes 262176 | tf_op jit(solution)/shard_map/ppermute | solution.py:534
  187.1 1.8 collective-permute-start.31
  188.9 2.1 collective-permute-start.27
  191.0 7.4 %collective-permute-start.28 = (bf16[256,512]{1,0:T(8,128)(2,1)S(1)}, bf16[256,512]{1,0:T(8,128)(2,1)S(1)}, u32[]{:S(2)}, u32[]{:S(2)}) collective-permute-start(bf16[256,512]{1,0:T(8,128)(2,1)S(1)} %get-tuple-element.75), channel_id=1, source_target_pairs={{0,4},{4,8},{8,12},{12,0},{1,5},{5,9},{9,13},{13,1},{2,6},{6,10},{... | collective-permute-start | bytes 786440 | tf_op jit(solution)/shard_map/ppermute | solution.py:536
  199.7 1.9 collective-permute-done.30.refs_7_
  201.6 6.2 %collective-permute-done.31.refs_8_ = bf16[256,512]{1,0:T(8,128)(2,1)S(1)} collective-permute-done((bf16[256,512]{1,0:T(8,128)(2,1)S(1)}, bf16[256,512]{1,0:T(8,128)(2,1)S(1)}, u32[]{:S(2)}, u32[]{:S(2)}) %collective-permute-start.31) | collective-permute-done | bytes 262176 | tf_op jit(solution)/shard_map/ppermute | solution.py:536
  207.7 5.9 %collective-permute-done.27.refs_3_ = bf16[256,512]{1,0:T(8,128)(2,1)S(1)} collective-permute-done((bf16[256,512]{1,0:T(8,128)(2,1)S(1)}, bf16[256,512]{1,0:T(8,128)(2,1)S(1)}, u32[]{:S(2)}, u32[]{:S(2)}) %collective-permute-start.27) | collective-permute-done | bytes 262176 | tf_op jit(solution)/shard_map/ppermute | solution.py:535
  213.7 2.3 %place.1 = bf16[512,1024]{1,0:T(8,128)(2,1)} custom-call(s32[1]{0:T(128)} %bitcast.seq_ref, s32[16]{0:T(128)} %order_ref.15, s32[1]{0:T(128)} %bitcast.1.ends_ref, bf16[256,512]{1,0:T(8,128)(2,1)S(1)} %fusion.13.refs_0_, bf16[256,512]{1,0:T(8,128)(2,1)S(1)} %fusion.19.refs_1_, bf16[256,512]{1,0:T(8,128)(2,1)S(1)} %get-tuple-element.65.refs_2_, ...), custom_call_target="tpu_custom_call" | custom-call | flops 1048576 | bytes 3670016 | tf_op jit(solution)/shard_map/place/pallas_call | solution.py:499
  (81 shorter events, 15.9 us)
Async XLA Ops:
  5.5 13.1 %copy-start.8 = (bf16[256,512]{1,0:T(8,128)(2,1)}, bf16[256,512]{1,0:T(8,128)(2,1)S(1)}, u32[]{:S(2)}) copy-start(bf16[256,512]{1,0:T(8,128)(2,1)S(1)} %get-tuple-element.41) | copy-start | bytes 786436
  5.5 17.1 %collective-permute-start.1 = (bf16[256,512]{1,0:T(8,128)(2,1)S(1)}, bf16[256,512]{1,0:T(8,128)(2,1)}, u32[]{:S(2)}, u32[]{:S(2)}) collective-permute-start(bf16[256,512]{1,0:T(8,128)(2,1)S(1)} %get-tuple-element.42), channel_id=1, source_target_pairs={{0,16},{1,17},{2,18},{3,19},{4,20},{5,21},{6,22},{7,23},{8,24},{9,... | collective-permute-start | bytes 786440 | tf_op jit(solution)/shard_map/ppermute | solution.py:563
  11.1 17.3 %collective-permute-start.17 = (bf16[256,1024]{1,0:T(8,128)(2,1)}, bf16[256,1024]{1,0:T(8,128)(2,1)S(1)}, u32[]{:S(2)}, u32[]{:S(2)}) collective-permute-start(bf16[256,1024]{1,0:T(8,128)(2,1)} %get-tuple-element.57), channel_id=1, source_target_pairs={{0,16},{1,17},{2,18},{3,19},{4,20},{5,21},{6,22},{7,23},{8,24},{9,... | collective-permute-start | bytes 1572872 | tf_op jit(solution)/shard_map/ppermute | solution.py:565
  18.5 0.7 copy-start.7
  19.2 27.5 %collective-permute-start.15 = (bf16[256,1024]{1,0:T(8,128)(2,1)}, bf16[256,1024]{1,0:T(8,128)(2,1)S(1)}, u32[]{:S(2)}, u32[]{:S(2)}) collective-permute-start(bf16[256,1024]{1,0:T(8,128)(2,1)} %get-tuple-element.53), channel_id=1, source_target_pairs={{0,16},{1,17},{2,18},{3,19},{4,20},{5,21},{6,22},{7,23},{8,24},{9,... | collective-permute-start | bytes 1572872 | tf_op jit(solution)/shard_map/ppermute | solution.py:565
  20.6 23.5 %collective-permute-start = (bf16[256,512]{1,0:T(8,128)(2,1)}, bf16[256,512]{1,0:T(8,128)(2,1)}, u32[]{:S(2)}, u32[]{:S(2)}) collective-permute-start(bf16[256,512]{1,0:T(8,128)(2,1)} %get-tuple-element.40), channel_id=1, source_target_pairs={{0,16},{1,17},{2,18},{3,19},{4,20},{5,21},{6,22},{7,23},{8,24},{9,... | collective-permute-start | bytes 786440 | tf_op jit(solution)/shard_map/ppermute | solution.py:563
  23.6 29.7 %collective-permute-start.3 = (bf16[256,512]{1,0:T(8,128)(2,1)S(1)}, bf16[256,512]{1,0:T(8,128)(2,1)}, u32[]{:S(2)}, u32[]{:S(2)}) collective-permute-start(bf16[256,512]{1,0:T(8,128)(2,1)S(1)} %broadcast_select_fusion.2.refs_1_), channel_id=1, source_target_pairs={{0,4},{4,8},{8,12},{12,0},{1,5},{5,9},{9,13},{13,1},{2,6},{6,10},{... | collective-permute-start | bytes 786440 | tf_op jit(solution)/shard_map/ppermute | solution.py:520
  25.2 29.3 %collective-permute-start.5 = (bf16[256,512]{1,0:T(8,128)(2,1)S(1)}, bf16[256,512]{1,0:T(8,128)(2,1)}, u32[]{:S(2)}, u32[]{:S(2)}) collective-permute-start(bf16[256,512]{1,0:T(8,128)(2,1)S(1)} %broadcast_select_fusion.2.refs_1_), channel_id=1, source_target_pairs={{4,0},{8,4},{12,8},{0,12},{5,1},{9,5},{13,9},{1,13},{6,2},{10,6},{... | collective-permute-start | bytes 786440 | tf_op jit(solution)/shard_map/ppermute | solution.py:521
  32.6 23.8 %collective-permute-start.18 = (bf16[256,512]{1,0:T(8,128)(2,1)S(1)}, bf16[256,512]{1,0:T(8,128)(2,1)S(1)}, u32[]{:S(2)}, u32[]{:S(2)}) collective-permute-start(bf16[256,512]{1,0:T(8,128)(2,1)S(1)} %get-tuple-element.60), channel_id=1, source_target_pairs={{16,0},{17,1},{18,2},{19,3},{20,4},{21,5},{22,6},{23,7},{24,8},{25... | collective-permute-start | bytes 786440 | tf_op jit(solution)/shard_map/ppermute | solution.py:575
  45.1 18.7 %collective-permute-start.2 = (bf16[256,512]{1,0:T(8,128)(2,1)S(1)}, bf16[256,512]{1,0:T(8,128)(2,1)S(1)}, u32[]{:S(2)}, u32[]{:S(2)}) collective-permute-start(bf16[256,512]{1,0:T(8,128)(2,1)S(1)} %broadcast_select_fusion.3.refs_0_), channel_id=1, source_target_pairs={{0,4},{4,8},{8,12},{12,0},{1,5},{5,9},{9,13},{13,1},{2,6},{6,10},{... | collective-permute-start | bytes 786440 | tf_op jit(solution)/shard_map/ppermute | solution.py:520
  46.7 17.4 %collective-permute-start.4 = (bf16[256,512]{1,0:T(8,128)(2,1)S(1)}, bf16[256,512]{1,0:T(8,128)(2,1)S(1)}, u32[]{:S(2)}, u32[]{:S(2)}) collective-permute-start(bf16[256,512]{1,0:T(8,128)(2,1)S(1)} %broadcast_select_fusion.3.refs_0_), channel_id=1, source_target_pairs={{4,0},{8,4},{12,8},{0,12},{5,1},{9,5},{13,9},{1,13},{6,2},{10,6},{... | collective-permute-start | bytes 786440 | tf_op jit(solution)/shard_map/ppermute | solution.py:521
  53.2 8.8 %collective-permute-start.16 = (bf16[256,512]{1,0:T(8,128)(2,1)S(1)}, bf16[256,512]{1,0:T(8,128)(2,1)S(1)}, u32[]{:S(2)}, u32[]{:S(2)}) collective-permute-start(bf16[256,512]{1,0:T(8,128)(2,1)S(1)} %get-tuple-element.56), channel_id=1, source_target_pairs={{16,0},{17,1},{18,2},{19,3},{20,4},{21,5},{22,6},{23,7},{24,8},{25... | collective-permute-start | bytes 786440 | tf_op jit(solution)/shard_map/ppermute | solution.py:575
  54.6 36.2 %collective-permute-start.7 = (bf16[256,512]{1,0:T(8,128)(2,1)S(1)}, bf16[256,512]{1,0:T(8,128)(2,1)S(1)}, u32[]{:S(2)}, u32[]{:S(2)}) collective-permute-start(bf16[256,512]{1,0:T(8,128)(2,1)S(1)} %select_select_fusion.2), channel_id=1, source_target_pairs={{4,0},{12,4},{8,12},{0,8},{5,1},{13,5},{9,13},{1,9},{6,2},{14,6},{... | collective-permute-start | bytes 786440 | tf_op jit(solution)/shard_map/ppermute | solution.py:523
  56.4 37.2 %copy-start.18 = (f32[2048]{0:T(1024)S(1)}, f32[2048]{0:T(1024)}, u32[]{:S(2)}) copy-start(f32[2048]{0:T(1024)} %param.9) | copy-start | bytes 24580
  56.4 16.6 %collective-permute-start.20 = (bf16[256,512]{1,0:T(8,128)(2,1)S(1)}, bf16[256,512]{1,0:T(8,128)(2,1)S(1)}, u32[]{:S(2)}, u32[]{:S(2)}) collective-permute-start(bf16[256,512]{1,0:T(8,128)(2,1)S(1)} %broadcast_select_fusion.refs_1_), channel_id=1, source_target_pairs={{0,4},{4,8},{8,12},{12,0},{1,5},{5,9},{9,13},{13,1},{2,6},{6,10},{... | collective-permute-start | bytes 786440 | tf_op jit(solution)/shard_map/ppermute | solution.py:520
  62.0 16.7 %collective-permute-start.22 = (bf16[256,512]{1,0:T(8,128)(2,1)S(1)}, bf16[256,512]{1,0:T(8,128)(2,1)S(1)}, u32[]{:S(2)}, u32[]{:S(2)}) collective-permute-start(bf16[256,512]{1,0:T(8,128)(2,1)S(1)} %broadcast_select_fusion.refs_1_), channel_id=1, source_target_pairs={{4,0},{8,4},{12,8},{0,12},{5,1},{9,5},{13,9},{1,13},{6,2},{10,6},{... | collective-permute-start | bytes 786440 | tf_op jit(solution)/shard_map/ppermute | solution.py:521
  63.7 20.6 %collective-permute-start.19 = (bf16[256,512]{1,0:T(8,128)(2,1)S(1)}, bf16[256,512]{1,0:T(8,128)(2,1)S(1)}, u32[]{:S(2)}, u32[]{:S(2)}) collective-permute-start(bf16[256,512]{1,0:T(8,128)(2,1)S(1)} %broadcast_select_fusion.1.refs_0_), channel_id=1, source_target_pairs={{0,4},{4,8},{8,12},{12,0},{1,5},{5,9},{9,13},{13,1},{2,6},{6,10},{... | collective-permute-start | bytes 786440 | tf_op jit(solution)/shard_map/ppermute | solution.py:520
  64.2 23.8 %collective-permute-start.21 = (bf16[256,512]{1,0:T(8,128)(2,1)S(1)}, bf16[256,512]{1,0:T(8,128)(2,1)S(1)}, u32[]{:S(2)}, u32[]{:S(2)}) collective-permute-start(bf16[256,512]{1,0:T(8,128)(2,1)S(1)} %broadcast_select_fusion.1.refs_0_), channel_id=1, source_target_pairs={{4,0},{8,4},{12,8},{0,12},{5,1},{9,5},{13,9},{1,13},{6,2},{10,6},{... | collective-permute-start | bytes 786440 | tf_op jit(solution)/shard_map/ppermute | solution.py:521
  73.0 20.6 %collective-permute-start.6 = (bf16[256,512]{1,0:T(8,128)(2,1)S(1)}, bf16[256,512]{1,0:T(8,128)(2,1)S(1)}, u32[]{:S(2)}, u32[]{:S(2)}) collective-permute-start(bf16[256,512]{1,0:T(8,128)(2,1)S(1)} %select_select_fusion.3), channel_id=1, source_target_pairs={{4,0},{12,4},{8,12},{0,8},{5,1},{13,5},{9,13},{1,9},{6,2},{14,6},{... | collective-permute-start | bytes 786440 | tf_op jit(solution)/shard_map/ppermute | solution.py:523
  78.7 24.8 %collective-permute-start.24 = (bf16[256,512]{1,0:T(8,128)(2,1)S(1)}, bf16[256,512]{1,0:T(8,128)(2,1)S(1)}, u32[]{:S(2)}, u32[]{:S(2)}) collective-permute-start(bf16[256,512]{1,0:T(8,128)(2,1)S(1)} %select_select_fusion), channel_id=1, source_target_pairs={{4,0},{12,4},{8,12},{0,8},{5,1},{13,5},{9,13},{1,9},{6,2},{14,6},{... | collective-permute-start | bytes 786440 | tf_op jit(solution)/shard_map/ppermute | solution.py:523
  88.0 16.2 %collective-permute-start.23 = (bf16[256,512]{1,0:T(8,128)(2,1)S(1)}, bf16[256,512]{1,0:T(8,128)(2,1)S(1)}, u32[]{:S(2)}, u32[]{:S(2)}) collective-permute-start(bf16[256,512]{1,0:T(8,128)(2,1)S(1)} %select_select_fusion.1), channel_id=1, source_target_pairs={{4,0},{12,4},{8,12},{0,8},{5,1},{13,5},{9,13},{1,9},{6,2},{14,6},{... | collective-permute-start | bytes 786440 | tf_op jit(solution)/shard_map/ppermute | solution.py:523
  101.0 13.3 %copy-start = (bf16[512,2048]{1,0:T(8,128)(2,1)S(1)}, bf16[512,2048]{1,0:T(8,128)(2,1)}, u32[]{:S(2)}) copy-start(bf16[512,2048]{1,0:T(8,128)(2,1)} %out_ref.1) | copy-start | bytes 6291460
  101.0 26.6 %collective-permute-start.8 = (bf16[1024,512]{1,0:T(8,128)(2,1)S(1)}, bf16[1024,512]{1,0:T(8,128)(2,1)S(1)}, u32[]{:S(2)}, u32[]{:S(2)}) collective-permute-start(bf16[1024,512]{1,0:T(8,128)(2,1)S(1)} %get-tuple-element.44.refs_0_), channel_id=1, source_target_pairs={{0,16},{16,0},{1,17},{17,1},{2,18},{18,2},{3,19},{19,3},{4,20},{20... | collective-permute-start | bytes 3145736 | tf_op jit(solution)/shard_map/ppermute | solution.py:580
  111.7 4.1 %copy-start.3 = (bf16[512,512]{1,0:T(8,128)(2,1)}, bf16[512,512]{1,0:T(8,128)(2,1)S(1)}, u32[]{:S(2)}) copy-start(bf16[512,512]{1,0:T(8,128)(2,1)S(1)} %get-tuple-element.61.query_ref) | copy-start | bytes 1572868
  111.7 39.2 %collective-permute-start.25 = (bf16[1024,512]{1,0:T(8,128)(2,1)}, bf16[1024,512]{1,0:T(8,128)(2,1)}, u32[]{:S(2)}, u32[]{:S(2)}) collective-permute-start(bf16[1024,512]{1,0:T(8,128)(2,1)} %get-tuple-element.62.refs_2_), channel_id=1, source_target_pairs={{0,16},{16,0},{1,17},{17,1},{2,18},{18,2},{3,19},{19,3},{4,20},{20... | collective-permute-start | bytes 3145736 | tf_op jit(solution)/shard_map/ppermute | solution.py:585
  127.5 7.1 %copy-start.1 = (bf16[1024,512]{1,0:T(8,128)(2,1)}, bf16[1024,512]{1,0:T(8,128)(2,1)S(1)}, u32[]{:S(2)}) copy-start(bf16[1024,512]{1,0:T(8,128)(2,1)S(1)} %collective-permute-done.8.refs_1_) | copy-start | bytes 3145732
  135.3 0.7 copy-start.9
  137.4 0.7 copy-start.15
  138.1 0.7 copy-start.17
  138.8 20.2 %collective-permute-start.12 = (bf16[256,512]{1,0:T(8,128)(2,1)}, bf16[256,512]{1,0:T(8,128)(2,1)}, u32[]{:S(2)}, u32[]{:S(2)}) collective-permute-start(bf16[256,512]{1,0:T(8,128)(2,1)} %get-tuple-element.51), channel_id=1, source_target_pairs={{0,4},{4,12},{12,8},{8,0},{1,5},{5,13},{13,9},{9,1},{2,6},{6,14},{... | collective-permute-start | bytes 786440 | tf_op jit(solution)/shard_map/ppermute | solution.py:534
  141.3 21.2 %collective-permute-start.9 = (bf16[256,512]{1,0:T(8,128)(2,1)}, bf16[256,512]{1,0:T(8,128)(2,1)S(1)}, u32[]{:S(2)}, u32[]{:S(2)}) collective-permute-start(bf16[256,512]{1,0:T(8,128)(2,1)} %copy-done.17), channel_id=1, source_target_pairs={{0,4},{4,12},{12,8},{8,0},{1,5},{5,13},{13,9},{9,1},{2,6},{6,14},{... | collective-permute-start | bytes 786440 | tf_op jit(solution)/shard_map/ppermute | solution.py:534
  141.4 1.2 copy-start.2
  142.6 1.0 copy-start.4
  150.9 8.1 %copy-start.14 = (bf16[256,512]{1,0:T(8,128)(2,1)S(1)}, bf16[256,512]{1,0:T(8,128)(2,1)}, u32[]{:S(2)}) copy-start(bf16[256,512]{1,0:T(8,128)(2,1)} %copy-done.13) | copy-start | bytes 786436
  150.9 8.1 %copy-start.16 = (bf16[256,512]{1,0:T(8,128)(2,1)S(1)}, bf16[256,512]{1,0:T(8,128)(2,1)}, u32[]{:S(2)}) copy-start(bf16[256,512]{1,0:T(8,128)(2,1)} %copy-done.15) | copy-start | bytes 786436
  150.9 11.6 %copy-start.10 = (bf16[256,512]{1,0:T(8,128)(2,1)S(1)}, bf16[256,512]{1,0:T(8,128)(2,1)}, u32[]{:S(2)}) copy-start(bf16[256,512]{1,0:T(8,128)(2,1)} %copy-done.9) | copy-start | bytes 786436
  150.9 11.6 %copy-start.12 = (bf16[256,512]{1,0:T(8,128)(2,1)S(1)}, bf16[256,512]{1,0:T(8,128)(2,1)}, u32[]{:S(2)}) copy-start(bf16[256,512]{1,0:T(8,128)(2,1)} %copy-done.11) | copy-start | bytes 786436
  156.6 13.2 %collective-permute-start.29 = (bf16[256,512]{1,0:T(8,128)(2,1)S(1)}, bf16[256,512]{1,0:T(8,128)(2,1)S(1)}, u32[]{:S(2)}, u32[]{:S(2)}) collective-permute-start(bf16[256,512]{1,0:T(8,128)(2,1)S(1)} %get-tuple-element.71), channel_id=1, source_target_pairs={{0,4},{4,12},{12,8},{8,0},{1,5},{5,13},{13,9},{9,1},{2,6},{6,14},{... | collective-permute-start | bytes 786440 | tf_op jit(solution)/shard_map/ppermute | solution.py:534
  160.1 38.3 %copy-start.6 = (bf16[256,512]{1,0:T(8,128)(2,1)S(1)}, bf16[256,512]{1,0:T(8,128)(2,1)}, u32[]{:S(2)}) copy-start(bf16[256,512]{1,0:T(8,128)(2,1)} %copy-done.5) | copy-start | bytes 786436
  160.1 26.9 %collective-permute-start.13 = (bf16[256,512]{1,0:T(8,128)(2,1)S(1)}, bf16[256,512]{1,0:T(8,128)(2,1)S(1)}, u32[]{:S(2)}, u32[]{:S(2)}) collective-permute-start(bf16[256,512]{1,0:T(8,128)(2,1)S(1)} %get-tuple-element.77), channel_id=1, source_target_pairs={{4,0},{8,4},{12,8},{0,12},{5,1},{9,5},{13,9},{1,13},{6,2},{10,6},{... | collective-permute-start | bytes 786440 | tf_op jit(solution)/shard_map/ppermute | solution.py:535
  162.4 26.4 %collective-permute-start.14 = (bf16[256,512]{1,0:T(8,128)(2,1)S(1)}, bf16[256,512]{1,0:T(8,128)(2,1)S(1)}, u32[]{:S(2)}, u32[]{:S(2)}) collective-permute-start(bf16[256,512]{1,0:T(8,128)(2,1)S(1)} %get-tuple-element.78), channel_id=1, source_target_pairs={{0,4},{4,8},{8,12},{12,0},{1,5},{5,9},{9,13},{13,1},{2,6},{6,10},{... | collective-permute-start | bytes 786440 | tf_op jit(solution)/shard_map/ppermute | solution.py:536
  162.4 24.2 %collective-permute-start.26 = (bf16[256,512]{1,0:T(8,128)(2,1)S(1)}, bf16[256,512]{1,0:T(8,128)(2,1)S(1)}, u32[]{:S(2)}, u32[]{:S(2)}) collective-permute-start(bf16[256,512]{1,0:T(8,128)(2,1)S(1)} %get-tuple-element.67), channel_id=1, source_target_pairs={{0,4},{4,12},{12,8},{8,0},{1,5},{5,13},{13,9},{9,1},{2,6},{6,14},{... | collective-permute-start | bytes 786440 | tf_op jit(solution)/shard_map/ppermute | solution.py:534
  162.7 28.3 %collective-permute-start.10 = (bf16[256,512]{1,0:T(8,128)(2,1)S(1)}, bf16[256,512]{1,0:T(8,128)(2,1)S(1)}, u32[]{:S(2)}, u32[]{:S(2)}) collective-permute-start(bf16[256,512]{1,0:T(8,128)(2,1)S(1)} %get-tuple-element.79), channel_id=1, source_target_pairs={{4,0},{8,4},{12,8},{0,12},{5,1},{9,5},{13,9},{1,13},{6,2},{10,6},{... | collective-permute-start | bytes 786440 | tf_op jit(solution)/shard_map/ppermute | solution.py:535
  169.8 29.8 %collective-permute-start.11 = (bf16[256,512]{1,0:T(8,128)(2,1)S(1)}, bf16[256,512]{1,0:T(8,128)(2,1)S(1)}, u32[]{:S(2)}, u32[]{:S(2)}) collective-permute-start(bf16[256,512]{1,0:T(8,128)(2,1)S(1)} %get-tuple-element.80), channel_id=1, source_target_pairs={{0,4},{4,8},{8,12},{12,0},{1,5},{5,9},{9,13},{13,1},{2,6},{6,10},{... | collective-permute-start | bytes 786440 | tf_op jit(solution)/shard_map/ppermute | solution.py:536
  186.6 14.9 %collective-permute-start.30 = (bf16[256,512]{1,0:T(8,128)(2,1)S(1)}, bf16[256,512]{1,0:T(8,128)(2,1)S(1)}, u32[]{:S(2)}, u32[]{:S(2)}) collective-permute-start(bf16[256,512]{1,0:T(8,128)(2,1)S(1)} %get-tuple-element.74), channel_id=1, source_target_pairs={{4,0},{8,4},{12,8},{0,12},{5,1},{9,5},{13,9},{1,13},{6,2},{10,6},{... | collective-permute-start | bytes 786440 | tf_op jit(solution)/shard_map/ppermute | solution.py:535
  187.1 20.6 %collective-permute-start.31 = (bf16[256,512]{1,0:T(8,128)(2,1)S(1)}, bf16[256,512]{1,0:T(8,128)(2,1)S(1)}, u32[]{:S(2)}, u32[]{:S(2)}) collective-permute-start(bf16[256,512]{1,0:T(8,128)(2,1)S(1)} %get-tuple-element.73), channel_id=1, source_target_pairs={{0,4},{4,8},{8,12},{12,0},{1,5},{5,9},{9,13},{13,1},{2,6},{6,10},{... | collective-permute-start | bytes 786440 | tf_op jit(solution)/shard_map/ppermute | solution.py:536
  188.9 24.8 %collective-permute-start.27 = (bf16[256,512]{1,0:T(8,128)(2,1)S(1)}, bf16[256,512]{1,0:T(8,128)(2,1)S(1)}, u32[]{:S(2)}, u32[]{:S(2)}) collective-permute-start(bf16[256,512]{1,0:T(8,128)(2,1)S(1)} %get-tuple-element.76), channel_id=1, source_target_pairs={{4,0},{8,4},{12,8},{0,12},{5,1},{9,5},{13,9},{1,13},{6,2},{10,6},{... | collective-permute-start | bytes 786440 | tf_op jit(solution)/shard_map/ppermute | solution.py:535
  191.0 22.7 %collective-permute-start.28 = (bf16[256,512]{1,0:T(8,128)(2,1)S(1)}, bf16[256,512]{1,0:T(8,128)(2,1)S(1)}, u32[]{:S(2)}, u32[]{:S(2)}) collective-permute-start(bf16[256,512]{1,0:T(8,128)(2,1)S(1)} %get-tuple-element.75), channel_id=1, source_target_pairs={{0,4},{4,8},{8,12},{12,0},{1,5},{5,9},{9,13},{13,1},{2,6},{6,10},{... | collective-permute-start | bytes 786440 | tf_op jit(solution)/shard_map/ppermute | solution.py:536
  (3 other events, 2.1 us)

commit v9 on v8

--- a/solution.py
+++ b/solution.py
@@ -256,14 +256,25 @@
     )(blocks, out_weight)
 
 
-def project_body(blocks_ref, weight_hbm, gains_ref, *refs):
-    shards, (query_ref, pair_ref, weight_ref, tokens_ref, arrived) = refs[:-5], refs[-5:]
-    copies = fetches(weight_hbm, weight_ref, arrived)
-    ahead, behind = copies[: len(copies) // 2], copies[len(copies) // 2 :]
-    for copy in ahead:
+ROWS = 256
+
+
+def products(weight_ref, tokens_ref, scale, copies, out_ref):
+    for index, copy in enumerate(copies):
+        copy.wait()
+        here = slice(index * ROWS, (index + 1) * ROWS)
+        total = jnp.dot(weight_ref[here, :], tokens_ref[...], preferred_element_type=jnp.float32)
+        out_ref[here, :] = (total * scale).astype(jnp.bfloat16)
+
+
+def pair_body(blocks_ref, weight_hbm, gains_ref, *refs):
+    shards, (pair_ref, tokens_ref, inverse_ref, weight_ref, arrived) = refs[:-5], refs[-5:]
+    rows = weight_ref.shape[0]
+    skipped = weight_hbm.shape[0] - rows
+    copies = fetches(weight_hbm.at[skipped : skipped + rows], weight_ref, arrived)
+    for copy in copies:
         copy.start()
     width, tokens = shards[0].shape
-    cols = query_ref.shape[0]
     lines = 128
     squares = jnp.zeros((1, tokens), jnp.float32)
     for index, shard in enumerate(shards):
@@ -276,51 +287,65 @@
             gain = jnp.concatenate([gains_ref[there, :]] * (tokens // 128), axis=1)
             tokens_ref[there, :] = (wide * gain).astype(jnp.bfloat16)
     inverse = lax.rsqrt(squares / (len(shards) * width) + EPSILON)
-    rows = 256
-    halfway = weight_ref.shape[0] // 2
-    for first in range(0, weight_ref.shape[0], rows):
-        if first == 0:
-            for copy in ahead:
-                copy.wait()
-            for copy in behind:
-                copy.start()
-        if first == halfway:
-            for copy in behind:
-                copy.wait()
-        here = slice(first, first + rows)
-        total = jnp.dot(weight_ref[here, :], tokens_ref[...], preferred_element_type=jnp.float32)
-        if first < cols:
-            query_ref[here, :] = (total * (inverse * (LOG2E / math.sqrt(HEAD)))).astype(jnp.bfloat16)
-        else:
-            there = slice(first - cols, first - cols + rows)
-            pair_ref[there, :] = (total * inverse).astype(jnp.bfloat16)
-
-
-def project_call(blocks, weights, gains, shards):
+    inverse_ref[...] = inverse
+    products(weight_ref, tokens_ref, inverse, copies, pair_ref)
+
+
+def query_body(weight_hbm, tokens_ref, inverse_ref, query_ref, weight_ref, arrived):
+    copies = fetches(weight_hbm.at[: weight_ref.shape[0]], weight_ref, arrived)
+    for copy in copies:
+        copy.start()
+    products(weight_ref, tokens_ref, inverse_ref[...] * (LOG2E / math.sqrt(HEAD)), copies, query_ref)
+
+
+def project_pair(blocks, weights, gains, shards):
     rows, channels = weights.shape
     tokens = shards[0].shape[1]
     cols = rows // 3
     return pl.pallas_call(
-        project_body,
+        pair_body,
         in_specs=[smem_spec(), off_chip_spec()] + [vmem_spec()] * (1 + len(shards)),
-        out_specs=[vmem_spec(), vmem_spec()],
+        out_specs=[vmem_spec()] * 3,
         scratch_shapes=[
-            pltpu.VMEM((rows, channels), jnp.bfloat16),
-            pltpu.VMEM((channels, tokens), jnp.bfloat16),
-            pltpu.SemaphoreType.DMA((6,)),
+            pltpu.VMEM((2 * cols, channels), jnp.bfloat16),
+            pltpu.SemaphoreType.DMA((2 * cols // ROWS,)),
         ],
         out_shape=[
-            jax.ShapeDtypeStruct((cols, tokens), jnp.bfloat16),
             jax.ShapeDtypeStruct((2 * cols, tokens), jnp.bfloat16),
+            jax.ShapeDtypeStruct((channels, tokens), jnp.bfloat16),
+            jax.ShapeDtypeStruct((1, tokens), jnp.float32),
         ],
         compiler_params=params(),
         cost_estimate=pl.CostEstimate(
-            flops=2 * rows * channels * tokens,
-            bytes_accessed=2 * (rows * channels + channels * tokens + rows * tokens),
+            flops=4 * cols * channels * tokens,
+            bytes_accessed=2 * (2 * cols * channels + 2 * channels * tokens + 2 * cols * tokens),
             transcendentals=0,
         ),
-        name="project",
+        name="pair",
     )(blocks, off_chip(weights), gains, *shards)
+
+
+def project_query(weights, scaled, inverse):
+    rows, channels = weights.shape
+    tokens = scaled.shape[1]
+    cols = rows // 3
+    return pl.pallas_call(
+        query_body,
+        in_specs=[off_chip_spec(), vmem_spec(), vmem_spec()],
+        out_specs=vmem_spec(),
+        scratch_shapes=[
+            pltpu.VMEM((cols, channels), jnp.bfloat16),
+            pltpu.SemaphoreType.DMA((cols // ROWS,)),
+        ],
+        out_shape=jax.ShapeDtypeStruct((cols, tokens), jnp.bfloat16),
+        compiler_params=params(),
+        cost_estimate=pl.CostEstimate(
+            flops=2 * cols * channels * tokens,
+            bytes_accessed=2 * (cols * channels + channels * tokens + cols * tokens),
+            transcendentals=0,
+        ),
+        name="query",
+    )(off_chip(weights), scaled, inverse)
 
 
 def tile_lists(order_ref, ids_ref, seq_here, tiles_dev):
@@ -576,13 +601,15 @@
         tokens_b.append(jnp.where(seq == 1, keep, got))
 
     swap = [(0, 1), (1, 0)]
-    query_a, pair_a = project_call(blocks, weights, gains, shards_a)
+    pair_a, *normed_a = project_pair(blocks, weights, gains, shards_a)
     peer_a = lax.ppermute(pair_a, "seq", swap)
+    query_a = project_query(weights, *normed_a)
     shards_b = gathered(tokens_b)
     partials_a = attend_call(0, tables, query_a, [(pair_a, 0), (peer_a, 1)], out_t=out_t)
     parts_a = reduced(partials_a)
-    query_b, pair_b = project_call(blocks, weights, gains, shards_b)
+    pair_b, *normed_b = project_pair(blocks, weights, gains, shards_b)
     peer_b = lax.ppermute(pair_b, "seq", swap)
+    query_b = project_query(weights, *normed_b)
     near = [(pair_a, 0), (peer_a, 1), (pair_b, 2)]
     state = attend_call(1, tables, query_b, near)
     partials_b = attend_call(1, tables, query_b, [(peer_b, 3)], state=state, out_t=out_t)

time: 217 us -> 206 us (0.949)
  starting transfers between devices: 61.2 us -> 55.7 us
  local copies, waits for them, and re-layouts: 7.57 us -> 3.25 us
  Pallas kernels: 58.4 us -> 61.7 us
  other arithmetic: 5.05 us -> 2.21 us
    ppermute x2, waiting for transfers between devices: 10.1 us -> 0.01 us  [per_device_fast(): got = lax.ppermute(send, 'seq', [(0, 1)])]
    ppermute x4, starting transfers between devices: 9.2 us -> 0.74 us  [reduce_blocks(): onward = lax.ppermute(plus(up, across, here == 1), 'tp', FORWARD)]
    ppermute x2, waiting for transfers between devices: 0.84 us -> 7.85 us  [per_device_fast(): before.append(lax.ppermute(tokens, 'seq', [(0, 1)]))]
    ppermute x4, waiting for transfers between devices: 7.59 us -> 12.6 us  [gather_blocks(): after = lax.ppermute(block, 'tp', BACKWARD)]
    unnamed x38 -> x10, local copies, waits for them, and re-layouts: 7.25 us -> 2.93 us
    ppermute x4, waiting for transfers between devices: 20 us -> 23.6 us  [reduce_blocks(): across = lax.ppermute(sent, 'tp', FOLDED)]
    ppermute x1, waiting for transfers between devices: 11.8 us -> 8.41 us  [per_device_fast(): peer_a = lax.ppermute(pair_a, 'seq', swap)]
    pallas_call x2 -> x4, Pallas kernels: 14.5 us -> 17.5 us  [the longest x2 12.1 us: project_pair(): pl.pallas_call(pair_body, in_specs=[smem_spec(), off_chip_spec()] + [vmem...]
  transfers between devices with their start and end apart: 32 -> 32, of which waited for: 15 -> 17; matrix products, arithmetic and copies ran while one was open for 2% -> 1% of each run, Pallas kernels for 23% -> 26%
where the time goes in v9:
time: 206 us
  waiting for transfers between devices  82.6 us (40%)
  Pallas kernels  61.7 us (30%)
  starting transfers between devices  55.7 us (27%)
  local copies, waits for them, and re-layouts  3.25 us (2%)
  other arithmetic  2.21 us (1%)
    ppermute x4, waiting for transfers between devices, reduce_blocks(): across = lax.ppermute(sent, 'tp', FOLDED)  23.6 us
    pallas_call x4, Pallas kernels, conv_call(): pl.pallas_call(functools.partial(conv_body, with_before, piece * channels...  20.3 us
    pallas_call x3, Pallas kernels, attend_call(): pl.pallas_call(functools.partial(attend_body, chunk, tuple((s for _, s in...  20 us
    ppermute x4, waiting for transfers between devices, gather_blocks(): after = lax.ppermute(block, 'tp', BACKWARD)  12.6 us
    pallas_call x2, Pallas kernels, project_pair(): pl.pallas_call(pair_body, in_specs=[smem_spec(), off_chip_spec()] + [vmem...  12.1 us
    ppermute x4, starting transfers between devices, reduce_blocks(): back = lax.ppermute(plus(down, across, here == 2), 'tp', BACKWARD)  11.3 us
    ppermute x4, starting transfers between devices, gather_blocks(): after = lax.ppermute(block, 'tp', BACKWARD)  11 us
    ppermute x4, waiting for transfers between devices, reduce_blocks(): back = lax.ppermute(plus(down, across, here == 2), 'tp', BACKWARD)  9.02 us
  transfers between devices with their start and end apart: 32, of which 17 were waited for; matrix products, arithmetic and copies ran while one was open for 1% of the time, Pallas kernels for 26%

profile of v9, /device:TPU:0, one launch (start us, length us, event | category | flops | bytes accessed | tf_op | source)
XLA Modules:
  0.0 205.8 jit_solution(12265664144093936315)
XLA Ops:
  0.0 5.5 %conv.5 = (f32[256,1024]{1,0:T(8,128)S(1)}, bf16[256,512]{1,0:T(8,128)(2,1)S(1)}, bf16[256,512]{1,0:T(8,128)(2,1)S(1)}, bf16[256,1024]{1,0:T(8,128)(2,1)}) custom-call(s32[1]{0:T(128)} %bitcast.seq_ref, s32[16]{0:T(128)} %order_ref.15, bf16[512,1024]{1,0:T(8,128)(2,1)} %tokens_ref.3, f32[27,512]{1,0:T(8,128)} %taps_ref.7), custom_call_target="tpu_custom_call" | custom-call | flops 7077888 | bytes 2097152 | tf_op jit(solution)/shard_map/conv/pallas_call | solution.py:220
  5.5 4.9 %collective-permute-start.1 = (bf16[256,512]{1,0:T(8,128)(2,1)S(1)}, bf16[256,512]{1,0:T(8,128)(2,1)S(1)}, u32[]{:S(2)}, u32[]{:S(2)}) collective-permute-start(bf16[256,512]{1,0:T(8,128)(2,1)S(1)} %get-tuple-element.44), channel_id=1, source_target_pairs={{0,16},{1,17},{2,18},{3,19},{4,20},{5,21},{6,22},{7,23},{8,24},{9,... | collective-permute-start | bytes 786440 | tf_op jit(solution)/shard_map/ppermute | solution.py:588
  10.4 2.1 %collective-permute-start.17 = (bf16[256,1024]{1,0:T(8,128)(2,1)}, bf16[256,1024]{1,0:T(8,128)(2,1)}, u32[]{:S(2)}, u32[]{:S(2)}) collective-permute-start(bf16[256,1024]{1,0:T(8,128)(2,1)} %get-tuple-element.60), channel_id=1, source_target_pairs={{0,16},{1,17},{2,18},{3,19},{4,20},{5,21},{6,22},{7,23},{8,24},{9,... | collective-permute-start | bytes 1572872 | tf_op jit(solution)/shard_map/ppermute | solution.py:590
  12.5 6.1 %conv.4 = (f32[256,1024]{1,0:T(8,128)S(1)}, bf16[256,512]{1,0:T(8,128)(2,1)S(1)}, bf16[256,512]{1,0:T(8,128)(2,1)}, bf16[256,1024]{1,0:T(8,128)(2,1)}) custom-call(s32[1]{0:T(128)} %bitcast.seq_ref, s32[16]{0:T(128)} %order_ref.15, bf16[512,1024]{1,0:T(8,128)(2,1)} %tokens_ref.3, f32[27,512]{1,0:T(8,128)} %taps_ref.7), custom_call_target="tpu_custom_call" | custom-call | flops 7077888 | bytes 2097152 | tf_op jit(solution)/shard_map/conv/pallas_call | solution.py:220
  18.6 2.0 collective-permute-start
  22.0 3.7 %collective-permute-start.5 = (bf16[256,512]{1,0:T(8,128)(2,1)S(1)}, bf16[256,512]{1,0:T(8,128)(2,1)S(1)}, u32[]{:S(2)}, u32[]{:S(2)}) collective-permute-start(bf16[256,512]{1,0:T(8,128)(2,1)S(1)} %broadcast_select_fusion.2.refs_1_), channel_id=1, source_target_pairs={{4,0},{8,4},{12,8},{0,12},{5,1},{9,5},{13,9},{1,13},{6,2},{10,6},{... | collective-permute-start | bytes 786440 | tf_op jit(solution)/shard_map/ppermute | solution.py:546
  25.8 2.6 %collective-permute-done.17.tokens_ref = bf16[256,1024]{1,0:T(8,128)(2,1)} collective-permute-done((bf16[256,1024]{1,0:T(8,128)(2,1)}, bf16[256,1024]{1,0:T(8,128)(2,1)}, u32[]{:S(2)}, u32[]{:S(2)}) %collective-permute-start.17) | collective-permute-done | bytes 524320 | tf_op jit(solution)/shard_map/ppermute | solution.py:590
  28.4 4.5 %conv.7 = (bf16[256,512]{1,0:T(8,128)(2,1)S(1)}, bf16[256,512]{1,0:T(8,128)(2,1)S(1)}) custom-call(s32[1]{0:T(128)} %bitcast.seq_ref, s32[16]{0:T(128)} %order_ref.15, bf16[256,1024]{1,0:T(8,128)(2,1)} %collective-permute-done.17.tokens_ref, f32[27,512]{1,0:T(8,128)} %taps_ref.7, f32[256,1024]{1,0:T(8,128)S(1)} %get-tuple-element.61.part_ref), custom_call_target="tpu_custom_call" | custom-call | flops 7077888 | bytes 2097152 | tf_op jit(solution)/shard_map/conv/pallas_call | solution.py:220
  35.1 3.7 %collective-permute-start.4 = (bf16[256,512]{1,0:T(8,128)(2,1)S(1)}, bf16[256,512]{1,0:T(8,128)(2,1)S(1)}, u32[]{:S(2)}, u32[]{:S(2)}) collective-permute-start(bf16[256,512]{1,0:T(8,128)(2,1)S(1)} %broadcast_select_fusion.3.refs_0_), channel_id=1, source_target_pairs={{4,0},{8,4},{12,8},{0,12},{5,1},{9,5},{13,9},{1,13},{6,2},{10,6},{... | collective-permute-start | bytes 786440 | tf_op jit(solution)/shard_map/ppermute | solution.py:546
  38.8 5.3 %collective-permute-done.15.tokens_ref = bf16[256,1024]{1,0:T(8,128)(2,1)S(1)} collective-permute-done((bf16[256,1024]{1,0:T(8,128)(2,1)}, bf16[256,1024]{1,0:T(8,128)(2,1)S(1)}, u32[]{:S(2)}, u32[]{:S(2)}) %collective-permute-start.15) | collective-permute-done | bytes 524320 | tf_op jit(solution)/shard_map/ppermute | solution.py:590
  44.1 1.6 collective-permute-start.2
  45.7 4.3 %conv.6 = (bf16[256,512]{1,0:T(8,128)(2,1)S(1)}, bf16[256,512]{1,0:T(8,128)(2,1)S(1)}) custom-call(s32[1]{0:T(128)} %bitcast.seq_ref, s32[16]{0:T(128)} %order_ref.15, bf16[256,1024]{1,0:T(8,128)(2,1)S(1)} %collective-permute-done.15.tokens_ref, f32[27,512]{1,0:T(8,128)} %taps_ref.7, f32[256,1024]{1,0:T(8,128)S(1)} %get-tuple-element.57.part_ref), custom_call_target="tpu_custom_call" | custom-call | flops 7077888 | bytes 2097152 | tf_op jit(solution)/shard_map/conv/pallas_call | solution.py:220
  51.3 2.6 %collective-permute-start.7 = (bf16[256,512]{1,0:T(8,128)(2,1)S(1)}, bf16[256,512]{1,0:T(8,128)(2,1)S(1)}, u32[]{:S(2)}, u32[]{:S(2)}) collective-permute-start(bf16[256,512]{1,0:T(8,128)(2,1)S(1)} %select_select_fusion.2), channel_id=1, source_target_pairs={{4,0},{12,4},{8,12},{0,8},{5,1},{13,5},{9,13},{1,9},{6,2},{14,6},{... | collective-permute-start | bytes 786440 | tf_op jit(solution)/shard_map/ppermute | solution.py:548
  55.4 3.4 %collective-permute-done.16 = bf16[256,512]{1,0:T(8,128)(2,1)S(1)} collective-permute-done((bf16[256,512]{1,0:T(8,128)(2,1)S(1)}, bf16[256,512]{1,0:T(8,128)(2,1)S(1)}, u32[]{:S(2)}, u32[]{:S(2)}) %collective-permute-start.16) | collective-permute-done | bytes 262176 | tf_op jit(solution)/shard_map/ppermute | solution.py:600
  58.8 1.6 collective-permute-start.20
  60.4 2.3 %collective-permute-start.21 = (bf16[256,512]{1,0:T(8,128)(2,1)S(1)}, bf16[256,512]{1,0:T(8,128)(2,1)S(1)}, u32[]{:S(2)}, u32[]{:S(2)}) collective-permute-start(bf16[256,512]{1,0:T(8,128)(2,1)S(1)} %broadcast_select_fusion.1.refs_0_), channel_id=1, source_target_pairs={{4,0},{8,4},{12,8},{0,12},{5,1},{9,5},{13,9},{1,13},{6,2},{10,6},{... | collective-permute-start | bytes 786440 | tf_op jit(solution)/shard_map/ppermute | solution.py:546
  62.8 7.0 %collective-permute-done.22.refs_5_ = bf16[256,512]{1,0:T(8,128)(2,1)S(1)} collective-permute-done((bf16[256,512]{1,0:T(8,128)(2,1)S(1)}, bf16[256,512]{1,0:T(8,128)(2,1)S(1)}, u32[]{:S(2)}, u32[]{:S(2)}) %collective-permute-start.22) | collective-permute-done | bytes 262176 | tf_op jit(solution)/shard_map/ppermute | solution.py:546
  69.8 3.9 %collective-permute-done.20.refs_3_ = bf16[256,512]{1,0:T(8,128)(2,1)S(1)} collective-permute-done((bf16[256,512]{1,0:T(8,128)(2,1)S(1)}, bf16[256,512]{1,0:T(8,128)(2,1)S(1)}, u32[]{:S(2)}, u32[]{:S(2)}) %collective-permute-start.20) | collective-permute-done | bytes 262176 | tf_op jit(solution)/shard_map/ppermute | solution.py:545
  73.8 1.7 collective-permute-start.24
  75.5 5.5 %collective-permute-done.21.refs_4_ = bf16[256,512]{1,0:T(8,128)(2,1)S(1)} collective-permute-done((bf16[256,512]{1,0:T(8,128)(2,1)S(1)}, bf16[256,512]{1,0:T(8,128)(2,1)S(1)}, u32[]{:S(2)}, u32[]{:S(2)}) %collective-permute-start.21) | collective-permute-done | bytes 262176 | tf_op jit(solution)/shard_map/ppermute | solution.py:546
  81.0 4.0 %collective-permute-done.19.refs_2_ = bf16[256,512]{1,0:T(8,128)(2,1)S(1)} collective-permute-done((bf16[256,512]{1,0:T(8,128)(2,1)S(1)}, bf16[256,512]{1,0:T(8,128)(2,1)S(1)}, u32[]{:S(2)}, u32[]{:S(2)}) %collective-permute-start.19) | collective-permute-done | bytes 262176 | tf_op jit(solution)/shard_map/ppermute | solution.py:545
  85.1 1.6 collective-permute-start.23
  86.7 2.1 %collective-permute-done.6.refs_6_ = bf16[256,512]{1,0:T(8,128)(2,1)S(1)} collective-permute-done((bf16[256,512]{1,0:T(8,128)(2,1)S(1)}, bf16[256,512]{1,0:T(8,128)(2,1)S(1)}, u32[]{:S(2)}, u32[]{:S(2)}) %collective-permute-start.6) | collective-permute-done | bytes 262176 | tf_op jit(solution)/shard_map/ppermute | solution.py:548
  89.1 6.0 %pair.2 = (bf16[1024,512]{1,0:T(8,128)(2,1)}, bf16[2048,512]{1,0:T(8,128)(2,1)S(1)}, f32[1,512]{1,0:T(1,128)S(1)}) custom-call(s32[4]{0:T(128)S(1)} %pad_add_fusion.blocks_ref, bf16[1536,2048]{1,0:T(8,128)(2,1)} %bitcast.8, f32[2048,128]{1,0:T(8,128)S(1)} %broadcast_in_dim.42.gains_ref, bf16[256,512]{1,0:T(8,128)(2,1)S(1)} %broadcast_select_fusion.3.refs_0_, ...), custom_call_target="tpu_custom_call" | custom-call | flops 2147483648 | bytes 9437184 | tf_op jit(solution)/shard_map/pair/pallas_call | solution.py:305
  95.2 2.7 %collective-permute-start.8 = (bf16[1024,512]{1,0:T(8,128)(2,1)}, bf16[1024,512]{1,0:T(8,128)(2,1)S(1)}, u32[]{:S(2)}, u32[]{:S(2)}) collective-permute-start(bf16[1024,512]{1,0:T(8,128)(2,1)} %get-tuple-element.47.refs_0_), channel_id=1, source_target_pairs={{0,16},{16,0},{1,17},{17,1},{2,18},{18,2},{3,19},{19,3},{4,20},{20... | collective-permute-start | bytes 3145736 | tf_op jit(solution)/shard_map/ppermute | solution.py:605
  98.1 6.1 %pair.3 = (bf16[1024,512]{1,0:T(8,128)(2,1)}, bf16[2048,512]{1,0:T(8,128)(2,1)S(1)}, f32[1,512]{1,0:T(1,128)S(1)}) custom-call(s32[4]{0:T(128)S(1)} %pad_add_fusion.blocks_ref, bf16[1536,2048]{1,0:T(8,128)(2,1)} %bitcast.9, f32[2048,128]{1,0:T(8,128)S(1)} %broadcast_in_dim.42.gains_ref, bf16[256,512]{1,0:T(8,128)(2,1)S(1)} %broadcast_select_fusion.1.refs_0_, ...), custom_call_target="tpu_custom_call" | custom-call | flops 2147483648 | bytes 9437184 | tf_op jit(solution)/shard_map/pair/pallas_call | solution.py:305
  105.5 2.4 %collective-permute-start.25 = (bf16[1024,512]{1,0:T(8,128)(2,1)}, bf16[1024,512]{1,0:T(8,128)(2,1)}, u32[]{:S(2)}, u32[]{:S(2)}) collective-permute-start(bf16[1024,512]{1,0:T(8,128)(2,1)} %get-tuple-element.66.refs_2_), channel_id=1, source_target_pairs={{0,16},{16,0},{1,17},{17,1},{2,18},{18,2},{3,19},{19,3},{4,20},{20... | collective-permute-start | bytes 3145736 | tf_op jit(solution)/shard_map/ppermute | solution.py:611
  107.9 1.6 copy-done.2
  109.5 1.5 prepare.1.refs_2_.refs_3_
  111.0 2.7 %query.2.query_ref = bf16[512,512]{1,0:T(8,128)(2,1)S(1)} custom-call(bf16[1536,2048]{1,0:T(8,128)(2,1)} %bitcast.10, bf16[2048,512]{1,0:T(8,128)(2,1)S(1)} %get-tuple-element.45.tokens_ref, f32[1,512]{1,0:T(1,128)S(1)} %get-tuple-element.46.inverse_ref), custom_call_target="tpu_custom_call" | custom-call | flops 1073741824 | bytes 4718592 | tf_op jit(solution)/shard_map/query/pallas_call | solution.py:332
  113.7 8.4 %collective-permute-done.8.refs_1_ = bf16[1024,512]{1,0:T(8,128)(2,1)S(1)} collective-permute-done((bf16[1024,512]{1,0:T(8,128)(2,1)}, bf16[1024,512]{1,0:T(8,128)(2,1)S(1)}, u32[]{:S(2)}, u32[]{:S(2)}) %collective-permute-start.8) | collective-permute-done | bytes 1048608 | tf_op jit(solution)/shard_map/ppermute | solution.py:605
  122.1 6.8 %attend.3 = (bf16[256,512]{1,0:T(8,128)(2,1)S(1)}, bf16[256,512]{1,0:T(8,128)(2,1)S(1)}, bf16[256,512]{1,0:T(8,128)(2,1)S(1)}, bf16[256,512]{1,0:T(8,128)(2,1)S(...) custom-call(s32[1]{0:T(128)} %bitcast.seq_ref, ...), custom_call_target="tpu_custom_call" | custom-call | flops 1073741824 | bytes 3145728 | tf_op jit(solution)/shard_map/attend/pallas_call | solution.py:472
  128.9 2.4 %collective-permute-start.9 = (bf16[256,512]{1,0:T(8,128)(2,1)S(1)}, bf16[256,512]{1,0:T(8,128)(2,1)S(1)}, u32[]{:S(2)}, u32[]{:S(2)}) collective-permute-start(bf16[256,512]{1,0:T(8,128)(2,1)S(1)} %get-tuple-element.50), channel_id=1, source_target_pairs={{0,4},{4,12},{12,8},{8,0},{1,5},{5,13},{13,9},{9,1},{2,6},{6,14},{... | collective-permute-start | bytes 786440 | tf_op jit(solution)/shard_map/ppermute | solution.py:559
  131.3 2.7 %query.3.query_ref = bf16[512,512]{1,0:T(8,128)(2,1)S(1)} custom-call(bf16[1536,2048]{1,0:T(8,128)(2,1)} %bitcast.11, bf16[2048,512]{1,0:T(8,128)(2,1)S(1)} %copy-done.1, f32[1,512]{1,0:T(1,128)S(1)} %get-tuple-element.65.inverse_ref), custom_call_target="tpu_custom_call" | custom-call | flops 1073741824 | bytes 4718592 | tf_op jit(solution)/shard_map/query/pallas_call | solution.py:332
  134.0 7.6 %attend.4 = (f32[4,2,512]{2,1,0:T(2,128)S(1)}, f32[512,512]{1,0:T(8,128)S(1)}) custom-call(s32[1]{0:T(128)} %bitcast.seq_ref, s32[16]{0:T(128)} %order_ref.15, s32[16,16]{1,0:T(8,128)} %mask_ref.5, bf16[512,512]{1,0:T(8,128)(2,1)S(1)} %query.3.query_ref, bf16[1024,512]{1,0:T(8,128)(2,1)} %get-tuple-element.47.refs_0_, ...), custom_call_target="tpu_custom_call" | custom-call | flops 1610612736 | bytes 4194304 | tf_op jit(solution)/shard_map/attend/pallas_call | solution.py:472
  141.7 5.6 %attend.5 = (bf16[256,512]{1,0:T(8,128)(2,1)S(1)}, bf16[256,512]{1,0:T(8,128)(2,1)S(1)}, bf16[256,512]{1,0:T(8,128)(2,1)S(1)}, bf16[256,512]{1,0:T(8,128)(2,1)S(...) custom-call(s32[1]{0:T(128)} %bitcast.seq_ref, ...), custom_call_target="tpu_custom_call" | custom-call | flops 536870912 | bytes 2097152 | tf_op jit(solution)/shard_map/attend/pallas_call | solution.py:472
  147.3 3.1 %collective-permute-start.26 = (bf16[256,512]{1,0:T(8,128)(2,1)S(1)}, bf16[256,512]{1,0:T(8,128)(2,1)S(1)}, u32[]{:S(2)}, u32[]{:S(2)}) collective-permute-start(bf16[256,512]{1,0:T(8,128)(2,1)S(1)} %get-tuple-element.71), channel_id=1, source_target_pairs={{0,4},{4,12},{12,8},{8,0},{1,5},{5,13},{13,9},{9,1},{2,6},{6,14},{... | collective-permute-start | bytes 786440 | tf_op jit(solution)/shard_map/ppermute | solution.py:559
  150.5 1.6 collective-permute-start.10
  153.0 3.1 %collective-permute-start.13 = (bf16[256,512]{1,0:T(8,128)(2,1)S(1)}, bf16[256,512]{1,0:T(8,128)(2,1)S(1)}, u32[]{:S(2)}, u32[]{:S(2)}) collective-permute-start(bf16[256,512]{1,0:T(8,128)(2,1)S(1)} %get-tuple-element.81), channel_id=1, source_target_pairs={{4,0},{8,4},{12,8},{0,12},{5,1},{9,5},{13,9},{1,13},{6,2},{10,6},{... | collective-permute-start | bytes 786440 | tf_op jit(solution)/shard_map/ppermute | solution.py:560
  156.1 4.1 %collective-permute-done.26.refs_5_ = bf16[256,512]{1,0:T(8,128)(2,1)S(1)} collective-permute-done((bf16[256,512]{1,0:T(8,128)(2,1)S(1)}, bf16[256,512]{1,0:T(8,128)(2,1)S(1)}, u32[]{:S(2)}, u32[]{:S(2)}) %collective-permute-start.26) | collective-permute-done | bytes 262176 | tf_op jit(solution)/shard_map/ppermute | solution.py:559
  160.4 19.5 %collective-permute-done.29.refs_9_ = bf16[256,512]{1,0:T(8,128)(2,1)S(1)} collective-permute-done((bf16[256,512]{1,0:T(8,128)(2,1)S(1)}, bf16[256,512]{1,0:T(8,128)(2,1)S(1)}, u32[]{:S(2)}, u32[]{:S(2)}) %collective-permute-start.29) | collective-permute-done | bytes 262176 | tf_op jit(solution)/shard_map/ppermute | solution.py:559
  180.0 3.9 %collective-permute-start.27 = (bf16[256,512]{1,0:T(8,128)(2,1)S(1)}, bf16[256,512]{1,0:T(8,128)(2,1)S(1)}, u32[]{:S(2)}, u32[]{:S(2)}) collective-permute-start(bf16[256,512]{1,0:T(8,128)(2,1)S(1)} %get-tuple-element.80), channel_id=1, source_target_pairs={{4,0},{8,4},{12,8},{0,12},{5,1},{9,5},{13,9},{1,13},{6,2},{10,6},{... | collective-permute-start | bytes 786440 | tf_op jit(solution)/shard_map/ppermute | solution.py:560
  185.0 2.7 %collective-permute-start.30 = (bf16[256,512]{1,0:T(8,128)(2,1)S(1)}, bf16[256,512]{1,0:T(8,128)(2,1)S(1)}, u32[]{:S(2)}, u32[]{:S(2)}) collective-permute-start(bf16[256,512]{1,0:T(8,128)(2,1)S(1)} %get-tuple-element.78), channel_id=1, source_target_pairs={{4,0},{8,4},{12,8},{0,12},{5,1},{9,5},{13,9},{1,13},{6,2},{10,6},{... | collective-permute-start | bytes 786440 | tf_op jit(solution)/shard_map/ppermute | solution.py:560
  188.1 4.6 %collective-permute-done.28.refs_4_ = bf16[256,512]{1,0:T(8,128)(2,1)S(1)} collective-permute-done((bf16[256,512]{1,0:T(8,128)(2,1)S(1)}, bf16[256,512]{1,0:T(8,128)(2,1)S(1)}, u32[]{:S(2)}, u32[]{:S(2)}) %collective-permute-start.28) | collective-permute-done | bytes 262176 | tf_op jit(solution)/shard_map/ppermute | solution.py:561
  192.6 4.6 %collective-permute-done.27.refs_3_ = bf16[256,512]{1,0:T(8,128)(2,1)S(1)} collective-permute-done((bf16[256,512]{1,0:T(8,128)(2,1)S(1)}, bf16[256,512]{1,0:T(8,128)(2,1)S(1)}, u32[]{:S(2)}, u32[]{:S(2)}) %collective-permute-start.27) | collective-permute-done | bytes 262176 | tf_op jit(solution)/shard_map/ppermute | solution.py:560
  197.2 2.9 %collective-permute-done.31.refs_8_ = bf16[256,512]{1,0:T(8,128)(2,1)S(1)} collective-permute-done((bf16[256,512]{1,0:T(8,128)(2,1)S(1)}, bf16[256,512]{1,0:T(8,128)(2,1)S(1)}, u32[]{:S(2)}, u32[]{:S(2)}) %collective-permute-start.31) | collective-permute-done | bytes 262176 | tf_op jit(solution)/shard_map/ppermute | solution.py:561
  200.2 3.3 %collective-permute-done.30.refs_7_ = bf16[256,512]{1,0:T(8,128)(2,1)S(1)} collective-permute-done((bf16[256,512]{1,0:T(8,128)(2,1)S(1)}, bf16[256,512]{1,0:T(8,128)(2,1)S(1)}, u32[]{:S(2)}, u32[]{:S(2)}) %collective-permute-start.30) | collective-permute-done | bytes 262176 | tf_op jit(solution)/shard_map/ppermute | solution.py:560
  203.5 2.3 %place.1 = bf16[512,1024]{1,0:T(8,128)(2,1)} custom-call(s32[1]{0:T(128)} %bitcast.seq_ref, s32[16]{0:T(128)} %order_ref.15, s32[1]{0:T(128)} %bitcast.1.ends_ref, bf16[256,512]{1,0:T(8,128)(2,1)S(1)} %fusion.13.refs_0_, bf16[256,512]{1,0:T(8,128)(2,1)S(1)} %fusion.19.refs_1_, bf16[256,512]{1,0:T(8,128)(2,1)S(1)} %get-tuple-element.69.refs_2_, ...), custom_call_target="tpu_custom_call" | custom-call | flops 1048576 | bytes 3670016 | tf_op jit(solution)/shard_map/place/pallas_call | solution.py:524
  (55 shorter events, 11.3 us)
Async XLA Ops:
  5.5 16.5 %collective-permute-start.1 = (bf16[256,512]{1,0:T(8,128)(2,1)S(1)}, bf16[256,512]{1,0:T(8,128)(2,1)S(1)}, u32[]{:S(2)}, u32[]{:S(2)}) collective-permute-start(bf16[256,512]{1,0:T(8,128)(2,1)S(1)} %get-tuple-element.44), channel_id=1, source_target_pairs={{0,16},{1,17},{2,18},{3,19},{4,20},{5,21},{6,22},{7,23},{8,24},{9,... | collective-permute-start | bytes 786440 | tf_op jit(solution)/shard_map/ppermute | solution.py:588
  10.4 18.0 %collective-permute-start.17 = (bf16[256,1024]{1,0:T(8,128)(2,1)}, bf16[256,1024]{1,0:T(8,128)(2,1)}, u32[]{:S(2)}, u32[]{:S(2)}) collective-permute-start(bf16[256,1024]{1,0:T(8,128)(2,1)} %get-tuple-element.60), channel_id=1, source_target_pairs={{0,16},{1,17},{2,18},{3,19},{4,20},{5,21},{6,22},{7,23},{8,24},{9,... | collective-permute-start | bytes 1572872 | tf_op jit(solution)/shard_map/ppermute | solution.py:590
  18.6 2.0 copy-start.3
  18.6 15.5 %collective-permute-start = (bf16[256,512]{1,0:T(8,128)(2,1)}, bf16[256,512]{1,0:T(8,128)(2,1)}, u32[]{:S(2)}, u32[]{:S(2)}) collective-permute-start(bf16[256,512]{1,0:T(8,128)(2,1)} %get-tuple-element.42), channel_id=1, source_target_pairs={{0,16},{1,17},{2,18},{3,19},{4,20},{5,21},{6,22},{7,23},{8,24},{9,... | collective-permute-start | bytes 786440 | tf_op jit(solution)/shard_map/ppermute | solution.py:588
  20.6 23.4 %collective-permute-start.15 = (bf16[256,1024]{1,0:T(8,128)(2,1)}, bf16[256,1024]{1,0:T(8,128)(2,1)S(1)}, u32[]{:S(2)}, u32[]{:S(2)}) collective-permute-start(bf16[256,1024]{1,0:T(8,128)(2,1)} %get-tuple-element.56), channel_id=1, source_target_pairs={{0,16},{1,17},{2,18},{3,19},{4,20},{5,21},{6,22},{7,23},{8,24},{9,... | collective-permute-start | bytes 1572872 | tf_op jit(solution)/shard_map/ppermute | solution.py:590
  22.0 27.9 %collective-permute-start.5 = (bf16[256,512]{1,0:T(8,128)(2,1)S(1)}, bf16[256,512]{1,0:T(8,128)(2,1)S(1)}, u32[]{:S(2)}, u32[]{:S(2)}) collective-permute-start(bf16[256,512]{1,0:T(8,128)(2,1)S(1)} %broadcast_select_fusion.2.refs_1_), channel_id=1, source_target_pairs={{4,0},{8,4},{12,8},{0,12},{5,1},{9,5},{13,9},{1,13},{6,2},{10,6},{... | collective-permute-start | bytes 786440 | tf_op jit(solution)/shard_map/ppermute | solution.py:546
  25.7 25.5 %collective-permute-start.3 = (bf16[256,512]{1,0:T(8,128)(2,1)S(1)}, bf16[256,512]{1,0:T(8,128)(2,1)S(1)}, u32[]{:S(2)}, u32[]{:S(2)}) collective-permute-start(bf16[256,512]{1,0:T(8,128)(2,1)S(1)} %broadcast_select_fusion.2.refs_1_), channel_id=1, source_target_pairs={{0,4},{4,8},{8,12},{12,0},{1,5},{5,9},{9,13},{13,1},{2,6},{6,10},{... | collective-permute-start | bytes 786440 | tf_op jit(solution)/shard_map/ppermute | solution.py:545
  32.8 21.1 %collective-permute-start.18 = (bf16[256,512]{1,0:T(8,128)(2,1)S(1)}, bf16[256,512]{1,0:T(8,128)(2,1)S(1)}, u32[]{:S(2)}, u32[]{:S(2)}) collective-permute-start(bf16[256,512]{1,0:T(8,128)(2,1)S(1)} %get-tuple-element.63), channel_id=1, source_target_pairs={{16,0},{17,1},{18,2},{19,3},{20,4},{21,5},{22,6},{23,7},{24,8},{25... | collective-permute-start | bytes 786440 | tf_op jit(solution)/shard_map/ppermute | solution.py:600
  35.1 25.2 %collective-permute-start.4 = (bf16[256,512]{1,0:T(8,128)(2,1)S(1)}, bf16[256,512]{1,0:T(8,128)(2,1)S(1)}, u32[]{:S(2)}, u32[]{:S(2)}) collective-permute-start(bf16[256,512]{1,0:T(8,128)(2,1)S(1)} %broadcast_select_fusion.3.refs_0_), channel_id=1, source_target_pairs={{4,0},{8,4},{12,8},{0,12},{5,1},{9,5},{13,9},{1,13},{6,2},{10,6},{... | collective-permute-start | bytes 786440 | tf_op jit(solution)/shard_map/ppermute | solution.py:546
  44.1 18.6 %collective-permute-start.2 = (bf16[256,512]{1,0:T(8,128)(2,1)S(1)}, bf16[256,512]{1,0:T(8,128)(2,1)S(1)}, u32[]{:S(2)}, u32[]{:S(2)}) collective-permute-start(bf16[256,512]{1,0:T(8,128)(2,1)S(1)} %broadcast_select_fusion.3.refs_0_), channel_id=1, source_target_pairs={{0,4},{4,8},{8,12},{12,0},{1,5},{5,9},{9,13},{13,1},{2,6},{6,10},{... | collective-permute-start | bytes 786440 | tf_op jit(solution)/shard_map/ppermute | solution.py:545
  49.9 8.8 %collective-permute-start.16 = (bf16[256,512]{1,0:T(8,128)(2,1)S(1)}, bf16[256,512]{1,0:T(8,128)(2,1)S(1)}, u32[]{:S(2)}, u32[]{:S(2)}) collective-permute-start(bf16[256,512]{1,0:T(8,128)(2,1)S(1)} %get-tuple-element.59), channel_id=1, source_target_pairs={{16,0},{17,1},{18,2},{19,3},{20,4},{21,5},{22,6},{23,7},{24,8},{25... | collective-permute-start | bytes 786440 | tf_op jit(solution)/shard_map/ppermute | solution.py:600
  51.3 35.4 %collective-permute-start.7 = (bf16[256,512]{1,0:T(8,128)(2,1)S(1)}, bf16[256,512]{1,0:T(8,128)(2,1)S(1)}, u32[]{:S(2)}, u32[]{:S(2)}) collective-permute-start(bf16[256,512]{1,0:T(8,128)(2,1)S(1)} %select_select_fusion.2), channel_id=1, source_target_pairs={{4,0},{12,4},{8,12},{0,8},{5,1},{13,5},{9,13},{1,9},{6,2},{14,6},{... | collective-permute-start | bytes 786440 | tf_op jit(solution)/shard_map/ppermute | solution.py:548
  54.0 34.8 %copy-start.4 = (f32[2048]{0:T(1024)S(1)}, f32[2048]{0:T(1024)}, u32[]{:S(2)}) copy-start(f32[2048]{0:T(1024)} %param.9) | copy-start | bytes 24580
  54.0 15.8 %collective-permute-start.22 = (bf16[256,512]{1,0:T(8,128)(2,1)S(1)}, bf16[256,512]{1,0:T(8,128)(2,1)S(1)}, u32[]{:S(2)}, u32[]{:S(2)}) collective-permute-start(bf16[256,512]{1,0:T(8,128)(2,1)S(1)} %broadcast_select_fusion.refs_1_), channel_id=1, source_target_pairs={{4,0},{8,4},{12,8},{0,12},{5,1},{9,5},{13,9},{1,13},{6,2},{10,6},{... | collective-permute-start | bytes 786440 | tf_op jit(solution)/shard_map/ppermute | solution.py:546
  58.8 15.0 %collective-permute-start.20 = (bf16[256,512]{1,0:T(8,128)(2,1)S(1)}, bf16[256,512]{1,0:T(8,128)(2,1)S(1)}, u32[]{:S(2)}, u32[]{:S(2)}) collective-permute-start(bf16[256,512]{1,0:T(8,128)(2,1)S(1)} %broadcast_select_fusion.refs_1_), channel_id=1, source_target_pairs={{0,4},{4,8},{8,12},{12,0},{1,5},{5,9},{9,13},{13,1},{2,6},{6,10},{... | collective-permute-start | bytes 786440 | tf_op jit(solution)/shard_map/ppermute | solution.py:545
  60.4 20.6 %collective-permute-start.21 = (bf16[256,512]{1,0:T(8,128)(2,1)S(1)}, bf16[256,512]{1,0:T(8,128)(2,1)S(1)}, u32[]{:S(2)}, u32[]{:S(2)}) collective-permute-start(bf16[256,512]{1,0:T(8,128)(2,1)S(1)} %broadcast_select_fusion.1.refs_0_), channel_id=1, source_target_pairs={{4,0},{8,4},{12,8},{0,12},{5,1},{9,5},{13,9},{1,13},{6,2},{10,6},{... | collective-permute-start | bytes 786440 | tf_op jit(solution)/shard_map/ppermute | solution.py:546
  62.7 22.3 %collective-permute-start.19 = (bf16[256,512]{1,0:T(8,128)(2,1)S(1)}, bf16[256,512]{1,0:T(8,128)(2,1)S(1)}, u32[]{:S(2)}, u32[]{:S(2)}) collective-permute-start(bf16[256,512]{1,0:T(8,128)(2,1)S(1)} %broadcast_select_fusion.1.refs_0_), channel_id=1, source_target_pairs={{0,4},{4,8},{8,12},{12,0},{1,5},{5,9},{9,13},{13,1},{2,6},{6,10},{... | collective-permute-start | bytes 786440 | tf_op jit(solution)/shard_map/ppermute | solution.py:545
  69.8 19.0 %collective-permute-start.6 = (bf16[256,512]{1,0:T(8,128)(2,1)S(1)}, bf16[256,512]{1,0:T(8,128)(2,1)S(1)}, u32[]{:S(2)}, u32[]{:S(2)}) collective-permute-start(bf16[256,512]{1,0:T(8,128)(2,1)S(1)} %select_select_fusion.3), channel_id=1, source_target_pairs={{4,0},{12,4},{8,12},{0,8},{5,1},{13,5},{9,13},{1,9},{6,2},{14,6},{... | collective-permute-start | bytes 786440 | tf_op jit(solution)/shard_map/ppermute | solution.py:548
  73.8 24.1 %collective-permute-start.24 = (bf16[256,512]{1,0:T(8,128)(2,1)S(1)}, bf16[256,512]{1,0:T(8,128)(2,1)S(1)}, u32[]{:S(2)}, u32[]{:S(2)}) collective-permute-start(bf16[256,512]{1,0:T(8,128)(2,1)S(1)} %select_select_fusion), channel_id=1, source_target_pairs={{4,0},{12,4},{8,12},{0,8},{5,1},{13,5},{9,13},{1,9},{6,2},{14,6},{... | collective-permute-start | bytes 786440 | tf_op jit(solution)/shard_map/ppermute | solution.py:548
  85.1 13.0 %collective-permute-start.23 = (bf16[256,512]{1,0:T(8,128)(2,1)S(1)}, bf16[256,512]{1,0:T(8,128)(2,1)S(1)}, u32[]{:S(2)}, u32[]{:S(2)}) collective-permute-start(bf16[256,512]{1,0:T(8,128)(2,1)S(1)} %select_select_fusion.1), channel_id=1, source_target_pairs={{4,0},{12,4},{8,12},{0,8},{5,1},{13,5},{9,13},{1,9},{6,2},{14,6},{... | collective-permute-start | bytes 786440 | tf_op jit(solution)/shard_map/ppermute | solution.py:548
  95.2 26.9 %collective-permute-start.8 = (bf16[1024,512]{1,0:T(8,128)(2,1)}, bf16[1024,512]{1,0:T(8,128)(2,1)S(1)}, u32[]{:S(2)}, u32[]{:S(2)}) collective-permute-start(bf16[1024,512]{1,0:T(8,128)(2,1)} %get-tuple-element.47.refs_0_), channel_id=1, source_target_pairs={{0,16},{16,0},{1,17},{17,1},{2,18},{18,2},{3,19},{19,3},{4,20},{20... | collective-permute-start | bytes 3145736 | tf_op jit(solution)/shard_map/ppermute | solution.py:605
  104.2 1.3 copy-start
  105.5 36.1 %collective-permute-start.25 = (bf16[1024,512]{1,0:T(8,128)(2,1)}, bf16[1024,512]{1,0:T(8,128)(2,1)}, u32[]{:S(2)}, u32[]{:S(2)}) collective-permute-start(bf16[1024,512]{1,0:T(8,128)(2,1)} %get-tuple-element.66.refs_2_), channel_id=1, source_target_pairs={{0,16},{16,0},{1,17},{17,1},{2,18},{18,2},{3,19},{19,3},{4,20},{20... | collective-permute-start | bytes 3145736 | tf_op jit(solution)/shard_map/ppermute | solution.py:611
  107.9 1.6 copy-start.2
  113.7 17.6 %copy-start.1 = (bf16[2048,512]{1,0:T(8,128)(2,1)S(1)}, bf16[2048,512]{1,0:T(8,128)(2,1)}, u32[]{:S(2)}) copy-start(bf16[2048,512]{1,0:T(8,128)(2,1)} %copy-done) | copy-start | bytes 6291460
  128.9 21.5 %collective-permute-start.9 = (bf16[256,512]{1,0:T(8,128)(2,1)S(1)}, bf16[256,512]{1,0:T(8,128)(2,1)S(1)}, u32[]{:S(2)}, u32[]{:S(2)}) collective-permute-start(bf16[256,512]{1,0:T(8,128)(2,1)S(1)} %get-tuple-element.50), channel_id=1, source_target_pairs={{0,4},{4,12},{12,8},{8,0},{1,5},{5,13},{13,9},{9,1},{2,6},{6,14},{... | collective-permute-start | bytes 786440 | tf_op jit(solution)/shard_map/ppermute | solution.py:559
  134.0 18.9 %collective-permute-start.12 = (bf16[256,512]{1,0:T(8,128)(2,1)S(1)}, bf16[256,512]{1,0:T(8,128)(2,1)S(1)}, u32[]{:S(2)}, u32[]{:S(2)}) collective-permute-start(bf16[256,512]{1,0:T(8,128)(2,1)S(1)} %get-tuple-element.54), channel_id=1, source_target_pairs={{0,4},{4,12},{12,8},{8,0},{1,5},{5,13},{13,9},{9,1},{2,6},{6,14},{... | collective-permute-start | bytes 786440 | tf_op jit(solution)/shard_map/ppermute | solution.py:559
  147.3 12.9 %collective-permute-start.26 = (bf16[256,512]{1,0:T(8,128)(2,1)S(1)}, bf16[256,512]{1,0:T(8,128)(2,1)S(1)}, u32[]{:S(2)}, u32[]{:S(2)}) collective-permute-start(bf16[256,512]{1,0:T(8,128)(2,1)S(1)} %get-tuple-element.71), channel_id=1, source_target_pairs={{0,4},{4,12},{12,8},{8,0},{1,5},{5,13},{13,9},{9,1},{2,6},{6,14},{... | collective-permute-start | bytes 786440 | tf_op jit(solution)/shard_map/ppermute | solution.py:559
  150.5 29.5 %collective-permute-start.10 = (bf16[256,512]{1,0:T(8,128)(2,1)S(1)}, bf16[256,512]{1,0:T(8,128)(2,1)S(1)}, u32[]{:S(2)}, u32[]{:S(2)}) collective-permute-start(bf16[256,512]{1,0:T(8,128)(2,1)S(1)} %get-tuple-element.83), channel_id=1, source_target_pairs={{4,0},{8,4},{12,8},{0,12},{5,1},{9,5},{13,9},{1,13},{6,2},{10,6},{... | collective-permute-start | bytes 786440 | tf_op jit(solution)/shard_map/ppermute | solution.py:560
  152.1 31.8 %collective-permute-start.11 = (bf16[256,512]{1,0:T(8,128)(2,1)S(1)}, bf16[256,512]{1,0:T(8,128)(2,1)S(1)}, u32[]{:S(2)}, u32[]{:S(2)}) collective-permute-start(bf16[256,512]{1,0:T(8,128)(2,1)S(1)} %get-tuple-element.84), channel_id=1, source_target_pairs={{0,4},{4,8},{8,12},{12,0},{1,5},{5,9},{9,13},{13,1},{2,6},{6,10},{... | collective-permute-start | bytes 786440 | tf_op jit(solution)/shard_map/ppermute | solution.py:561
  152.8 27.0 %collective-permute-start.29 = (bf16[256,512]{1,0:T(8,128)(2,1)S(1)}, bf16[256,512]{1,0:T(8,128)(2,1)S(1)}, u32[]{:S(2)}, u32[]{:S(2)}) collective-permute-start(bf16[256,512]{1,0:T(8,128)(2,1)S(1)} %get-tuple-element.75), channel_id=1, source_target_pairs={{0,4},{4,12},{12,8},{8,0},{1,5},{5,13},{13,9},{9,1},{2,6},{6,14},{... | collective-permute-start | bytes 786440 | tf_op jit(solution)/shard_map/ppermute | solution.py:559
  153.0 32.0 %collective-permute-start.13 = (bf16[256,512]{1,0:T(8,128)(2,1)S(1)}, bf16[256,512]{1,0:T(8,128)(2,1)S(1)}, u32[]{:S(2)}, u32[]{:S(2)}) collective-permute-start(bf16[256,512]{1,0:T(8,128)(2,1)S(1)} %get-tuple-element.81), channel_id=1, source_target_pairs={{4,0},{8,4},{12,8},{0,12},{5,1},{9,5},{13,9},{1,13},{6,2},{10,6},{... | collective-permute-start | bytes 786440 | tf_op jit(solution)/shard_map/ppermute | solution.py:560
  160.2 27.7 %collective-permute-start.14 = (bf16[256,512]{1,0:T(8,128)(2,1)S(1)}, bf16[256,512]{1,0:T(8,128)(2,1)S(1)}, u32[]{:S(2)}, u32[]{:S(2)}) collective-permute-start(bf16[256,512]{1,0:T(8,128)(2,1)S(1)} %get-tuple-element.82), channel_id=1, source_target_pairs={{0,4},{4,8},{8,12},{12,0},{1,5},{5,9},{9,13},{13,1},{2,6},{6,10},{... | collective-permute-start | bytes 786440 | tf_op jit(solution)/shard_map/ppermute | solution.py:561
  179.9 12.8 %collective-permute-start.28 = (bf16[256,512]{1,0:T(8,128)(2,1)S(1)}, bf16[256,512]{1,0:T(8,128)(2,1)S(1)}, u32[]{:S(2)}, u32[]{:S(2)}) collective-permute-start(bf16[256,512]{1,0:T(8,128)(2,1)S(1)} %get-tuple-element.79), channel_id=1, source_target_pairs={{0,4},{4,8},{8,12},{12,0},{1,5},{5,9},{9,13},{13,1},{2,6},{6,10},{... | collective-permute-start | bytes 786440 | tf_op jit(solution)/shard_map/ppermute | solution.py:561
  180.0 17.2 %collective-permute-start.27 = (bf16[256,512]{1,0:T(8,128)(2,1)S(1)}, bf16[256,512]{1,0:T(8,128)(2,1)S(1)}, u32[]{:S(2)}, u32[]{:S(2)}) collective-permute-start(bf16[256,512]{1,0:T(8,128)(2,1)S(1)} %get-tuple-element.80), channel_id=1, source_target_pairs={{4,0},{8,4},{12,8},{0,12},{5,1},{9,5},{13,9},{1,13},{6,2},{10,6},{... | collective-permute-start | bytes 786440 | tf_op jit(solution)/shard_map/ppermute | solution.py:560
  183.9 16.2 %collective-permute-start.31 = (bf16[256,512]{1,0:T(8,128)(2,1)S(1)}, bf16[256,512]{1,0:T(8,128)(2,1)S(1)}, u32[]{:S(2)}, u32[]{:S(2)}) collective-permute-start(bf16[256,512]{1,0:T(8,128)(2,1)S(1)} %get-tuple-element.77), channel_id=1, source_target_pairs={{0,4},{4,8},{8,12},{12,0},{1,5},{5,9},{9,13},{13,1},{2,6},{6,10},{... | collective-permute-start | bytes 786440 | tf_op jit(solution)/shard_map/ppermute | solution.py:561
  185.0 18.5 %collective-permute-start.30 = (bf16[256,512]{1,0:T(8,128)(2,1)S(1)}, bf16[256,512]{1,0:T(8,128)(2,1)S(1)}, u32[]{:S(2)}, u32[]{:S(2)}) collective-permute-start(bf16[256,512]{1,0:T(8,128)(2,1)S(1)} %get-tuple-element.78), channel_id=1, source_target_pairs={{4,0},{8,4},{12,8},{0,12},{5,1},{9,5},{13,9},{1,13},{6,2},{10,6},{... | collective-permute-start | bytes 786440 | tf_op jit(solution)/shard_map/ppermute | solution.py:560

commit v10 on v9

--- a/solution.py
+++ b/solution.py
@@ -99,12 +99,14 @@
 PIECES = 2
 
 
-def conv_body(with_before, first_row, seq_ref, order_ref, tokens_ref, taps_ref, part_ref, keep_ref, send_ref, *refs):
+def conv_body(with_before, first_row, seq_ref, order_ref, tokens_ref, taps_ref, part_hbm, keep_ref, send_ref, *refs):
     if with_before:
-        slots_ref, taps_scr, packed = refs
+        slots_ref, taps_scr, packed, part_ref, moving = refs
         source_ref = tokens_ref
+        for copy in fetches(part_hbm, part_ref, moving):
+            copy.start()
     else:
-        copy_ref, slots_ref, taps_scr, packed, source_ref, arrived, taps_in, taps_arrived, left = refs
+        copy_ref, slots_ref, taps_scr, packed, part_ref, moving, source_ref, arrived, taps_in, taps_arrived, left = refs
     channels, tokens = packed.shape
     tiles_dev = tokens // TILE
     per_frame = FRAME // TILE
@@ -163,32 +165,52 @@
                 packed[rows, place] = value.astype(jnp.bfloat16)
         return carry
 
-    steps = channels // GROUP
-    if with_before:
-        lax.fori_loop(0, steps, advance, 0, unroll=2)
-    else:
-        each = steps // CHUNKS
-
-        def leaving(begin, index):
-            block = pl.ds(begin, each * GROUP)
-            return pltpu.make_async_copy(source_ref.at[block], copy_ref.at[block], left.at[index])
-
-        def chunk(index, carry):
-            begin = index * each * GROUP
-            pltpu.make_async_copy(
-                tokens_ref.at[pl.ds(first_row + begin, each * GROUP)],
-                source_ref.at[pl.ds(begin, each * GROUP)],
-                arrived.at[index],
-            ).wait()
-            leaving(begin, index).start()
-            later = functools.partial(advance, base=begin)
-            return lax.fori_loop(0, each, later, carry, unroll=2)
-
-        lax.fori_loop(0, CHUNKS, chunk, 0)
-        for index in range(CHUNKS):
-            leaving(index * each * GROUP, index).wait()
+    each = channels // CHUNKS
+
+    def block_of(index):
+        return pl.ds(index * each, each)
+
+    def part_copy(index):
+        block = block_of(index)
+        if with_before:
+            return pltpu.make_async_copy(part_hbm.at[block], part_ref.at[block], moving.at[index])
+        return pltpu.make_async_copy(part_ref.at[block], part_hbm.at[block], moving.at[index])
+
+    def arriving(index):
+        theirs = pl.ds(first_row + index * each, each)
+        return pltpu.make_async_copy(
+            tokens_ref.at[theirs], source_ref.at[block_of(index)], arrived.at[index]
+        )
+
+    def leaving(index):
+        block = block_of(index)
+        return pltpu.make_async_copy(source_ref.at[block], copy_ref.at[block], left.at[index])
+
+    def chunk(index, carry):
+        if with_before:
+            part_copy(index).wait()
+        else:
+            arriving(index).wait()
+            leaving(index).start()
+        later = functools.partial(advance, base=index * each)
+        carry = lax.fori_loop(0, each // GROUP, later, carry, unroll=2)
+        if not with_before:
+
+            @pl.when(index > 0)
+            def _():
+                part_copy(index - 1).start()
+
+        return carry
+
+    lax.fori_loop(0, CHUNKS, chunk, 0)
+    if not with_before:
+        part_copy(CHUNKS - 1).start()
     keep_ref[...] = packed[:, : tokens // 2]
     send_ref[...] = packed[:, tokens // 2 :]
+    if not with_before:
+        for index in range(CHUNKS):
+            leaving(index).wait()
+            part_copy(index).wait()
 
 
 def conv_call(seq_here, stripe_order, tokens, conv_taps, piece, part=None):
@@ -202,14 +224,16 @@
         pltpu.SMEM((count // TILE,), jnp.int32),
         pltpu.VMEM((channels, 128), jnp.float32),
         pltpu.VMEM((channels, count), jnp.bfloat16),
+        pltpu.VMEM((channels, count), jnp.float32),
+        pltpu.SemaphoreType.DMA((CHUNKS,)),
     ]
-    in_specs = [smem_spec(), smem_spec(), vmem_spec(), vmem_spec(), vmem_spec()]
+    in_specs = [smem_spec(), smem_spec(), vmem_spec(), vmem_spec(), off_chip_spec()]
     if not with_before:
         in_specs = [smem_spec(), smem_spec(), off_chip_spec(), off_chip_spec()]
         tokens = off_chip(tokens)
-        sum_shape = jax.ShapeDtypeStruct((channels, count), jnp.float32)
+        sum_shape = pltpu.HBM((channels, count), jnp.float32)
         out_shape = [sum_shape] + out_shape + [pltpu.HBM((channels, count), jnp.bfloat16)]
-        out_specs = [vmem_spec()] * 3 + [off_chip_spec()]
+        out_specs = [off_chip_spec(), vmem_spec(), vmem_spec(), off_chip_spec()]
         scratch += [
             pltpu.VMEM((channels, count), jnp.bfloat16),
             pltpu.SemaphoreType.DMA((CHUNKS,)),
@@ -228,7 +252,7 @@
             flops=channels * count * TAPS, bytes_accessed=channels * count * 8, transcendentals=0
         ),
         name="conv",
-    )(seq_here, stripe_order, tokens, conv_taps, *([part] if with_before else []))
+    )(seq_here, stripe_order, tokens, conv_taps, *([off_chip(part)] if with_before else []))
 
 
 def prepare_body(blocks_ref, out_ref, out_out):

time: 206 us -> 208 us (level)
  Pallas kernels: 61.7 us -> 64.2 us
    pallas_call x4, Pallas kernels: 20.3 us -> 22.8 us  [conv_call(): pl.pallas_call(functools.partial(conv_body, with_before, piece * channels...]
  transfers between devices with their start and end apart: 32 -> 32, of which waited for: 17 -> 16; matrix products, arithmetic and copies ran while one was open for 1% -> 1% of each run, Pallas kernels for 26% -> 27%
where the time goes in v10:
time: 208 us
  waiting for transfers between devices  84.3 us (41%)
  Pallas kernels  64.2 us (31%)
  starting transfers between devices  54.1 us (26%)
  local copies, waits for them, and re-layouts  3.25 us (2%)
    ppermute x4, waiting for transfers between devices, reduce_blocks(): across = lax.ppermute(sent, 'tp', FOLDED)  23.6 us
    pallas_call x4, Pallas kernels, conv_call(): pl.pallas_call(functools.partial(conv_body, with_before, piece * channels...  22.8 us
    pallas_call x3, Pallas kernels, attend_call(): pl.pallas_call(functools.partial(attend_body, chunk, tuple((s for _, s in...  20 us
    ppermute x4, waiting for transfers between devices, gather_blocks(): after = lax.ppermute(block, 'tp', BACKWARD)  12.6 us
    pallas_call x2, Pallas kernels, project_pair(): pl.pallas_call(pair_body, in_specs=[smem_spec(), off_chip_spec()] + [vmem...  12.2 us
    ppermute x4, starting transfers between devices, reduce_blocks(): back = lax.ppermute(plus(down, across, here == 2), 'tp', BACKWARD)  11.4 us
    ppermute x4, starting transfers between devices, gather_blocks(): after = lax.ppermute(block, 'tp', BACKWARD)  11 us
    ppermute x2, waiting for transfers between devices, per_device_fast(): before.append(lax.ppermute(tokens, 'seq', [(0, 1)]))  9.52 us
  transfers between devices with their start and end apart: 32, of which 16 were waited for; matrix products, arithmetic and copies ran while one was open for 1% of the time, Pallas kernels for 27%

profile of v10, /device:TPU:0, one launch (start us, length us, event | category | flops | bytes accessed | tf_op | source)
XLA Modules:
  0.0 207.5 jit_solution(12342392083642172905)
XLA Ops:
  0.0 6.3 %conv.5 = (f32[256,1024]{1,0:T(8,128)}, bf16[256,512]{1,0:T(8,128)(2,1)S(1)}, bf16[256,512]{1,0:T(8,128)(2,1)S(1)}, bf16[256,1024]{1,0:T(8,128)(2,1)}) custom-call(s32[1]{0:T(128)} %bitcast.seq_ref, s32[16]{0:T(128)} %order_ref.15, bf16[512,1024]{1,0:T(8,128)(2,1)} %tokens_ref.3, f32[27,512]{1,0:T(8,128)} %taps_ref.7), custom_call_target="tpu_custom_call" | custom-call | flops 7077888 | bytes 2097152 | tf_op jit(solution)/shard_map/conv/pallas_call | solution.py:244
  6.3 4.9 %collective-permute-start.1 = (bf16[256,512]{1,0:T(8,128)(2,1)S(1)}, bf16[256,512]{1,0:T(8,128)(2,1)S(1)}, u32[]{:S(2)}, u32[]{:S(2)}) collective-permute-start(bf16[256,512]{1,0:T(8,128)(2,1)S(1)} %get-tuple-element.44), channel_id=1, source_target_pairs={{0,16},{1,17},{2,18},{3,19},{4,20},{5,21},{6,22},{7,23},{8,24},{9,... | collective-permute-start | bytes 786440 | tf_op jit(solution)/shard_map/ppermute | solution.py:612
  12.5 6.2 %conv.4 = (f32[256,1024]{1,0:T(8,128)}, bf16[256,512]{1,0:T(8,128)(2,1)S(1)}, bf16[256,512]{1,0:T(8,128)(2,1)S(1)}, bf16[256,1024]{1,0:T(8,128)(2,1)}) custom-call(s32[1]{0:T(128)} %bitcast.seq_ref, s32[16]{0:T(128)} %order_ref.15, bf16[512,1024]{1,0:T(8,128)(2,1)} %tokens_ref.3, f32[27,512]{1,0:T(8,128)} %taps_ref.7), custom_call_target="tpu_custom_call" | custom-call | flops 7077888 | bytes 2097152 | tf_op jit(solution)/shard_map/conv/pallas_call | solution.py:244
  21.5 3.7 %collective-permute-start.5 = (bf16[256,512]{1,0:T(8,128)(2,1)S(1)}, bf16[256,512]{1,0:T(8,128)(2,1)S(1)}, u32[]{:S(2)}, u32[]{:S(2)}) collective-permute-start(bf16[256,512]{1,0:T(8,128)(2,1)S(1)} %broadcast_select_fusion.2.refs_1_), channel_id=1, source_target_pairs={{4,0},{8,4},{12,8},{0,12},{5,1},{9,5},{13,9},{1,13},{6,2},{10,6},{... | collective-permute-start | bytes 786440 | tf_op jit(solution)/shard_map/ppermute | solution.py:570
  25.2 4.0 %collective-permute-done.17.tokens_ref = bf16[256,1024]{1,0:T(8,128)(2,1)S(1)} collective-permute-done((bf16[256,1024]{1,0:T(8,128)(2,1)}, bf16[256,1024]{1,0:T(8,128)(2,1)S(1)}, u32[]{:S(2)}, u32[]{:S(2)}) %collective-permute-start.17) | collective-permute-done | bytes 524320 | tf_op jit(solution)/shard_map/ppermute | solution.py:614
  29.2 5.1 %conv.7 = (bf16[256,512]{1,0:T(8,128)(2,1)S(1)}, bf16[256,512]{1,0:T(8,128)(2,1)S(1)}) custom-call(s32[1]{0:T(128)} %bitcast.seq_ref, s32[16]{0:T(128)} %order_ref.15, bf16[256,1024]{1,0:T(8,128)(2,1)S(1)} %collective-permute-done.17.tokens_ref, f32[27,512]{1,0:T(8,128)} %taps_ref.7, f32[256,1024]{1,0:T(8,128)} %get-tuple-element.61.part_hbm), custom_call_target="tpu_custom_call" | custom-call | flops 7077888 | bytes 2097152 | tf_op jit(solution)/shard_map/conv/pallas_call | solution.py:244
  35.7 3.7 %collective-permute-start.4 = (bf16[256,512]{1,0:T(8,128)(2,1)S(1)}, bf16[256,512]{1,0:T(8,128)(2,1)S(1)}, u32[]{:S(2)}, u32[]{:S(2)}) collective-permute-start(bf16[256,512]{1,0:T(8,128)(2,1)S(1)} %broadcast_select_fusion.3.refs_0_), channel_id=1, source_target_pairs={{4,0},{8,4},{12,8},{0,12},{5,1},{9,5},{13,9},{1,13},{6,2},{10,6},{... | collective-permute-start | bytes 786440 | tf_op jit(solution)/shard_map/ppermute | solution.py:570
  39.3 5.6 %collective-permute-done.15.tokens_ref = bf16[256,1024]{1,0:T(8,128)(2,1)S(1)} collective-permute-done((bf16[256,1024]{1,0:T(8,128)(2,1)}, bf16[256,1024]{1,0:T(8,128)(2,1)S(1)}, u32[]{:S(2)}, u32[]{:S(2)}) %collective-permute-start.15) | collective-permute-done | bytes 524320 | tf_op jit(solution)/shard_map/ppermute | solution.py:614
  44.9 1.6 collective-permute-start.2
  46.5 5.1 %conv.6 = (bf16[256,512]{1,0:T(8,128)(2,1)S(1)}, bf16[256,512]{1,0:T(8,128)(2,1)S(1)}) custom-call(s32[1]{0:T(128)} %bitcast.seq_ref, s32[16]{0:T(128)} %order_ref.15, bf16[256,1024]{1,0:T(8,128)(2,1)S(1)} %collective-permute-done.15.tokens_ref, f32[27,512]{1,0:T(8,128)} %taps_ref.7, f32[256,1024]{1,0:T(8,128)} %get-tuple-element.57.part_hbm), custom_call_target="tpu_custom_call" | custom-call | flops 7077888 | bytes 2097152 | tf_op jit(solution)/shard_map/conv/pallas_call | solution.py:244
  53.0 2.6 %collective-permute-start.7 = (bf16[256,512]{1,0:T(8,128)(2,1)S(1)}, bf16[256,512]{1,0:T(8,128)(2,1)S(1)}, u32[]{:S(2)}, u32[]{:S(2)}) collective-permute-start(bf16[256,512]{1,0:T(8,128)(2,1)S(1)} %select_select_fusion.2), channel_id=1, source_target_pairs={{4,0},{12,4},{8,12},{0,8},{5,1},{13,5},{9,13},{1,9},{6,2},{14,6},{... | collective-permute-start | bytes 786440 | tf_op jit(solution)/shard_map/ppermute | solution.py:572
  55.7 1.4 collective-permute-start.22
  57.1 3.4 %collective-permute-done.16 = bf16[256,512]{1,0:T(8,128)(2,1)S(1)} collective-permute-done((bf16[256,512]{1,0:T(8,128)(2,1)S(1)}, bf16[256,512]{1,0:T(8,128)(2,1)S(1)}, u32[]{:S(2)}, u32[]{:S(2)}) %collective-permute-start.16) | collective-permute-done | bytes 262176 | tf_op jit(solution)/shard_map/ppermute | solution.py:624
  60.5 1.6 collective-permute-start.20
  62.1 2.3 %collective-permute-start.21 = (bf16[256,512]{1,0:T(8,128)(2,1)S(1)}, bf16[256,512]{1,0:T(8,128)(2,1)S(1)}, u32[]{:S(2)}, u32[]{:S(2)}) collective-permute-start(bf16[256,512]{1,0:T(8,128)(2,1)S(1)} %broadcast_select_fusion.1.refs_0_), channel_id=1, source_target_pairs={{4,0},{8,4},{12,8},{0,12},{5,1},{9,5},{13,9},{1,13},{6,2},{10,6},{... | collective-permute-start | bytes 786440 | tf_op jit(solution)/shard_map/ppermute | solution.py:570
  64.4 7.1 %collective-permute-done.22.refs_5_ = bf16[256,512]{1,0:T(8,128)(2,1)S(1)} collective-permute-done((bf16[256,512]{1,0:T(8,128)(2,1)S(1)}, bf16[256,512]{1,0:T(8,128)(2,1)S(1)}, u32[]{:S(2)}, u32[]{:S(2)}) %collective-permute-start.22) | collective-permute-done | bytes 262176 | tf_op jit(solution)/shard_map/ppermute | solution.py:570
  71.5 3.9 %collective-permute-done.20.refs_3_ = bf16[256,512]{1,0:T(8,128)(2,1)S(1)} collective-permute-done((bf16[256,512]{1,0:T(8,128)(2,1)S(1)}, bf16[256,512]{1,0:T(8,128)(2,1)S(1)}, u32[]{:S(2)}, u32[]{:S(2)}) %collective-permute-start.20) | collective-permute-done | bytes 262176 | tf_op jit(solution)/shard_map/ppermute | solution.py:569
  75.5 1.7 collective-permute-start.24
  77.2 5.5 %collective-permute-done.21.refs_4_ = bf16[256,512]{1,0:T(8,128)(2,1)S(1)} collective-permute-done((bf16[256,512]{1,0:T(8,128)(2,1)S(1)}, bf16[256,512]{1,0:T(8,128)(2,1)S(1)}, u32[]{:S(2)}, u32[]{:S(2)}) %collective-permute-start.21) | collective-permute-done | bytes 262176 | tf_op jit(solution)/shard_map/ppermute | solution.py:570
  82.7 4.0 %collective-permute-done.19.refs_2_ = bf16[256,512]{1,0:T(8,128)(2,1)S(1)} collective-permute-done((bf16[256,512]{1,0:T(8,128)(2,1)S(1)}, bf16[256,512]{1,0:T(8,128)(2,1)S(1)}, u32[]{:S(2)}, u32[]{:S(2)}) %collective-permute-start.19) | collective-permute-done | bytes 262176 | tf_op jit(solution)/shard_map/ppermute | solution.py:569
  86.7 1.6 collective-permute-start.23
  88.4 2.1 %collective-permute-done.6.refs_6_ = bf16[256,512]{1,0:T(8,128)(2,1)S(1)} collective-permute-done((bf16[256,512]{1,0:T(8,128)(2,1)S(1)}, bf16[256,512]{1,0:T(8,128)(2,1)S(1)}, u32[]{:S(2)}, u32[]{:S(2)}) %collective-permute-start.6) | collective-permute-done | bytes 262176 | tf_op jit(solution)/shard_map/ppermute | solution.py:572
  90.8 6.0 %pair.2 = (bf16[1024,512]{1,0:T(8,128)(2,1)}, bf16[2048,512]{1,0:T(8,128)(2,1)S(1)}, f32[1,512]{1,0:T(1,128)S(1)}) custom-call(s32[4]{0:T(128)S(1)} %pad_add_fusion.blocks_ref, bf16[1536,2048]{1,0:T(8,128)(2,1)} %bitcast.8, f32[2048,128]{1,0:T(8,128)S(1)} %broadcast_in_dim.42.gains_ref, bf16[256,512]{1,0:T(8,128)(2,1)S(1)} %broadcast_select_fusion.3.refs_0_, ...), custom_call_target="tpu_custom_call" | custom-call | flops 2147483648 | bytes 9437184 | tf_op jit(solution)/shard_map/pair/pallas_call | solution.py:329
  96.9 2.7 %collective-permute-start.8 = (bf16[1024,512]{1,0:T(8,128)(2,1)}, bf16[1024,512]{1,0:T(8,128)(2,1)S(1)}, u32[]{:S(2)}, u32[]{:S(2)}) collective-permute-start(bf16[1024,512]{1,0:T(8,128)(2,1)} %get-tuple-element.47.refs_0_), channel_id=1, source_target_pairs={{0,16},{16,0},{1,17},{17,1},{2,18},{18,2},{3,19},{19,3},{4,20},{20... | collective-permute-start | bytes 3145736 | tf_op jit(solution)/shard_map/ppermute | solution.py:629
  99.6 6.1 %pair.3 = (bf16[1024,512]{1,0:T(8,128)(2,1)}, bf16[2048,512]{1,0:T(8,128)(2,1)S(1)}, f32[1,512]{1,0:T(1,128)S(1)}) custom-call(s32[4]{0:T(128)S(1)} %pad_add_fusion.blocks_ref, bf16[1536,2048]{1,0:T(8,128)(2,1)} %bitcast.9, f32[2048,128]{1,0:T(8,128)S(1)} %broadcast_in_dim.42.gains_ref, bf16[256,512]{1,0:T(8,128)(2,1)S(1)} %broadcast_select_fusion.1.refs_0_, ...), custom_call_target="tpu_custom_call" | custom-call | flops 2147483648 | bytes 9437184 | tf_op jit(solution)/shard_map/pair/pallas_call | solution.py:329
  105.7 1.3 copy-done
  107.0 2.2 %collective-permute-start.25 = (bf16[1024,512]{1,0:T(8,128)(2,1)}, bf16[1024,512]{1,0:T(8,128)(2,1)}, u32[]{:S(2)}, u32[]{:S(2)}) collective-permute-start(bf16[1024,512]{1,0:T(8,128)(2,1)} %get-tuple-element.66.refs_2_), channel_id=1, source_target_pairs={{0,16},{16,0},{1,17},{17,1},{2,18},{18,2},{3,19},{19,3},{4,20},{20... | collective-permute-start | bytes 3145736 | tf_op jit(solution)/shard_map/ppermute | solution.py:635
  109.3 1.6 copy-done.2
  110.9 1.5 prepare.1.refs_2_.refs_3_
  112.4 2.7 %query.2.query_ref = bf16[512,512]{1,0:T(8,128)(2,1)S(1)} custom-call(bf16[1536,2048]{1,0:T(8,128)(2,1)} %bitcast.10, bf16[2048,512]{1,0:T(8,128)(2,1)S(1)} %get-tuple-element.45.tokens_ref, f32[1,512]{1,0:T(1,128)S(1)} %get-tuple-element.46.inverse_ref), custom_call_target="tpu_custom_call" | custom-call | flops 1073741824 | bytes 4718592 | tf_op jit(solution)/shard_map/query/pallas_call | solution.py:356
  115.1 8.7 %collective-permute-done.8.refs_1_ = bf16[1024,512]{1,0:T(8,128)(2,1)S(1)} collective-permute-done((bf16[1024,512]{1,0:T(8,128)(2,1)}, bf16[1024,512]{1,0:T(8,128)(2,1)S(1)}, u32[]{:S(2)}, u32[]{:S(2)}) %collective-permute-start.8) | collective-permute-done | bytes 1048608 | tf_op jit(solution)/shard_map/ppermute | solution.py:629
  123.8 6.8 %attend.3 = (bf16[256,512]{1,0:T(8,128)(2,1)S(1)}, bf16[256,512]{1,0:T(8,128)(2,1)S(1)}, bf16[256,512]{1,0:T(8,128)(2,1)S(1)}, bf16[256,512]{1,0:T(8,128)(2,1)S(...) custom-call(s32[1]{0:T(128)} %bitcast.seq_ref, ...), custom_call_target="tpu_custom_call" | custom-call | flops 1073741824 | bytes 3145728 | tf_op jit(solution)/shard_map/attend/pallas_call | solution.py:496
  130.6 2.4 %collective-permute-start.9 = (bf16[256,512]{1,0:T(8,128)(2,1)S(1)}, bf16[256,512]{1,0:T(8,128)(2,1)S(1)}, u32[]{:S(2)}, u32[]{:S(2)}) collective-permute-start(bf16[256,512]{1,0:T(8,128)(2,1)S(1)} %get-tuple-element.50), channel_id=1, source_target_pairs={{0,4},{4,12},{12,8},{8,0},{1,5},{5,13},{13,9},{9,1},{2,6},{6,14},{... | collective-permute-start | bytes 786440 | tf_op jit(solution)/shard_map/ppermute | solution.py:583
  133.0 2.7 %query.3.query_ref = bf16[512,512]{1,0:T(8,128)(2,1)S(1)} custom-call(bf16[1536,2048]{1,0:T(8,128)(2,1)} %bitcast.11, bf16[2048,512]{1,0:T(8,128)(2,1)S(1)} %copy-done.1, f32[1,512]{1,0:T(1,128)S(1)} %get-tuple-element.65.inverse_ref), custom_call_target="tpu_custom_call" | custom-call | flops 1073741824 | bytes 4718592 | tf_op jit(solution)/shard_map/query/pallas_call | solution.py:356
  135.7 7.6 %attend.4 = (f32[4,2,512]{2,1,0:T(2,128)S(1)}, f32[512,512]{1,0:T(8,128)S(1)}) custom-call(s32[1]{0:T(128)} %bitcast.seq_ref, s32[16]{0:T(128)} %order_ref.15, s32[16,16]{1,0:T(8,128)} %mask_ref.5, bf16[512,512]{1,0:T(8,128)(2,1)S(1)} %query.3.query_ref, bf16[1024,512]{1,0:T(8,128)(2,1)} %get-tuple-element.47.refs_0_, ...), custom_call_target="tpu_custom_call" | custom-call | flops 1610612736 | bytes 4194304 | tf_op jit(solution)/shard_map/attend/pallas_call | solution.py:496
  143.4 5.6 %attend.5 = (bf16[256,512]{1,0:T(8,128)(2,1)S(1)}, bf16[256,512]{1,0:T(8,128)(2,1)S(1)}, bf16[256,512]{1,0:T(8,128)(2,1)S(1)}, bf16[256,512]{1,0:T(8,128)(2,1)S(...) custom-call(s32[1]{0:T(128)} %bitcast.seq_ref, ...), custom_call_target="tpu_custom_call" | custom-call | flops 536870912 | bytes 2097152 | tf_op jit(solution)/shard_map/attend/pallas_call | solution.py:496
  149.0 3.1 %collective-permute-start.26 = (bf16[256,512]{1,0:T(8,128)(2,1)S(1)}, bf16[256,512]{1,0:T(8,128)(2,1)S(1)}, u32[]{:S(2)}, u32[]{:S(2)}) collective-permute-start(bf16[256,512]{1,0:T(8,128)(2,1)S(1)} %get-tuple-element.71), channel_id=1, source_target_pairs={{0,4},{4,12},{12,8},{8,0},{1,5},{5,13},{13,9},{9,1},{2,6},{6,14},{... | collective-permute-start | bytes 786440 | tf_op jit(solution)/shard_map/ppermute | solution.py:583
  152.2 1.6 collective-permute-start.10
  154.7 3.1 %collective-permute-start.13 = (bf16[256,512]{1,0:T(8,128)(2,1)S(1)}, bf16[256,512]{1,0:T(8,128)(2,1)S(1)}, u32[]{:S(2)}, u32[]{:S(2)}) collective-permute-start(bf16[256,512]{1,0:T(8,128)(2,1)S(1)} %get-tuple-element.81), channel_id=1, source_target_pairs={{4,0},{8,4},{12,8},{0,12},{5,1},{9,5},{13,9},{1,13},{6,2},{10,6},{... | collective-permute-start | bytes 786440 | tf_op jit(solution)/shard_map/ppermute | solution.py:584
  157.9 4.1 %collective-permute-done.26.refs_5_ = bf16[256,512]{1,0:T(8,128)(2,1)S(1)} collective-permute-done((bf16[256,512]{1,0:T(8,128)(2,1)S(1)}, bf16[256,512]{1,0:T(8,128)(2,1)S(1)}, u32[]{:S(2)}, u32[]{:S(2)}) %collective-permute-start.26) | collective-permute-done | bytes 262176 | tf_op jit(solution)/shard_map/ppermute | solution.py:583
  162.1 19.5 %collective-permute-done.29.refs_9_ = bf16[256,512]{1,0:T(8,128)(2,1)S(1)} collective-permute-done((bf16[256,512]{1,0:T(8,128)(2,1)S(1)}, bf16[256,512]{1,0:T(8,128)(2,1)S(1)}, u32[]{:S(2)}, u32[]{:S(2)}) %collective-permute-start.29) | collective-permute-done | bytes 262176 | tf_op jit(solution)/shard_map/ppermute | solution.py:583
  181.7 3.9 %collective-permute-start.27 = (bf16[256,512]{1,0:T(8,128)(2,1)S(1)}, bf16[256,512]{1,0:T(8,128)(2,1)S(1)}, u32[]{:S(2)}, u32[]{:S(2)}) collective-permute-start(bf16[256,512]{1,0:T(8,128)(2,1)S(1)} %get-tuple-element.80), channel_id=1, source_target_pairs={{4,0},{8,4},{12,8},{0,12},{5,1},{9,5},{13,9},{1,13},{6,2},{10,6},{... | collective-permute-start | bytes 786440 | tf_op jit(solution)/shard_map/ppermute | solution.py:584
  186.7 2.8 %collective-permute-start.30 = (bf16[256,512]{1,0:T(8,128)(2,1)S(1)}, bf16[256,512]{1,0:T(8,128)(2,1)S(1)}, u32[]{:S(2)}, u32[]{:S(2)}) collective-permute-start(bf16[256,512]{1,0:T(8,128)(2,1)S(1)} %get-tuple-element.78), channel_id=1, source_target_pairs={{4,0},{8,4},{12,8},{0,12},{5,1},{9,5},{13,9},{1,13},{6,2},{10,6},{... | collective-permute-start | bytes 786440 | tf_op jit(solution)/shard_map/ppermute | solution.py:584
  189.8 4.6 %collective-permute-done.28.refs_4_ = bf16[256,512]{1,0:T(8,128)(2,1)S(1)} collective-permute-done((bf16[256,512]{1,0:T(8,128)(2,1)S(1)}, bf16[256,512]{1,0:T(8,128)(2,1)S(1)}, u32[]{:S(2)}, u32[]{:S(2)}) %collective-permute-start.28) | collective-permute-done | bytes 262176 | tf_op jit(solution)/shard_map/ppermute | solution.py:585
  194.4 4.6 %collective-permute-done.27.refs_3_ = bf16[256,512]{1,0:T(8,128)(2,1)S(1)} collective-permute-done((bf16[256,512]{1,0:T(8,128)(2,1)S(1)}, bf16[256,512]{1,0:T(8,128)(2,1)S(1)}, u32[]{:S(2)}, u32[]{:S(2)}) %collective-permute-start.27) | collective-permute-done | bytes 262176 | tf_op jit(solution)/shard_map/ppermute | solution.py:584
  198.9 2.9 %collective-permute-done.31.refs_8_ = bf16[256,512]{1,0:T(8,128)(2,1)S(1)} collective-permute-done((bf16[256,512]{1,0:T(8,128)(2,1)S(1)}, bf16[256,512]{1,0:T(8,128)(2,1)S(1)}, u32[]{:S(2)}, u32[]{:S(2)}) %collective-permute-start.31) | collective-permute-done | bytes 262176 | tf_op jit(solution)/shard_map/ppermute | solution.py:585
  201.9 3.3 %collective-permute-done.30.refs_7_ = bf16[256,512]{1,0:T(8,128)(2,1)S(1)} collective-permute-done((bf16[256,512]{1,0:T(8,128)(2,1)S(1)}, bf16[256,512]{1,0:T(8,128)(2,1)S(1)}, u32[]{:S(2)}, u32[]{:S(2)}) %collective-permute-start.30) | collective-permute-done | bytes 262176 | tf_op jit(solution)/shard_map/ppermute | solution.py:584
  205.2 2.3 %place.1 = bf16[512,1024]{1,0:T(8,128)(2,1)} custom-call(s32[1]{0:T(128)} %bitcast.seq_ref, s32[16]{0:T(128)} %order_ref.15, s32[1]{0:T(128)} %bitcast.1.ends_ref, bf16[256,512]{1,0:T(8,128)(2,1)S(1)} %fusion.13.refs_0_, bf16[256,512]{1,0:T(8,128)(2,1)S(1)} %fusion.19.refs_1_, bf16[256,512]{1,0:T(8,128)(2,1)S(1)} %get-tuple-element.69.refs_2_, ...), custom_call_target="tpu_custom_call" | custom-call | flops 1048576 | bytes 3670016 | tf_op jit(solution)/shard_map/place/pallas_call | solution.py:548
  (53 shorter events, 10.0 us)
Async XLA Ops:
  6.3 15.2 %collective-permute-start.1 = (bf16[256,512]{1,0:T(8,128)(2,1)S(1)}, bf16[256,512]{1,0:T(8,128)(2,1)S(1)}, u32[]{:S(2)}, u32[]{:S(2)}) collective-permute-start(bf16[256,512]{1,0:T(8,128)(2,1)S(1)} %get-tuple-element.44), channel_id=1, source_target_pairs={{0,16},{1,17},{2,18},{3,19},{4,20},{5,21},{6,22},{7,23},{8,24},{9,... | collective-permute-start | bytes 786440 | tf_op jit(solution)/shard_map/ppermute | solution.py:612
  11.2 18.0 %collective-permute-start.17 = (bf16[256,1024]{1,0:T(8,128)(2,1)}, bf16[256,1024]{1,0:T(8,128)(2,1)S(1)}, u32[]{:S(2)}, u32[]{:S(2)}) collective-permute-start(bf16[256,1024]{1,0:T(8,128)(2,1)} %get-tuple-element.60), channel_id=1, source_target_pairs={{0,16},{1,17},{2,18},{3,19},{4,20},{5,21},{6,22},{7,23},{8,24},{9,... | collective-permute-start | bytes 1572872 | tf_op jit(solution)/shard_map/ppermute | solution.py:614
  18.8 16.9 %collective-permute-start = (bf16[256,512]{1,0:T(8,128)(2,1)S(1)}, bf16[256,512]{1,0:T(8,128)(2,1)S(1)}, u32[]{:S(2)}, u32[]{:S(2)}) collective-permute-start(bf16[256,512]{1,0:T(8,128)(2,1)S(1)} %get-tuple-element.42), channel_id=1, source_target_pairs={{0,16},{1,17},{2,18},{3,19},{4,20},{5,21},{6,22},{7,23},{8,24},{9,... | collective-permute-start | bytes 786440 | tf_op jit(solution)/shard_map/ppermute | solution.py:612
  20.1 24.8 %collective-permute-start.15 = (bf16[256,1024]{1,0:T(8,128)(2,1)}, bf16[256,1024]{1,0:T(8,128)(2,1)S(1)}, u32[]{:S(2)}, u32[]{:S(2)}) collective-permute-start(bf16[256,1024]{1,0:T(8,128)(2,1)} %get-tuple-element.56), channel_id=1, source_target_pairs={{0,16},{1,17},{2,18},{3,19},{4,20},{5,21},{6,22},{7,23},{8,24},{9,... | collective-permute-start | bytes 1572872 | tf_op jit(solution)/shard_map/ppermute | solution.py:614
  21.5 30.1 %collective-permute-start.5 = (bf16[256,512]{1,0:T(8,128)(2,1)S(1)}, bf16[256,512]{1,0:T(8,128)(2,1)S(1)}, u32[]{:S(2)}, u32[]{:S(2)}) collective-permute-start(bf16[256,512]{1,0:T(8,128)(2,1)S(1)} %broadcast_select_fusion.2.refs_1_), channel_id=1, source_target_pairs={{4,0},{8,4},{12,8},{0,12},{5,1},{9,5},{13,9},{1,13},{6,2},{10,6},{... | collective-permute-start | bytes 786440 | tf_op jit(solution)/shard_map/ppermute | solution.py:570
  25.1 27.8 %collective-permute-start.3 = (bf16[256,512]{1,0:T(8,128)(2,1)S(1)}, bf16[256,512]{1,0:T(8,128)(2,1)S(1)}, u32[]{:S(2)}, u32[]{:S(2)}) collective-permute-start(bf16[256,512]{1,0:T(8,128)(2,1)S(1)} %broadcast_select_fusion.2.refs_1_), channel_id=1, source_target_pairs={{0,4},{4,8},{8,12},{12,0},{1,5},{5,9},{9,13},{13,1},{2,6},{6,10},{... | collective-permute-start | bytes 786440 | tf_op jit(solution)/shard_map/ppermute | solution.py:569
  34.3 21.3 %collective-permute-start.18 = (bf16[256,512]{1,0:T(8,128)(2,1)S(1)}, bf16[256,512]{1,0:T(8,128)(2,1)S(1)}, u32[]{:S(2)}, u32[]{:S(2)}) collective-permute-start(bf16[256,512]{1,0:T(8,128)(2,1)S(1)} %get-tuple-element.63), channel_id=1, source_target_pairs={{16,0},{17,1},{18,2},{19,3},{20,4},{21,5},{22,6},{23,7},{24,8},{25... | collective-permute-start | bytes 786440 | tf_op jit(solution)/shard_map/ppermute | solution.py:624
  35.7 26.4 %collective-permute-start.4 = (bf16[256,512]{1,0:T(8,128)(2,1)S(1)}, bf16[256,512]{1,0:T(8,128)(2,1)S(1)}, u32[]{:S(2)}, u32[]{:S(2)}) collective-permute-start(bf16[256,512]{1,0:T(8,128)(2,1)S(1)} %broadcast_select_fusion.3.refs_0_), channel_id=1, source_target_pairs={{4,0},{8,4},{12,8},{0,12},{5,1},{9,5},{13,9},{1,13},{6,2},{10,6},{... | collective-permute-start | bytes 786440 | tf_op jit(solution)/shard_map/ppermute | solution.py:570
  44.9 19.5 %collective-permute-start.2 = (bf16[256,512]{1,0:T(8,128)(2,1)S(1)}, bf16[256,512]{1,0:T(8,128)(2,1)S(1)}, u32[]{:S(2)}, u32[]{:S(2)}) collective-permute-start(bf16[256,512]{1,0:T(8,128)(2,1)S(1)} %broadcast_select_fusion.3.refs_0_), channel_id=1, source_target_pairs={{0,4},{4,8},{8,12},{12,0},{1,5},{5,9},{9,13},{13,1},{2,6},{6,10},{... | collective-permute-start | bytes 786440 | tf_op jit(solution)/shard_map/ppermute | solution.py:569
  51.6 8.8 %collective-permute-start.16 = (bf16[256,512]{1,0:T(8,128)(2,1)S(1)}, bf16[256,512]{1,0:T(8,128)(2,1)S(1)}, u32[]{:S(2)}, u32[]{:S(2)}) collective-permute-start(bf16[256,512]{1,0:T(8,128)(2,1)S(1)} %get-tuple-element.59), channel_id=1, source_target_pairs={{16,0},{17,1},{18,2},{19,3},{20,4},{21,5},{22,6},{23,7},{24,8},{25... | collective-permute-start | bytes 786440 | tf_op jit(solution)/shard_map/ppermute | solution.py:624
  53.0 35.4 %collective-permute-start.7 = (bf16[256,512]{1,0:T(8,128)(2,1)S(1)}, bf16[256,512]{1,0:T(8,128)(2,1)S(1)}, u32[]{:S(2)}, u32[]{:S(2)}) collective-permute-start(bf16[256,512]{1,0:T(8,128)(2,1)S(1)} %select_select_fusion.2), channel_id=1, source_target_pairs={{4,0},{12,4},{8,12},{0,8},{5,1},{13,5},{9,13},{1,9},{6,2},{14,6},{... | collective-permute-start | bytes 786440 | tf_op jit(solution)/shard_map/ppermute | solution.py:572
  55.7 34.8 %copy-start.3 = (f32[2048]{0:T(1024)S(1)}, f32[2048]{0:T(1024)}, u32[]{:S(2)}) copy-start(f32[2048]{0:T(1024)} %param.9) | copy-start | bytes 24580
  55.7 15.8 %collective-permute-start.22 = (bf16[256,512]{1,0:T(8,128)(2,1)S(1)}, bf16[256,512]{1,0:T(8,128)(2,1)S(1)}, u32[]{:S(2)}, u32[]{:S(2)}) collective-permute-start(bf16[256,512]{1,0:T(8,128)(2,1)S(1)} %broadcast_select_fusion.refs_1_), channel_id=1, source_target_pairs={{4,0},{8,4},{12,8},{0,12},{5,1},{9,5},{13,9},{1,13},{6,2},{10,6},{... | collective-permute-start | bytes 786440 | tf_op jit(solution)/shard_map/ppermute | solution.py:570
  60.5 15.0 %collective-permute-start.20 = (bf16[256,512]{1,0:T(8,128)(2,1)S(1)}, bf16[256,512]{1,0:T(8,128)(2,1)S(1)}, u32[]{:S(2)}, u32[]{:S(2)}) collective-permute-start(bf16[256,512]{1,0:T(8,128)(2,1)S(1)} %broadcast_select_fusion.refs_1_), channel_id=1, source_target_pairs={{0,4},{4,8},{8,12},{12,0},{1,5},{5,9},{9,13},{13,1},{2,6},{6,10},{... | collective-permute-start | bytes 786440 | tf_op jit(solution)/shard_map/ppermute | solution.py:569
  62.1 20.6 %collective-permute-start.21 = (bf16[256,512]{1,0:T(8,128)(2,1)S(1)}, bf16[256,512]{1,0:T(8,128)(2,1)S(1)}, u32[]{:S(2)}, u32[]{:S(2)}) collective-permute-start(bf16[256,512]{1,0:T(8,128)(2,1)S(1)} %broadcast_select_fusion.1.refs_0_), channel_id=1, source_target_pairs={{4,0},{8,4},{12,8},{0,12},{5,1},{9,5},{13,9},{1,13},{6,2},{10,6},{... | collective-permute-start | bytes 786440 | tf_op jit(solution)/shard_map/ppermute | solution.py:570
  64.4 22.3 %collective-permute-start.19 = (bf16[256,512]{1,0:T(8,128)(2,1)S(1)}, bf16[256,512]{1,0:T(8,128)(2,1)S(1)}, u32[]{:S(2)}, u32[]{:S(2)}) collective-permute-start(bf16[256,512]{1,0:T(8,128)(2,1)S(1)} %broadcast_select_fusion.1.refs_0_), channel_id=1, source_target_pairs={{0,4},{4,8},{8,12},{12,0},{1,5},{5,9},{9,13},{13,1},{2,6},{6,10},{... | collective-permute-start | bytes 786440 | tf_op jit(solution)/shard_map/ppermute | solution.py:569
  71.5 19.0 %collective-permute-start.6 = (bf16[256,512]{1,0:T(8,128)(2,1)S(1)}, bf16[256,512]{1,0:T(8,128)(2,1)S(1)}, u32[]{:S(2)}, u32[]{:S(2)}) collective-permute-start(bf16[256,512]{1,0:T(8,128)(2,1)S(1)} %select_select_fusion.3), channel_id=1, source_target_pairs={{4,0},{12,4},{8,12},{0,8},{5,1},{13,5},{9,13},{1,9},{6,2},{14,6},{... | collective-permute-start | bytes 786440 | tf_op jit(solution)/shard_map/ppermute | solution.py:572
  75.5 24.1 %collective-permute-start.24 = (bf16[256,512]{1,0:T(8,128)(2,1)S(1)}, bf16[256,512]{1,0:T(8,128)(2,1)S(1)}, u32[]{:S(2)}, u32[]{:S(2)}) collective-permute-start(bf16[256,512]{1,0:T(8,128)(2,1)S(1)} %select_select_fusion), channel_id=1, source_target_pairs={{4,0},{12,4},{8,12},{0,8},{5,1},{13,5},{9,13},{1,9},{6,2},{14,6},{... | collective-permute-start | bytes 786440 | tf_op jit(solution)/shard_map/ppermute | solution.py:572
  86.7 12.8 %collective-permute-start.23 = (bf16[256,512]{1,0:T(8,128)(2,1)S(1)}, bf16[256,512]{1,0:T(8,128)(2,1)S(1)}, u32[]{:S(2)}, u32[]{:S(2)}) collective-permute-start(bf16[256,512]{1,0:T(8,128)(2,1)S(1)} %select_select_fusion.1), channel_id=1, source_target_pairs={{4,0},{12,4},{8,12},{0,8},{5,1},{13,5},{9,13},{1,9},{6,2},{14,6},{... | collective-permute-start | bytes 786440 | tf_op jit(solution)/shard_map/ppermute | solution.py:572
  96.9 26.9 %collective-permute-start.8 = (bf16[1024,512]{1,0:T(8,128)(2,1)}, bf16[1024,512]{1,0:T(8,128)(2,1)S(1)}, u32[]{:S(2)}, u32[]{:S(2)}) collective-permute-start(bf16[1024,512]{1,0:T(8,128)(2,1)} %get-tuple-element.47.refs_0_), channel_id=1, source_target_pairs={{0,16},{16,0},{1,17},{17,1},{2,18},{18,2},{3,19},{19,3},{4,20},{20... | collective-permute-start | bytes 3145736 | tf_op jit(solution)/shard_map/ppermute | solution.py:629
  105.7 1.3 copy-start
  107.0 36.3 %collective-permute-start.25 = (bf16[1024,512]{1,0:T(8,128)(2,1)}, bf16[1024,512]{1,0:T(8,128)(2,1)}, u32[]{:S(2)}, u32[]{:S(2)}) collective-permute-start(bf16[1024,512]{1,0:T(8,128)(2,1)} %get-tuple-element.66.refs_2_), channel_id=1, source_target_pairs={{0,16},{16,0},{1,17},{17,1},{2,18},{18,2},{3,19},{19,3},{4,20},{20... | collective-permute-start | bytes 3145736 | tf_op jit(solution)/shard_map/ppermute | solution.py:635
  109.3 1.6 copy-start.2
  115.1 17.9 %copy-start.1 = (bf16[2048,512]{1,0:T(8,128)(2,1)S(1)}, bf16[2048,512]{1,0:T(8,128)(2,1)}, u32[]{:S(2)}) copy-start(bf16[2048,512]{1,0:T(8,128)(2,1)} %copy-done) | copy-start | bytes 6291460
  130.6 21.5 %collective-permute-start.9 = (bf16[256,512]{1,0:T(8,128)(2,1)S(1)}, bf16[256,512]{1,0:T(8,128)(2,1)S(1)}, u32[]{:S(2)}, u32[]{:S(2)}) collective-permute-start(bf16[256,512]{1,0:T(8,128)(2,1)S(1)} %get-tuple-element.50), channel_id=1, source_target_pairs={{0,4},{4,12},{12,8},{8,0},{1,5},{5,13},{13,9},{9,1},{2,6},{6,14},{... | collective-permute-start | bytes 786440 | tf_op jit(solution)/shard_map/ppermute | solution.py:583
  135.7 18.9 %collective-permute-start.12 = (bf16[256,512]{1,0:T(8,128)(2,1)S(1)}, bf16[256,512]{1,0:T(8,128)(2,1)S(1)}, u32[]{:S(2)}, u32[]{:S(2)}) collective-permute-start(bf16[256,512]{1,0:T(8,128)(2,1)S(1)} %get-tuple-element.54), channel_id=1, source_target_pairs={{0,4},{4,12},{12,8},{8,0},{1,5},{5,13},{13,9},{9,1},{2,6},{6,14},{... | collective-permute-start | bytes 786440 | tf_op jit(solution)/shard_map/ppermute | solution.py:583
  149.0 12.9 %collective-permute-start.26 = (bf16[256,512]{1,0:T(8,128)(2,1)S(1)}, bf16[256,512]{1,0:T(8,128)(2,1)S(1)}, u32[]{:S(2)}, u32[]{:S(2)}) collective-permute-start(bf16[256,512]{1,0:T(8,128)(2,1)S(1)} %get-tuple-element.71), channel_id=1, source_target_pairs={{0,4},{4,12},{12,8},{8,0},{1,5},{5,13},{13,9},{9,1},{2,6},{6,14},{... | collective-permute-start | bytes 786440 | tf_op jit(solution)/shard_map/ppermute | solution.py:583
  152.2 29.5 %collective-permute-start.10 = (bf16[256,512]{1,0:T(8,128)(2,1)S(1)}, bf16[256,512]{1,0:T(8,128)(2,1)S(1)}, u32[]{:S(2)}, u32[]{:S(2)}) collective-permute-start(bf16[256,512]{1,0:T(8,128)(2,1)S(1)} %get-tuple-element.83), channel_id=1, source_target_pairs={{4,0},{8,4},{12,8},{0,12},{5,1},{9,5},{13,9},{1,13},{6,2},{10,6},{... | collective-permute-start | bytes 786440 | tf_op jit(solution)/shard_map/ppermute | solution.py:584
  153.8 31.8 %collective-permute-start.11 = (bf16[256,512]{1,0:T(8,128)(2,1)S(1)}, bf16[256,512]{1,0:T(8,128)(2,1)S(1)}, u32[]{:S(2)}, u32[]{:S(2)}) collective-permute-start(bf16[256,512]{1,0:T(8,128)(2,1)S(1)} %get-tuple-element.84), channel_id=1, source_target_pairs={{0,4},{4,8},{8,12},{12,0},{1,5},{5,9},{9,13},{13,1},{2,6},{6,10},{... | collective-permute-start | bytes 786440 | tf_op jit(solution)/shard_map/ppermute | solution.py:585
  154.5 27.0 %collective-permute-start.29 = (bf16[256,512]{1,0:T(8,128)(2,1)S(1)}, bf16[256,512]{1,0:T(8,128)(2,1)S(1)}, u32[]{:S(2)}, u32[]{:S(2)}) collective-permute-start(bf16[256,512]{1,0:T(8,128)(2,1)S(1)} %get-tuple-element.75), channel_id=1, source_target_pairs={{0,4},{4,12},{12,8},{8,0},{1,5},{5,13},{13,9},{9,1},{2,6},{6,14},{... | collective-permute-start | bytes 786440 | tf_op jit(solution)/shard_map/ppermute | solution.py:583
  154.7 32.0 %collective-permute-start.13 = (bf16[256,512]{1,0:T(8,128)(2,1)S(1)}, bf16[256,512]{1,0:T(8,128)(2,1)S(1)}, u32[]{:S(2)}, u32[]{:S(2)}) collective-permute-start(bf16[256,512]{1,0:T(8,128)(2,1)S(1)} %get-tuple-element.81), channel_id=1, source_target_pairs={{4,0},{8,4},{12,8},{0,12},{5,1},{9,5},{13,9},{1,13},{6,2},{10,6},{... | collective-permute-start | bytes 786440 | tf_op jit(solution)/shard_map/ppermute | solution.py:584
  161.9 27.7 %collective-permute-start.14 = (bf16[256,512]{1,0:T(8,128)(2,1)S(1)}, bf16[256,512]{1,0:T(8,128)(2,1)S(1)}, u32[]{:S(2)}, u32[]{:S(2)}) collective-permute-start(bf16[256,512]{1,0:T(8,128)(2,1)S(1)} %get-tuple-element.82), channel_id=1, source_target_pairs={{0,4},{4,8},{8,12},{12,0},{1,5},{5,9},{9,13},{13,1},{2,6},{6,10},{... | collective-permute-start | bytes 786440 | tf_op jit(solution)/shard_map/ppermute | solution.py:585
  181.6 12.8 %collective-permute-start.28 = (bf16[256,512]{1,0:T(8,128)(2,1)S(1)}, bf16[256,512]{1,0:T(8,128)(2,1)S(1)}, u32[]{:S(2)}, u32[]{:S(2)}) collective-permute-start(bf16[256,512]{1,0:T(8,128)(2,1)S(1)} %get-tuple-element.79), channel_id=1, source_target_pairs={{0,4},{4,8},{8,12},{12,0},{1,5},{5,9},{9,13},{13,1},{2,6},{6,10},{... | collective-permute-start | bytes 786440 | tf_op jit(solution)/shard_map/ppermute | solution.py:585
  181.7 17.2 %collective-permute-start.27 = (bf16[256,512]{1,0:T(8,128)(2,1)S(1)}, bf16[256,512]{1,0:T(8,128)(2,1)S(1)}, u32[]{:S(2)}, u32[]{:S(2)}) collective-permute-start(bf16[256,512]{1,0:T(8,128)(2,1)S(1)} %get-tuple-element.80), channel_id=1, source_target_pairs={{4,0},{8,4},{12,8},{0,12},{5,1},{9,5},{13,9},{1,13},{6,2},{10,6},{... | collective-permute-start | bytes 786440 | tf_op jit(solution)/shard_map/ppermute | solution.py:584
  185.6 16.2 %collective-permute-start.31 = (bf16[256,512]{1,0:T(8,128)(2,1)S(1)}, bf16[256,512]{1,0:T(8,128)(2,1)S(1)}, u32[]{:S(2)}, u32[]{:S(2)}) collective-permute-start(bf16[256,512]{1,0:T(8,128)(2,1)S(1)} %get-tuple-element.77), channel_id=1, source_target_pairs={{0,4},{4,8},{8,12},{12,0},{1,5},{5,9},{9,13},{13,1},{2,6},{6,10},{... | collective-permute-start | bytes 786440 | tf_op jit(solution)/shard_map/ppermute | solution.py:585
  186.7 18.5 %collective-permute-start.30 = (bf16[256,512]{1,0:T(8,128)(2,1)S(1)}, bf16[256,512]{1,0:T(8,128)(2,1)S(1)}, u32[]{:S(2)}, u32[]{:S(2)}) collective-permute-start(bf16[256,512]{1,0:T(8,128)(2,1)S(1)} %get-tuple-element.78), channel_id=1, source_target_pairs={{4,0},{8,4},{12,8},{0,12},{5,1},{9,5},{13,9},{1,13},{6,2},{10,6},{... | collective-permute-start | bytes 786440 | tf_op jit(solution)/shard_map/ppermute | solution.py:584

commit v11 on v9

--- a/solution.py
+++ b/solution.py
@@ -21,7 +21,7 @@
 MASKED_SCORE = -1e30
 LOG2E = math.log2(math.e)
 
-VMEM_LIMIT = 14 * 1024 * 1024
+VMEM_LIMIT = 10 * 1024 * 1024
 
 
 def vmem_spec():
@@ -165,7 +165,7 @@
 
     steps = channels // GROUP
     if with_before:
-        lax.fori_loop(0, steps, advance, 0, unroll=2)
+        lax.fori_loop(0, steps, advance, 0, unroll=4)
     else:
         each = steps // CHUNKS
 
@@ -182,7 +182,7 @@
             ).wait()
             leaving(begin, index).start()
             later = functools.partial(advance, base=begin)
-            return lax.fori_loop(0, each, later, carry, unroll=2)
+            return lax.fori_loop(0, each, later, carry, unroll=4)
 
         lax.fori_loop(0, CHUNKS, chunk, 0)
         for index in range(CHUNKS):

time: 206 us -> 207 us (level)
  no operation moved by 1% of the time
where the time goes in v11:
time: 207 us
  waiting for transfers between devices  82 us (40%)
  Pallas kernels  63 us (30%)
  starting transfers between devices  55.7 us (27%)
  local copies, waits for them, and re-layouts  3.25 us (2%)
  other arithmetic  2.21 us (1%)
    ppermute x4, waiting for transfers between devices, reduce_blocks(): across = lax.ppermute(sent, 'tp', FOLDED)  23.6 us
    pallas_call x4, Pallas kernels, conv_call(): pl.pallas_call(functools.partial(conv_body, with_before, piece * channels...  21.7 us
    pallas_call x3, Pallas kernels, attend_call(): pl.pallas_call(functools.partial(attend_body, chunk, tuple((s for _, s in...  20 us
    ppermute x4, waiting for transfers between devices, gather_blocks(): after = lax.ppermute(block, 'tp', BACKWARD)  12.6 us
    pallas_call x2, Pallas kernels, project_pair(): pl.pallas_call(pair_body, in_specs=[smem_spec(), off_chip_spec()] + [vmem...  12.1 us
    ppermute x4, starting transfers between devices, reduce_blocks(): back = lax.ppermute(plus(down, across, here == 2), 'tp', BACKWARD)  11.3 us
    ppermute x4, starting transfers between devices, gather_blocks(): after = lax.ppermute(block, 'tp', BACKWARD)  11 us
    ppermute x4, waiting for transfers between devices, reduce_blocks(): back = lax.ppermute(plus(down, across, here == 2), 'tp', BACKWARD)  9.01 us
  transfers between devices with their start and end apart: 32, of which 17 were waited for; matrix products, arithmetic and copies ran while one was open for 1% of the time, Pallas kernels for 26%

profile of v11, /device:TPU:0, one launch (start us, length us, event | category | flops | bytes accessed | tf_op | source)
XLA Modules:
  0.0 206.5 jit_solution(17763353733794126017)
XLA Ops:
  0.0 6.2 %conv.5 = (f32[256,1024]{1,0:T(8,128)S(1)}, bf16[256,512]{1,0:T(8,128)(2,1)S(1)}, bf16[256,512]{1,0:T(8,128)(2,1)S(1)}, bf16[256,1024]{1,0:T(8,128)(2,1)}) custom-call(s32[1]{0:T(128)} %bitcast.seq_ref, s32[16]{0:T(128)} %order_ref.15, bf16[512,1024]{1,0:T(8,128)(2,1)} %tokens_ref.3, f32[27,512]{1,0:T(8,128)} %taps_ref.7), custom_call_target="tpu_custom_call" | custom-call | flops 7077888 | bytes 2097152 | tf_op jit(solution)/shard_map/conv/pallas_call | solution.py:220
  6.2 4.9 %collective-permute-start.1 = (bf16[256,512]{1,0:T(8,128)(2,1)S(1)}, bf16[256,512]{1,0:T(8,128)(2,1)S(1)}, u32[]{:S(2)}, u32[]{:S(2)}) collective-permute-start(bf16[256,512]{1,0:T(8,128)(2,1)S(1)} %get-tuple-element.44), channel_id=1, source_target_pairs={{0,16},{1,17},{2,18},{3,19},{4,20},{5,21},{6,22},{7,23},{8,24},{9,... | collective-permute-start | bytes 786440 | tf_op jit(solution)/shard_map/ppermute | solution.py:588
  11.1 2.1 %collective-permute-start.17 = (bf16[256,1024]{1,0:T(8,128)(2,1)}, bf16[256,1024]{1,0:T(8,128)(2,1)}, u32[]{:S(2)}, u32[]{:S(2)}) collective-permute-start(bf16[256,1024]{1,0:T(8,128)(2,1)} %get-tuple-element.60), channel_id=1, source_target_pairs={{0,16},{1,17},{2,18},{3,19},{4,20},{5,21},{6,22},{7,23},{8,24},{9,... | collective-permute-start | bytes 1572872 | tf_op jit(solution)/shard_map/ppermute | solution.py:590
  13.2 6.9 %conv.4 = (f32[256,1024]{1,0:T(8,128)S(1)}, bf16[256,512]{1,0:T(8,128)(2,1)S(1)}, bf16[256,512]{1,0:T(8,128)(2,1)}, bf16[256,1024]{1,0:T(8,128)(2,1)}) custom-call(s32[1]{0:T(128)} %bitcast.seq_ref, s32[16]{0:T(128)} %order_ref.15, bf16[512,1024]{1,0:T(8,128)(2,1)} %tokens_ref.3, f32[27,512]{1,0:T(8,128)} %taps_ref.7), custom_call_target="tpu_custom_call" | custom-call | flops 7077888 | bytes 2097152 | tf_op jit(solution)/shard_map/conv/pallas_call | solution.py:220
  20.1 2.0 collective-permute-start
  23.5 3.7 %collective-permute-start.5 = (bf16[256,512]{1,0:T(8,128)(2,1)S(1)}, bf16[256,512]{1,0:T(8,128)(2,1)S(1)}, u32[]{:S(2)}, u32[]{:S(2)}) collective-permute-start(bf16[256,512]{1,0:T(8,128)(2,1)S(1)} %broadcast_select_fusion.2.refs_1_), channel_id=1, source_target_pairs={{4,0},{8,4},{12,8},{0,12},{5,1},{9,5},{13,9},{1,13},{6,2},{10,6},{... | collective-permute-start | bytes 786440 | tf_op jit(solution)/shard_map/ppermute | solution.py:546
  27.2 1.8 collective-permute-done.17.tokens_ref
  29.1 4.4 %conv.7 = (bf16[256,512]{1,0:T(8,128)(2,1)S(1)}, bf16[256,512]{1,0:T(8,128)(2,1)S(1)}) custom-call(s32[1]{0:T(128)} %bitcast.seq_ref, s32[16]{0:T(128)} %order_ref.15, bf16[256,1024]{1,0:T(8,128)(2,1)} %collective-permute-done.17.tokens_ref, f32[27,512]{1,0:T(8,128)} %taps_ref.7, f32[256,1024]{1,0:T(8,128)S(1)} %get-tuple-element.61.part_ref), custom_call_target="tpu_custom_call" | custom-call | flops 7077888 | bytes 2097152 | tf_op jit(solution)/shard_map/conv/pallas_call | solution.py:220
  35.8 3.7 %collective-permute-start.4 = (bf16[256,512]{1,0:T(8,128)(2,1)S(1)}, bf16[256,512]{1,0:T(8,128)(2,1)S(1)}, u32[]{:S(2)}, u32[]{:S(2)}) collective-permute-start(bf16[256,512]{1,0:T(8,128)(2,1)S(1)} %broadcast_select_fusion.3.refs_0_), channel_id=1, source_target_pairs={{4,0},{8,4},{12,8},{0,12},{5,1},{9,5},{13,9},{1,13},{6,2},{10,6},{... | collective-permute-start | bytes 786440 | tf_op jit(solution)/shard_map/ppermute | solution.py:546
  39.5 5.3 %collective-permute-done.15.tokens_ref = bf16[256,1024]{1,0:T(8,128)(2,1)S(1)} collective-permute-done((bf16[256,1024]{1,0:T(8,128)(2,1)}, bf16[256,1024]{1,0:T(8,128)(2,1)S(1)}, u32[]{:S(2)}, u32[]{:S(2)}) %collective-permute-start.15) | collective-permute-done | bytes 524320 | tf_op jit(solution)/shard_map/ppermute | solution.py:590
  44.8 1.6 collective-permute-start.2
  46.4 4.2 %conv.6 = (bf16[256,512]{1,0:T(8,128)(2,1)S(1)}, bf16[256,512]{1,0:T(8,128)(2,1)S(1)}) custom-call(s32[1]{0:T(128)} %bitcast.seq_ref, s32[16]{0:T(128)} %order_ref.15, bf16[256,1024]{1,0:T(8,128)(2,1)S(1)} %collective-permute-done.15.tokens_ref, f32[27,512]{1,0:T(8,128)} %taps_ref.7, f32[256,1024]{1,0:T(8,128)S(1)} %get-tuple-element.57.part_ref), custom_call_target="tpu_custom_call" | custom-call | flops 7077888 | bytes 2097152 | tf_op jit(solution)/shard_map/conv/pallas_call | solution.py:220
  52.0 2.6 %collective-permute-start.7 = (bf16[256,512]{1,0:T(8,128)(2,1)S(1)}, bf16[256,512]{1,0:T(8,128)(2,1)S(1)}, u32[]{:S(2)}, u32[]{:S(2)}) collective-permute-start(bf16[256,512]{1,0:T(8,128)(2,1)S(1)} %select_select_fusion.2), channel_id=1, source_target_pairs={{4,0},{12,4},{8,12},{0,8},{5,1},{13,5},{9,13},{1,9},{6,2},{14,6},{... | collective-permute-start | bytes 786440 | tf_op jit(solution)/shard_map/ppermute | solution.py:548
  56.1 3.4 %collective-permute-done.16 = bf16[256,512]{1,0:T(8,128)(2,1)S(1)} collective-permute-done((bf16[256,512]{1,0:T(8,128)(2,1)S(1)}, bf16[256,512]{1,0:T(8,128)(2,1)S(1)}, u32[]{:S(2)}, u32[]{:S(2)}) %collective-permute-start.16) | collective-permute-done | bytes 262176 | tf_op jit(solution)/shard_map/ppermute | solution.py:600
  59.4 1.6 collective-permute-start.20
  61.1 2.3 %collective-permute-start.21 = (bf16[256,512]{1,0:T(8,128)(2,1)S(1)}, bf16[256,512]{1,0:T(8,128)(2,1)S(1)}, u32[]{:S(2)}, u32[]{:S(2)}) collective-permute-start(bf16[256,512]{1,0:T(8,128)(2,1)S(1)} %broadcast_select_fusion.1.refs_0_), channel_id=1, source_target_pairs={{4,0},{8,4},{12,8},{0,12},{5,1},{9,5},{13,9},{1,13},{6,2},{10,6},{... | collective-permute-start | bytes 786440 | tf_op jit(solution)/shard_map/ppermute | solution.py:546
  63.4 7.0 %collective-permute-done.22.refs_5_ = bf16[256,512]{1,0:T(8,128)(2,1)S(1)} collective-permute-done((bf16[256,512]{1,0:T(8,128)(2,1)S(1)}, bf16[256,512]{1,0:T(8,128)(2,1)S(1)}, u32[]{:S(2)}, u32[]{:S(2)}) %collective-permute-start.22) | collective-permute-done | bytes 262176 | tf_op jit(solution)/shard_map/ppermute | solution.py:546
  70.5 3.9 %collective-permute-done.20.refs_3_ = bf16[256,512]{1,0:T(8,128)(2,1)S(1)} collective-permute-done((bf16[256,512]{1,0:T(8,128)(2,1)S(1)}, bf16[256,512]{1,0:T(8,128)(2,1)S(1)}, u32[]{:S(2)}, u32[]{:S(2)}) %collective-permute-start.20) | collective-permute-done | bytes 262176 | tf_op jit(solution)/shard_map/ppermute | solution.py:545
  74.4 1.7 collective-permute-start.24
  76.1 5.5 %collective-permute-done.21.refs_4_ = bf16[256,512]{1,0:T(8,128)(2,1)S(1)} collective-permute-done((bf16[256,512]{1,0:T(8,128)(2,1)S(1)}, bf16[256,512]{1,0:T(8,128)(2,1)S(1)}, u32[]{:S(2)}, u32[]{:S(2)}) %collective-permute-start.21) | collective-permute-done | bytes 262176 | tf_op jit(solution)/shard_map/ppermute | solution.py:546
  81.7 4.0 %collective-permute-done.19.refs_2_ = bf16[256,512]{1,0:T(8,128)(2,1)S(1)} collective-permute-done((bf16[256,512]{1,0:T(8,128)(2,1)S(1)}, bf16[256,512]{1,0:T(8,128)(2,1)S(1)}, u32[]{:S(2)}, u32[]{:S(2)}) %collective-permute-start.19) | collective-permute-done | bytes 262176 | tf_op jit(solution)/shard_map/ppermute | solution.py:545
  85.7 1.6 collective-permute-start.23
  87.4 2.1 %collective-permute-done.6.refs_6_ = bf16[256,512]{1,0:T(8,128)(2,1)S(1)} collective-permute-done((bf16[256,512]{1,0:T(8,128)(2,1)S(1)}, bf16[256,512]{1,0:T(8,128)(2,1)S(1)}, u32[]{:S(2)}, u32[]{:S(2)}) %collective-permute-start.6) | collective-permute-done | bytes 262176 | tf_op jit(solution)/shard_map/ppermute | solution.py:548
  89.8 6.0 %pair.2 = (bf16[1024,512]{1,0:T(8,128)(2,1)}, bf16[2048,512]{1,0:T(8,128)(2,1)S(1)}, f32[1,512]{1,0:T(1,128)S(1)}) custom-call(s32[4]{0:T(128)S(1)} %pad_add_fusion.blocks_ref, bf16[1536,2048]{1,0:T(8,128)(2,1)} %bitcast.8, f32[2048,128]{1,0:T(8,128)S(1)} %broadcast_in_dim.42.gains_ref, bf16[256,512]{1,0:T(8,128)(2,1)S(1)} %broadcast_select_fusion.3.refs_0_, ...), custom_call_target="tpu_custom_call" | custom-call | flops 2147483648 | bytes 9437184 | tf_op jit(solution)/shard_map/pair/pallas_call | solution.py:305
  95.9 2.7 %collective-permute-start.8 = (bf16[1024,512]{1,0:T(8,128)(2,1)}, bf16[1024,512]{1,0:T(8,128)(2,1)S(1)}, u32[]{:S(2)}, u32[]{:S(2)}) collective-permute-start(bf16[1024,512]{1,0:T(8,128)(2,1)} %get-tuple-element.47.refs_0_), channel_id=1, source_target_pairs={{0,16},{16,0},{1,17},{17,1},{2,18},{18,2},{3,19},{19,3},{4,20},{20... | collective-permute-start | bytes 3145736 | tf_op jit(solution)/shard_map/ppermute | solution.py:605
  98.8 6.1 %pair.3 = (bf16[1024,512]{1,0:T(8,128)(2,1)}, bf16[2048,512]{1,0:T(8,128)(2,1)S(1)}, f32[1,512]{1,0:T(1,128)S(1)}) custom-call(s32[4]{0:T(128)S(1)} %pad_add_fusion.blocks_ref, bf16[1536,2048]{1,0:T(8,128)(2,1)} %bitcast.9, f32[2048,128]{1,0:T(8,128)S(1)} %broadcast_in_dim.42.gains_ref, bf16[256,512]{1,0:T(8,128)(2,1)S(1)} %broadcast_select_fusion.1.refs_0_, ...), custom_call_target="tpu_custom_call" | custom-call | flops 2147483648 | bytes 9437184 | tf_op jit(solution)/shard_map/pair/pallas_call | solution.py:305
  106.2 2.4 %collective-permute-start.25 = (bf16[1024,512]{1,0:T(8,128)(2,1)}, bf16[1024,512]{1,0:T(8,128)(2,1)}, u32[]{:S(2)}, u32[]{:S(2)}) collective-permute-start(bf16[1024,512]{1,0:T(8,128)(2,1)} %get-tuple-element.66.refs_2_), channel_id=1, source_target_pairs={{0,16},{16,0},{1,17},{17,1},{2,18},{18,2},{3,19},{19,3},{4,20},{20... | collective-permute-start | bytes 3145736 | tf_op jit(solution)/shard_map/ppermute | solution.py:611
  108.6 1.6 copy-done.2
  110.2 1.5 prepare.1.refs_2_.refs_3_
  111.7 2.7 %query.2.query_ref = bf16[512,512]{1,0:T(8,128)(2,1)S(1)} custom-call(bf16[1536,2048]{1,0:T(8,128)(2,1)} %bitcast.10, bf16[2048,512]{1,0:T(8,128)(2,1)S(1)} %get-tuple-element.45.tokens_ref, f32[1,512]{1,0:T(1,128)S(1)} %get-tuple-element.46.inverse_ref), custom_call_target="tpu_custom_call" | custom-call | flops 1073741824 | bytes 4718592 | tf_op jit(solution)/shard_map/query/pallas_call | solution.py:332
  114.4 8.4 %collective-permute-done.8.refs_1_ = bf16[1024,512]{1,0:T(8,128)(2,1)S(1)} collective-permute-done((bf16[1024,512]{1,0:T(8,128)(2,1)}, bf16[1024,512]{1,0:T(8,128)(2,1)S(1)}, u32[]{:S(2)}, u32[]{:S(2)}) %collective-permute-start.8) | collective-permute-done | bytes 1048608 | tf_op jit(solution)/shard_map/ppermute | solution.py:605
  122.8 6.8 %attend.3 = (bf16[256,512]{1,0:T(8,128)(2,1)S(1)}, bf16[256,512]{1,0:T(8,128)(2,1)S(1)}, bf16[256,512]{1,0:T(8,128)(2,1)S(1)}, bf16[256,512]{1,0:T(8,128)(2,1)S(...) custom-call(s32[1]{0:T(128)} %bitcast.seq_ref, ...), custom_call_target="tpu_custom_call" | custom-call | flops 1073741824 | bytes 3145728 | tf_op jit(solution)/shard_map/attend/pallas_call | solution.py:472
  129.6 2.4 %collective-permute-start.9 = (bf16[256,512]{1,0:T(8,128)(2,1)S(1)}, bf16[256,512]{1,0:T(8,128)(2,1)S(1)}, u32[]{:S(2)}, u32[]{:S(2)}) collective-permute-start(bf16[256,512]{1,0:T(8,128)(2,1)S(1)} %get-tuple-element.50), channel_id=1, source_target_pairs={{0,4},{4,12},{12,8},{8,0},{1,5},{5,13},{13,9},{9,1},{2,6},{6,14},{... | collective-permute-start | bytes 786440 | tf_op jit(solution)/shard_map/ppermute | solution.py:559
  132.0 2.7 %query.3.query_ref = bf16[512,512]{1,0:T(8,128)(2,1)S(1)} custom-call(bf16[1536,2048]{1,0:T(8,128)(2,1)} %bitcast.11, bf16[2048,512]{1,0:T(8,128)(2,1)S(1)} %copy-done.1, f32[1,512]{1,0:T(1,128)S(1)} %get-tuple-element.65.inverse_ref), custom_call_target="tpu_custom_call" | custom-call | flops 1073741824 | bytes 4718592 | tf_op jit(solution)/shard_map/query/pallas_call | solution.py:332
  134.7 7.6 %attend.4 = (f32[4,2,512]{2,1,0:T(2,128)S(1)}, f32[512,512]{1,0:T(8,128)S(1)}) custom-call(s32[1]{0:T(128)} %bitcast.seq_ref, s32[16]{0:T(128)} %order_ref.15, s32[16,16]{1,0:T(8,128)} %mask_ref.5, bf16[512,512]{1,0:T(8,128)(2,1)S(1)} %query.3.query_ref, bf16[1024,512]{1,0:T(8,128)(2,1)} %get-tuple-element.47.refs_0_, ...), custom_call_target="tpu_custom_call" | custom-call | flops 1610612736 | bytes 4194304 | tf_op jit(solution)/shard_map/attend/pallas_call | solution.py:472
  142.3 5.6 %attend.5 = (bf16[256,512]{1,0:T(8,128)(2,1)S(1)}, bf16[256,512]{1,0:T(8,128)(2,1)S(1)}, bf16[256,512]{1,0:T(8,128)(2,1)S(1)}, bf16[256,512]{1,0:T(8,128)(2,1)S(...) custom-call(s32[1]{0:T(128)} %bitcast.seq_ref, ...), custom_call_target="tpu_custom_call" | custom-call | flops 536870912 | bytes 2097152 | tf_op jit(solution)/shard_map/attend/pallas_call | solution.py:472
  148.0 3.1 %collective-permute-start.26 = (bf16[256,512]{1,0:T(8,128)(2,1)S(1)}, bf16[256,512]{1,0:T(8,128)(2,1)S(1)}, u32[]{:S(2)}, u32[]{:S(2)}) collective-permute-start(bf16[256,512]{1,0:T(8,128)(2,1)S(1)} %get-tuple-element.71), channel_id=1, source_target_pairs={{0,4},{4,12},{12,8},{8,0},{1,5},{5,13},{13,9},{9,1},{2,6},{6,14},{... | collective-permute-start | bytes 786440 | tf_op jit(solution)/shard_map/ppermute | solution.py:559
  151.2 1.6 collective-permute-start.10
  153.7 3.1 %collective-permute-start.13 = (bf16[256,512]{1,0:T(8,128)(2,1)S(1)}, bf16[256,512]{1,0:T(8,128)(2,1)S(1)}, u32[]{:S(2)}, u32[]{:S(2)}) collective-permute-start(bf16[256,512]{1,0:T(8,128)(2,1)S(1)} %get-tuple-element.81), channel_id=1, source_target_pairs={{4,0},{8,4},{12,8},{0,12},{5,1},{9,5},{13,9},{1,13},{6,2},{10,6},{... | collective-permute-start | bytes 786440 | tf_op jit(solution)/shard_map/ppermute | solution.py:560
  156.8 4.1 %collective-permute-done.26.refs_5_ = bf16[256,512]{1,0:T(8,128)(2,1)S(1)} collective-permute-done((bf16[256,512]{1,0:T(8,128)(2,1)S(1)}, bf16[256,512]{1,0:T(8,128)(2,1)S(1)}, u32[]{:S(2)}, u32[]{:S(2)}) %collective-permute-start.26) | collective-permute-done | bytes 262176 | tf_op jit(solution)/shard_map/ppermute | solution.py:559
  161.0 19.5 %collective-permute-done.29.refs_9_ = bf16[256,512]{1,0:T(8,128)(2,1)S(1)} collective-permute-done((bf16[256,512]{1,0:T(8,128)(2,1)S(1)}, bf16[256,512]{1,0:T(8,128)(2,1)S(1)}, u32[]{:S(2)}, u32[]{:S(2)}) %collective-permute-start.29) | collective-permute-done | bytes 262176 | tf_op jit(solution)/shard_map/ppermute | solution.py:559
  180.7 3.9 %collective-permute-start.27 = (bf16[256,512]{1,0:T(8,128)(2,1)S(1)}, bf16[256,512]{1,0:T(8,128)(2,1)S(1)}, u32[]{:S(2)}, u32[]{:S(2)}) collective-permute-start(bf16[256,512]{1,0:T(8,128)(2,1)S(1)} %get-tuple-element.80), channel_id=1, source_target_pairs={{4,0},{8,4},{12,8},{0,12},{5,1},{9,5},{13,9},{1,13},{6,2},{10,6},{... | collective-permute-start | bytes 786440 | tf_op jit(solution)/shard_map/ppermute | solution.py:560
  185.7 2.7 %collective-permute-start.30 = (bf16[256,512]{1,0:T(8,128)(2,1)S(1)}, bf16[256,512]{1,0:T(8,128)(2,1)S(1)}, u32[]{:S(2)}, u32[]{:S(2)}) collective-permute-start(bf16[256,512]{1,0:T(8,128)(2,1)S(1)} %get-tuple-element.78), channel_id=1, source_target_pairs={{4,0},{8,4},{12,8},{0,12},{5,1},{9,5},{13,9},{1,13},{6,2},{10,6},{... | collective-permute-start | bytes 786440 | tf_op jit(solution)/shard_map/ppermute | solution.py:560
  188.7 4.6 %collective-permute-done.28.refs_4_ = bf16[256,512]{1,0:T(8,128)(2,1)S(1)} collective-permute-done((bf16[256,512]{1,0:T(8,128)(2,1)S(1)}, bf16[256,512]{1,0:T(8,128)(2,1)S(1)}, u32[]{:S(2)}, u32[]{:S(2)}) %collective-permute-start.28) | collective-permute-done | bytes 262176 | tf_op jit(solution)/shard_map/ppermute | solution.py:561
  193.3 4.6 %collective-permute-done.27.refs_3_ = bf16[256,512]{1,0:T(8,128)(2,1)S(1)} collective-permute-done((bf16[256,512]{1,0:T(8,128)(2,1)S(1)}, bf16[256,512]{1,0:T(8,128)(2,1)S(1)}, u32[]{:S(2)}, u32[]{:S(2)}) %collective-permute-start.27) | collective-permute-done | bytes 262176 | tf_op jit(solution)/shard_map/ppermute | solution.py:560
  197.9 2.9 %collective-permute-done.31.refs_8_ = bf16[256,512]{1,0:T(8,128)(2,1)S(1)} collective-permute-done((bf16[256,512]{1,0:T(8,128)(2,1)S(1)}, bf16[256,512]{1,0:T(8,128)(2,1)S(1)}, u32[]{:S(2)}, u32[]{:S(2)}) %collective-permute-start.31) | collective-permute-done | bytes 262176 | tf_op jit(solution)/shard_map/ppermute | solution.py:561
  200.9 3.3 %collective-permute-done.30.refs_7_ = bf16[256,512]{1,0:T(8,128)(2,1)S(1)} collective-permute-done((bf16[256,512]{1,0:T(8,128)(2,1)S(1)}, bf16[256,512]{1,0:T(8,128)(2,1)S(1)}, u32[]{:S(2)}, u32[]{:S(2)}) %collective-permute-start.30) | collective-permute-done | bytes 262176 | tf_op jit(solution)/shard_map/ppermute | solution.py:560
  204.2 2.3 %place.1 = bf16[512,1024]{1,0:T(8,128)(2,1)} custom-call(s32[1]{0:T(128)} %bitcast.seq_ref, s32[16]{0:T(128)} %order_ref.15, s32[1]{0:T(128)} %bitcast.1.ends_ref, bf16[256,512]{1,0:T(8,128)(2,1)S(1)} %fusion.13.refs_0_, bf16[256,512]{1,0:T(8,128)(2,1)S(1)} %fusion.19.refs_1_, bf16[256,512]{1,0:T(8,128)(2,1)S(1)} %get-tuple-element.69.refs_2_, ...), custom_call_target="tpu_custom_call" | custom-call | flops 1048576 | bytes 3670016 | tf_op jit(solution)/shard_map/place/pallas_call | solution.py:524
  (55 shorter events, 11.4 us)
Async XLA Ops:
  6.2 17.3 %collective-permute-start.1 = (bf16[256,512]{1,0:T(8,128)(2,1)S(1)}, bf16[256,512]{1,0:T(8,128)(2,1)S(1)}, u32[]{:S(2)}, u32[]{:S(2)}) collective-permute-start(bf16[256,512]{1,0:T(8,128)(2,1)S(1)} %get-tuple-element.44), channel_id=1, source_target_pairs={{0,16},{1,17},{2,18},{3,19},{4,20},{5,21},{6,22},{7,23},{8,24},{9,... | collective-permute-start | bytes 786440 | tf_op jit(solution)/shard_map/ppermute | solution.py:588
  11.1 18.0 %collective-permute-start.17 = (bf16[256,1024]{1,0:T(8,128)(2,1)}, bf16[256,1024]{1,0:T(8,128)(2,1)}, u32[]{:S(2)}, u32[]{:S(2)}) collective-permute-start(bf16[256,1024]{1,0:T(8,128)(2,1)} %get-tuple-element.60), channel_id=1, source_target_pairs={{0,16},{1,17},{2,18},{3,19},{4,20},{5,21},{6,22},{7,23},{8,24},{9,... | collective-permute-start | bytes 1572872 | tf_op jit(solution)/shard_map/ppermute | solution.py:590
  20.1 2.0 copy-start.3
  20.1 14.7 %collective-permute-start = (bf16[256,512]{1,0:T(8,128)(2,1)}, bf16[256,512]{1,0:T(8,128)(2,1)}, u32[]{:S(2)}, u32[]{:S(2)}) collective-permute-start(bf16[256,512]{1,0:T(8,128)(2,1)} %get-tuple-element.42), channel_id=1, source_target_pairs={{0,16},{1,17},{2,18},{3,19},{4,20},{5,21},{6,22},{7,23},{8,24},{9,... | collective-permute-start | bytes 786440 | tf_op jit(solution)/shard_map/ppermute | solution.py:588
  22.1 22.7 %collective-permute-start.15 = (bf16[256,1024]{1,0:T(8,128)(2,1)}, bf16[256,1024]{1,0:T(8,128)(2,1)S(1)}, u32[]{:S(2)}, u32[]{:S(2)}) collective-permute-start(bf16[256,1024]{1,0:T(8,128)(2,1)} %get-tuple-element.56), channel_id=1, source_target_pairs={{0,16},{1,17},{2,18},{3,19},{4,20},{5,21},{6,22},{7,23},{8,24},{9,... | collective-permute-start | bytes 1572872 | tf_op jit(solution)/shard_map/ppermute | solution.py:590
  23.5 27.1 %collective-permute-start.5 = (bf16[256,512]{1,0:T(8,128)(2,1)S(1)}, bf16[256,512]{1,0:T(8,128)(2,1)S(1)}, u32[]{:S(2)}, u32[]{:S(2)}) collective-permute-start(bf16[256,512]{1,0:T(8,128)(2,1)S(1)} %broadcast_select_fusion.2.refs_1_), channel_id=1, source_target_pairs={{4,0},{8,4},{12,8},{0,12},{5,1},{9,5},{13,9},{1,13},{6,2},{10,6},{... | collective-permute-start | bytes 786440 | tf_op jit(solution)/shard_map/ppermute | solution.py:546
  27.2 24.8 %collective-permute-start.3 = (bf16[256,512]{1,0:T(8,128)(2,1)S(1)}, bf16[256,512]{1,0:T(8,128)(2,1)S(1)}, u32[]{:S(2)}, u32[]{:S(2)}) collective-permute-start(bf16[256,512]{1,0:T(8,128)(2,1)S(1)} %broadcast_select_fusion.2.refs_1_), channel_id=1, source_target_pairs={{0,4},{4,8},{8,12},{12,0},{1,5},{5,9},{9,13},{13,1},{2,6},{6,10},{... | collective-permute-start | bytes 786440 | tf_op jit(solution)/shard_map/ppermute | solution.py:545
  33.5 21.1 %collective-permute-start.18 = (bf16[256,512]{1,0:T(8,128)(2,1)S(1)}, bf16[256,512]{1,0:T(8,128)(2,1)S(1)}, u32[]{:S(2)}, u32[]{:S(2)}) collective-permute-start(bf16[256,512]{1,0:T(8,128)(2,1)S(1)} %get-tuple-element.63), channel_id=1, source_target_pairs={{16,0},{17,1},{18,2},{19,3},{20,4},{21,5},{22,6},{23,7},{24,8},{25... | collective-permute-start | bytes 786440 | tf_op jit(solution)/shard_map/ppermute | solution.py:600
  35.8 25.2 %collective-permute-start.4 = (bf16[256,512]{1,0:T(8,128)(2,1)S(1)}, bf16[256,512]{1,0:T(8,128)(2,1)S(1)}, u32[]{:S(2)}, u32[]{:S(2)}) collective-permute-start(bf16[256,512]{1,0:T(8,128)(2,1)S(1)} %broadcast_select_fusion.3.refs_0_), channel_id=1, source_target_pairs={{4,0},{8,4},{12,8},{0,12},{5,1},{9,5},{13,9},{1,13},{6,2},{10,6},{... | collective-permute-start | bytes 786440 | tf_op jit(solution)/shard_map/ppermute | solution.py:546
  44.8 18.5 %collective-permute-start.2 = (bf16[256,512]{1,0:T(8,128)(2,1)S(1)}, bf16[256,512]{1,0:T(8,128)(2,1)S(1)}, u32[]{:S(2)}, u32[]{:S(2)}) collective-permute-start(bf16[256,512]{1,0:T(8,128)(2,1)S(1)} %broadcast_select_fusion.3.refs_0_), channel_id=1, source_target_pairs={{0,4},{4,8},{8,12},{12,0},{1,5},{5,9},{9,13},{13,1},{2,6},{6,10},{... | collective-permute-start | bytes 786440 | tf_op jit(solution)/shard_map/ppermute | solution.py:545
  50.6 8.8 %collective-permute-start.16 = (bf16[256,512]{1,0:T(8,128)(2,1)S(1)}, bf16[256,512]{1,0:T(8,128)(2,1)S(1)}, u32[]{:S(2)}, u32[]{:S(2)}) collective-permute-start(bf16[256,512]{1,0:T(8,128)(2,1)S(1)} %get-tuple-element.59), channel_id=1, source_target_pairs={{16,0},{17,1},{18,2},{19,3},{20,4},{21,5},{22,6},{23,7},{24,8},{25... | collective-permute-start | bytes 786440 | tf_op jit(solution)/shard_map/ppermute | solution.py:600
  52.0 35.4 %collective-permute-start.7 = (bf16[256,512]{1,0:T(8,128)(2,1)S(1)}, bf16[256,512]{1,0:T(8,128)(2,1)S(1)}, u32[]{:S(2)}, u32[]{:S(2)}) collective-permute-start(bf16[256,512]{1,0:T(8,128)(2,1)S(1)} %select_select_fusion.2), channel_id=1, source_target_pairs={{4,0},{12,4},{8,12},{0,8},{5,1},{13,5},{9,13},{1,9},{6,2},{14,6},{... | collective-permute-start | bytes 786440 | tf_op jit(solution)/shard_map/ppermute | solution.py:548
  54.7 34.8 %copy-start.4 = (f32[2048]{0:T(1024)S(1)}, f32[2048]{0:T(1024)}, u32[]{:S(2)}) copy-start(f32[2048]{0:T(1024)} %param.9) | copy-start | bytes 24580
  54.7 15.8 %collective-permute-start.22 = (bf16[256,512]{1,0:T(8,128)(2,1)S(1)}, bf16[256,512]{1,0:T(8,128)(2,1)S(1)}, u32[]{:S(2)}, u32[]{:S(2)}) collective-permute-start(bf16[256,512]{1,0:T(8,128)(2,1)S(1)} %broadcast_select_fusion.refs_1_), channel_id=1, source_target_pairs={{4,0},{8,4},{12,8},{0,12},{5,1},{9,5},{13,9},{1,13},{6,2},{10,6},{... | collective-permute-start | bytes 786440 | tf_op jit(solution)/shard_map/ppermute | solution.py:546
  59.4 15.0 %collective-permute-start.20 = (bf16[256,512]{1,0:T(8,128)(2,1)S(1)}, bf16[256,512]{1,0:T(8,128)(2,1)S(1)}, u32[]{:S(2)}, u32[]{:S(2)}) collective-permute-start(bf16[256,512]{1,0:T(8,128)(2,1)S(1)} %broadcast_select_fusion.refs_1_), channel_id=1, source_target_pairs={{0,4},{4,8},{8,12},{12,0},{1,5},{5,9},{9,13},{13,1},{2,6},{6,10},{... | collective-permute-start | bytes 786440 | tf_op jit(solution)/shard_map/ppermute | solution.py:545
  61.1 20.6 %collective-permute-start.21 = (bf16[256,512]{1,0:T(8,128)(2,1)S(1)}, bf16[256,512]{1,0:T(8,128)(2,1)S(1)}, u32[]{:S(2)}, u32[]{:S(2)}) collective-permute-start(bf16[256,512]{1,0:T(8,128)(2,1)S(1)} %broadcast_select_fusion.1.refs_0_), channel_id=1, source_target_pairs={{4,0},{8,4},{12,8},{0,12},{5,1},{9,5},{13,9},{1,13},{6,2},{10,6},{... | collective-permute-start | bytes 786440 | tf_op jit(solution)/shard_map/ppermute | solution.py:546
  63.4 22.3 %collective-permute-start.19 = (bf16[256,512]{1,0:T(8,128)(2,1)S(1)}, bf16[256,512]{1,0:T(8,128)(2,1)S(1)}, u32[]{:S(2)}, u32[]{:S(2)}) collective-permute-start(bf16[256,512]{1,0:T(8,128)(2,1)S(1)} %broadcast_select_fusion.1.refs_0_), channel_id=1, source_target_pairs={{0,4},{4,8},{8,12},{12,0},{1,5},{5,9},{9,13},{13,1},{2,6},{6,10},{... | collective-permute-start | bytes 786440 | tf_op jit(solution)/shard_map/ppermute | solution.py:545
  70.5 19.0 %collective-permute-start.6 = (bf16[256,512]{1,0:T(8,128)(2,1)S(1)}, bf16[256,512]{1,0:T(8,128)(2,1)S(1)}, u32[]{:S(2)}, u32[]{:S(2)}) collective-permute-start(bf16[256,512]{1,0:T(8,128)(2,1)S(1)} %select_select_fusion.3), channel_id=1, source_target_pairs={{4,0},{12,4},{8,12},{0,8},{5,1},{13,5},{9,13},{1,9},{6,2},{14,6},{... | collective-permute-start | bytes 786440 | tf_op jit(solution)/shard_map/ppermute | solution.py:548
  74.4 24.1 %collective-permute-start.24 = (bf16[256,512]{1,0:T(8,128)(2,1)S(1)}, bf16[256,512]{1,0:T(8,128)(2,1)S(1)}, u32[]{:S(2)}, u32[]{:S(2)}) collective-permute-start(bf16[256,512]{1,0:T(8,128)(2,1)S(1)} %select_select_fusion), channel_id=1, source_target_pairs={{4,0},{12,4},{8,12},{0,8},{5,1},{13,5},{9,13},{1,9},{6,2},{14,6},{... | collective-permute-start | bytes 786440 | tf_op jit(solution)/shard_map/ppermute | solution.py:548
  85.7 13.1 %collective-permute-start.23 = (bf16[256,512]{1,0:T(8,128)(2,1)S(1)}, bf16[256,512]{1,0:T(8,128)(2,1)S(1)}, u32[]{:S(2)}, u32[]{:S(2)}) collective-permute-start(bf16[256,512]{1,0:T(8,128)(2,1)S(1)} %select_select_fusion.1), channel_id=1, source_target_pairs={{4,0},{12,4},{8,12},{0,8},{5,1},{13,5},{9,13},{1,9},{6,2},{14,6},{... | collective-permute-start | bytes 786440 | tf_op jit(solution)/shard_map/ppermute | solution.py:548
  95.9 26.9 %collective-permute-start.8 = (bf16[1024,512]{1,0:T(8,128)(2,1)}, bf16[1024,512]{1,0:T(8,128)(2,1)S(1)}, u32[]{:S(2)}, u32[]{:S(2)}) collective-permute-start(bf16[1024,512]{1,0:T(8,128)(2,1)} %get-tuple-element.47.refs_0_), channel_id=1, source_target_pairs={{0,16},{16,0},{1,17},{17,1},{2,18},{18,2},{3,19},{19,3},{4,20},{20... | collective-permute-start | bytes 3145736 | tf_op jit(solution)/shard_map/ppermute | solution.py:605
  104.9 1.3 copy-start
  106.2 36.1 %collective-permute-start.25 = (bf16[1024,512]{1,0:T(8,128)(2,1)}, bf16[1024,512]{1,0:T(8,128)(2,1)}, u32[]{:S(2)}, u32[]{:S(2)}) collective-permute-start(bf16[1024,512]{1,0:T(8,128)(2,1)} %get-tuple-element.66.refs_2_), channel_id=1, source_target_pairs={{0,16},{16,0},{1,17},{17,1},{2,18},{18,2},{3,19},{19,3},{4,20},{20... | collective-permute-start | bytes 3145736 | tf_op jit(solution)/shard_map/ppermute | solution.py:611
  108.6 1.6 copy-start.2
  114.4 17.5 %copy-start.1 = (bf16[2048,512]{1,0:T(8,128)(2,1)S(1)}, bf16[2048,512]{1,0:T(8,128)(2,1)}, u32[]{:S(2)}) copy-start(bf16[2048,512]{1,0:T(8,128)(2,1)} %copy-done) | copy-start | bytes 6291460
  129.6 21.5 %collective-permute-start.9 = (bf16[256,512]{1,0:T(8,128)(2,1)S(1)}, bf16[256,512]{1,0:T(8,128)(2,1)S(1)}, u32[]{:S(2)}, u32[]{:S(2)}) collective-permute-start(bf16[256,512]{1,0:T(8,128)(2,1)S(1)} %get-tuple-element.50), channel_id=1, source_target_pairs={{0,4},{4,12},{12,8},{8,0},{1,5},{5,13},{13,9},{9,1},{2,6},{6,14},{... | collective-permute-start | bytes 786440 | tf_op jit(solution)/shard_map/ppermute | solution.py:559
  134.6 18.9 %collective-permute-start.12 = (bf16[256,512]{1,0:T(8,128)(2,1)S(1)}, bf16[256,512]{1,0:T(8,128)(2,1)S(1)}, u32[]{:S(2)}, u32[]{:S(2)}) collective-permute-start(bf16[256,512]{1,0:T(8,128)(2,1)S(1)} %get-tuple-element.54), channel_id=1, source_target_pairs={{0,4},{4,12},{12,8},{8,0},{1,5},{5,13},{13,9},{9,1},{2,6},{6,14},{... | collective-permute-start | bytes 786440 | tf_op jit(solution)/shard_map/ppermute | solution.py:559
  148.0 12.9 %collective-permute-start.26 = (bf16[256,512]{1,0:T(8,128)(2,1)S(1)}, bf16[256,512]{1,0:T(8,128)(2,1)S(1)}, u32[]{:S(2)}, u32[]{:S(2)}) collective-permute-start(bf16[256,512]{1,0:T(8,128)(2,1)S(1)} %get-tuple-element.71), channel_id=1, source_target_pairs={{0,4},{4,12},{12,8},{8,0},{1,5},{5,13},{13,9},{9,1},{2,6},{6,14},{... | collective-permute-start | bytes 786440 | tf_op jit(solution)/shard_map/ppermute | solution.py:559
  151.2 29.5 %collective-permute-start.10 = (bf16[256,512]{1,0:T(8,128)(2,1)S(1)}, bf16[256,512]{1,0:T(8,128)(2,1)S(1)}, u32[]{:S(2)}, u32[]{:S(2)}) collective-permute-start(bf16[256,512]{1,0:T(8,128)(2,1)S(1)} %get-tuple-element.83), channel_id=1, source_target_pairs={{4,0},{8,4},{12,8},{0,12},{5,1},{9,5},{13,9},{1,13},{6,2},{10,6},{... | collective-permute-start | bytes 786440 | tf_op jit(solution)/shard_map/ppermute | solution.py:560
  152.8 31.8 %collective-permute-start.11 = (bf16[256,512]{1,0:T(8,128)(2,1)S(1)}, bf16[256,512]{1,0:T(8,128)(2,1)S(1)}, u32[]{:S(2)}, u32[]{:S(2)}) collective-permute-start(bf16[256,512]{1,0:T(8,128)(2,1)S(1)} %get-tuple-element.84), channel_id=1, source_target_pairs={{0,4},{4,8},{8,12},{12,0},{1,5},{5,9},{9,13},{13,1},{2,6},{6,10},{... | collective-permute-start | bytes 786440 | tf_op jit(solution)/shard_map/ppermute | solution.py:561
  153.5 27.0 %collective-permute-start.29 = (bf16[256,512]{1,0:T(8,128)(2,1)S(1)}, bf16[256,512]{1,0:T(8,128)(2,1)S(1)}, u32[]{:S(2)}, u32[]{:S(2)}) collective-permute-start(bf16[256,512]{1,0:T(8,128)(2,1)S(1)} %get-tuple-element.75), channel_id=1, source_target_pairs={{0,4},{4,12},{12,8},{8,0},{1,5},{5,13},{13,9},{9,1},{2,6},{6,14},{... | collective-permute-start | bytes 786440 | tf_op jit(solution)/shard_map/ppermute | solution.py:559
  153.7 32.0 %collective-permute-start.13 = (bf16[256,512]{1,0:T(8,128)(2,1)S(1)}, bf16[256,512]{1,0:T(8,128)(2,1)S(1)}, u32[]{:S(2)}, u32[]{:S(2)}) collective-permute-start(bf16[256,512]{1,0:T(8,128)(2,1)S(1)} %get-tuple-element.81), channel_id=1, source_target_pairs={{4,0},{8,4},{12,8},{0,12},{5,1},{9,5},{13,9},{1,13},{6,2},{10,6},{... | collective-permute-start | bytes 786440 | tf_op jit(solution)/shard_map/ppermute | solution.py:560
  160.9 27.7 %collective-permute-start.14 = (bf16[256,512]{1,0:T(8,128)(2,1)S(1)}, bf16[256,512]{1,0:T(8,128)(2,1)S(1)}, u32[]{:S(2)}, u32[]{:S(2)}) collective-permute-start(bf16[256,512]{1,0:T(8,128)(2,1)S(1)} %get-tuple-element.82), channel_id=1, source_target_pairs={{0,4},{4,8},{8,12},{12,0},{1,5},{5,9},{9,13},{13,1},{2,6},{6,10},{... | collective-permute-start | bytes 786440 | tf_op jit(solution)/shard_map/ppermute | solution.py:561
  180.6 12.8 %collective-permute-start.28 = (bf16[256,512]{1,0:T(8,128)(2,1)S(1)}, bf16[256,512]{1,0:T(8,128)(2,1)S(1)}, u32[]{:S(2)}, u32[]{:S(2)}) collective-permute-start(bf16[256,512]{1,0:T(8,128)(2,1)S(1)} %get-tuple-element.79), channel_id=1, source_target_pairs={{0,4},{4,8},{8,12},{12,0},{1,5},{5,9},{9,13},{13,1},{2,6},{6,10},{... | collective-permute-start | bytes 786440 | tf_op jit(solution)/shard_map/ppermute | solution.py:561
  180.7 17.2 %collective-permute-start.27 = (bf16[256,512]{1,0:T(8,128)(2,1)S(1)}, bf16[256,512]{1,0:T(8,128)(2,1)S(1)}, u32[]{:S(2)}, u32[]{:S(2)}) collective-permute-start(bf16[256,512]{1,0:T(8,128)(2,1)S(1)} %get-tuple-element.80), channel_id=1, source_target_pairs={{4,0},{8,4},{12,8},{0,12},{5,1},{9,5},{13,9},{1,13},{6,2},{10,6},{... | collective-permute-start | bytes 786440 | tf_op jit(solution)/shard_map/ppermute | solution.py:560
  184.6 16.3 %collective-permute-start.31 = (bf16[256,512]{1,0:T(8,128)(2,1)S(1)}, bf16[256,512]{1,0:T(8,128)(2,1)S(1)}, u32[]{:S(2)}, u32[]{:S(2)}) collective-permute-start(bf16[256,512]{1,0:T(8,128)(2,1)S(1)} %get-tuple-element.77), channel_id=1, source_target_pairs={{0,4},{4,8},{8,12},{12,0},{1,5},{5,9},{9,13},{13,1},{2,6},{6,10},{... | collective-permute-start | bytes 786440 | tf_op jit(solution)/shard_map/ppermute | solution.py:561
  185.7 18.5 %collective-permute-start.30 = (bf16[256,512]{1,0:T(8,128)(2,1)S(1)}, bf16[256,512]{1,0:T(8,128)(2,1)S(1)}, u32[]{:S(2)}, u32[]{:S(2)}) collective-permute-start(bf16[256,512]{1,0:T(8,128)(2,1)S(1)} %get-tuple-element.78), channel_id=1, source_target_pairs={{4,0},{8,4},{12,8},{0,12},{5,1},{9,5},{13,9},{1,13},{6,2},{10,6},{... | collective-permute-start | bytes 786440 | tf_op jit(solution)/shard_map/ppermute | solution.py:560
